TPU v7x, 128 devices: a whole 4x4x4 slice. The times are simulated.
128 devices in a mesh: row: 16 (over x, y_hi, core), col: 8 (over z, y_lo).
Axes of the slice: x: 4, y: 4 (y_hi: 2, y_lo: 2; y = y_hi * 2 + y_lo), z: 4, core: 2. Of those that a mesh axis runs over, the one named last changes fastest.
Arguments:
- counts: int32 [16384, 16384], P('row', 'col'), may hold values from 0 to 33, as said below
- row_emb: float32 [256, 16384], P('col', 'row'), may hold values from -2 to 2
- col_emb: float32 [256, 16384], P('row', 'col'), may hold values from -2 to 2
- row_accum: float32 [256, 16384], P('col', 'row'), may hold values from 100 to 10000
- col_accum: float32 [256, 16384], P('row', 'col'), may hold values from 100 to 10000
Outputs:
- new_row_emb: float32 [256, 16384], P('col', 'row')
- new_col_emb: float32 [256, 16384], P('row', 'col')
Inputs may be any that keep to these rules, and one draw needn't show every extreme that they name: `counts`: every row word and every column word has a positive count with some partner.
All inputs are finite; a program needn't handle non-finite values.
Results may differ from a plain program's by a relative error of at most 0.0015.
Values may be sent and summed in bfloat16 or wider, within the bound.
No kernel may reach another device: no remote copies, remote signals or barrier semaphores. Data moves between devices by JAX's collectives and lax.ppermute only.
A program may use at most 64 MiB of HBM per device.

v0:
```python
import jax
import jax.numpy as jnp
from jax import lax
from jax.sharding import PartitionSpec as P

SWEEPS = 2


def copy_for_each(value, axis):
    length = lax.axis_size(axis)
    return lax.all_to_all(
        jnp.broadcast_to(value[None], (length, *value.shape)), axis, 0, 0, tiled=True
    )


def in_order(tiles, dim):
    tiles = jnp.moveaxis(tiles, 0, dim)
    lengths = tiles.shape
    return tiles.reshape(*lengths[:dim], lengths[dim] * lengths[dim + 1], *lengths[dim + 2 :])


def gathered_copies(value, axis, dim):
    tiles = copy_for_each(value, axis)
    return in_order(tiles, dim)


def split_up(value, dim, length):
    before, after = (value.shape[:dim], value.shape[dim + 1 :])
    return jnp.moveaxis(value.reshape(*before, length, -1, *after), dim, 0)


def sent_and_summed(value, axis, dim):
    tiles = split_up(value, dim, lax.axis_size(axis))
    arrived = lax.all_to_all(tiles, axis, split_axis=0, concat_axis=0, tiled=True)
    return arrived.astype(jnp.float32).sum(axis=0)


def over_copies(value, axis):
    everything = copy_for_each(value, axis)
    return jnp.sum(everything, axis=0)


def sweep_once(row_emb, col_emb, row_accum, col_accum, positive, target, weight):
    row_half = row_emb.astype(jnp.bfloat16)
    col_half = col_emb.astype(jnp.bfloat16)
    row_block = gathered_copies(row_half, "col", 0)
    col_block = lax.all_gather(col_half, "row", axis=0, tiled=True)
    scores = lax.dot_general(
        row_block, col_block, (((0,), (0,)), ((), ())), preferred_element_type=jnp.float32
    )
    errors = scores - target
    grads = jnp.where(positive, weight * errors, jax.nn.sigmoid(errors)).astype(jnp.bfloat16)
    piece = col_block
    row_grad = sent_and_summed(
        lax.dot_general(
            piece, grads, (((1,), (1,)), ((), ())), preferred_element_type=jnp.float32
        ).astype(jnp.bfloat16),
        "col",
        0,
    )
    piece = row_block
    col_grad = sent_and_summed(
        jnp.dot(piece, grads, preferred_element_type=jnp.float32).astype(jnp.bfloat16), "row", 0
    )
    row_accum = row_accum + row_grad * row_grad
    row_emb = row_emb - 0.05 * row_grad / jnp.sqrt(row_accum)
    col_accum = col_accum + col_grad * col_grad
    col_emb = col_emb - 0.05 * col_grad / jnp.sqrt(col_accum)
    return (row_emb, col_emb, row_accum, col_accum)


def on_device(counts, row_emb, col_emb, row_accum, col_accum):
    values = counts.astype(jnp.float32)
    local_rows = jnp.sum(values, axis=1)
    local_cols = jnp.sum(values, axis=0)
    row_marg = over_copies(local_rows, "col")
    col_marg = over_copies(local_cols, "row")
    total = over_copies(jnp.sum(row_marg), "row")
    target = (
        jnp.log(jnp.maximum(values, 1.0))
        + jnp.log(total)
        - jnp.log(row_marg)[:, None]
        - jnp.log(col_marg)[None, :]
    )
    weight = 0.1 + 0.25 * jnp.sqrt(values)
    positive = counts > 0
    for sweep in range(SWEEPS):
        row_emb, col_emb, row_accum, col_accum = sweep_once(
            row_emb, col_emb, row_accum, col_accum, positive, target, weight
        )
    return (row_emb, col_emb)


def solution(mesh):
    in_specs = (P("row", "col"), P("col", "row"), P("row", "col"), P("col", "row"), P("row", "col"))
    out_specs = (P("col", "row"), P("row", "col"))
    return jax.shard_map(
        on_device, mesh=mesh, in_specs=in_specs, out_specs=out_specs, check_vma=False
    )
```

profile of v0, /device:TPU:0, one launch (start us, length us, event | category | flops | bytes accessed | tf_op | source)
XLA Modules:
  0.0 206.2 jit_solution(5882931983976948135)
XLA Ops:
  7.2 0.0 copy-start
  7.2 0.0 all-gather.3.cloned.1.call-start
  7.2 1.6 convert_element_type.53
  8.8 0.0 all-gather.3.cloned.1.call-update
  8.8 4.6 %convert_reduce_fusion.1 = (f32[1024]{0:T(1024)S(1)}, f32[2048]{0:T(1024)S(1)}) fusion(s32[1024,2048]{1,0:T(8,128)} %param.5), kind=kLoop, calls=%fused_computation.5 | loop fusion | flops 6288384 | bytes 8400896 | tf_op jit(solution)/shard_map/reduce_sum | solution.py:74
  13.5 12.5 %all_to_all.48 = f32[8,1,1024]{2,1,0:T(1,128)S(1)} all-to-all(f32[8,1,1024]{2,1,0:T(1,128)S(1)} %broadcast_in_dim.11), channel_id=1, replica_groups=mesh['row'=16,'col'=8] {'col'}, dimensions={0} | all-to-all | bytes 65536 | tf_op jit(solution)/shard_map/all_to_all | solution.py:11
  26.0 0.7 fusion.2
  26.6 0.6 broadcast_in_dim.12
  27.3 14.1 %all_to_all.49 = f32[16,1,1]{2,1,0:T(1,128)S(1)} all-to-all(f32[16,1,1]{2,1,0:T(1,128)S(1)} %broadcast_in_dim.12), channel_id=1, replica_groups=mesh['row'=16,'col'=8] {'row'}, dimensions={0} | all-to-all | bytes 128 | tf_op jit(solution)/shard_map/all_to_all | solution.py:11
  41.4 0.7 broadcast_in_dim.13
  42.2 3.5 %all-to-all-start.3 = ((f32[16,1,2048]{2,1,0:T(1,128)}), f32[16,1,2048]{2,1,0:T(1,128)S(1)}, u32[]{:S(2)}, u32[]{:S(2)}) async-start(f32[16,1,2048]{2,1,0:T(1,128)} %broadcast_in_dim.13), calls=%async_computation.3 | async-start | bytes 262144 | tf_op jit(solution)/shard_map/all_to_all | solution.py:11
  45.7 0.0 copy-done
  45.7 8.3 %all-to-all-done.3 = f32[16,1,2048]{2,1,0:T(1,128)S(1)} async-done(((f32[16,1,2048]{2,1,0:T(1,128)}), f32[16,1,2048]{2,1,0:T(1,128)S(1)}, u32[]{:S(2)}, u32[]{:S(2)}) %all-to-all-start.3) | async-done | bytes 131104 | tf_op jit(solution)/shard_map/all_to_all | solution.py:11
  54.0 0.8 broadcast_in_dim.10
  54.9 3.5 %all-to-all-start = ((bf16[8,32,1024]{2,1,0:T(8,128)(2,1)}), bf16[8,32,1024]{2,1,0:T(8,128)(2,1)S(1)}, u32[]{:S(2)}, u32[]{:S(2)}) async-start(bf16[8,32,1024]{2,1,0:T(8,128)(2,1)} %broadcast_in_dim.10), calls=%async_computation | async-start | bytes 1048576 | tf_op jit(solution)/shard_map/all_to_all | solution.py:11
  58.4 0.0 all-gather.5.cloned.1.call-start
  58.4 0.6 reduce_sum.92
  59.7 0.1 reduce_sum.95
  59.8 9.2 %all-to-all-done = bf16[8,32,1024]{2,1,0:T(8,128)(2,1)S(1)} async-done(((bf16[8,32,1024]{2,1,0:T(8,128)(2,1)}), bf16[8,32,1024]{2,1,0:T(8,128)(2,1)S(1)}, u32[]{:S(2)}, u32[]{:S(2)}) %all-to-all-start) | async-done | bytes 524320 | tf_op jit(solution)/shard_map/all_to_all | solution.py:11
  69.0 12.8 %select_convert_fusion.1 = bf16[1024,2048]{1,0:T(8,128)(2,1)S(1)} fusion(s32[1024,2048]{1,0:T(8,128)} %param.5, bf16[256,1024]{1,0:T(8,128)(2,1)S(1)} %bitcast.23, bf16[256,2048]{1,0:T(8,128)(2,1)} %all-gather.3.cloned.1.call-done, f32[2048]{0:T(1024)S(1)} %log.23, f32[1024]{0:T(1024)S(1)} %log.22, f32[]{:T(128)S(6)} %log.21), kind=kOutput, calls=%fused_computation.1 | convolution fusion | flops 1105199104 | bytes 14168068 | tf_op jit(solution)/shard_map/dot_general | solution.py:48
  81.9 0.0 copy-start.6
  81.9 0.0 copy-start.1
  81.9 0.0 copy-start.3
  81.9 0.0 copy-start.4
  81.9 0.0 copy-start.2
  81.9 1.3 convolution_convert_fusion
  83.2 20.9 %all_to_all.50 = bf16[16,16,2048]{2,1,0:T(8,128)(2,1)S(1)} all-to-all(bf16[16,16,2048]{2,1,0:T(8,128)(2,1)S(1)} %bitcast.22), channel_id=1, replica_groups=mesh['row'=16,'col'=8] {'row'}, dimensions={0} | all-to-all | bytes 2097152 | tf_op jit(solution)/shard_map/all_to_all | solution.py:34
  104.1 0.1 convert_reduce_fusion.3
  104.3 0.7 fusion.1
  105.0 0.0 all-gather.5.cloned.1.call-update
  105.0 0.0 copy-done.4
  105.0 3.5 %convolution_convert_fusion.3 = bf16[1024,256]{0,1:T(8,128)(2,1)S(1)} fusion(bf16[1024,2048]{1,0:T(8,128)(2,1)} %copy-done.6, bf16[256,2048]{1,0:T(8,128)(2,1)S(1)} %copy-done.4), kind=kOutput, calls=%fused_computation.12 | convolution fusion | flops 1074003968 | bytes 5767168 | tf_op jit(solution)/shard_map/dot_general | solution.py:55
  108.5 12.8 %all_to_all.51 = bf16[8,32,1024]{2,1,0:T(8,128)(2,1)S(1)} all-to-all(bf16[8,32,1024]{2,1,0:T(8,128)(2,1)S(1)} %bitcast.27), channel_id=1, replica_groups=mesh['row'=16,'col'=8] {'col'}, dimensions={0} | all-to-all | bytes 1048576 | tf_op jit(solution)/shard_map/all_to_all | solution.py:34
  121.2 0.1 convert_reduce_fusion.5
  121.3 0.1 broadcast_in_dim.14
  121.4 11.7 %all_to_all.52 = bf16[8,32,1024]{2,1,0:T(8,128)(2,1)S(1)} all-to-all(bf16[8,32,1024]{2,1,0:T(8,128)(2,1)S(1)} %broadcast_in_dim.14), channel_id=1, replica_groups=mesh['row'=16,'col'=8] {'col'}, dimensions={0} | all-to-all | bytes 1048576 | tf_op jit(solution)/shard_map/all_to_all | solution.py:11
  133.1 12.0 %all-gather.5.cloned.1.call-done = bf16[256,2048]{1,0:T(8,128)(2,1)} async-done(((bf16[16,2048]{1,0:T(8,128)(2,1)}), bf16[256,2048]{1,0:T(8,128)(2,1)}) %all-gather.5.cloned.1.call-update) | async-done | bytes 1048592 | tf_op jit(solution)/shard_map/all_gather | solution.py:47
  145.0 13.2 %select_convert_fusion = bf16[1024,2048]{1,0:T(8,128)(2,1)S(1)} fusion(s32[1024,2048]{1,0:T(8,128)} %param.5, bf16[256,1024]{1,0:T(8,128)(2,1)S(1)} %bitcast.25, bf16[256,2048]{1,0:T(8,128)(2,1)} %all-gather.5.cloned.1.call-done, f32[2048]{0:T(1024)S(1)} %log.23, f32[1024]{0:T(1024)S(1)} %log.22, f32[]{:T(128)S(6)} %log.21), kind=kOutput, calls=%fused_computation | convolution fusion | flops 1105199104 | bytes 14168068 | tf_op jit(solution)/shard_map/dot_general | solution.py:48
  158.3 2.1 %convolution_convert_fusion.2 = bf16[256,1024]{1,0:T(8,128)(2,1)} fusion(bf16[256,2048]{1,0:T(8,128)(2,1)S(1)} %copy-done.5, bf16[1024,2048]{1,0:T(8,128)(2,1)S(1)} %select_convert_fusion), kind=kOutput, calls=%fused_computation.11 | convolution fusion | flops 1074003968 | bytes 5767168 | tf_op jit(solution)/shard_map/dot_general | solution.py:55
  160.3 4.4 %all-to-all-start.7 = ((bf16[8,32,1024]{2,1,0:T(8,128)(2,1)}), bf16[8,32,1024]{2,1,0:T(8,128)(2,1)S(1)}, u32[]{:S(2)}, u32[]{:S(2)}) async-start(bf16[8,32,1024]{2,1,0:T(8,128)(2,1)} %bitcast.6), calls=%async_computation.7 | async-start | bytes 1048576 | tf_op jit(solution)/shard_map/all_to_all | solution.py:34
  164.8 4.4 %convolution_convert_fusion.1 = bf16[256,2048]{1,0:T(8,128)(2,1)} fusion(bf16[256,1024]{1,0:T(8,128)(2,1)S(1)} %bitcast.26, bf16[1024,2048]{1,0:T(8,128)(2,1)} %copy-done.7), kind=kOutput, calls=%fused_computation.8 | convolution fusion | flops 1074266112 | bytes 5767168 | tf_op jit(solution)/shard_map/dot_general | solution.py:63
  169.2 6.1 %all-to-all-done.7 = bf16[8,32,1024]{2,1,0:T(8,128)(2,1)S(1)} async-done(((bf16[8,32,1024]{2,1,0:T(8,128)(2,1)}), bf16[8,32,1024]{2,1,0:T(8,128)(2,1)S(1)}, u32[]{:S(2)}, u32[]{:S(2)}) %all-to-all-start.7) | async-done | bytes 524320 | tf_op jit(solution)/shard_map/all_to_all | solution.py:34
  175.3 5.2 %all-to-all-start.8 = ((bf16[16,16,2048]{2,1,0:T(8,128)(2,1)}), bf16[16,16,2048]{2,1,0:T(8,128)(2,1)S(1)}, u32[]{:S(2)}, u32[]{:S(2)}) async-start(bf16[16,16,2048]{2,1,0:T(8,128)(2,1)} %bitcast.7), calls=%async_computation.8 | async-start | bytes 2097152 | tf_op jit(solution)/shard_map/all_to_all | solution.py:34
  180.5 0.1 convert_reduce_fusion.4
  180.6 0.7 multiply_subtract_fusion.1
  181.3 17.1 %all-to-all-done.8 = bf16[16,16,2048]{2,1,0:T(8,128)(2,1)S(1)} async-done(((bf16[16,16,2048]{2,1,0:T(8,128)(2,1)}), bf16[16,16,2048]{2,1,0:T(8,128)(2,1)S(1)}, u32[]{:S(2)}, u32[]{:S(2)}) %all-to-all-start.8) | async-done | bytes 1048608 | tf_op jit(solution)/shard_map/all_to_all | solution.py:34
  198.4 0.1 convert_reduce_fusion.2
  198.6 0.7 multiply_subtract_fusion
  (14 shorter events, 0.1 us)
Async XLA Ops:
  7.2 38.5 %copy-start = (f32[32,1024]{1,0:T(8,128)S(1)}, f32[32,1024]{1,0:T(8,128)}, u32[]{:S(2)}) copy-start(f32[32,1024]{1,0:T(8,128)} %param.6) | copy-start | bytes 393220
  7.2 61.8 %all-gather.3.cloned.1.call-start = ((), (), s32[]{:S(2)}) async-start(), calls=%async_computation.9 | async-start | bytes 1114112 | tf_op jit(solution)/shard_map/all_gather | solution.py:47
  42.2 11.9 %all-to-all-start.3 = ((f32[16,1,2048]{2,1,0:T(1,128)}), f32[16,1,2048]{2,1,0:T(1,128)S(1)}, u32[]{:S(2)}, u32[]{:S(2)}) async-start(f32[16,1,2048]{2,1,0:T(1,128)} %broadcast_in_dim.13), calls=%async_computation.3 | async-start | bytes 262144 | tf_op jit(solution)/shard_map/all_to_all | solution.py:11
  54.9 14.2 %all-to-all-start = ((bf16[8,32,1024]{2,1,0:T(8,128)(2,1)}), bf16[8,32,1024]{2,1,0:T(8,128)(2,1)S(1)}, u32[]{:S(2)}, u32[]{:S(2)}) async-start(bf16[8,32,1024]{2,1,0:T(8,128)(2,1)} %broadcast_in_dim.10), calls=%async_computation | async-start | bytes 1048576 | tf_op jit(solution)/shard_map/all_to_all | solution.py:11
  58.4 86.7 %all-gather.5.cloned.1.call-start = ((), (), s32[]{:S(2)}) async-start(), calls=%async_computation.10 | async-start | bytes 1114112 | tf_op jit(solution)/shard_map/all_gather | solution.py:47
  81.9 22.4 %copy-start.6 = (bf16[1024,2048]{1,0:T(8,128)(2,1)}, bf16[1024,2048]{1,0:T(8,128)(2,1)S(1)}, u32[]{:S(2)}) copy-start(bf16[1024,2048]{1,0:T(8,128)(2,1)S(1)} %select_convert_fusion.1) | copy-start | bytes 12582916
  81.9 22.4 %copy-start.1 = (f32[16,2048]{1,0:T(8,128)S(1)}, f32[16,2048]{1,0:T(8,128)}, u32[]{:S(2)}) copy-start(f32[16,2048]{1,0:T(8,128)} %param.7) | copy-start | bytes 393220
  81.9 22.4 %copy-start.3 = (f32[16,2048]{1,0:T(8,128)S(1)}, f32[16,2048]{1,0:T(8,128)}, u32[]{:S(2)}) copy-start(f32[16,2048]{1,0:T(8,128)} %param.9) | copy-start | bytes 393220
  81.9 23.1 %copy-start.4 = (bf16[256,2048]{1,0:T(8,128)(2,1)S(1)}, bf16[256,2048]{1,0:T(8,128)(2,1)}, u32[]{:S(2)}) copy-start(bf16[256,2048]{1,0:T(8,128)(2,1)} %all-gather.3.cloned.1.call-done) | copy-start | bytes 3145732
  81.9 39.4 %copy-start.2 = (f32[32,1024]{1,0:T(8,128)S(1)}, f32[32,1024]{1,0:T(8,128)}, u32[]{:S(2)}) copy-start(f32[32,1024]{1,0:T(8,128)} %param.8) | copy-start | bytes 393220
  145.0 13.2 %copy-start.5 = (bf16[256,2048]{1,0:T(8,128)(2,1)S(1)}, bf16[256,2048]{1,0:T(8,128)(2,1)}, u32[]{:S(2)}) copy-start(bf16[256,2048]{1,0:T(8,128)(2,1)} %all-gather.5.cloned.1.call-done) | copy-start | bytes 3145732
  158.2 2.1 %copy-start.7 = (bf16[1024,2048]{1,0:T(8,128)(2,1)}, bf16[1024,2048]{1,0:T(8,128)(2,1)S(1)}, u32[]{:S(2)}) copy-start(bf16[1024,2048]{1,0:T(8,128)(2,1)S(1)} %select_convert_fusion) | copy-start | bytes 12582916
  160.3 14.9 %all-to-all-start.7 = ((bf16[8,32,1024]{2,1,0:T(8,128)(2,1)}), bf16[8,32,1024]{2,1,0:T(8,128)(2,1)S(1)}, u32[]{:S(2)}, u32[]{:S(2)}) async-start(bf16[8,32,1024]{2,1,0:T(8,128)(2,1)} %bitcast.6), calls=%async_computation.7 | async-start | bytes 1048576 | tf_op jit(solution)/shard_map/all_to_all | solution.py:34
  175.3 23.2 %all-to-all-start.8 = ((bf16[16,16,2048]{2,1,0:T(8,128)(2,1)}), bf16[16,16,2048]{2,1,0:T(8,128)(2,1)S(1)}, u32[]{:S(2)}, u32[]{:S(2)}) async-start(bf16[16,16,2048]{2,1,0:T(8,128)(2,1)} %bitcast.7), calls=%async_computation.8 | async-start | bytes 2097152 | tf_op jit(solution)/shard_map/all_to_all | solution.py:34
Sparse Core Ops, SparseCore 0:
  10.9 47.2 all-gather.2
  105.1 39.8 all-gather.4
where the time goes:
time: 207 us; the launch traced here: 206 us
  blocking collectives  71.9 us (35%)
  waiting for transfers between devices  52.7 us (25%)
  matrix products  37.3 us (18%)
  starting transfers between devices  16.7 us (8%)
  between operations  15 us (7%)
  other arithmetic  10.2 us (5%)
  local copies, waits for them, and re-layouts  2.34 us (1%)
    all_to_all x3, blocking collectives, copy_for_each(): lax.all_to_all(jnp.broadcast_to(value[None], (length, *value.shape)), axi...  38.3 us
    all_to_all x2, blocking collectives, sent_and_summed(): lax.all_to_all(tiles, axis, split_axis=0, concat_axis=0, tiled=True)  33.7 us
    dot_general x2, matrix products, sweep_once(): lax.dot_general(row_block, col_block, (((0,), (0,)), ((), ())), preferred...  26 us
    all_to_all x2, waiting for transfers between devices, sent_and_summed(): lax.all_to_all(tiles, axis, split_axis=0, concat_axis=0, tiled=True)  23.2 us
    all_to_all x2, waiting for transfers between devices, copy_for_each(): lax.all_to_all(jnp.broadcast_to(value[None], (length, *value.shape)), axi...  17.5 us
    all_gather x2, waiting for transfers between devices, sweep_once(): col_block = lax.all_gather(col_half, 'row', axis=0, tiled=True)  12 us
    all_to_all x2, starting transfers between devices, sent_and_summed(): lax.all_to_all(tiles, axis, split_axis=0, concat_axis=0, tiled=True)  9.65 us
    all_to_all x2, starting transfers between devices, copy_for_each(): lax.all_to_all(jnp.broadcast_to(value[None], (length, *value.shape)), axi...  7.01 us
  transfers between devices with their start and end apart: 6, of which 5 were waited for; matrix products, arithmetic and copies ran while one was open for 8% of the time, Pallas kernels for 0%

commit v1 on v0

v1 whole, which is shorter than its diff:
```python
import jax
import jax.numpy as jnp
from jax import lax
from jax.sharding import Mesh, PartitionSpec as P

SWEEPS = 2
ROW = ("x", "yh", "c")
COL = ("z", "yl")
CHIPS = ("x", "yh")
AXES = (*ROW, *COL)
SIZES = (4, 2, 2, 4, 2)
OTHER_CORE = [(0, 1), (1, 0)]


def sent_to_all(value, axes, length):
    copies = jnp.broadcast_to(value[None], (length, *value.shape))
    return lax.all_to_all(copies, axes, 0, 0, tiled=True)


def digits_of(value, base, length):
    parts = []
    for _ in range(length):
        parts.append((value % base).astype(jnp.bfloat16))
        value = value // base
    return jnp.stack(parts)


def value_of(digits, base):
    total = digits[-1]
    for at in range(digits.shape[0] - 2, -1, -1):
        total = total * base + digits[at]
    return total


def over_col(value):
    return sent_to_all(value, COL, 8)


def over_row(value):
    mine = sent_to_all(value, CHIPS, 8)
    theirs = lax.ppermute(mine, "c", OTHER_CORE)
    first = lax.axis_index("c") == 0
    return jnp.where(first, mine, theirs), jnp.where(first, theirs, mine)


def in_one(even, odd):
    return jnp.stack([even, odd], axis=1).reshape(256, -1)


def row_pieces_summed(grad):
    tiles = grad.reshape(8, 32, -1)
    arrived = lax.all_to_all(tiles, COL, 0, 0, tiled=True)
    return arrived.astype(jnp.float32).sum(axis=0)


def col_pieces_summed(grad):
    halves = grad.reshape(8, 2, 16, -1)
    core = lax.axis_index("c")
    away = lax.dynamic_index_in_dim(halves, 1 - core, 1, False)
    home = lax.dynamic_index_in_dim(halves, core, 1, False)
    theirs = lax.ppermute(away.astype(jnp.bfloat16), "c", OTHER_CORE)
    both = (home.astype(jnp.float32) + theirs.astype(jnp.float32)).astype(jnp.bfloat16)
    arrived = lax.all_to_all(both, CHIPS, 0, 0, tiled=True)
    return arrived.astype(jnp.float32).sum(axis=0)


def stepped(emb, accum, grad):
    accum = accum + grad * grad
    return emb - 0.05 * grad / jnp.sqrt(accum), accum


def on_device(counts, row_emb, col_emb, row_accum, col_accum):
    local_rows = jnp.sum(counts, axis=1)
    local_cols = jnp.sum(counts, axis=0)
    parcel = jnp.concatenate(
        [
            row_emb.astype(jnp.bfloat16),
            digits_of(local_rows, 128, 3),
            jnp.zeros((5, row_emb.shape[1]), jnp.bfloat16),
        ]
    )
    arrived = over_col(parcel)
    row_block = arrived[:, :32].reshape(256, -1)
    row_marg = value_of(arrived[:, 32:35].astype(jnp.float32).sum(axis=0), 128.0)
    block_total = jnp.sum(row_marg.astype(jnp.int32))
    lanes = lax.broadcasted_iota(jnp.int32, (1, col_emb.shape[1]), 1)
    total_digits = digits_of(block_total, 256, 4)
    total_row = jnp.zeros((1, col_emb.shape[1]), jnp.bfloat16)
    for at in range(4):
        total_row = jnp.where(lanes == at, total_digits[at], total_row)
    parcel = jnp.concatenate(
        [
            col_emb.astype(jnp.bfloat16),
            digits_of(local_cols, 256, 2),
            total_row,
            jnp.zeros((5, col_emb.shape[1]), jnp.bfloat16),
        ]
    )
    even, odd = over_row(parcel)
    col_block = in_one(even[:, :16], odd[:, :16])
    rest = even[:, 16:19].astype(jnp.float32).sum(axis=0) + odd[:, 16:19].astype(jnp.float32).sum(axis=0)
    col_marg = value_of(rest[:2], 256.0)
    total = value_of(rest[2, :4], 256.0)

    values = counts.astype(jnp.float32)
    target = (
        jnp.log(jnp.maximum(values, 1.0))
        + jnp.log(total)
        - jnp.log(row_marg)[:, None]
        - jnp.log(col_marg)[None, :]
    )
    weight = 0.1 + 0.25 * jnp.sqrt(values)
    positive = counts > 0
    for sweep in range(SWEEPS):
        scores = lax.dot_general(
            row_block, col_block, (((0,), (0,)), ((), ())), preferred_element_type=jnp.float32
        )
        errors = scores - target
        grads = jnp.where(positive, weight * errors, jax.nn.sigmoid(errors)).astype(jnp.bfloat16)
        row_grad = lax.dot_general(
            col_block, grads, (((1,), (1,)), ((), ())), preferred_element_type=jnp.float32
        ).astype(jnp.bfloat16)
        col_grad = jnp.dot(row_block, grads, preferred_element_type=jnp.float32).astype(jnp.bfloat16)
        row_emb, row_accum = stepped(row_emb, row_accum, row_pieces_summed(row_grad))
        col_emb, col_accum = stepped(col_emb, col_accum, col_pieces_summed(col_grad))
        if sweep + 1 < SWEEPS:
            row_block = over_col(row_emb.astype(jnp.bfloat16)).reshape(256, -1)
            col_block = in_one(*over_row(col_emb.astype(jnp.bfloat16)))
    return row_emb, col_emb


def solution(mesh):
    fine = Mesh(mesh.devices.reshape(SIZES), AXES)
    tall, wide = P(ROW, COL), P(COL, ROW)
    return jax.shard_map(
        on_device,
        mesh=fine,
        in_specs=(tall, wide, tall, wide, tall),
        out_specs=(wide, tall),
        check_vma=False,
    )
```

time: 207 us -> 174 us (0.84)
  blocking collectives: 71.9 us -> 33.5 us
  starting transfers between devices: 16.7 us -> 26.2 us
  between operations: 15 us -> 6.28 us
  waiting for transfers between devices: 52.7 us -> 58.1 us
  local copies, waits for them, and re-layouts: 2.34 us -> 5.93 us
  matrix products: 37.3 us -> 34.6 us
    all_to_all x5 -> x2, blocking collectives: 71.9 us -> 33.5 us  [the longest x1 19 us: sent_to_all(): return lax.all_to_all(copies, axes, 0, 0, tiled=True)]
    all_to_all x4 -> x6, waiting for transfers between devices: 40.7 us -> 53.9 us  [the longest x3 25.4 us: sent_to_all(): return lax.all_to_all(copies, axes, 0, 0, tiled=True)]
    all_gather x2 -> x0, waiting for transfers between devices: 12 us -> none  [sweep_once(): col_block = lax.all_gather(col_half, 'row', axis=0, tiled=True)]
    all_to_all x4 -> x6, starting transfers between devices: 16.7 us -> 25.9 us  [the longest x3 13.6 us: sent_to_all(): return lax.all_to_all(copies, axes, 0, 0, tiled=True)]
    ppermute x0 -> x4, waiting for transfers between devices: none -> 4.21 us  [the longest x2 2.24 us: over_row(): theirs = lax.ppermute(mine, 'c', OTHER_CORE)]
    dot_general x6, matrix products: 37.3 us -> 34.6 us  [the longest x2 25.7 us: on_device(): lax.dot_general(row_block, col_block, (((0,), (0,)), ((), ())), preferred...]
    reduce_sum x8 -> x9, other arithmetic: 6.47 us -> 5.17 us  [the longest x1 4.05 us: on_device(): local_cols = jnp.sum(counts, axis=0)]
  transfers between devices with their start and end apart: 6 -> 10, of which waited for: 5 -> 8; matrix products, arithmetic and copies ran while one was open for 8% -> 5% of each run, Pallas kernels for 0% -> 0%
where the time goes in v1:
time: 174 us; the launch traced here: 173 us
  waiting for transfers between devices  58.1 us (33%)
  matrix products  34.6 us (20%)
  blocking collectives  33.5 us (19%)
  starting transfers between devices  26.2 us (15%)
  other arithmetic  8.39 us (5%)
  between operations  6.28 us (4%)
  local copies, waits for them, and re-layouts  5.93 us (3%)
    dot_general x2, matrix products, on_device(): lax.dot_general(row_block, col_block, (((0,), (0,)), ((), ())), preferred...  25.7 us
    all_to_all x3, waiting for transfers between devices, sent_to_all(): return lax.all_to_all(copies, axes, 0, 0, tiled=True)  25.4 us
    all_to_all x1, blocking collectives, sent_to_all(): return lax.all_to_all(copies, axes, 0, 0, tiled=True)  19 us
    all_to_all x2, waiting for transfers between devices, row_pieces_summed(): arrived = lax.all_to_all(tiles, COL, 0, 0, tiled=True)  18.6 us
    all_to_all x1, blocking collectives, col_pieces_summed(): arrived = lax.all_to_all(both, CHIPS, 0, 0, tiled=True)  14.5 us
    all_to_all x3, starting transfers between devices, sent_to_all(): return lax.all_to_all(copies, axes, 0, 0, tiled=True)  13.6 us
    all_to_all x1, waiting for transfers between devices, col_pieces_summed(): arrived = lax.all_to_all(both, CHIPS, 0, 0, tiled=True)  9.9 us
    all_to_all x2, starting transfers between devices, row_pieces_summed(): arrived = lax.all_to_all(tiles, COL, 0, 0, tiled=True)  6.98 us
  transfers between devices with their start and end apart: 10, of which 8 were waited for; matrix products, arithmetic and copies ran while one was open for 5% of the time, Pallas kernels for 0%

profile of v1, /device:TPU:0, one launch (start us, length us, event | category | flops | bytes accessed | tf_op | source)
XLA Modules:
  0.0 173.0 jit_solution(2115318864782738612)
XLA Ops:
  0.6 4.1 %fusion.13 = (s32[2048]{0:T(1024)S(1)}, s32[1024]{0:T(1024)S(1)}) fusion(s32[1024,2048]{1,0:T(8,128)} %param.5), kind=kLoop, calls=%fused_computation.78 | loop fusion | flops 4191232 | bytes 8400896 | tf_op jit(solution)/shard_map/reduce_sum | solution.py:74
  4.9 0.9 broadcast_in_dim.49
  5.8 6.4 %all-to-all-start = ((bf16[8,40,1024]{2,1,0:T(8,128)(2,1)}), bf16[8,40,1024]{2,1,0:T(8,128)(2,1)S(1)}, u32[]{:S(2)}, u32[]{:S(2)}) async-start(bf16[8,40,1024]{2,1,0:T(8,128)(2,1)} %broadcast_in_dim.49), calls=%async_computation | async-start | bytes 1310720 | tf_op jit(solution)/shard_map/all_to_all | solution.py:17
  12.2 0.1 fusion.5
  12.4 11.4 %all-to-all-done = bf16[8,40,1024]{2,1,0:T(8,128)(2,1)S(1)} async-done(((bf16[8,40,1024]{2,1,0:T(8,128)(2,1)}), bf16[8,40,1024]{2,1,0:T(8,128)(2,1)S(1)}, u32[]{:S(2)}, u32[]{:S(2)}) %all-to-all-start) | async-done | bytes 655392 | tf_op jit(solution)/shard_map/all_to_all | solution.py:17
  23.8 0.6 convert_reduce_fusion.7
  27.3 0.1 broadcast_in_dim.56
  27.4 19.0 %all_to_all.40 = bf16[8,24,2048]{2,1,0:T(8,128)(2,1)S(1)} all-to-all(bf16[8,24,2048]{2,1,0:T(8,128)(2,1)S(1)} %broadcast_in_dim.56), channel_id=1, replica_groups=mesh['x'=4,'yh'=2,'c'=2,'z'=4,'yl'=2] {'x','yh'}, dimensions={0} | all-to-all | bytes 1572864 | tf_op jit(solution)/shard_map/all_to_all | solution.py:17
  46.4 2.2 %collective-permute-done = bf16[8,24,2048]{2,1,0:T(8,128)(2,1)S(1)} collective-permute-done((bf16[8,24,2048]{2,1,0:T(8,128)(2,1)S(1)}, bf16[8,24,2048]{2,1,0:T(8,128)(2,1)S(1)}, u32[]{:S(2)}, u32[]{:S(2)}) %collective-permute-start) | collective-permute-done | bytes 786464 | tf_op jit(solution)/shard_map/ppermute | solution.py:41
  48.7 0.1 broadcast_select_fusion.1
  48.8 0.1 convert_reduce_fusion.5
  49.0 0.7 fusion.15
  52.3 0.1 pad_maximum_fusion
  52.4 12.9 %select_convert_fusion.1 = bf16[1024,2048]{1,0:T(8,128)(2,1)S(1)} fusion(s32[1024,2048]{1,0:T(8,128)} %param.5, bf16[256,1024]{1,0:T(8,128)(2,1)S(1)} %bitcast.55, bf16[256,2048]{1,0:T(8,128)(2,1)S(1)} %bitcast.47, f32[2048]{0:T(1024)S(1)} %bitcast.62, f32[1024]{0:T(1024)S(1)} %bitcast.64, f32[]{:T(128)} %bitcast.7), kind=kOutput, calls=%fused_computation.1 | convolution fusion | flops 1105199104 | bytes 14168068 | tf_op jit(solution)/shard_map/dot_general | solution.py:115
  65.3 1.3 convolution_convert_fusion.1
  66.6 0.6 copy-done.4
  67.2 0.8 dynamic-slice_bitcast_fusion.1
  68.1 0.2 collective-permute-start.1
  68.2 2.0 %collective-permute-done.1 = bf16[8,16,2048]{2,1,0:T(8,128)(2,1)S(1)} collective-permute-done((bf16[8,16,2048]{2,1,0:T(8,128)(2,1)}, bf16[8,16,2048]{2,1,0:T(8,128)(2,1)S(1)}, u32[]{:S(2)}, u32[]{:S(2)}) %collective-permute-start.1) | collective-permute-done | bytes 524320 | tf_op jit(solution)/shard_map/ppermute | solution.py:61
  70.2 0.1 fusion.1
  70.3 14.5 %all_to_all.41 = bf16[8,16,2048]{2,1,0:T(8,128)(2,1)S(1)} all-to-all(bf16[8,16,2048]{2,1,0:T(8,128)(2,1)S(1)} %fusion.1), channel_id=1, replica_groups=mesh['x'=4,'yh'=2,'c'=2,'z'=4,'yl'=2] {'x','yh'}, dimensions={0} | all-to-all | bytes 1048576 | tf_op jit(solution)/shard_map/all_to_all | solution.py:63
  84.8 0.1 convert_reduce_fusion.2
  84.9 0.8 broadcast_in_dim.57
  85.8 3.5 %all-to-all-start.4 = ((bf16[8,16,2048]{2,1,0:T(8,128)(2,1)}), bf16[8,16,2048]{2,1,0:T(8,128)(2,1)S(1)}, u32[]{:S(2)}, u32[]{:S(2)}) async-start(bf16[8,16,2048]{2,1,0:T(8,128)(2,1)} %broadcast_in_dim.57), calls=%async_computation.4 | async-start | bytes 1048576 | tf_op jit(solution)/shard_map/all_to_all | solution.py:17
  89.3 4.3 %convolution_convert_fusion.3 = bf16[256,1024]{1,0:T(8,128)(2,1)} fusion(bf16[256,2048]{1,0:T(8,128)(2,1)S(1)} %bitcast.48, bf16[1024,2048]{1,0:T(8,128)(2,1)} %copy-done.4), kind=kOutput, calls=%fused_computation.8 | convolution fusion | flops 1074003968 | bytes 5767168 | tf_op jit(solution)/shard_map/dot_general | solution.py:120
  93.6 5.8 %all-to-all-done.4 = bf16[8,16,2048]{2,1,0:T(8,128)(2,1)S(1)} async-done(((bf16[8,16,2048]{2,1,0:T(8,128)(2,1)}), bf16[8,16,2048]{2,1,0:T(8,128)(2,1)S(1)}, u32[]{:S(2)}, u32[]{:S(2)}) %all-to-all-start.4) | async-done | bytes 524320 | tf_op jit(solution)/shard_map/all_to_all | solution.py:17
  99.4 3.5 %all-to-all-start.2 = ((bf16[8,32,1024]{2,1,0:T(8,128)(2,1)}), bf16[8,32,1024]{2,1,0:T(8,128)(2,1)S(1)}, u32[]{:S(2)}, u32[]{:S(2)}) async-start(bf16[8,32,1024]{2,1,0:T(8,128)(2,1)} %bitcast.10), calls=%async_computation.2 | async-start | bytes 1048576 | tf_op jit(solution)/shard_map/all_to_all | solution.py:52
  102.9 0.1 collective-permute-start.2
  103.0 8.5 %all-to-all-done.2 = bf16[8,32,1024]{2,1,0:T(8,128)(2,1)S(1)} async-done(((bf16[8,32,1024]{2,1,0:T(8,128)(2,1)}), bf16[8,32,1024]{2,1,0:T(8,128)(2,1)S(1)}, u32[]{:S(2)}, u32[]{:S(2)}) %all-to-all-start.2) | async-done | bytes 524320 | tf_op jit(solution)/shard_map/all_to_all | solution.py:52
  111.5 0.1 convert_reduce_fusion.3
  111.7 0.8 broadcast_in_dim.58
  112.5 3.7 %all-to-all-start.5 = ((bf16[8,32,1024]{2,1,0:T(8,128)(2,1)}), bf16[8,32,1024]{2,1,0:T(8,128)(2,1)S(1)}, u32[]{:S(2)}, u32[]{:S(2)}) async-start(bf16[8,32,1024]{2,1,0:T(8,128)(2,1)} %broadcast_in_dim.58), calls=%async_computation.5 | async-start | bytes 1048576 | tf_op jit(solution)/shard_map/all_to_all | solution.py:17
  116.2 0.1 select_bitcast_fusion.1
  116.3 0.1 pad_maximum_fusion.1
  116.4 8.2 %all-to-all-done.5 = bf16[8,32,1024]{2,1,0:T(8,128)(2,1)S(1)} async-done(((bf16[8,32,1024]{2,1,0:T(8,128)(2,1)}), bf16[8,32,1024]{2,1,0:T(8,128)(2,1)S(1)}, u32[]{:S(2)}, u32[]{:S(2)}) %all-to-all-start.5) | async-done | bytes 524320 | tf_op jit(solution)/shard_map/all_to_all | solution.py:17
  124.6 12.9 %select_convert_fusion = bf16[1024,2048]{1,0:T(8,128)(2,1)S(1)} fusion(s32[1024,2048]{1,0:T(8,128)} %param.5, bf16[256,1024]{1,0:T(8,128)(2,1)S(1)} %bitcast.57, bf16[256,2048]{1,0:T(8,128)(2,1)S(1)} %bitcast.49, f32[2048]{0:T(1024)S(1)} %bitcast.63, f32[1024]{0:T(1024)S(1)} %bitcast.65, f32[]{:T(128)} %bitcast.7), kind=kOutput, calls=%fused_computation | convolution fusion | flops 1105199104 | bytes 14168068 | tf_op jit(solution)/shard_map/dot_general | solution.py:115
  137.5 1.3 convolution_convert_fusion
  138.8 0.9 dynamic-slice_bitcast_fusion
  139.6 2.1 %convolution_convert_fusion.2 = bf16[256,1024]{1,0:T(8,128)(2,1)} fusion(bf16[256,2048]{1,0:T(8,128)(2,1)S(1)} %bitcast.50, bf16[1024,2048]{1,0:T(8,128)(2,1)S(1)} %select_convert_fusion), kind=kOutput, calls=%fused_computation.7 | convolution fusion | flops 1074003968 | bytes 5767168 | tf_op jit(solution)/shard_map/dot_general | solution.py:120
  141.7 3.5 %all-to-all-start.6 = ((bf16[8,32,1024]{2,1,0:T(8,128)(2,1)}), bf16[8,32,1024]{2,1,0:T(8,128)(2,1)S(1)}, u32[]{:S(2)}, u32[]{:S(2)}) async-start(bf16[8,32,1024]{2,1,0:T(8,128)(2,1)} %bitcast.59), calls=%async_computation.6 | async-start | bytes 1048576 | tf_op jit(solution)/shard_map/all_to_all | solution.py:52
  145.2 0.9 fusion
  146.1 10.1 %all-to-all-done.6 = bf16[8,32,1024]{2,1,0:T(8,128)(2,1)S(1)} async-done(((bf16[8,32,1024]{2,1,0:T(8,128)(2,1)}), bf16[8,32,1024]{2,1,0:T(8,128)(2,1)S(1)}, u32[]{:S(2)}, u32[]{:S(2)}) %all-to-all-start.6) | async-done | bytes 524320 | tf_op jit(solution)/shard_map/all_to_all | solution.py:52
  156.2 5.3 %all-to-all-start.7 = ((bf16[8,16,2048]{2,1,0:T(8,128)(2,1)}), bf16[8,16,2048]{2,1,0:T(8,128)(2,1)S(1)}, u32[]{:S(2)}, u32[]{:S(2)}) async-start(bf16[8,16,2048]{2,1,0:T(8,128)(2,1)} %fusion), calls=%async_computation.7 | async-start | bytes 1048576 | tf_op jit(solution)/shard_map/all_to_all | solution.py:63
  161.5 0.1 convert_reduce_fusion.1
  161.6 0.7 multiply_subtract_fusion.1
  162.3 9.9 %all-to-all-done.7 = bf16[8,16,2048]{2,1,0:T(8,128)(2,1)S(1)} async-done(((bf16[8,16,2048]{2,1,0:T(8,128)(2,1)}), bf16[8,16,2048]{2,1,0:T(8,128)(2,1)S(1)}, u32[]{:S(2)}, u32[]{:S(2)}) %all-to-all-start.7) | async-done | bytes 524320 | tf_op jit(solution)/shard_map/all_to_all | solution.py:63
  172.2 0.1 convert_reduce_fusion
  172.3 0.7 multiply_subtract_fusion
  (35 shorter events, 0.7 us)
Async XLA Ops:
  0.6 4.2 %copy-start = (f32[32,1024]{1,0:T(8,128)S(1)}, f32[32,1024]{1,0:T(8,128)}, u32[]{:S(2)}) copy-start(f32[32,1024]{1,0:T(8,128)} %param.6) | copy-start | bytes 393220
  0.6 11.7 %copy-start.1 = (f32[16,2048]{1,0:T(8,128)S(1)}, f32[16,2048]{1,0:T(8,128)}, u32[]{:S(2)}) copy-start(f32[16,2048]{1,0:T(8,128)} %param.7) | copy-start | bytes 393220
  5.8 17.9 %all-to-all-start = ((bf16[8,40,1024]{2,1,0:T(8,128)(2,1)}), bf16[8,40,1024]{2,1,0:T(8,128)(2,1)S(1)}, u32[]{:S(2)}, u32[]{:S(2)}) async-start(bf16[8,40,1024]{2,1,0:T(8,128)(2,1)} %broadcast_in_dim.49), calls=%async_computation | async-start | bytes 1310720 | tf_op jit(solution)/shard_map/all_to_all | solution.py:17
  46.4 2.3 %collective-permute-start = (bf16[8,24,2048]{2,1,0:T(8,128)(2,1)S(1)}, bf16[8,24,2048]{2,1,0:T(8,128)(2,1)S(1)}, u32[]{:S(2)}, u32[]{:S(2)}) collective-permute-start(bf16[8,24,2048]{2,1,0:T(8,128)(2,1)S(1)} %all_to_all.40), channel_id=1, source_target_pairs={{0,8},{8,0},{1,9},{9,1},{2,10},{10,2},{3,11},{11,3},{4,12},{12,4},... | collective-permute-start | bytes 2359304 | tf_op jit(solution)/shard_map/ppermute | solution.py:41
  65.3 1.9 %copy-start.4 = (bf16[1024,2048]{1,0:T(8,128)(2,1)}, bf16[1024,2048]{1,0:T(8,128)(2,1)S(1)}, u32[]{:S(2)}) copy-start(bf16[1024,2048]{1,0:T(8,128)(2,1)S(1)} %select_convert_fusion.1) | copy-start | bytes 12582916
  65.3 19.5 %copy-start.3 = (f32[16,2048]{1,0:T(8,128)S(1)}, f32[16,2048]{1,0:T(8,128)}, u32[]{:S(2)}) copy-start(f32[16,2048]{1,0:T(8,128)} %param.9) | copy-start | bytes 393220
  66.6 45.0 %copy-start.2 = (f32[32,1024]{1,0:T(8,128)S(1)}, f32[32,1024]{1,0:T(8,128)}, u32[]{:S(2)}) copy-start(f32[32,1024]{1,0:T(8,128)} %param.8) | copy-start | bytes 393220
  68.1 2.1 %collective-permute-start.1 = (bf16[8,16,2048]{2,1,0:T(8,128)(2,1)}, bf16[8,16,2048]{2,1,0:T(8,128)(2,1)S(1)}, u32[]{:S(2)}, u32[]{:S(2)}) collective-permute-start(bf16[8,16,2048]{2,1,0:T(8,128)(2,1)} %dynamic-slice_bitcast_fusion.1), channel_id=1, source_target_pairs={{0,8},{8,0},{1,9},{9,1},{2,10},{10,2},{3,11},{11,3},{4,12},{12,4},... | collective-permute-start | bytes 1572872 | tf_op jit(solution)/shard_map/ppermute | solution.py:61
  85.8 13.6 %all-to-all-start.4 = ((bf16[8,16,2048]{2,1,0:T(8,128)(2,1)}), bf16[8,16,2048]{2,1,0:T(8,128)(2,1)S(1)}, u32[]{:S(2)}, u32[]{:S(2)}) async-start(bf16[8,16,2048]{2,1,0:T(8,128)(2,1)} %broadcast_in_dim.57), calls=%async_computation.4 | async-start | bytes 1048576 | tf_op jit(solution)/shard_map/all_to_all | solution.py:17
  99.4 12.1 %all-to-all-start.2 = ((bf16[8,32,1024]{2,1,0:T(8,128)(2,1)}), bf16[8,32,1024]{2,1,0:T(8,128)(2,1)S(1)}, u32[]{:S(2)}, u32[]{:S(2)}) async-start(bf16[8,32,1024]{2,1,0:T(8,128)(2,1)} %bitcast.10), calls=%async_computation.2 | async-start | bytes 1048576 | tf_op jit(solution)/shard_map/all_to_all | solution.py:52
  102.9 13.3 %collective-permute-start.2 = (bf16[8,16,2048]{2,1,0:T(8,128)(2,1)S(1)}, bf16[8,16,2048]{2,1,0:T(8,128)(2,1)S(1)}, u32[]{:S(2)}, u32[]{:S(2)}) collective-permute-start(bf16[8,16,2048]{2,1,0:T(8,128)(2,1)S(1)} %all-to-all-done.4), channel_id=1, source_target_pairs={{0,8},{8,0},{1,9},{9,1},{2,10},{10,2},{3,11},{11,3},{4,12},{12,4},... | collective-permute-start | bytes 1572872 | tf_op jit(solution)/shard_map/ppermute | solution.py:41
  112.5 12.1 %all-to-all-start.5 = ((bf16[8,32,1024]{2,1,0:T(8,128)(2,1)}), bf16[8,32,1024]{2,1,0:T(8,128)(2,1)S(1)}, u32[]{:S(2)}, u32[]{:S(2)}) async-start(bf16[8,32,1024]{2,1,0:T(8,128)(2,1)} %broadcast_in_dim.58), calls=%async_computation.5 | async-start | bytes 1048576 | tf_op jit(solution)/shard_map/all_to_all | solution.py:17
  139.6 5.6 %collective-permute-start.3 = (bf16[8,16,2048]{2,1,0:T(8,128)(2,1)}, bf16[8,16,2048]{2,1,0:T(8,128)(2,1)S(1)}, u32[]{:S(2)}, u32[]{:S(2)}) collective-permute-start(bf16[8,16,2048]{2,1,0:T(8,128)(2,1)} %dynamic-slice_bitcast_fusion), channel_id=1, source_target_pairs={{0,8},{8,0},{1,9},{9,1},{2,10},{10,2},{3,11},{11,3},{4,12},{12,4},... | collective-permute-start | bytes 1572872 | tf_op jit(solution)/shard_map/ppermute | solution.py:61
  141.7 14.5 %all-to-all-start.6 = ((bf16[8,32,1024]{2,1,0:T(8,128)(2,1)}), bf16[8,32,1024]{2,1,0:T(8,128)(2,1)S(1)}, u32[]{:S(2)}, u32[]{:S(2)}) async-start(bf16[8,32,1024]{2,1,0:T(8,128)(2,1)} %bitcast.59), calls=%async_computation.6 | async-start | bytes 1048576 | tf_op jit(solution)/shard_map/all_to_all | solution.py:52
  156.2 16.0 %all-to-all-start.7 = ((bf16[8,16,2048]{2,1,0:T(8,128)(2,1)}), bf16[8,16,2048]{2,1,0:T(8,128)(2,1)S(1)}, u32[]{:S(2)}, u32[]{:S(2)}) async-start(bf16[8,16,2048]{2,1,0:T(8,128)(2,1)} %fusion), calls=%async_computation.7 | async-start | bytes 1048576 | tf_op jit(solution)/shard_map/all_to_all | solution.py:63

commit v2 on v1

v2 whole, which is shorter than its diff:
```python
import jax
import jax.numpy as jnp
from jax import lax
from jax.experimental import pallas as pl
from jax.experimental.pallas import tpu as pltpu
from jax.sharding import Mesh, PartitionSpec as P

SWEEPS = 2
ROW = ("x", "yh", "c")
COL = ("z", "yl")
CHIPS = ("x", "yh")
AXES = (*ROW, *COL)
SIZES = (4, 2, 2, 4, 2)
OTHER_CORE = [(0, 1), (1, 0)]
D, BR, COLS = 256, 1024, 2048
TN, RC = 256, 256
VMEM_LIMIT = 32 * 2**20


def sent_to_all(value, axes, length):
    copies = jnp.broadcast_to(value[None], (length, *value.shape))
    return lax.all_to_all(copies, axes, 0, 0, tiled=True)


def digits_of(value, base, length):
    parts = []
    for _ in range(length):
        parts.append((value % base).astype(jnp.bfloat16))
        value = value // base
    return jnp.stack(parts)


def value_of(digits, base):
    total = digits[-1]
    for at in range(digits.shape[0] - 2, -1, -1):
        total = total * base + digits[at]
    return total


def over_col(value):
    return sent_to_all(value, COL, 8)


def over_row(value):
    mine = sent_to_all(value, CHIPS, 8)
    theirs = lax.ppermute(mine, "c", OTHER_CORE)
    return mine, theirs


def row_pieces_summed(tiles):
    arrived = lax.all_to_all(tiles, COL, 0, 0, tiled=True)
    return arrived.astype(jnp.float32).sum(axis=0)


def col_pieces_summed(home, away):
    theirs = lax.ppermute(away, "c", OTHER_CORE)
    both = (home + theirs.astype(jnp.float32)).astype(jnp.bfloat16)
    arrived = lax.all_to_all(both, CHIPS, 0, 0, tiled=True)
    return arrived.astype(jnp.float32).sum(axis=0)


def stepped(emb, accum, grad):
    accum = accum + grad * grad
    return emb - 0.05 * grad / jnp.sqrt(accum), accum


def sweep_kernel(core_ref, row_ref, mine_ref, theirs_ref, u_ref, v_ref, logs_ref, weight_ref,
                 row_out, home_out, away_out, row_flat, row_tall, col_flat, grads, row_total):
    core = core_ref[0]
    flat = row_ref[:, :32, :].reshape(D, BR)
    row_flat[...] = flat
    row_tall[...] = (flat * jnp.bfloat16(0.5)).T
    col_flat[:, pl.ds(core, 1)] = mine_ref[:, :16, :][:, None]
    col_flat[:, pl.ds(1 - core, 1)] = theirs_ref[:, :16, :][:, None]
    row_total[...] = jnp.zeros_like(row_total)

    def tile(at, _):
        start = pl.multiple_of(at * TN, TN)
        here = pl.ds(start, TN)
        col = col_flat[:, :, :, here].reshape(D, TN)
        shift = v_ref[:, here]
        for chunk in range(BR // RC):
            rows = pl.ds(chunk * RC, RC)
            scores = jnp.dot(row_tall[rows, :], col, preferred_element_type=jnp.float32)
            errors = scores - logs_ref[rows, here] + (shift - jnp.tile(u_ref[rows, :], (1, TN // 128)))
            weight = weight_ref[rows, here]
            grad = jnp.where(weight > 0.0, weight * errors, 0.5 * jnp.tanh(errors) + 0.5)
            grads[rows, :] = grad.astype(jnp.bfloat16)
        both = grads[...]
        row_total[...] += jnp.dot(both, col.T, preferred_element_type=jnp.float32)
        col_grad = jnp.dot(row_flat[...], both, preferred_element_type=jnp.float32).reshape(8, 2, 16, TN)
        even, odd = col_grad[:, 0], col_grad[:, 1]
        first = core == 0
        home_out[:, :, here] = jnp.where(first, even, odd).astype(home_out.dtype)
        away_out[:, :, here] = jnp.where(first, odd, even).astype(away_out.dtype)
        return 0

    lax.fori_loop(0, COLS // TN, tile, 0)
    row_out[...] = row_total[...].astype(jnp.bfloat16).T.reshape(8, 32, BR)


def swept(core, row, mine, theirs, u, v, logs, weight):
    vmem = pl.BlockSpec(memory_space=pltpu.VMEM)
    return pl.pallas_call(
        sweep_kernel,
        out_shape=(
            jax.ShapeDtypeStruct((8, 32, BR), jnp.bfloat16),
            jax.ShapeDtypeStruct((8, 16, COLS), jnp.float32),
            jax.ShapeDtypeStruct((8, 16, COLS), jnp.bfloat16),
        ),
        in_specs=[pl.BlockSpec(memory_space=pltpu.SMEM)] + [vmem] * 7,
        out_specs=(vmem,) * 3,
        scratch_shapes=[
            pltpu.VMEM((D, BR), jnp.bfloat16),
            pltpu.VMEM((BR, D), jnp.bfloat16),
            pltpu.VMEM((8, 2, 16, COLS), jnp.bfloat16),
            pltpu.VMEM((BR, TN), jnp.bfloat16),
            pltpu.VMEM((BR, D), jnp.float32),
        ],
        compiler_params=pltpu.CompilerParams(vmem_limit_bytes=VMEM_LIMIT),
        cost_estimate=pl.CostEstimate(flops=6 * D * BR * COLS, bytes_accessed=20 * 2**20, transcendentals=BR * COLS),
        name="sweep",
    )(core, row, mine, theirs, u, v, logs, weight)


def on_device(counts, row_emb, col_emb, row_accum, col_accum):
    local_rows = jnp.sum(counts, axis=1)
    local_cols = jnp.sum(counts, axis=0)
    parcel = jnp.concatenate(
        [
            row_emb.astype(jnp.bfloat16),
            digits_of(local_rows, 128, 3),
            jnp.zeros((5, row_emb.shape[1]), jnp.bfloat16),
        ]
    )
    arrived = over_col(parcel)
    row_block = arrived
    row_marg = value_of(arrived[:, 32:35].astype(jnp.float32).sum(axis=0), 128.0)
    block_total = jnp.sum(row_marg.astype(jnp.int32))
    lanes = lax.broadcasted_iota(jnp.int32, (1, col_emb.shape[1]), 1)
    total_digits = digits_of(block_total, 256, 4)
    total_row = jnp.zeros((1, col_emb.shape[1]), jnp.bfloat16)
    for at in range(4):
        total_row = jnp.where(lanes == at, total_digits[at], total_row)
    parcel = jnp.concatenate(
        [
            col_emb.astype(jnp.bfloat16),
            digits_of(local_cols, 256, 2),
            total_row,
            jnp.zeros((5, col_emb.shape[1]), jnp.bfloat16),
        ]
    )
    mine, theirs = over_row(parcel)
    rest = mine[:, 16:19].astype(jnp.float32).sum(axis=0) + theirs[:, 16:19].astype(jnp.float32).sum(axis=0)
    col_marg = value_of(rest[:2], 256.0)
    total = value_of(rest[2, :4], 256.0)

    values = counts.astype(jnp.float32)
    logs = 0.5 * jnp.log(jnp.maximum(values, 1.0))
    weight = jnp.where(counts > 0, 0.2 + 0.5 * jnp.sqrt(values), 0.0)
    u = 0.5 * (jnp.log(total) - jnp.log(row_marg))
    u = jnp.broadcast_to(u[:, None], (BR, 128))
    v = 0.5 * jnp.log(col_marg)[None, :]
    core = lax.axis_index("c").astype(jnp.int32)[None]
    for sweep in range(SWEEPS):
        row_grad, home, away = swept(core, row_block, mine, theirs, u, v, logs, weight)
        row_emb, row_accum = stepped(row_emb, row_accum, row_pieces_summed(row_grad))
        col_emb, col_accum = stepped(col_emb, col_accum, col_pieces_summed(home, away))
        if sweep + 1 < SWEEPS:
            row_block = over_col(row_emb.astype(jnp.bfloat16))
            mine, theirs = over_row(col_emb.astype(jnp.bfloat16))
    return row_emb, col_emb


def solution(mesh):
    fine = Mesh(mesh.devices.reshape(SIZES), AXES)
    tall, wide = P(ROW, COL), P(COL, ROW)
    return jax.shard_map(
        on_device,
        mesh=fine,
        in_specs=(tall, wide, tall, wide, tall),
        out_specs=(wide, tall),
        check_vma=False,
    )
```

time: 174 us -> 174 us (level)
  matrix products: 34.6 us -> 0 us
  Pallas kernels: 0 us -> 16.8 us
  other arithmetic: 8.39 us -> 18 us
  waiting for transfers between devices: 58.1 us -> 64.7 us
  blocking collectives: 33.5 us -> 28.5 us
  local copies, waits for them, and re-layouts: 5.93 us -> 10.7 us
    dot_general x6 -> x0, matrix products: 34.6 us -> none  [the longest x2 25.7 us: on_device(): lax.dot_general(row_block, col_block, (((0,), (0,)), ((), ())), preferred...]
    pallas_call x0 -> x2, Pallas kernels: none -> 16.8 us  [swept(): pl.pallas_call(sweep_kernel, out_shape=(jax.ShapeDtypeStruct((8, 32, BR),...]
    select_n x1, other arithmetic: 0.11 us -> 10.1 us  [on_device(): weight = jnp.where(counts > 0, 0.2 + 0.5 * jnp.sqrt(values), 0.0)]
    all_to_all x3, waiting for transfers between devices: 25.4 us -> 33.7 us  [sent_to_all(): return lax.all_to_all(copies, axes, 0, 0, tiled=True)]
    unnamed x10 -> x16, local copies, waits for them, and re-layouts: 0.66 us -> 6.79 us
    all_to_all x1, blocking collectives: 19 us -> 13.4 us  [sent_to_all(): return lax.all_to_all(copies, axes, 0, 0, tiled=True)]
    all_to_all x3, starting transfers between devices: 13.6 us -> 16.7 us  [sent_to_all(): return lax.all_to_all(copies, axes, 0, 0, tiled=True)]
    ppermute x2, waiting for transfers between devices: 2.24 us -> 0.01 us  [over_row(): theirs = lax.ppermute(mine, 'c', OTHER_CORE)]
  transfers between devices with their start and end apart: 10 -> 10, of which waited for: 8 -> 7; matrix products, arithmetic and copies ran while one was open for 5% -> 7% of each run, Pallas kernels for 0% -> 0%
where the time goes in v2:
time: 174 us; the launch traced here: 173 us
  waiting for transfers between devices  64.7 us (37%)
  blocking collectives  28.5 us (16%)
  starting transfers between devices  27.7 us (16%)
  other arithmetic  18 us (10%)
  Pallas kernels  16.8 us (10%)
  local copies, waits for them, and re-layouts  10.7 us (6%)
  between operations  6.27 us (4%)
    all_to_all x3, waiting for transfers between devices, sent_to_all(): return lax.all_to_all(copies, axes, 0, 0, tiled=True)  33.7 us
    all_to_all x2, waiting for transfers between devices, row_pieces_summed(): arrived = lax.all_to_all(tiles, COL, 0, 0, tiled=True)  19.4 us
    pallas_call x2, Pallas kernels, swept(): pl.pallas_call(sweep_kernel, out_shape=(jax.ShapeDtypeStruct((8, 32, BR),...  16.8 us
    all_to_all x3, starting transfers between devices, sent_to_all(): return lax.all_to_all(copies, axes, 0, 0, tiled=True)  16.7 us
    all_to_all x1, blocking collectives, col_pieces_summed(): arrived = lax.all_to_all(both, CHIPS, 0, 0, tiled=True)  15.1 us
    all_to_all x1, blocking collectives, sent_to_all(): return lax.all_to_all(copies, axes, 0, 0, tiled=True)  13.4 us
    select_n x1, other arithmetic, on_device(): weight = jnp.where(counts > 0, 0.2 + 0.5 * jnp.sqrt(values), 0.0)  10.1 us
    all_to_all x1, waiting for transfers between devices, col_pieces_summed(): arrived = lax.all_to_all(both, CHIPS, 0, 0, tiled=True)  10 us
  transfers between devices with their start and end apart: 10, of which 7 were waited for; matrix products, arithmetic and copies ran while one was open for 7% of the time, Pallas kernels for 0%

profile of v2, /device:TPU:0, one launch (start us, length us, event | category | flops | bytes accessed | tf_op | source)
XLA Modules:
  0.0 172.7 jit_solution(10575505181564986095)
XLA Ops:
  0.6 4.1 %fusion.12 = (s32[2048]{0:T(1024)S(1)}, s32[1024]{0:T(1024)S(1)}) fusion(s32[1024,2048]{1,0:T(8,128)} %param.5), kind=kLoop, calls=%fused_computation.61 | loop fusion | flops 4191232 | bytes 8400896 | tf_op jit(solution)/shard_map/reduce_sum | solution.py:128
  4.9 0.9 broadcast_in_dim.62
  5.8 6.4 %all-to-all-start = ((bf16[8,40,1024]{2,1,0:T(8,128)(2,1)}), bf16[8,40,1024]{2,1,0:T(8,128)(2,1)S(1)}, u32[]{:S(2)}, u32[]{:S(2)}) async-start(bf16[8,40,1024]{2,1,0:T(8,128)(2,1)} %broadcast_in_dim.62), calls=%async_computation | async-start | bytes 1310720 | tf_op jit(solution)/shard_map/all_to_all | solution.py:22
  12.2 0.1 fusion.3
  12.4 11.4 %all-to-all-done.row_ref = bf16[8,40,1024]{2,1,0:T(8,128)(2,1)S(1)} async-done(((bf16[8,40,1024]{2,1,0:T(8,128)(2,1)}), bf16[8,40,1024]{2,1,0:T(8,128)(2,1)S(1)}, u32[]{:S(2)}, u32[]{:S(2)}) %all-to-all-start) | async-done | bytes 655392 | tf_op jit(solution)/shard_map/all_to_all | solution.py:22
  23.8 0.6 convert_reduce_fusion.7
  27.1 0.1 concatenate.7
  27.2 1.0 broadcast_in_dim.69
  28.2 6.6 %all-to-all-start.1 = ((bf16[8,24,2048]{2,1,0:T(8,128)(2,1)}), bf16[8,24,2048]{2,1,0:T(8,128)(2,1)S(1)}, u32[]{:S(2)}, u32[]{:S(2)}) async-start(bf16[8,24,2048]{2,1,0:T(8,128)(2,1)} %broadcast_in_dim.69), calls=%async_computation.1 | async-start | bytes 1572864 | tf_op jit(solution)/shard_map/all_to_all | solution.py:22
  34.8 12.3 %all-to-all-done.1.mine_ref = bf16[8,24,2048]{2,1,0:T(8,128)(2,1)S(1)} async-done(((bf16[8,24,2048]{2,1,0:T(8,128)(2,1)}), bf16[8,24,2048]{2,1,0:T(8,128)(2,1)S(1)}, u32[]{:S(2)}, u32[]{:S(2)}) %all-to-all-start.1) | async-done | bytes 786464 | tf_op jit(solution)/shard_map/all_to_all | solution.py:22
  47.1 0.0 collective-permute-start
  47.1 10.1 %add_select_fusion = (f32[1024,2048]{1,0:T(8,128)S(1)}, f32[1024,2048]{1,0:T(8,128)S(1)}) fusion(s32[1024,2048]{1,0:T(8,128)} %param.5), kind=kLoop, calls=%fused_computation | loop fusion | flops 14680064 | bytes 25165824 | tf_op jit(solution)/shard_map/jit(_where)/select_n | solution.py:160
  57.2 0.1 convert_reduce_fusion.5
  57.3 0.1 convert_reduce_fusion.4
  57.4 0.9 fusion.13
  61.0 0.2 broadcast_in_dim.70.u_ref
  61.2 0.0 copy-start.7
  61.2 0.0 copy-start.6
  61.2 8.4 %sweep.2 = (bf16[8,32,1024]{2,1,0:T(8,128)(2,1)}, f32[8,16,2048]{2,1,0:T(8,128)S(1)}, bf16[8,16,2048]{2,1,0:T(8,128)(2,1)S(1)}) custom-call(s32[1]{0:T(128)} %bitcast.core_ref, bf16[8,40,1024]{2,1,0:T(8,128)(2,1)S(1)} %all-to-all-done.row_ref, bf16[8,24,2048]{2,1,0:T(8,128)(2,1)S(1)} %all-to-all-done.1.mine_ref, ...), custom_call_target="tpu_custom_call" | custom-call | flops 3221225472 | bytes 20971520 | tf_op jit(solution)/shard_map/sweep/pallas_call | solution.py:104
  69.6 0.5 collective-permute-start.1
  70.1 1.5 collective-permute-done.1
  71.7 0.1 add_convert_fusion.1
  71.8 15.1 %all_to_all.40 = bf16[8,16,2048]{2,1,0:T(8,128)(2,1)S(1)} all-to-all(bf16[8,16,2048]{2,1,0:T(8,128)(2,1)S(1)} %add_convert_fusion.1), channel_id=1, replica_groups=mesh['x'=4,'yh'=2,'c'=2,'z'=4,'yl'=2] {'x','yh'}, dimensions={0} | all-to-all | bytes 1048576 | tf_op jit(solution)/shard_map/all_to_all | solution.py:58
  86.8 3.5 %all-to-all-start.2 = ((bf16[8,32,1024]{2,1,0:T(8,128)(2,1)}), bf16[8,32,1024]{2,1,0:T(8,128)(2,1)S(1)}, u32[]{:S(2)}, u32[]{:S(2)}) async-start(bf16[8,32,1024]{2,1,0:T(8,128)(2,1)} %get-tuple-element.8), calls=%async_computation.2 | async-start | bytes 1048576 | tf_op jit(solution)/shard_map/all_to_all | solution.py:51
  90.3 0.1 convert_reduce_fusion.2
  90.5 9.3 %all-to-all-done.2 = bf16[8,32,1024]{2,1,0:T(8,128)(2,1)S(1)} async-done(((bf16[8,32,1024]{2,1,0:T(8,128)(2,1)}), bf16[8,32,1024]{2,1,0:T(8,128)(2,1)S(1)}, u32[]{:S(2)}, u32[]{:S(2)}) %all-to-all-start.2) | async-done | bytes 524320 | tf_op jit(solution)/shard_map/all_to_all | solution.py:51
  99.8 0.8 broadcast_in_dim.73
  100.6 3.6 %all-to-all-start.5 = ((bf16[8,16,2048]{2,1,0:T(8,128)(2,1)}), bf16[8,16,2048]{2,1,0:T(8,128)(2,1)S(1)}, u32[]{:S(2)}, u32[]{:S(2)}) async-start(bf16[8,16,2048]{2,1,0:T(8,128)(2,1)} %broadcast_in_dim.73), calls=%async_computation.5 | async-start | bytes 1048576 | tf_op jit(solution)/shard_map/all_to_all | solution.py:22
  104.2 0.1 convert_reduce_fusion.3
  104.3 10.0 %all-to-all-done.5.mine_ref = bf16[8,16,2048]{2,1,0:T(8,128)(2,1)S(1)} async-done(((bf16[8,16,2048]{2,1,0:T(8,128)(2,1)}), bf16[8,16,2048]{2,1,0:T(8,128)(2,1)S(1)}, u32[]{:S(2)}, u32[]{:S(2)}) %all-to-all-start.5) | async-done | bytes 524320 | tf_op jit(solution)/shard_map/all_to_all | solution.py:22
  114.3 0.0 collective-permute-start.2
  114.3 0.1 broadcast_in_dim.72
  114.4 13.4 %all_to_all.41.row_ref = bf16[8,32,1024]{2,1,0:T(8,128)(2,1)S(1)} all-to-all(bf16[8,32,1024]{2,1,0:T(8,128)(2,1)S(1)} %broadcast_in_dim.72), channel_id=1, replica_groups=mesh['x'=4,'yh'=2,'c'=2,'z'=4,'yl'=2] {'z','yl'}, dimensions={0} | all-to-all | bytes 1048576 | tf_op jit(solution)/shard_map/all_to_all | solution.py:22
  127.8 0.0 collective-permute-done.2.theirs_ref
  127.8 3.4 %copy-done.1 = f32[1024,2048]{1,0:T(8,128)S(1)} copy-done((f32[1024,2048]{1,0:T(8,128)S(1)}, f32[1024,2048]{1,0:T(8,128)}, u32[]{:S(2)}) %copy-start.1) | copy-done | bytes 8388632
  131.2 3.4 %copy-done.3 = f32[1024,2048]{1,0:T(8,128)S(1)} copy-done((f32[1024,2048]{1,0:T(8,128)S(1)}, f32[1024,2048]{1,0:T(8,128)}, u32[]{:S(2)}) %copy-start.3) | copy-done | bytes 8388632
  134.6 8.4 %sweep.3 = (bf16[8,32,1024]{2,1,0:T(8,128)(2,1)}, f32[8,16,2048]{2,1,0:T(8,128)S(1)}, bf16[8,16,2048]{2,1,0:T(8,128)(2,1)S(1)}) custom-call(s32[1]{0:T(128)} %bitcast.core_ref, bf16[8,32,1024]{2,1,0:T(8,128)(2,1)S(1)} %all_to_all.41.row_ref, bf16[8,16,2048]{2,1,0:T(8,128)(2,1)S(1)} %all-to-all-done.5.mine_ref, ...), custom_call_target="tpu_custom_call" | custom-call | flops 3221225472 | bytes 20971520 | tf_op jit(solution)/shard_map/sweep/pallas_call | solution.py:104
  143.0 0.0 collective-permute-start.3
  143.0 3.5 %all-to-all-start.6 = ((bf16[8,32,1024]{2,1,0:T(8,128)(2,1)}), bf16[8,32,1024]{2,1,0:T(8,128)(2,1)S(1)}, u32[]{:S(2)}, u32[]{:S(2)}) async-start(bf16[8,32,1024]{2,1,0:T(8,128)(2,1)} %get-tuple-element.11), calls=%async_computation.6 | async-start | bytes 1048576 | tf_op jit(solution)/shard_map/all_to_all | solution.py:51
  146.5 0.0 collective-permute-done.3
  146.5 0.9 add_convert_fusion
  147.4 10.1 %all-to-all-done.6 = bf16[8,32,1024]{2,1,0:T(8,128)(2,1)S(1)} async-done(((bf16[8,32,1024]{2,1,0:T(8,128)(2,1)}), bf16[8,32,1024]{2,1,0:T(8,128)(2,1)S(1)}, u32[]{:S(2)}, u32[]{:S(2)}) %all-to-all-start.6) | async-done | bytes 524320 | tf_op jit(solution)/shard_map/all_to_all | solution.py:51
  157.5 3.6 %all-to-all-start.7 = ((bf16[8,16,2048]{2,1,0:T(8,128)(2,1)}), bf16[8,16,2048]{2,1,0:T(8,128)(2,1)S(1)}, u32[]{:S(2)}, u32[]{:S(2)}) async-start(bf16[8,16,2048]{2,1,0:T(8,128)(2,1)} %add_convert_fusion), calls=%async_computation.7 | async-start | bytes 1048576 | tf_op jit(solution)/shard_map/all_to_all | solution.py:58
  161.1 0.1 convert_reduce_fusion.1
  161.2 0.7 multiply_subtract_fusion.1
  161.9 10.0 %all-to-all-done.7 = bf16[8,16,2048]{2,1,0:T(8,128)(2,1)S(1)} async-done(((bf16[8,16,2048]{2,1,0:T(8,128)(2,1)}), bf16[8,16,2048]{2,1,0:T(8,128)(2,1)S(1)}, u32[]{:S(2)}, u32[]{:S(2)}) %all-to-all-start.7) | async-done | bytes 524320 | tf_op jit(solution)/shard_map/all_to_all | solution.py:58
  171.9 0.1 convert_reduce_fusion
  172.0 0.7 multiply_subtract_fusion
  (29 shorter events, 0.4 us)
Async XLA Ops:
  0.6 4.2 %copy-start.4 = (f32[32,1024]{1,0:T(8,128)S(1)}, f32[32,1024]{1,0:T(8,128)}, u32[]{:S(2)}) copy-start(f32[32,1024]{1,0:T(8,128)} %param.6) | copy-start | bytes 393220
  0.6 11.7 %copy-start.5 = (f32[16,2048]{1,0:T(8,128)S(1)}, f32[16,2048]{1,0:T(8,128)}, u32[]{:S(2)}) copy-start(f32[16,2048]{1,0:T(8,128)} %param.7) | copy-start | bytes 393220
  5.8 17.9 %all-to-all-start = ((bf16[8,40,1024]{2,1,0:T(8,128)(2,1)}), bf16[8,40,1024]{2,1,0:T(8,128)(2,1)S(1)}, u32[]{:S(2)}, u32[]{:S(2)}) async-start(bf16[8,40,1024]{2,1,0:T(8,128)(2,1)} %broadcast_in_dim.62), calls=%async_computation | async-start | bytes 1310720 | tf_op jit(solution)/shard_map/all_to_all | solution.py:22
  28.2 18.9 %all-to-all-start.1 = ((bf16[8,24,2048]{2,1,0:T(8,128)(2,1)}), bf16[8,24,2048]{2,1,0:T(8,128)(2,1)S(1)}, u32[]{:S(2)}, u32[]{:S(2)}) async-start(bf16[8,24,2048]{2,1,0:T(8,128)(2,1)} %broadcast_in_dim.69), calls=%async_computation.1 | async-start | bytes 1572864 | tf_op jit(solution)/shard_map/all_to_all | solution.py:22
  47.1 10.2 %collective-permute-start = (bf16[8,24,2048]{2,1,0:T(8,128)(2,1)S(1)}, bf16[8,24,2048]{2,1,0:T(8,128)(2,1)S(1)}, u32[]{:S(2)}, u32[]{:S(2)}) collective-permute-start(bf16[8,24,2048]{2,1,0:T(8,128)(2,1)S(1)} %all-to-all-done.1.mine_ref), channel_id=1, source_target_pairs={{0,8},{8,0},{1,9},{9,1},{2,10},{10,2},{3,11},{11,3},{4,12},{12,4},... | collective-permute-start | bytes 2359304 | tf_op jit(solution)/shard_map/ppermute | solution.py:46
  57.2 12.4 %copy-start = (f32[1024,2048]{1,0:T(8,128)}, f32[1024,2048]{1,0:T(8,128)S(1)}, u32[]{:S(2)}) copy-start(f32[1024,2048]{1,0:T(8,128)S(1)} %get-tuple-element.24.weight_ref) | copy-start | bytes 25165828
  57.2 12.4 %copy-start.2 = (f32[1024,2048]{1,0:T(8,128)}, f32[1024,2048]{1,0:T(8,128)S(1)}, u32[]{:S(2)}) copy-start(f32[1024,2048]{1,0:T(8,128)S(1)} %get-tuple-element.25.logs_ref) | copy-start | bytes 25165828
  61.2 29.3 %copy-start.7 = (f32[16,2048]{1,0:T(8,128)S(1)}, f32[16,2048]{1,0:T(8,128)}, u32[]{:S(2)}) copy-start(f32[16,2048]{1,0:T(8,128)} %param.9) | copy-start | bytes 393220
  61.2 53.1 %copy-start.6 = (f32[32,1024]{1,0:T(8,128)S(1)}, f32[32,1024]{1,0:T(8,128)}, u32[]{:S(2)}) copy-start(f32[32,1024]{1,0:T(8,128)} %param.8) | copy-start | bytes 393220
  69.6 2.0 %collective-permute-start.1 = (bf16[8,16,2048]{2,1,0:T(8,128)(2,1)S(1)}, bf16[8,16,2048]{2,1,0:T(8,128)(2,1)S(1)}, u32[]{:S(2)}, u32[]{:S(2)}) collective-permute-start(bf16[8,16,2048]{2,1,0:T(8,128)(2,1)S(1)} %get-tuple-element.10), channel_id=1, source_target_pairs={{0,8},{8,0},{1,9},{9,1},{2,10},{10,2},{3,11},{11,3},{4,12},{12,4},... | collective-permute-start | bytes 1572872 | tf_op jit(solution)/shard_map/ppermute | solution.py:56
  86.8 12.9 %all-to-all-start.2 = ((bf16[8,32,1024]{2,1,0:T(8,128)(2,1)}), bf16[8,32,1024]{2,1,0:T(8,128)(2,1)S(1)}, u32[]{:S(2)}, u32[]{:S(2)}) async-start(bf16[8,32,1024]{2,1,0:T(8,128)(2,1)} %get-tuple-element.8), calls=%async_computation.2 | async-start | bytes 1048576 | tf_op jit(solution)/shard_map/all_to_all | solution.py:51
  100.6 13.7 %all-to-all-start.5 = ((bf16[8,16,2048]{2,1,0:T(8,128)(2,1)}), bf16[8,16,2048]{2,1,0:T(8,128)(2,1)S(1)}, u32[]{:S(2)}, u32[]{:S(2)}) async-start(bf16[8,16,2048]{2,1,0:T(8,128)(2,1)} %broadcast_in_dim.73), calls=%async_computation.5 | async-start | bytes 1048576 | tf_op jit(solution)/shard_map/all_to_all | solution.py:22
  114.3 13.6 %collective-permute-start.2 = (bf16[8,16,2048]{2,1,0:T(8,128)(2,1)S(1)}, bf16[8,16,2048]{2,1,0:T(8,128)(2,1)S(1)}, u32[]{:S(2)}, u32[]{:S(2)}) collective-permute-start(bf16[8,16,2048]{2,1,0:T(8,128)(2,1)S(1)} %all-to-all-done.5.mine_ref), channel_id=1, source_target_pairs={{0,8},{8,0},{1,9},{9,1},{2,10},{10,2},{3,11},{11,3},{4,12},{12,4},... | collective-permute-start | bytes 1572872 | tf_op jit(solution)/shard_map/ppermute | solution.py:46
  127.8 3.4 %copy-start.1 = (f32[1024,2048]{1,0:T(8,128)S(1)}, f32[1024,2048]{1,0:T(8,128)}, u32[]{:S(2)}) copy-start(f32[1024,2048]{1,0:T(8,128)} %copy-done) | copy-start | bytes 25165828
  131.2 3.4 %copy-start.3 = (f32[1024,2048]{1,0:T(8,128)S(1)}, f32[1024,2048]{1,0:T(8,128)}, u32[]{:S(2)}) copy-start(f32[1024,2048]{1,0:T(8,128)} %copy-done.2) | copy-start | bytes 25165828
  143.0 3.5 %collective-permute-start.3 = (bf16[8,16,2048]{2,1,0:T(8,128)(2,1)S(1)}, bf16[8,16,2048]{2,1,0:T(8,128)(2,1)S(1)}, u32[]{:S(2)}, u32[]{:S(2)}) collective-permute-start(bf16[8,16,2048]{2,1,0:T(8,128)(2,1)S(1)} %get-tuple-element.13), channel_id=1, source_target_pairs={{0,8},{8,0},{1,9},{9,1},{2,10},{10,2},{3,11},{11,3},{4,12},{12,4},... | collective-permute-start | bytes 1572872 | tf_op jit(solution)/shard_map/ppermute | solution.py:56
  143.0 14.5 %all-to-all-start.6 = ((bf16[8,32,1024]{2,1,0:T(8,128)(2,1)}), bf16[8,32,1024]{2,1,0:T(8,128)(2,1)S(1)}, u32[]{:S(2)}, u32[]{:S(2)}) async-start(bf16[8,32,1024]{2,1,0:T(8,128)(2,1)} %get-tuple-element.11), calls=%async_computation.6 | async-start | bytes 1048576 | tf_op jit(solution)/shard_map/all_to_all | solution.py:51
  157.5 14.4 %all-to-all-start.7 = ((bf16[8,16,2048]{2,1,0:T(8,128)(2,1)}), bf16[8,16,2048]{2,1,0:T(8,128)(2,1)S(1)}, u32[]{:S(2)}, u32[]{:S(2)}) async-start(bf16[8,16,2048]{2,1,0:T(8,128)(2,1)} %add_convert_fusion), calls=%async_computation.7 | async-start | bytes 1048576 | tf_op jit(solution)/shard_map/all_to_all | solution.py:58

commit v3 on v0

v3 whole, which is shorter than its diff:
```python
import jax
import jax.numpy as jnp
from jax import lax
from jax.experimental import pallas as pl
from jax.experimental.pallas import tpu as pltpu
from jax.sharding import Mesh, PartitionSpec as P


ROW = ("x", "yh", "c")
COL = ("z", "yl")
CHIPS = ("x", "yh")
AXES = (*ROW, *COL)
SIZES = (4, 2, 2, 4, 2)
SWAP = [(0, 1), (1, 0)]
D, BR, COLS = 256, 1024, 2048
TN, RC, BLOCK = 256, 256, 128
VMEM = pl.BlockSpec(memory_space=pltpu.VMEM)


def shape(dims, kind):
    return jax.ShapeDtypeStruct(dims, kind)


def cost(flops, moved):
    return pl.CostEstimate(flops=flops, bytes_accessed=moved, transcendentals=0)


def in_hbm(value):
    return pltpu.with_memory_space_constraint(value, pltpu.HBM)


def to_each(copies, axes):
    return lax.all_to_all(copies, axes, 0, 0, tiled=True)


def over_z(value, shift):
    return lax.ppermute(value, "z", [(at, (at + shift) % 4) for at in range(4)])


def logs_kernel(counts_ref, logs_ref):
    values = counts_ref[...].astype(jnp.float32)
    logs_ref[...] = 0.5 * jnp.log(jnp.maximum(values, 1.0))


def weight_kernel(counts_ref, weight_ref):
    values = counts_ref[...].astype(jnp.float32)
    weight_ref[...] = jnp.where(values > 0.0, 0.2 + 0.5 * jnp.sqrt(values), 0.0)


def prepared(kernel, counts):
    spec = pl.BlockSpec((BLOCK, COLS), lambda at: (at, 0))
    return pl.pallas_call(
        kernel,
        grid=(BR // BLOCK,),
        out_shape=pltpu.HBM((BR, COLS), jnp.float32),
        in_specs=[spec],
        out_specs=spec,
        compiler_params=pltpu.CompilerParams(vmem_limit_bytes=24 * 2**20),
        cost_estimate=cost(4 * BR * COLS, 16 * 2**20),
    )(in_hbm(counts))


def first_kernel(emb_ref, sums_ref, out_ref):
    sums = sums_ref[...]
    digits = [sums & 127, (sums >> 7) & 127, sums >> 14]
    rows = [emb_ref[...]] + [digit.astype(jnp.float32) for digit in digits]
    parcel = jnp.concatenate(rows + [jnp.zeros((5, BR), jnp.float32)]).astype(jnp.bfloat16)
    for at in range(8):
        out_ref[at] = parcel


def second_kernel(arrived_ref, emb_ref, sums_ref, out_ref, row_log_ref):
    digits = arrived_ref[0, 32:40, :].astype(jnp.float32)
    for at in range(1, 8):
        digits += arrived_ref[at, 32:40, :].astype(jnp.float32)
    marg = digits[0:1] + 128.0 * digits[1:2] + 16384.0 * digits[2:3]
    total = jnp.sum(marg.astype(jnp.int32), axis=1, keepdims=True)
    lane = lax.broadcasted_iota(jnp.int32, (1, COLS), 1)
    total = jnp.broadcast_to(total, (1, COLS))
    parts = jnp.where(lane < 4, (total >> (8 * jnp.minimum(lane, 3))) & 255, 0)
    sums = sums_ref[...]
    rows = [emb_ref[...], (sums & 255).astype(jnp.float32), (sums >> 8).astype(jnp.float32), parts.astype(jnp.float32)]
    parcel = jnp.concatenate(rows + [jnp.zeros((5, COLS), jnp.float32)]).astype(jnp.bfloat16)
    for at in range(8):
        out_ref[at] = parcel
    logs = 0.5 * jnp.log(marg)
    for at in range(BR // 128):
        here = slice(at * 128, at * 128 + 128)
        row_log_ref[here, :] = jnp.broadcast_to(logs[:, here], (128, 128)).T


def col_log_kernel(mine_ref, theirs_ref, out_ref):
    digits = mine_ref[0, 16:24, :].astype(jnp.float32) + theirs_ref[0, 16:24, :].astype(jnp.float32)
    for at in range(1, 8):
        digits += mine_ref[at, 16:24, :].astype(jnp.float32) + theirs_ref[at, 16:24, :].astype(jnp.float32)
    marg = digits[0:1] + 256.0 * digits[1:2]
    lane = lax.broadcasted_iota(jnp.int32, (1, 128), 1)
    scale = jnp.where(lane == 0, 1.0, jnp.where(lane == 1, 256.0, jnp.where(lane == 2, 65536.0, 16777216.0)))
    total = jnp.sum(jnp.where(lane < 4, digits[2:3, :128] * scale, 0.0), axis=1, keepdims=True)
    out_ref[...] = 0.5 * jnp.log(marg) - 0.5 * jnp.log(total)


def arranged_kernel(*refs):
    row_refs, (flat_ref, tall_ref) = refs[:-2], refs[-2:]
    z, yl = lax.axis_index("z"), lax.axis_index("yl")
    if len(row_refs) == 1:
        flat_ref[...] = row_refs[0][:, :32, :]
    else:
        for shift in range(4):
            for other in range(2):
                place = lax.rem(z + 4 - shift, 4) * 2 + lax.rem(yl + other, 2)
                flat_ref[pl.ds(place, 1)] = row_refs[shift][other : other + 1]
    tall_ref[...] = (flat_ref[...].reshape(D, BR) * jnp.bfloat16(0.5)).T


def arranged(row):
    outs = (shape((8, 32, BR), jnp.bfloat16), shape((BR, D), jnp.bfloat16))
    return small(arranged_kernel, outs)(*row)


def sweep_kernel(*refs):
    row_flat, row_tall, mine_ref, theirs_ref, row_log_ref, col_log_ref, logs_ref, weight_ref = refs[:8]
    outs, home_out, away_out = refs[8:12], refs[12], refs[13]
    col_flat, grads, row_total, turned = refs[14:]
    step = pl.program_id(0)
    core, z, yl = lax.axis_index("c"), lax.axis_index("z"), lax.axis_index("yl")

    @pl.when(step == 0)
    def _():
        col_flat[:, pl.ds(core, 1)] = mine_ref[:, :16, :][:, None]
        col_flat[:, pl.ds(1 - core, 1)] = theirs_ref[:, :16, :][:, None]
        row_total[...] = jnp.zeros_like(row_total)

    start = pl.multiple_of(step * TN, TN)
    here = pl.ds(start, TN)
    col = col_flat[:, :, :, here].reshape(D, TN)
    shift = col_log_ref[...]
    for chunk in range(BR // RC):
        rows = pl.ds(chunk * RC, RC)
        scores = jnp.dot(row_tall[rows, :], col, preferred_element_type=jnp.float32)
        errors = scores - logs_ref[rows, :] + (shift + jnp.tile(row_log_ref[rows, :], (1, TN // 128)))
        weight = weight_ref[rows, :]
        grad = jnp.where(weight > 0.0, weight * errors, 0.5 * jnp.tanh(errors) + 0.5)
        grads[rows, :] = grad.astype(jnp.bfloat16)
    both = grads[...]
    row_total[...] += jnp.dot(both, col.T, preferred_element_type=jnp.float32)
    col_grad = jnp.dot(row_flat[...].reshape(D, BR), both, preferred_element_type=jnp.float32).reshape(8, 2, 16, TN)
    even, odd = col_grad[:, 0], col_grad[:, 1]
    home_out[...] = jnp.where(core == 0, even, odd)
    away_out[...] = jnp.where(core == 0, odd, even).astype(jnp.bfloat16)

    @pl.when(step == COLS // TN - 1)
    def _():
        turned[...] = row_total[...].astype(jnp.bfloat16).T.reshape(8, 32, BR)
        for shift in range(4):
            for other in range(2):
                place = lax.rem(z + shift, 4) * 2 + lax.rem(yl + other, 2)
                outs[shift][other : other + 1] = turned[pl.ds(place, 1)]


def swept(row, mine, theirs, row_log, col_log, logs, weight):
    tile = pl.BlockSpec((BR, TN), lambda at: (0, at))
    out_tile = pl.BlockSpec((8, 16, TN), lambda at: (0, 0, at))
    return pl.pallas_call(
        sweep_kernel,
        grid=(COLS // TN,),
        out_shape=(shape((2, 32, BR), jnp.bfloat16),) * 4
        + (shape((8, 16, COLS), jnp.float32), shape((8, 16, COLS), jnp.bfloat16)),
        in_specs=[VMEM] * 5 + [pl.BlockSpec((1, TN), lambda at: (0, at)), tile, tile],
        out_specs=(VMEM,) * 4 + (out_tile,) * 2,
        scratch_shapes=[
            pltpu.VMEM((8, 2, 16, COLS), jnp.bfloat16),
            pltpu.VMEM((BR, TN), jnp.bfloat16),
            pltpu.VMEM((BR, D), jnp.float32),
            pltpu.VMEM((8, 32, BR), jnp.bfloat16),
        ],
        compiler_params=pltpu.CompilerParams(vmem_limit_bytes=24 * 2**20),
        cost_estimate=cost(6 * D * BR * COLS, 20 * 2**20),
        name="sweep",
    )(*row, mine, theirs, row_log, col_log, in_hbm(logs), in_hbm(weight))


def home_kernel(home_ref, theirs_ref, out_ref):
    out_ref[...] = (home_ref[...] + theirs_ref[...].astype(jnp.float32)).astype(jnp.bfloat16)


def z_kernel(a_ref, b_ref, c_ref, d_ref, keep_ref, send_ref):
    total = a_ref[...].astype(jnp.float32) + b_ref[...].astype(jnp.float32)
    total += c_ref[...].astype(jnp.float32) + d_ref[...].astype(jnp.float32)
    keep_ref[...] = total[0]
    send_ref[...] = total[1].astype(jnp.bfloat16)


def moved(emb_ref, accum_ref, grad):
    accum = accum_ref[...] + grad * grad
    return emb_ref[...] - 0.05 * grad / jnp.sqrt(accum), accum


def row_kernel(keep_ref, came_ref, emb_ref, accum_ref, new_emb_ref, new_accum_ref, half_ref):
    emb, accum = moved(emb_ref, accum_ref, keep_ref[...] + came_ref[...].astype(jnp.float32))
    new_emb_ref[...] = emb
    new_accum_ref[...] = accum
    half_ref[...] = emb.astype(jnp.bfloat16)


def col_kernel(came_ref, emb_ref, accum_ref, new_emb_ref, new_accum_ref, half_ref):
    grad = came_ref[0].astype(jnp.float32)
    for at in range(1, 8):
        grad += came_ref[at].astype(jnp.float32)
    emb, accum = moved(emb_ref, accum_ref, grad)
    new_emb_ref[...] = emb
    new_accum_ref[...] = accum
    half = emb.astype(jnp.bfloat16)
    for at in range(8):
        half_ref[at] = half


def small(kernel, outs):
    return pl.pallas_call(
        kernel,
        out_shape=outs,
        compiler_params=pltpu.CompilerParams(vmem_limit_bytes=8 * 2**20),
        cost_estimate=cost(2**20, 2**20),
    )


def on_device(counts, row_emb, col_emb, row_accum, col_accum):
    local_rows = jnp.sum(counts, axis=1)[None]
    local_cols = jnp.sum(counts, axis=0)[None]
    copies = small(first_kernel, shape((8, 40, BR), jnp.bfloat16))(row_emb, local_rows)
    row_block = to_each(copies, COL)
    logs = prepared(logs_kernel, counts)
    row_block, logs = lax.optimization_barrier((row_block, logs))
    copies, row_log = small(
        second_kernel, (shape((8, 24, COLS), jnp.bfloat16), shape((BR, 128), jnp.float32))
    )(row_block, col_emb, local_cols)
    mine = to_each(copies, CHIPS)
    weight = prepared(weight_kernel, counts)
    mine, weight = lax.optimization_barrier((mine, weight))
    theirs = lax.ppermute(mine, "c", SWAP)
    col_log = small(col_log_kernel, shape((1, COLS), jnp.float32))(mine, theirs)
    row = arranged([row_block])
    for sweep in range(2):
        *parts, home, away = swept(row, mine, theirs, row_log, col_log, logs, weight)
        theirs = lax.ppermute(away, "c", SWAP)
        parts = parts[:1] + [over_z(parts[shift], shift) for shift in (1, 3, 2)]
        both = small(home_kernel, shape((8, 16, COLS), jnp.bfloat16))(home, theirs)
        came = to_each(both, CHIPS)
        outs = (shape((32, BR), jnp.float32), shape((32, BR), jnp.bfloat16))
        keep, send = small(z_kernel, outs)(*parts)
        from_pair = lax.ppermute(send, "yl", SWAP)
        outs = (shape((32, BR), jnp.float32),) * 2 + (shape((32, BR), jnp.bfloat16),)
        row_emb, row_accum, half = small(row_kernel, outs)(keep, from_pair, row_emb, row_accum)
        outs = (shape((16, COLS), jnp.float32),) * 2 + (shape((8, 16, COLS), jnp.bfloat16),)
        col_emb, col_accum, copies = small(col_kernel, outs)(came, col_emb, col_accum)
        if sweep == 0:
            pair = lax.ppermute(half, "yl", SWAP)
            pair = jnp.stack([half, pair])
            mine = to_each(copies, CHIPS)
            row = [pair, over_z(pair, 1), over_z(pair, 2), over_z(pair, 3)]
            row = arranged(row)
            theirs = lax.ppermute(mine, "c", SWAP)
    return row_emb, col_emb


def solution(mesh):
    fine = Mesh(mesh.devices.reshape(SIZES), AXES)
    tall, wide = P(ROW, COL), P(COL, ROW)
    return jax.shard_map(
        on_device,
        mesh=fine,
        in_specs=(tall, wide, tall, wide, tall),
        out_specs=(wide, tall),
        check_vma=False,
    )
```

time: 207 us -> 155 us (0.75)
  Pallas kernels: 0 us -> 48.3 us
  blocking collectives: 71.9 us -> 30.1 us
  matrix products: 37.3 us -> 0 us
  between operations: 15 us -> 0.78 us
  starting transfers between devices: 16.7 us -> 28.8 us
  waiting for transfers between devices: 52.7 us -> 41.3 us
  other arithmetic: 10.2 us -> 4.06 us
  local copies, waits for them, and re-layouts: 2.34 us -> 0.02 us
    pallas_call x0 -> x17, Pallas kernels: none -> 48.3 us  [the longest x2 22.8 us: swept(): pl.pallas_call(sweep_kernel, grid=(COLS // TN,), out_shape=(shape((2, 32,...]
    all_to_all x5 -> x2, blocking collectives: 71.9 us -> 30.1 us  [to_each(): return lax.all_to_all(copies, axes, 0, 0, tiled=True)]
    dot_general x6 -> x0, matrix products: 37.3 us -> none  [the longest x2 26 us: sweep_once(): lax.dot_general(row_block, col_block, (((0,), (0,)), ((), ())), preferred...]
    ppermute x0 -> x16, waiting for transfers between devices: none -> 37.2 us  [the longest x9 19.7 us: over_z(): return lax.ppermute(value, 'z', [(at, (at + shift) % 4) for at in range(4)])]
    all_to_all x4 -> x3, waiting for transfers between devices: 40.7 us -> 4.1 us  [to_each(): return lax.all_to_all(copies, axes, 0, 0, tiled=True)]
    ppermute x0 -> x16, starting transfers between devices: none -> 12.2 us  [the longest x9 10.6 us: over_z(): return lax.ppermute(value, 'z', [(at, (at + shift) % 4) for at in range(4)])]
    all_gather x2 -> x0, waiting for transfers between devices: 12 us -> none  [sweep_once(): col_block = lax.all_gather(col_half, 'row', axis=0, tiled=True)]
    reduce_sum x8 -> x1, other arithmetic: 6.47 us -> 4.04 us  [on_device(): local_cols = jnp.sum(counts, axis=0)[None]]
  transfers between devices with their start and end apart: 6 -> 19, of which waited for: 5 -> 17; matrix products, arithmetic and copies ran while one was open for 8% -> 0% of each run, Pallas kernels for 0% -> 14%
where the time goes in v3:
time: 155 us; the launch traced here: 153 us
  Pallas kernels  48.3 us (31%)
  waiting for transfers between devices  41.3 us (27%)
  blocking collectives  30.1 us (19%)
  starting transfers between devices  28.8 us (19%)
  other arithmetic  4.06 us (3%)
    all_to_all x2, blocking collectives, to_each(): return lax.all_to_all(copies, axes, 0, 0, tiled=True)  30.1 us
    pallas_call x2, Pallas kernels, swept(): pl.pallas_call(sweep_kernel, grid=(COLS // TN,), out_shape=(shape((2, 32,...  22.8 us
    pallas_call x2, Pallas kernels, prepared(): pl.pallas_call(kernel, grid=(BR // BLOCK,), out_shape=pltpu.HBM((BR, COLS...  19.7 us
    ppermute x9, waiting for transfers between devices, over_z(): return lax.ppermute(value, 'z', [(at, (at + shift) % 4) for at in range(4)])  19.7 us
    all_to_all x3, starting transfers between devices, to_each(): return lax.all_to_all(copies, axes, 0, 0, tiled=True)  16.6 us
    ppermute x9, starting transfers between devices, over_z(): return lax.ppermute(value, 'z', [(at, (at + shift) % 4) for at in range(4)])  10.6 us
    ppermute x2, waiting for transfers between devices, on_device(): from_pair = lax.ppermute(send, 'yl', SWAP)  7.75 us
    all_to_all x3, waiting for transfers between devices, to_each(): return lax.all_to_all(copies, axes, 0, 0, tiled=True)  4.1 us
  transfers between devices with their start and end apart: 19, of which 17 were waited for; matrix products, arithmetic and copies ran while one was open for 0% of the time, Pallas kernels for 14%

profile of v3, /device:TPU:0, one launch (start us, length us, event | category | flops | bytes accessed | tf_op | source)
XLA Modules:
  0.0 153.3 jit_solution(5926627606771657285)
XLA Ops:
  0.6 4.0 %fusion = (s32[2048]{0:T(1024)S(1)}, s32[1024]{0:T(1024)S(1)}) fusion(s32[1024,2048]{1,0:T(8,128)} %counts_ref.3), kind=kLoop, calls=%fused_computation.1 | loop fusion | flops 4191232 | bytes 8400896 | tf_op jit(solution)/shard_map/reduce_sum | solution.py:229
  4.7 1.0 shard_map.68
  5.7 6.4 %all-to-all-start = ((bf16[8,40,1024]{2,1,0:T(8,128)(2,1)}), bf16[8,40,1024]{2,1,0:T(8,128)(2,1)S(1)}, u32[]{:S(2)}, u32[]{:S(2)}) async-start(bf16[8,40,1024]{2,1,0:T(8,128)(2,1)} %shard_map.68), calls=%async_computation | async-start | bytes 1310720 | tf_op jit(solution)/shard_map/all_to_all | solution.py:33
  12.1 9.4 %shard_map.69.refs_6_ = f32[1024,2048]{1,0:T(8,128)} custom-call(s32[1024,2048]{1,0:T(8,128)} %counts_ref.3), custom_call_target="tpu_custom_call" | custom-call | flops 8388608 | bytes 16777216 | tf_op jit(solution)/shard_map/pallas_call | solution.py:52
  21.6 2.0 %all-to-all-done.refs_0_.arrived_ref = bf16[8,40,1024]{2,1,0:T(8,128)(2,1)S(1)} async-done(((bf16[8,40,1024]{2,1,0:T(8,128)(2,1)}), bf16[8,40,1024]{2,1,0:T(8,128)(2,1)S(1)}, u32[]{:S(2)}, u32[]{:S(2)}) %all-to-all-start) | async-done | bytes 655392 | tf_op jit(solution)/shard_map/all_to_all | solution.py:33
  23.6 1.1 shard_map.71
  24.7 6.6 %all-to-all-start.1 = ((bf16[8,24,2048]{2,1,0:T(8,128)(2,1)}), bf16[8,24,2048]{2,1,0:T(8,128)(2,1)S(1)}, u32[]{:S(2)}, u32[]{:S(2)}) async-start(bf16[8,24,2048]{2,1,0:T(8,128)(2,1)} %get-tuple-element.39), calls=%async_computation.1 | async-start | bytes 1572864 | tf_op jit(solution)/shard_map/all_to_all | solution.py:33
  31.3 10.2 %shard_map.72.refs_7_ = f32[1024,2048]{1,0:T(8,128)} custom-call(s32[1024,2048]{1,0:T(8,128)} %counts_ref.3), custom_call_target="tpu_custom_call" | custom-call | flops 8388608 | bytes 16777216 | tf_op jit(solution)/shard_map/pallas_call | solution.py:52
  41.6 2.1 %all-to-all-done.1.mine_ref.refs_2_ = bf16[8,24,2048]{2,1,0:T(8,128)(2,1)S(1)} async-done(((bf16[8,24,2048]{2,1,0:T(8,128)(2,1)}), bf16[8,24,2048]{2,1,0:T(8,128)(2,1)S(1)}, u32[]{:S(2)}, u32[]{:S(2)}) %all-to-all-start.1) | async-done | bytes 786464 | tf_op jit(solution)/shard_map/all_to_all | solution.py:33
  43.6 0.2 shard_map.70
  43.8 2.1 %collective-permute-done.theirs_ref.refs_3_ = bf16[8,24,2048]{2,1,0:T(8,128)(2,1)S(1)} collective-permute-done((bf16[8,24,2048]{2,1,0:T(8,128)(2,1)S(1)}, bf16[8,24,2048]{2,1,0:T(8,128)(2,1)S(1)}, u32[]{:S(2)}, u32[]{:S(2)}) %collective-permute-start) | collective-permute-done | bytes 786464 | tf_op jit(solution)/shard_map/ppermute | solution.py:240
  45.9 0.2 shard_map.73.refs_5_
  46.1 11.4 %sweep.2 = (bf16[2,32,1024]{2,1,0:T(8,128)(2,1)S(1)}, bf16[2,32,1024]{2,1,0:T(8,128)(2,1)S(1)}, bf16[2,32,1024]{2,1,0:T(8,128)(2,1)S(1)}, bf16[2,32,1024]{2,1,0:...) custom-call(bf16[8,32,1024]{2,1,0:T(8,128)(2,1)S(1)} %get-tuple-element.37.refs_0_, ...), custom_call_target="tpu_custom_call" | custom-call | flops 3221225472 | bytes 20971520 | tf_op jit(solution)/shard_map/sweep/pallas_call | solution.py:164
  57.5 0.2 collective-permute-start.9
  57.8 1.8 %collective-permute-done.9.theirs_ref = bf16[8,16,2048]{2,1,0:T(8,128)(2,1)S(1)} collective-permute-done((bf16[8,16,2048]{2,1,0:T(8,128)(2,1)S(1)}, bf16[8,16,2048]{2,1,0:T(8,128)(2,1)S(1)}, u32[]{:S(2)}, u32[]{:S(2)}) %collective-permute-start.9) | collective-permute-done | bytes 524320 | tf_op jit(solution)/shard_map/ppermute | solution.py:245
  59.5 0.1 shard_map.77
  59.7 16.5 %all_to_all.25.came_ref = bf16[8,16,2048]{2,1,0:T(8,128)(2,1)S(1)} all-to-all(bf16[8,16,2048]{2,1,0:T(8,128)(2,1)S(1)} %shard_map.77), channel_id=1, replica_groups=mesh['x'=4,'yh'=2,'c'=2,'z'=4,'yl'=2] {'x','yh'}, dimensions={0} | all-to-all | bytes 1048576 | tf_op jit(solution)/shard_map/all_to_all | solution.py:33
  76.1 0.1 shard_map.78
  76.3 13.6 %all_to_all.26.refs_2_ = bf16[8,16,2048]{2,1,0:T(8,128)(2,1)S(1)} all-to-all(bf16[8,16,2048]{2,1,0:T(8,128)(2,1)S(1)} %get-tuple-element.55), channel_id=1, replica_groups=mesh['x'=4,'yh'=2,'c'=2,'z'=4,'yl'=2] {'x','yh'}, dimensions={0} | all-to-all | bytes 1048576 | tf_op jit(solution)/shard_map/all_to_all | solution.py:33
  89.9 3.2 %collective-permute-start.2 = (bf16[2,32,1024]{2,1,0:T(8,128)(2,1)S(1)}, bf16[2,32,1024]{2,1,0:T(8,128)(2,1)S(1)}, u32[]{:S(2)}, u32[]{:S(2)}) collective-permute-start(bf16[2,32,1024]{2,1,0:T(8,128)(2,1)S(1)} %get-tuple-element.46), channel_id=1, source_target_pairs={{0,6},{2,0},{4,2},{6,4},{1,7},{3,1},{5,3},{7,5},{8,14},{10,8},{12,... | collective-permute-start | bytes 393224 | tf_op jit(solution)/shard_map/ppermute | solution.py:37
  93.1 0.3 collective-permute-start.3
  93.4 3.6 %collective-permute-done.1.b_ref = bf16[2,32,1024]{2,1,0:T(8,128)(2,1)S(1)} collective-permute-done((bf16[2,32,1024]{2,1,0:T(8,128)(2,1)S(1)}, bf16[2,32,1024]{2,1,0:T(8,128)(2,1)S(1)}, u32[]{:S(2)}, u32[]{:S(2)}) %collective-permute-start.1) | collective-permute-done | bytes 131104 | tf_op jit(solution)/shard_map/ppermute | solution.py:37
  97.0 2.1 %collective-permute-done.2.c_ref = bf16[2,32,1024]{2,1,0:T(8,128)(2,1)S(1)} collective-permute-done((bf16[2,32,1024]{2,1,0:T(8,128)(2,1)S(1)}, bf16[2,32,1024]{2,1,0:T(8,128)(2,1)S(1)}, u32[]{:S(2)}, u32[]{:S(2)}) %collective-permute-start.2) | collective-permute-done | bytes 131104 | tf_op jit(solution)/shard_map/ppermute | solution.py:37
  99.1 0.9 collective-permute-done.3.d_ref
  100.1 0.3 collective-permute-start.4
  100.4 4.0 %collective-permute-done.4.came_ref = bf16[32,1024]{1,0:T(8,128)(2,1)S(1)} collective-permute-done((bf16[32,1024]{1,0:T(8,128)(2,1)S(1)}, bf16[32,1024]{1,0:T(8,128)(2,1)S(1)}, u32[]{:S(2)}, u32[]{:S(2)}) %collective-permute-start.4) | collective-permute-done | bytes 65568 | tf_op jit(solution)/shard_map/ppermute | solution.py:251
  104.4 0.1 shard_map.75
  104.5 0.3 collective-permute-start.5
  104.8 4.0 %collective-permute-done.5 = bf16[32,1024]{1,0:T(8,128)(2,1)S(1)} collective-permute-done((bf16[32,1024]{1,0:T(8,128)(2,1)S(1)}, bf16[32,1024]{1,0:T(8,128)(2,1)S(1)}, u32[]{:S(2)}, u32[]{:S(2)}) %collective-permute-start.5) | collective-permute-done | bytes 65568 | tf_op jit(solution)/shard_map/ppermute | solution.py:257
  108.9 2.9 %collective-permute-start.8 = (bf16[2,32,1024]{2,1,0:T(8,128)(2,1)S(1)}, bf16[2,32,1024]{2,1,0:T(8,128)(2,1)S(1)}, u32[]{:S(2)}, u32[]{:S(2)}) collective-permute-start(bf16[2,32,1024]{2,1,0:T(8,128)(2,1)S(1)} %pad_maximum_fusion.refs_0_), channel_id=1, source_target_pairs={{0,6},{2,0},{4,2},{6,4},{1,7},{3,1},{5,3},{7,5},{8,14},{10,8},{12,... | collective-permute-start | bytes 393224 | tf_op jit(solution)/shard_map/ppermute | solution.py:37
  111.7 0.9 collective-permute-start.6
  112.7 3.0 %collective-permute-done.8.refs_3_ = bf16[2,32,1024]{2,1,0:T(8,128)(2,1)S(1)} collective-permute-done((bf16[2,32,1024]{2,1,0:T(8,128)(2,1)S(1)}, bf16[2,32,1024]{2,1,0:T(8,128)(2,1)S(1)}, u32[]{:S(2)}, u32[]{:S(2)}) %collective-permute-start.8) | collective-permute-done | bytes 131104 | tf_op jit(solution)/shard_map/ppermute | solution.py:37
  115.6 2.6 %collective-permute-done.7.refs_2_ = bf16[2,32,1024]{2,1,0:T(8,128)(2,1)S(1)} collective-permute-done((bf16[2,32,1024]{2,1,0:T(8,128)(2,1)S(1)}, bf16[2,32,1024]{2,1,0:T(8,128)(2,1)S(1)}, u32[]{:S(2)}, u32[]{:S(2)}) %collective-permute-start.7) | collective-permute-done | bytes 131104 | tf_op jit(solution)/shard_map/ppermute | solution.py:37
  118.3 1.0 collective-permute-done.6.refs_1_
  119.3 0.2 shard_map.76
  119.6 11.4 %sweep.3 = (bf16[2,32,1024]{2,1,0:T(8,128)(2,1)S(1)}, bf16[2,32,1024]{2,1,0:T(8,128)(2,1)S(1)}, bf16[2,32,1024]{2,1,0:T(8,128)(2,1)S(1)}, bf16[2,32,1024]{2,1,0:...) custom-call(bf16[8,32,1024]{2,1,0:T(8,128)(2,1)S(1)} %get-tuple-element.51.refs_0_, ...), custom_call_target="tpu_custom_call" | custom-call | flops 3221225472 | bytes 20971520 | tf_op jit(solution)/shard_map/sweep/pallas_call | solution.py:164
  131.0 0.1 collective-permute-start.15
  131.1 1.9 %collective-permute-done.15.theirs_ref = bf16[8,16,2048]{2,1,0:T(8,128)(2,1)S(1)} collective-permute-done((bf16[8,16,2048]{2,1,0:T(8,128)(2,1)S(1)}, bf16[8,16,2048]{2,1,0:T(8,128)(2,1)S(1)}, u32[]{:S(2)}, u32[]{:S(2)}) %collective-permute-start.15) | collective-permute-done | bytes 524320 | tf_op jit(solution)/shard_map/ppermute | solution.py:245
  133.0 0.9 shard_map.81
  133.9 3.5 %all-to-all-start.4 = ((bf16[8,16,2048]{2,1,0:T(8,128)(2,1)}), bf16[8,16,2048]{2,1,0:T(8,128)(2,1)S(1)}, u32[]{:S(2)}, u32[]{:S(2)}) async-start(bf16[8,16,2048]{2,1,0:T(8,128)(2,1)} %shard_map.81), calls=%async_computation.4 | async-start | bytes 1048576 | tf_op jit(solution)/shard_map/all_to_all | solution.py:33
  137.5 3.2 %collective-permute-start.12 = (bf16[2,32,1024]{2,1,0:T(8,128)(2,1)S(1)}, bf16[2,32,1024]{2,1,0:T(8,128)(2,1)S(1)}, u32[]{:S(2)}, u32[]{:S(2)}) collective-permute-start(bf16[2,32,1024]{2,1,0:T(8,128)(2,1)S(1)} %get-tuple-element.58), channel_id=1, source_target_pairs={{0,6},{2,0},{4,2},{6,4},{1,7},{3,1},{5,3},{7,5},{8,14},{10,8},{12,... | collective-permute-start | bytes 393224 | tf_op jit(solution)/shard_map/ppermute | solution.py:37
  140.7 3.5 %collective-permute-done.11.b_ref = bf16[2,32,1024]{2,1,0:T(8,128)(2,1)S(1)} collective-permute-done((bf16[2,32,1024]{2,1,0:T(8,128)(2,1)S(1)}, bf16[2,32,1024]{2,1,0:T(8,128)(2,1)S(1)}, u32[]{:S(2)}, u32[]{:S(2)}) %collective-permute-start.11) | collective-permute-done | bytes 131104 | tf_op jit(solution)/shard_map/ppermute | solution.py:37
  144.2 2.1 %collective-permute-done.12.c_ref = bf16[2,32,1024]{2,1,0:T(8,128)(2,1)S(1)} collective-permute-done((bf16[2,32,1024]{2,1,0:T(8,128)(2,1)S(1)}, bf16[2,32,1024]{2,1,0:T(8,128)(2,1)S(1)}, u32[]{:S(2)}, u32[]{:S(2)}) %collective-permute-start.12) | collective-permute-done | bytes 131104 | tf_op jit(solution)/shard_map/ppermute | solution.py:37
  146.3 0.9 collective-permute-done.13.d_ref
  147.3 0.6 collective-permute-start.14
  147.9 3.7 %collective-permute-done.14.came_ref = bf16[32,1024]{1,0:T(8,128)(2,1)S(1)} collective-permute-done((bf16[32,1024]{1,0:T(8,128)(2,1)S(1)}, bf16[32,1024]{1,0:T(8,128)(2,1)S(1)}, u32[]{:S(2)}, u32[]{:S(2)}) %collective-permute-start.14) | collective-permute-done | bytes 65568 | tf_op jit(solution)/shard_map/ppermute | solution.py:251
  151.6 0.8 shard_map.80
  152.4 1.0 shard_map.82
  (19 shorter events, 0.3 us)
Async XLA Ops:
  0.6 4.1 %copy-start.1 = (f32[32,1024]{1,0:T(8,128)S(1)}, f32[32,1024]{1,0:T(8,128)}, u32[]{:S(2)}) copy-start(f32[32,1024]{1,0:T(8,128)} %emb_ref.6) | copy-start | bytes 393220
  5.7 17.9 %all-to-all-start = ((bf16[8,40,1024]{2,1,0:T(8,128)(2,1)}), bf16[8,40,1024]{2,1,0:T(8,128)(2,1)S(1)}, u32[]{:S(2)}, u32[]{:S(2)}) async-start(bf16[8,40,1024]{2,1,0:T(8,128)(2,1)} %shard_map.68), calls=%async_computation | async-start | bytes 1310720 | tf_op jit(solution)/shard_map/all_to_all | solution.py:33
  12.1 11.5 %copy-start = (f32[16,2048]{1,0:T(8,128)S(1)}, f32[16,2048]{1,0:T(8,128)}, u32[]{:S(2)}) copy-start(f32[16,2048]{1,0:T(8,128)} %emb_ref.7) | copy-start | bytes 393220
  24.7 18.9 %all-to-all-start.1 = ((bf16[8,24,2048]{2,1,0:T(8,128)(2,1)}), bf16[8,24,2048]{2,1,0:T(8,128)(2,1)S(1)}, u32[]{:S(2)}, u32[]{:S(2)}) async-start(bf16[8,24,2048]{2,1,0:T(8,128)(2,1)} %get-tuple-element.39), calls=%async_computation.1 | async-start | bytes 1572864 | tf_op jit(solution)/shard_map/all_to_all | solution.py:33
  43.6 2.3 %collective-permute-start = (bf16[8,24,2048]{2,1,0:T(8,128)(2,1)S(1)}, bf16[8,24,2048]{2,1,0:T(8,128)(2,1)S(1)}, u32[]{:S(2)}, u32[]{:S(2)}) collective-permute-start(bf16[8,24,2048]{2,1,0:T(8,128)(2,1)S(1)} %all-to-all-done.1.mine_ref.refs_2_), channel_id=1, source_target_pairs={{0,8},{8,0},{1,9},{9,1},{2,10},{10,2},{3,11},{11,3},{4,12},{12,4},... | collective-permute-start | bytes 2359304 | tf_op jit(solution)/shard_map/ppermute | solution.py:240
  46.1 30.0 %copy-start.3 = (f32[16,2048]{1,0:T(8,128)S(1)}, f32[16,2048]{1,0:T(8,128)}, u32[]{:S(2)}) copy-start(f32[16,2048]{1,0:T(8,128)} %accum_ref.3) | copy-start | bytes 393220
  46.1 58.3 %copy-start.2 = (f32[32,1024]{1,0:T(8,128)S(1)}, f32[32,1024]{1,0:T(8,128)}, u32[]{:S(2)}) copy-start(f32[32,1024]{1,0:T(8,128)} %accum_ref.2) | copy-start | bytes 393220
  57.5 2.0 %collective-permute-start.9 = (bf16[8,16,2048]{2,1,0:T(8,128)(2,1)S(1)}, bf16[8,16,2048]{2,1,0:T(8,128)(2,1)S(1)}, u32[]{:S(2)}, u32[]{:S(2)}) collective-permute-start(bf16[8,16,2048]{2,1,0:T(8,128)(2,1)S(1)} %get-tuple-element.54), channel_id=1, source_target_pairs={{0,8},{8,0},{1,9},{9,1},{2,10},{10,2},{3,11},{11,3},{4,12},{12,4},... | collective-permute-start | bytes 1572872 | tf_op jit(solution)/shard_map/ppermute | solution.py:245
  89.9 29.7 %collective-permute-start.10 = (bf16[8,16,2048]{2,1,0:T(8,128)(2,1)S(1)}, bf16[8,16,2048]{2,1,0:T(8,128)(2,1)S(1)}, u32[]{:S(2)}, u32[]{:S(2)}) collective-permute-start(bf16[8,16,2048]{2,1,0:T(8,128)(2,1)S(1)} %all_to_all.26.refs_2_), channel_id=1, source_target_pairs={{0,8},{8,0},{1,9},{9,1},{2,10},{10,2},{3,11},{11,3},{4,12},{12,4},... | collective-permute-start | bytes 1572872 | tf_op jit(solution)/shard_map/ppermute | solution.py:262
  89.9 7.1 %collective-permute-start.1 = (bf16[2,32,1024]{2,1,0:T(8,128)(2,1)S(1)}, bf16[2,32,1024]{2,1,0:T(8,128)(2,1)S(1)}, u32[]{:S(2)}, u32[]{:S(2)}) collective-permute-start(bf16[2,32,1024]{2,1,0:T(8,128)(2,1)S(1)} %get-tuple-element.45), channel_id=1, source_target_pairs={{0,2},{2,4},{4,6},{6,0},{1,3},{3,5},{5,7},{7,1},{8,10},{10,12},{12... | collective-permute-start | bytes 393224 | tf_op jit(solution)/shard_map/ppermute | solution.py:37
  89.9 9.2 %collective-permute-start.2 = (bf16[2,32,1024]{2,1,0:T(8,128)(2,1)S(1)}, bf16[2,32,1024]{2,1,0:T(8,128)(2,1)S(1)}, u32[]{:S(2)}, u32[]{:S(2)}) collective-permute-start(bf16[2,32,1024]{2,1,0:T(8,128)(2,1)S(1)} %get-tuple-element.46), channel_id=1, source_target_pairs={{0,6},{2,0},{4,2},{6,4},{1,7},{3,1},{5,3},{7,5},{8,14},{10,8},{12,... | collective-permute-start | bytes 393224 | tf_op jit(solution)/shard_map/ppermute | solution.py:37
  93.1 6.9 %collective-permute-start.3 = (bf16[2,32,1024]{2,1,0:T(8,128)(2,1)S(1)}, bf16[2,32,1024]{2,1,0:T(8,128)(2,1)S(1)}, u32[]{:S(2)}, u32[]{:S(2)}) collective-permute-start(bf16[2,32,1024]{2,1,0:T(8,128)(2,1)S(1)} %get-tuple-element.47), channel_id=1, source_target_pairs={{0,4},{2,6},{4,0},{6,2},{1,5},{3,7},{5,1},{7,3},{8,12},{10,14},{12... | collective-permute-start | bytes 393224 | tf_op jit(solution)/shard_map/ppermute | solution.py:37
  100.1 4.3 %collective-permute-start.4 = (bf16[32,1024]{1,0:T(8,128)(2,1)S(1)}, bf16[32,1024]{1,0:T(8,128)(2,1)S(1)}, u32[]{:S(2)}, u32[]{:S(2)}) collective-permute-start(bf16[32,1024]{1,0:T(8,128)(2,1)S(1)} %get-tuple-element.49), channel_id=1, source_target_pairs={{0,1},{1,0},{2,3},{3,2},{4,5},{5,4},{6,7},{7,6},{8,9},{9,8},{10,11... | collective-permute-start | bytes 196616 | tf_op jit(solution)/shard_map/ppermute | solution.py:251
  104.5 4.3 %collective-permute-start.5 = (bf16[32,1024]{1,0:T(8,128)(2,1)S(1)}, bf16[32,1024]{1,0:T(8,128)(2,1)S(1)}, u32[]{:S(2)}, u32[]{:S(2)}) collective-permute-start(bf16[32,1024]{1,0:T(8,128)(2,1)S(1)} %get-tuple-element.50), channel_id=1, source_target_pairs={{0,1},{1,0},{2,3},{3,2},{4,5},{5,4},{6,7},{7,6},{8,9},{9,8},{10,11... | collective-permute-start | bytes 196616 | tf_op jit(solution)/shard_map/ppermute | solution.py:257
  108.9 6.8 %collective-permute-start.8 = (bf16[2,32,1024]{2,1,0:T(8,128)(2,1)S(1)}, bf16[2,32,1024]{2,1,0:T(8,128)(2,1)S(1)}, u32[]{:S(2)}, u32[]{:S(2)}) collective-permute-start(bf16[2,32,1024]{2,1,0:T(8,128)(2,1)S(1)} %pad_maximum_fusion.refs_0_), channel_id=1, source_target_pairs={{0,6},{2,0},{4,2},{6,4},{1,7},{3,1},{5,3},{7,5},{8,14},{10,8},{12,... | collective-permute-start | bytes 393224 | tf_op jit(solution)/shard_map/ppermute | solution.py:37
  111.7 6.6 %collective-permute-start.7 = (bf16[2,32,1024]{2,1,0:T(8,128)(2,1)S(1)}, bf16[2,32,1024]{2,1,0:T(8,128)(2,1)S(1)}, u32[]{:S(2)}, u32[]{:S(2)}) collective-permute-start(bf16[2,32,1024]{2,1,0:T(8,128)(2,1)S(1)} %pad_maximum_fusion.refs_0_), channel_id=1, source_target_pairs={{0,4},{2,6},{4,0},{6,2},{1,5},{3,7},{5,1},{7,3},{8,12},{10,14},{12... | collective-permute-start | bytes 393224 | tf_op jit(solution)/shard_map/ppermute | solution.py:37
  111.7 7.6 %collective-permute-start.6 = (bf16[2,32,1024]{2,1,0:T(8,128)(2,1)S(1)}, bf16[2,32,1024]{2,1,0:T(8,128)(2,1)S(1)}, u32[]{:S(2)}, u32[]{:S(2)}) collective-permute-start(bf16[2,32,1024]{2,1,0:T(8,128)(2,1)S(1)} %pad_maximum_fusion.refs_0_), channel_id=1, source_target_pairs={{0,2},{2,4},{4,6},{6,0},{1,3},{3,5},{5,7},{7,1},{8,10},{10,12},{12... | collective-permute-start | bytes 393224 | tf_op jit(solution)/shard_map/ppermute | solution.py:37
  131.0 2.0 %collective-permute-start.15 = (bf16[8,16,2048]{2,1,0:T(8,128)(2,1)S(1)}, bf16[8,16,2048]{2,1,0:T(8,128)(2,1)S(1)}, u32[]{:S(2)}, u32[]{:S(2)}) collective-permute-start(bf16[8,16,2048]{2,1,0:T(8,128)(2,1)S(1)} %get-tuple-element.66), channel_id=1, source_target_pairs={{0,8},{8,0},{1,9},{9,1},{2,10},{10,2},{3,11},{11,3},{4,12},{12,4},... | collective-permute-start | bytes 1572872 | tf_op jit(solution)/shard_map/ppermute | solution.py:245
  133.9 18.5 %all-to-all-start.4 = ((bf16[8,16,2048]{2,1,0:T(8,128)(2,1)}), bf16[8,16,2048]{2,1,0:T(8,128)(2,1)S(1)}, u32[]{:S(2)}, u32[]{:S(2)}) async-start(bf16[8,16,2048]{2,1,0:T(8,128)(2,1)} %shard_map.81), calls=%async_computation.4 | async-start | bytes 1048576 | tf_op jit(solution)/shard_map/all_to_all | solution.py:33
  137.4 6.8 %collective-permute-start.11 = (bf16[2,32,1024]{2,1,0:T(8,128)(2,1)S(1)}, bf16[2,32,1024]{2,1,0:T(8,128)(2,1)S(1)}, u32[]{:S(2)}, u32[]{:S(2)}) collective-permute-start(bf16[2,32,1024]{2,1,0:T(8,128)(2,1)S(1)} %get-tuple-element.57), channel_id=1, source_target_pairs={{0,2},{2,4},{4,6},{6,0},{1,3},{3,5},{5,7},{7,1},{8,10},{10,12},{12... | collective-permute-start | bytes 393224 | tf_op jit(solution)/shard_map/ppermute | solution.py:37
  137.5 8.8 %collective-permute-start.12 = (bf16[2,32,1024]{2,1,0:T(8,128)(2,1)S(1)}, bf16[2,32,1024]{2,1,0:T(8,128)(2,1)S(1)}, u32[]{:S(2)}, u32[]{:S(2)}) collective-permute-start(bf16[2,32,1024]{2,1,0:T(8,128)(2,1)S(1)} %get-tuple-element.58), channel_id=1, source_target_pairs={{0,6},{2,0},{4,2},{6,4},{1,7},{3,1},{5,3},{7,5},{8,14},{10,8},{12,... | collective-permute-start | bytes 393224 | tf_op jit(solution)/shard_map/ppermute | solution.py:37
  140.7 6.5 %collective-permute-start.13 = (bf16[2,32,1024]{2,1,0:T(8,128)(2,1)S(1)}, bf16[2,32,1024]{2,1,0:T(8,128)(2,1)S(1)}, u32[]{:S(2)}, u32[]{:S(2)}) collective-permute-start(bf16[2,32,1024]{2,1,0:T(8,128)(2,1)S(1)} %get-tuple-element.59), channel_id=1, source_target_pairs={{0,4},{2,6},{4,0},{6,2},{1,5},{3,7},{5,1},{7,3},{8,12},{10,14},{12... | collective-permute-start | bytes 393224 | tf_op jit(solution)/shard_map/ppermute | solution.py:37
  147.3 4.3 %collective-permute-start.14 = (bf16[32,1024]{1,0:T(8,128)(2,1)S(1)}, bf16[32,1024]{1,0:T(8,128)(2,1)S(1)}, u32[]{:S(2)}, u32[]{:S(2)}) collective-permute-start(bf16[32,1024]{1,0:T(8,128)(2,1)S(1)} %get-tuple-element.61), channel_id=1, source_target_pairs={{0,1},{1,0},{2,3},{3,2},{4,5},{5,4},{6,7},{7,6},{8,9},{9,8},{10,11... | collective-permute-start | bytes 196616 | tf_op jit(solution)/shard_map/ppermute | solution.py:251

commit v4 on v3

v4 whole, which is shorter than its diff:
```python
import jax
import jax.numpy as jnp
from jax import lax
from jax.experimental import pallas as pl
from jax.experimental.pallas import tpu as pltpu
from jax.sharding import Mesh, PartitionSpec as P


ROW = ("x", "yh", "c")
COL = ("z", "yl")
CHIPS = ("x", "yh")
AXES = (*ROW, *COL)
SIZES = (4, 2, 2, 4, 2)
SWAP = [(0, 1), (1, 0)]
D, BR, COLS = 256, 1024, 2048
TN, RC, BLOCK = 256, 256, 128
VMEM = pl.BlockSpec(memory_space=pltpu.VMEM)


def shape(dims, kind):
    return jax.ShapeDtypeStruct(dims, kind)


def cost(flops, moved):
    return pl.CostEstimate(flops=flops, bytes_accessed=moved, transcendentals=0)


def in_hbm(value):
    return pltpu.with_memory_space_constraint(value, pltpu.HBM)


def to_each(copies, axes):
    return lax.all_to_all(copies, axes, 0, 0, tiled=True)


def over_z(value, shift):
    return lax.ppermute(value, "z", [(at, (at + shift) % 4) for at in range(4)])


def rows_sum(ref, rows):
    total = ref[0, rows, :].astype(jnp.float32)
    for at in range(1, ref.shape[0]):
        total += ref[at, rows, :].astype(jnp.float32)
    return total


def prepared_kernel(counts_ref, out_ref):
    values = counts_ref[...].astype(jnp.float32).astype(jnp.bfloat16)
    for at in range(COLS // TN):
        out_ref[at] = values[:, at * TN : at * TN + TN]


def prepared(counts):
    return pl.pallas_call(
        prepared_kernel,
        grid=(BR // BLOCK,),
        out_shape=pltpu.HBM((COLS // TN, BR, TN), jnp.bfloat16),
        in_specs=[pl.BlockSpec((BLOCK, COLS), lambda at: (at, 0))],
        out_specs=pl.BlockSpec((COLS // TN, BLOCK, TN), lambda at: (0, at, 0)),
        compiler_params=pltpu.CompilerParams(vmem_limit_bytes=6 * 2**20),
        cost_estimate=cost(BR * COLS, 12 * 2**20),
        name="prepared",
    )(in_hbm(counts))


def first_kernel(row_emb_ref, row_sums_ref, col_emb_ref, col_sums_ref, row_ref, col_ref):
    sums = row_sums_ref[...]
    digits = [(sums & 127).astype(jnp.float32), ((sums >> 7) & 127).astype(jnp.float32), (sums >> 14).astype(jnp.float32)]
    rows = [row_emb_ref[...]] + digits + [jnp.zeros((5, BR), jnp.float32)]
    row_ref[...] = jnp.concatenate(rows).astype(jnp.bfloat16)
    sums = col_sums_ref[...]
    rows = [col_emb_ref[...], (sums & 255).astype(jnp.float32), (sums >> 8).astype(jnp.float32), jnp.zeros((6, COLS), jnp.float32)]
    parcel = jnp.concatenate(rows).astype(jnp.bfloat16)
    for at in range(8):
        col_ref[at] = parcel


def joined_first_kernel(own_ref, other_ref, out_ref):
    out_ref[:32] = own_ref[:32]
    out_ref[32:64] = other_ref[:32]
    out_ref[64:] = (own_ref[32:].astype(jnp.float32) + other_ref[32:].astype(jnp.float32)).astype(jnp.bfloat16)


def placed(row_refs, flat_ref, tall_ref):
    z, yl = lax.axis_index("z"), lax.axis_index("yl")
    for shift in range(4):
        for other in range(2):
            place = lax.rem(z + 4 - shift, 4) * 2 + lax.rem(yl + other, 2)
            flat_ref[pl.ds(place, 1)] = row_refs[shift][pl.ds(32 * other, 32), :][None]
    tall_ref[...] = (flat_ref[...].reshape(D, BR) * jnp.bfloat16(0.5)).T


def arranged_first_kernel(*refs):
    row_refs, (flat_ref, tall_ref, row_log_ref, total_ref) = refs[:4], refs[4:]
    placed(row_refs, flat_ref, tall_ref)
    digits = row_refs[0][64:, :].astype(jnp.float32)
    for ref in row_refs[1:]:
        digits += ref[64:, :].astype(jnp.float32)
    marg = digits[0:1] + 128.0 * digits[1:2] + 16384.0 * digits[2:3]
    total = jnp.sum(marg.astype(jnp.int32), axis=1, keepdims=True)
    lane = lax.broadcasted_iota(jnp.int32, (8, 128), 1)
    total = jnp.broadcast_to(total, (8, 128))
    parts = jnp.where(lane < 4, (total >> (8 * jnp.minimum(lane, 3))) & 255, 0)
    parcel = parts.astype(jnp.float32).astype(jnp.bfloat16)
    for at in range(16):
        total_ref[at] = parcel
    logs = 0.5 * jnp.log(marg)
    for at in range(BR // 128):
        here = slice(at * 128, at * 128 + 128)
        row_log_ref[here, :] = jnp.broadcast_to(logs[:, here], (128, 128)).T


def arranged_kernel(*refs):
    placed(refs[:4], refs[4], refs[5])


def col_log_kernel(mine_ref, theirs_ref, out_ref):
    digits = rows_sum(mine_ref, slice(16, 24)) + rows_sum(theirs_ref, slice(16, 24))
    out_ref[...] = 0.5 * jnp.log(digits[0:1] + 256.0 * digits[1:2])


def sweep_kernel(row_flat, row_tall, mine_ref, theirs_ref, row_log_ref, col_log_ref, total_ref, counts_ref, *refs):
    outs, home_out, away_out = refs[:4], refs[4], refs[5]
    col_flat, col_tall, grads, turned, counts, arrived = refs[6:]
    copies = [pltpu.make_async_copy(counts_ref.at[at], counts.at[at], arrived.at[at]) for at in range(COLS // TN)]
    for copy in copies:
        copy.start()
    core, z, yl = lax.axis_index("c"), lax.axis_index("z"), lax.axis_index("yl")
    col_flat[:, pl.ds(core, 1)] = mine_ref[:, :16, :][:, None]
    col_flat[:, pl.ds(1 - core, 1)] = theirs_ref[:, :16, :][:, None]
    lane = lax.broadcasted_iota(jnp.int32, (1, 128), 1)
    scale = jnp.where(lane == 0, 1.0, jnp.where(lane == 1, 256.0, jnp.where(lane == 2, 65536.0, 16777216.0)))
    parts = rows_sum(total_ref, slice(0, 8))[0:1]
    total = jnp.sum(jnp.where(lane < 4, parts * scale, 0.0), axis=1, keepdims=True)
    total_log = 0.5 * jnp.log(jnp.broadcast_to(total, (1, TN)))

    for at in range(COLS // TN):
        here = slice(at * TN, at * TN + TN)
        col = col_flat[:, :, :, here].reshape(D, TN)
        col_tall[here, :] = col.T
        shift = col_log_ref[:, here] - total_log
        copies[at].wait()
        for chunk in range(BR // RC):
            rows = slice(chunk * RC, chunk * RC + RC)
            scores = jnp.dot(row_tall[rows, :], col, preferred_element_type=jnp.float32)
            values = counts[at, rows, :].astype(jnp.float32)
            least = jnp.maximum(values, 1.0)
            errors = scores - 0.5 * jnp.log(least) + (shift + jnp.tile(row_log_ref[rows, :], (1, TN // 128)))
            weight = 0.2 + 0.5 * (least * lax.rsqrt(least))
            grad = jnp.where(values > 0.0, weight * errors, 0.5 * jnp.tanh(errors) + 0.5)
            grads[rows, here] = grad.astype(jnp.bfloat16)
    col_grad = jnp.dot(row_flat[...].reshape(D, BR), grads[...], preferred_element_type=jnp.float32).reshape(8, 2, 16, COLS)
    even, odd = col_grad[:, 0], col_grad[:, 1]
    home_out[...] = jnp.where(core == 0, even, odd)
    away_out[...] = jnp.where(core == 0, odd, even).astype(jnp.bfloat16)
    for chunk in range(BR // 256):
        rows = slice(chunk * 256, chunk * 256 + 256)
        part = jnp.dot(grads[rows, :], col_tall[...], preferred_element_type=jnp.float32)
        turned[:, :, rows] = part.astype(jnp.bfloat16).T.reshape(8, 32, 256)
    for shift in range(4):
        for other in range(2):
            place = lax.rem(z + shift, 4) * 2 + lax.rem(yl + other, 2)
            outs[shift][other : other + 1] = turned[pl.ds(place, 1)]


def swept(*args):
    return pl.pallas_call(
        sweep_kernel,
        out_shape=(shape((2, 32, BR), jnp.bfloat16),) * 4
        + (shape((8, 16, COLS), jnp.float32), shape((8, 16, COLS), jnp.bfloat16)),
        in_specs=[VMEM] * 7 + [pl.BlockSpec(memory_space=pltpu.HBM)],
        out_specs=(VMEM,) * 6,
        scratch_shapes=[
            pltpu.VMEM((8, 2, 16, COLS), jnp.bfloat16),
            pltpu.VMEM((COLS, D), jnp.bfloat16),
            pltpu.VMEM((BR, COLS), jnp.bfloat16),
            pltpu.VMEM((8, 32, BR), jnp.bfloat16),
            pltpu.VMEM((COLS // TN, BR, TN), jnp.bfloat16),
            pltpu.SemaphoreType.DMA((COLS // TN,)),
        ],
        compiler_params=pltpu.CompilerParams(vmem_limit_bytes=24 * 2**20),
        cost_estimate=cost(6 * D * BR * COLS, 20 * 2**20),
        name="sweep",
    )(*args)


def joined_kernel(own_ref, other_ref, out_ref):
    out_ref[:32] = own_ref[...]
    out_ref[32:] = other_ref[...]


def home_kernel(home_ref, theirs_ref, out_ref):
    out_ref[...] = (home_ref[...] + theirs_ref[...].astype(jnp.float32)).astype(jnp.bfloat16)


def z_kernel(a_ref, b_ref, c_ref, d_ref, keep_ref, send_ref):
    total = a_ref[...].astype(jnp.float32) + b_ref[...].astype(jnp.float32)
    total += c_ref[...].astype(jnp.float32) + d_ref[...].astype(jnp.float32)
    keep_ref[...] = total[0]
    send_ref[...] = total[1].astype(jnp.bfloat16)


def moved(emb_ref, accum_ref, grad):
    accum = accum_ref[...] + grad * grad
    return emb_ref[...] - 0.05 * grad / jnp.sqrt(accum), accum


def row_kernel(keep_ref, came_ref, emb_ref, accum_ref, new_emb_ref, new_accum_ref, half_ref):
    emb, accum = moved(emb_ref, accum_ref, keep_ref[...] + came_ref[...].astype(jnp.float32))
    new_emb_ref[...] = emb
    new_accum_ref[...] = accum
    half_ref[...] = emb.astype(jnp.bfloat16)


def col_kernel(came_ref, emb_ref, accum_ref, new_emb_ref, new_accum_ref, half_ref):
    grad = came_ref[0].astype(jnp.float32)
    for at in range(1, 8):
        grad += came_ref[at].astype(jnp.float32)
    emb, accum = moved(emb_ref, accum_ref, grad)
    new_emb_ref[...] = emb
    new_accum_ref[...] = accum
    half = emb.astype(jnp.bfloat16)
    for at in range(8):
        half_ref[at] = half


def small(kernel, outs):
    return pl.pallas_call(
        kernel,
        out_shape=outs,
        compiler_params=pltpu.CompilerParams(vmem_limit_bytes=6 * 2**20),
        cost_estimate=cost(2**20, 2**20),
    )


def on_device(counts, row_emb, col_emb, row_accum, col_accum):
    row_sums = jnp.sum(counts, axis=1)[None]
    col_sums = jnp.sum(counts, axis=0)[None]
    outs = (shape((40, BR), jnp.bfloat16), shape((8, 24, COLS), jnp.bfloat16))
    parcel, copies = small(first_kernel, outs)(row_emb, row_sums, col_emb, col_sums)
    other = lax.ppermute(parcel, "yl", SWAP)
    mine = to_each(copies, CHIPS)
    pair = small(joined_first_kernel, shape((72, BR), jnp.bfloat16))(parcel, other)
    row = [pair, over_z(pair, 1), over_z(pair, 2), over_z(pair, 3)]
    outs = (shape((8, 32, BR), jnp.bfloat16), shape((BR, D), jnp.bfloat16), shape((BR, 128), jnp.float32), shape((16, 8, 128), jnp.bfloat16))
    *row, row_log, total = small(arranged_first_kernel, outs)(*row)
    theirs = lax.ppermute(mine, "c", SWAP)
    total = to_each(total, ROW)
    small_counts = prepared(counts)
    col_log = small(col_log_kernel, shape((1, COLS), jnp.float32))(mine, theirs)
    for sweep in range(2):
        *parts, home, away = swept(*row, mine, theirs, row_log, col_log, total, in_hbm(small_counts))
        theirs = lax.ppermute(away, "c", SWAP)
        far = over_z(parts[2], 2)
        both = small(home_kernel, shape((8, 16, COLS), jnp.bfloat16))(home, theirs)
        came = to_each(both, CHIPS)
        parts = [parts[0], far, over_z(parts[1], 1), over_z(parts[3], 3)]
        outs = (shape((32, BR), jnp.float32), shape((32, BR), jnp.bfloat16))
        keep, send = small(z_kernel, outs)(*parts)
        from_pair = lax.ppermute(send, "yl", SWAP)
        outs = (shape((32, BR), jnp.float32),) * 2 + (shape((32, BR), jnp.bfloat16),)
        row_emb, row_accum, half = small(row_kernel, outs)(keep, from_pair, row_emb, row_accum)
        outs = (shape((16, COLS), jnp.float32),) * 2 + (shape((8, 16, COLS), jnp.bfloat16),)
        col_emb, col_accum, copies = small(col_kernel, outs)(came, col_emb, col_accum)
        if sweep == 0:
            pair = lax.ppermute(half, "yl", SWAP)
            pair = small(joined_kernel, shape((64, BR), jnp.bfloat16))(half, pair)
            mine = to_each(copies, CHIPS)
            row = [pair, over_z(pair, 1), over_z(pair, 2), over_z(pair, 3)]
            outs = (shape((8, 32, BR), jnp.bfloat16), shape((BR, D), jnp.bfloat16))
            row = small(arranged_kernel, outs)(*row)
            theirs = lax.ppermute(mine, "c", SWAP)
    return row_emb, col_emb


def solution(mesh):
    fine = Mesh(mesh.devices.reshape(SIZES), AXES)
    tall, wide = P(ROW, COL), P(COL, ROW)
    return jax.shard_map(
        on_device,
        mesh=fine,
        in_specs=(tall, wide, tall, wide, tall),
        out_specs=(wide, tall),
        check_vma=False,
    )
```

time: 155 us -> 162 us (1.045)
  blocking collectives: 30.1 us -> 52.9 us
  Pallas kernels: 48.3 us -> 30.1 us
  waiting for transfers between devices: 41.3 us -> 45.8 us
  starting transfers between devices: 28.8 us -> 25.6 us
  local copies, waits for them, and re-layouts: 0.02 us -> 1.86 us
    all_to_all x2 -> x3, blocking collectives: 30.1 us -> 52.9 us  [to_each(): return lax.all_to_all(copies, axes, 0, 0, tiled=True)]
    pallas_call x8, Pallas kernels: 45 us -> 26.9 us  [the longest x2 18.1 us: swept(): pl.pallas_call(sweep_kernel, out_shape=(shape((2, 32, BR), jnp.bfloat16),...]
    all_to_all x3 -> x2, starting transfers between devices: 16.6 us -> 6.99 us  [to_each(): return lax.all_to_all(copies, axes, 0, 0, tiled=True)]
    ppermute x9 -> x12, waiting for transfers between devices: 19.7 us -> 27.4 us  [over_z(): return lax.ppermute(value, 'z', [(at, (at + shift) % 4) for at in range(4)])]
    ppermute x9 -> x12, starting transfers between devices: 10.6 us -> 15.2 us  [over_z(): return lax.ppermute(value, 'z', [(at, (at + shift) % 4) for at in range(4)])]
    ppermute x0 -> x1, waiting for transfers between devices: none -> 4.18 us  [on_device(): other = lax.ppermute(parcel, 'yl', SWAP)]
    all_to_all x3 -> x2, waiting for transfers between devices: 4.1 us -> 0.01 us  [to_each(): return lax.all_to_all(copies, axes, 0, 0, tiled=True)]
    ppermute x2, waiting for transfers between devices: 2.08 us -> 0.01 us  [on_device(): theirs = lax.ppermute(mine, 'c', SWAP)]
  transfers between devices with their start and end apart: 19 -> 22, of which waited for: 17 -> 16; matrix products, arithmetic and copies ran while one was open for 0% -> 0% of each run, Pallas kernels for 14% -> 6%
where the time goes in v4:
time: 162 us; the launch traced here: 161 us
  blocking collectives  52.9 us (33%)
  waiting for transfers between devices  45.8 us (28%)
  Pallas kernels  30.1 us (19%)
  starting transfers between devices  25.6 us (16%)
  other arithmetic  4.05 us (2%)
  local copies, waits for them, and re-layouts  1.86 us (1%)
    all_to_all x3, blocking collectives, to_each(): return lax.all_to_all(copies, axes, 0, 0, tiled=True)  52.9 us
    ppermute x12, waiting for transfers between devices, over_z(): return lax.ppermute(value, 'z', [(at, (at + shift) % 4) for at in range(4)])  27.4 us
    pallas_call x2, Pallas kernels, swept(): pl.pallas_call(sweep_kernel, out_shape=(shape((2, 32, BR), jnp.bfloat16),...  18.1 us
    ppermute x12, starting transfers between devices, over_z(): return lax.ppermute(value, 'z', [(at, (at + shift) % 4) for at in range(4)])  15.2 us
    pallas_call x1, Pallas kernels, prepared(): pl.pallas_call(prepared_kernel, grid=(BR // BLOCK,), out_shape=pltpu.HBM(...  7.77 us
    ppermute x2, waiting for transfers between devices, on_device(): from_pair = lax.ppermute(send, 'yl', SWAP)  7.19 us
    all_to_all x2, starting transfers between devices, to_each(): return lax.all_to_all(copies, axes, 0, 0, tiled=True)  6.99 us
    ppermute x1, waiting for transfers between devices, on_device(): other = lax.ppermute(parcel, 'yl', SWAP)  4.18 us
  transfers between devices with their start and end apart: 22, of which 16 were waited for; matrix products, arithmetic and copies ran while one was open for 0% of the time, Pallas kernels for 6%

profile of v4, /device:TPU:0, one launch (start us, length us, event | category | flops | bytes accessed | tf_op | source)
XLA Modules:
  0.0 161.1 jit_solution(7067888011591492235)
XLA Ops:
  0.6 4.1 %fusion = (s32[2048]{0:T(1024)S(1)}, s32[1024]{0:T(1024)S(1)}) fusion(s32[1024,2048]{1,0:T(8,128)} %counts_ref.1), kind=kLoop, calls=%fused_computation | loop fusion | flops 4191232 | bytes 8400896 | tf_op jit(solution)/shard_map/reduce_sum | solution.py:238
  4.8 20.9 %all_to_all.25.mine_ref = bf16[8,24,2048]{2,1,0:T(8,128)(2,1)S(1)} all-to-all(bf16[8,24,2048]{2,1,0:T(8,128)(2,1)S(1)} %get-tuple-element.37), channel_id=1, replica_groups=mesh['x'=4,'yh'=2,'c'=2,'z'=4,'yl'=2] {'x','yh'}, dimensions={0} | all-to-all | bytes 1572864 | tf_op jit(solution)/shard_map/all_to_all | solution.py:33
  25.7 0.7 collective-permute-start
  26.4 4.2 %collective-permute-done.other_ref = bf16[40,1024]{1,0:T(8,128)(2,1)S(1)} collective-permute-done((bf16[40,1024]{1,0:T(8,128)(2,1)S(1)}, bf16[40,1024]{1,0:T(8,128)(2,1)S(1)}, u32[]{:S(2)}, u32[]{:S(2)}) %collective-permute-start) | collective-permute-done | bytes 81952 | tf_op jit(solution)/shard_map/ppermute | solution.py:241
  30.6 4.1 %collective-permute-start.3 = (bf16[72,1024]{1,0:T(8,128)(2,1)S(1)}, bf16[72,1024]{1,0:T(8,128)(2,1)S(1)}, u32[]{:S(2)}, u32[]{:S(2)}) collective-permute-start(bf16[72,1024]{1,0:T(8,128)(2,1)S(1)} %shard_map.69.refs_0_), channel_id=1, source_target_pairs={{0,6},{2,0},{4,2},{6,4},{1,7},{3,1},{5,3},{7,5},{8,14},{10,8},{12,... | collective-permute-start | bytes 442376 | tf_op jit(solution)/shard_map/ppermute | solution.py:37
  34.7 1.3 collective-permute-start.1
  35.9 4.8 %collective-permute-done.3.refs_3_ = bf16[72,1024]{1,0:T(8,128)(2,1)S(1)} collective-permute-done((bf16[72,1024]{1,0:T(8,128)(2,1)S(1)}, bf16[72,1024]{1,0:T(8,128)(2,1)S(1)}, u32[]{:S(2)}, u32[]{:S(2)}) %collective-permute-start.3) | collective-permute-done | bytes 147488 | tf_op jit(solution)/shard_map/ppermute | solution.py:37
  40.7 2.1 %collective-permute-done.2.refs_2_ = bf16[72,1024]{1,0:T(8,128)(2,1)S(1)} collective-permute-done((bf16[72,1024]{1,0:T(8,128)(2,1)S(1)}, bf16[72,1024]{1,0:T(8,128)(2,1)S(1)}, u32[]{:S(2)}, u32[]{:S(2)}) %collective-permute-start.2) | collective-permute-done | bytes 147488 | tf_op jit(solution)/shard_map/ppermute | solution.py:37
  42.9 1.3 collective-permute-done.1.refs_1_
  44.2 0.7 shard_map.70
  44.9 0.8 copy-done.4
  45.7 3.5 %all-to-all-start.1 = ((bf16[16,8,128]{2,1,0:T(8,128)(2,1)}), bf16[16,8,128]{2,1,0:T(8,128)(2,1)S(1)}, u32[]{:S(2)}, u32[]{:S(2)}) async-start(bf16[16,8,128]{2,1,0:T(8,128)(2,1)} %get-tuple-element.39), calls=%async_computation.1 | async-start | bytes 65536 | tf_op jit(solution)/shard_map/all_to_all | solution.py:33
  49.2 7.8 %prepared.1.counts_ref = bf16[8,1024,256]{2,1,0:T(8,128)(2,1)} custom-call(s32[1024,2048]{1,0:T(8,128)} %counts_ref.1), custom_call_target="tpu_custom_call" | custom-call | flops 2097152 | bytes 12582912 | tf_op jit(solution)/shard_map/prepared/pallas_call | solution.py:54
  57.1 1.0 copy-done.5
  58.1 9.0 %sweep.2 = (bf16[2,32,1024]{2,1,0:T(8,128)(2,1)S(1)}, bf16[2,32,1024]{2,1,0:T(8,128)(2,1)S(1)}, bf16[2,32,1024]{2,1,0:T(8,128)(2,1)S(1)}, bf16[2,32,1024]{2,1,0:...) custom-call(bf16[8,32,1024]{2,1,0:T(8,128)(2,1)S(1)} %get-tuple-element.35.row_flat, ...), custom_call_target="tpu_custom_call" | custom-call | flops 3221225472 | bytes 20971520 | tf_op jit(solution)/shard_map/sweep/pallas_call | solution.py:167
  67.2 0.4 collective-permute-start.13
  67.6 1.6 %collective-permute-done.13.theirs_ref = bf16[8,16,2048]{2,1,0:T(8,128)(2,1)S(1)} collective-permute-done((bf16[8,16,2048]{2,1,0:T(8,128)(2,1)S(1)}, bf16[8,16,2048]{2,1,0:T(8,128)(2,1)S(1)}, u32[]{:S(2)}, u32[]{:S(2)}) %collective-permute-start.13) | collective-permute-done | bytes 524320 | tf_op jit(solution)/shard_map/ppermute | solution.py:253
  69.3 18.4 %all_to_all.26.came_ref = bf16[8,16,2048]{2,1,0:T(8,128)(2,1)S(1)} all-to-all(bf16[8,16,2048]{2,1,0:T(8,128)(2,1)S(1)} %shard_map.76), channel_id=1, replica_groups=mesh['x'=4,'yh'=2,'c'=2,'z'=4,'yl'=2] {'x','yh'}, dimensions={0} | all-to-all | bytes 1048576 | tf_op jit(solution)/shard_map/all_to_all | solution.py:33
  87.8 13.6 %all_to_all.27.mine_ref = bf16[8,16,2048]{2,1,0:T(8,128)(2,1)S(1)} all-to-all(bf16[8,16,2048]{2,1,0:T(8,128)(2,1)S(1)} %get-tuple-element.51), channel_id=1, replica_groups=mesh['x'=4,'yh'=2,'c'=2,'z'=4,'yl'=2] {'x','yh'}, dimensions={0} | all-to-all | bytes 1048576 | tf_op jit(solution)/shard_map/all_to_all | solution.py:33
  101.4 0.6 collective-permute-start.5
  102.0 1.2 collective-permute-start.6
  103.2 2.1 %collective-permute-start.7 = (bf16[2,32,1024]{2,1,0:T(8,128)(2,1)S(1)}, bf16[2,32,1024]{2,1,0:T(8,128)(2,1)S(1)}, u32[]{:S(2)}, u32[]{:S(2)}) collective-permute-start(bf16[2,32,1024]{2,1,0:T(8,128)(2,1)S(1)} %get-tuple-element.43), channel_id=1, source_target_pairs={{0,6},{2,0},{4,2},{6,4},{1,7},{3,1},{5,3},{7,5},{8,14},{10,8},{12,... | collective-permute-start | bytes 393224 | tf_op jit(solution)/shard_map/ppermute | solution.py:37
  105.3 4.1 %collective-permute-done.5.b_ref = bf16[2,32,1024]{2,1,0:T(8,128)(2,1)S(1)} collective-permute-done((bf16[2,32,1024]{2,1,0:T(8,128)(2,1)S(1)}, bf16[2,32,1024]{2,1,0:T(8,128)(2,1)S(1)}, u32[]{:S(2)}, u32[]{:S(2)}) %collective-permute-start.5) | collective-permute-done | bytes 131104 | tf_op jit(solution)/shard_map/ppermute | solution.py:37
  109.4 2.3 %collective-permute-done.6.c_ref = bf16[2,32,1024]{2,1,0:T(8,128)(2,1)S(1)} collective-permute-done((bf16[2,32,1024]{2,1,0:T(8,128)(2,1)S(1)}, bf16[2,32,1024]{2,1,0:T(8,128)(2,1)S(1)}, u32[]{:S(2)}, u32[]{:S(2)}) %collective-permute-start.6) | collective-permute-done | bytes 131104 | tf_op jit(solution)/shard_map/ppermute | solution.py:37
  111.7 0.8 collective-permute-start.8
  112.5 3.6 %collective-permute-done.8.came_ref = bf16[32,1024]{1,0:T(8,128)(2,1)S(1)} collective-permute-done((bf16[32,1024]{1,0:T(8,128)(2,1)S(1)}, bf16[32,1024]{1,0:T(8,128)(2,1)S(1)}, u32[]{:S(2)}, u32[]{:S(2)}) %collective-permute-start.8) | collective-permute-done | bytes 65568 | tf_op jit(solution)/shard_map/ppermute | solution.py:260
  116.2 0.8 collective-permute-start.9
  116.9 3.6 %collective-permute-done.9.other_ref = bf16[32,1024]{1,0:T(8,128)(2,1)S(1)} collective-permute-done((bf16[32,1024]{1,0:T(8,128)(2,1)S(1)}, bf16[32,1024]{1,0:T(8,128)(2,1)S(1)}, u32[]{:S(2)}, u32[]{:S(2)}) %collective-permute-start.9) | collective-permute-done | bytes 65568 | tf_op jit(solution)/shard_map/ppermute | solution.py:266
  120.5 1.0 collective-permute-start.12
  121.5 0.3 collective-permute-start.11
  121.7 0.9 collective-permute-start.10
  122.6 2.9 %collective-permute-done.12.refs_3_ = bf16[64,1024]{1,0:T(8,128)(2,1)S(1)} collective-permute-done((bf16[64,1024]{1,0:T(8,128)(2,1)S(1)}, bf16[64,1024]{1,0:T(8,128)(2,1)S(1)}, u32[]{:S(2)}, u32[]{:S(2)}) %collective-permute-start.12) | collective-permute-done | bytes 131104 | tf_op jit(solution)/shard_map/ppermute | solution.py:37
  125.6 2.5 %collective-permute-done.11.refs_2_ = bf16[64,1024]{1,0:T(8,128)(2,1)S(1)} collective-permute-done((bf16[64,1024]{1,0:T(8,128)(2,1)S(1)}, bf16[64,1024]{1,0:T(8,128)(2,1)S(1)}, u32[]{:S(2)}, u32[]{:S(2)}) %collective-permute-start.11) | collective-permute-done | bytes 131104 | tf_op jit(solution)/shard_map/ppermute | solution.py:37
  128.1 1.3 collective-permute-done.10.refs_1_
  129.4 0.2 shard_map.75
  129.6 9.0 %sweep.3 = (bf16[2,32,1024]{2,1,0:T(8,128)(2,1)S(1)}, bf16[2,32,1024]{2,1,0:T(8,128)(2,1)S(1)}, bf16[2,32,1024]{2,1,0:T(8,128)(2,1)S(1)}, bf16[2,32,1024]{2,1,0:...) custom-call(bf16[8,32,1024]{2,1,0:T(8,128)(2,1)S(1)} %get-tuple-element.47.row_flat, ...), custom_call_target="tpu_custom_call" | custom-call | flops 3221225472 | bytes 20971520 | tf_op jit(solution)/shard_map/sweep/pallas_call | solution.py:167
  138.8 1.9 %collective-permute-done.19.theirs_ref = bf16[8,16,2048]{2,1,0:T(8,128)(2,1)S(1)} collective-permute-done((bf16[8,16,2048]{2,1,0:T(8,128)(2,1)S(1)}, bf16[8,16,2048]{2,1,0:T(8,128)(2,1)S(1)}, u32[]{:S(2)}, u32[]{:S(2)}) %collective-permute-start.19) | collective-permute-done | bytes 524320 | tf_op jit(solution)/shard_map/ppermute | solution.py:253
  140.6 0.9 shard_map.80
  141.6 3.5 %all-to-all-start.4 = ((bf16[8,16,2048]{2,1,0:T(8,128)(2,1)}), bf16[8,16,2048]{2,1,0:T(8,128)(2,1)S(1)}, u32[]{:S(2)}, u32[]{:S(2)}) async-start(bf16[8,16,2048]{2,1,0:T(8,128)(2,1)} %shard_map.80), calls=%async_computation.4 | async-start | bytes 1048576 | tf_op jit(solution)/shard_map/all_to_all | solution.py:33
  145.1 0.7 collective-permute-start.15
  145.8 1.1 collective-permute-start.16
  146.9 2.1 %collective-permute-start.17 = (bf16[2,32,1024]{2,1,0:T(8,128)(2,1)S(1)}, bf16[2,32,1024]{2,1,0:T(8,128)(2,1)S(1)}, u32[]{:S(2)}, u32[]{:S(2)}) collective-permute-start(bf16[2,32,1024]{2,1,0:T(8,128)(2,1)S(1)} %get-tuple-element.55), channel_id=1, source_target_pairs={{0,6},{2,0},{4,2},{6,4},{1,7},{3,1},{5,3},{7,5},{8,14},{10,8},{12,... | collective-permute-start | bytes 393224 | tf_op jit(solution)/shard_map/ppermute | solution.py:37
  149.0 4.1 %collective-permute-done.15.b_ref = bf16[2,32,1024]{2,1,0:T(8,128)(2,1)S(1)} collective-permute-done((bf16[2,32,1024]{2,1,0:T(8,128)(2,1)S(1)}, bf16[2,32,1024]{2,1,0:T(8,128)(2,1)S(1)}, u32[]{:S(2)}, u32[]{:S(2)}) %collective-permute-start.15) | collective-permute-done | bytes 131104 | tf_op jit(solution)/shard_map/ppermute | solution.py:37
  153.1 1.9 %collective-permute-done.16.c_ref = bf16[2,32,1024]{2,1,0:T(8,128)(2,1)S(1)} collective-permute-done((bf16[2,32,1024]{2,1,0:T(8,128)(2,1)S(1)}, bf16[2,32,1024]{2,1,0:T(8,128)(2,1)S(1)}, u32[]{:S(2)}, u32[]{:S(2)}) %collective-permute-start.16) | collective-permute-done | bytes 131104 | tf_op jit(solution)/shard_map/ppermute | solution.py:37
  155.1 0.7 collective-permute-start.18
  155.8 3.6 %collective-permute-done.18.came_ref = bf16[32,1024]{1,0:T(8,128)(2,1)S(1)} collective-permute-done((bf16[32,1024]{1,0:T(8,128)(2,1)S(1)}, bf16[32,1024]{1,0:T(8,128)(2,1)S(1)}, u32[]{:S(2)}, u32[]{:S(2)}) %collective-permute-start.18) | collective-permute-done | bytes 65568 | tf_op jit(solution)/shard_map/ppermute | solution.py:260
  159.4 0.7 shard_map.79
  160.2 1.0 shard_map.81
  (29 shorter events, 0.8 us)
Async XLA Ops:
  0.6 4.1 %copy-start.1 = (f32[16,2048]{1,0:T(8,128)S(1)}, f32[16,2048]{1,0:T(8,128)}, u32[]{:S(2)}) copy-start(f32[16,2048]{1,0:T(8,128)} %emb_ref.3) | copy-start | bytes 393220
  0.6 4.1 %copy-start = (f32[32,1024]{1,0:T(8,128)S(1)}, f32[32,1024]{1,0:T(8,128)}, u32[]{:S(2)}) copy-start(f32[32,1024]{1,0:T(8,128)} %emb_ref.2) | copy-start | bytes 393220
  25.7 31.3 %collective-permute-start.4 = (bf16[8,24,2048]{2,1,0:T(8,128)(2,1)S(1)}, bf16[8,24,2048]{2,1,0:T(8,128)(2,1)S(1)}, u32[]{:S(2)}, u32[]{:S(2)}) collective-permute-start(bf16[8,24,2048]{2,1,0:T(8,128)(2,1)S(1)} %all_to_all.25.mine_ref), channel_id=1, source_target_pairs={{0,8},{8,0},{1,9},{9,1},{2,10},{10,2},{3,11},{11,3},{4,12},{12,4},... | collective-permute-start | bytes 2359304 | tf_op jit(solution)/shard_map/ppermute | solution.py:247
  25.7 4.9 %collective-permute-start = (bf16[40,1024]{1,0:T(8,128)(2,1)S(1)}, bf16[40,1024]{1,0:T(8,128)(2,1)S(1)}, u32[]{:S(2)}, u32[]{:S(2)}) collective-permute-start(bf16[40,1024]{1,0:T(8,128)(2,1)S(1)} %get-tuple-element.34.own_ref), channel_id=1, source_target_pairs={{0,1},{1,0},{2,3},{3,2},{4,5},{5,4},{6,7},{7,6},{8,9},{9,8},{10,11... | collective-permute-start | bytes 245768 | tf_op jit(solution)/shard_map/ppermute | solution.py:241
  30.6 10.2 %collective-permute-start.3 = (bf16[72,1024]{1,0:T(8,128)(2,1)S(1)}, bf16[72,1024]{1,0:T(8,128)(2,1)S(1)}, u32[]{:S(2)}, u32[]{:S(2)}) collective-permute-start(bf16[72,1024]{1,0:T(8,128)(2,1)S(1)} %shard_map.69.refs_0_), channel_id=1, source_target_pairs={{0,6},{2,0},{4,2},{6,4},{1,7},{3,1},{5,3},{7,5},{8,14},{10,8},{12,... | collective-permute-start | bytes 442376 | tf_op jit(solution)/shard_map/ppermute | solution.py:37
  34.7 8.2 %collective-permute-start.2 = (bf16[72,1024]{1,0:T(8,128)(2,1)S(1)}, bf16[72,1024]{1,0:T(8,128)(2,1)S(1)}, u32[]{:S(2)}, u32[]{:S(2)}) collective-permute-start(bf16[72,1024]{1,0:T(8,128)(2,1)S(1)} %shard_map.69.refs_0_), channel_id=1, source_target_pairs={{0,4},{2,6},{4,0},{6,2},{1,5},{3,7},{5,1},{7,3},{8,12},{10,14},{12... | collective-permute-start | bytes 442376 | tf_op jit(solution)/shard_map/ppermute | solution.py:37
  34.7 9.5 %collective-permute-start.1 = (bf16[72,1024]{1,0:T(8,128)(2,1)S(1)}, bf16[72,1024]{1,0:T(8,128)(2,1)S(1)}, u32[]{:S(2)}, u32[]{:S(2)}) collective-permute-start(bf16[72,1024]{1,0:T(8,128)(2,1)S(1)} %shard_map.69.refs_0_), channel_id=1, source_target_pairs={{0,2},{2,4},{4,6},{6,0},{1,3},{3,5},{5,7},{7,1},{8,10},{10,12},{12... | collective-permute-start | bytes 442376 | tf_op jit(solution)/shard_map/ppermute | solution.py:37
  44.9 0.8 copy-start.4
  45.7 11.4 %all-to-all-start.1 = ((bf16[16,8,128]{2,1,0:T(8,128)(2,1)}), bf16[16,8,128]{2,1,0:T(8,128)(2,1)S(1)}, u32[]{:S(2)}, u32[]{:S(2)}) async-start(bf16[16,8,128]{2,1,0:T(8,128)(2,1)} %get-tuple-element.39), calls=%async_computation.1 | async-start | bytes 65536 | tf_op jit(solution)/shard_map/all_to_all | solution.py:33
  57.0 30.7 %copy-start.3 = (f32[16,2048]{1,0:T(8,128)S(1)}, f32[16,2048]{1,0:T(8,128)}, u32[]{:S(2)}) copy-start(f32[16,2048]{1,0:T(8,128)} %accum_ref.3) | copy-start | bytes 393220
  57.1 1.0 copy-start.5
  58.1 58.0 %copy-start.2 = (f32[32,1024]{1,0:T(8,128)S(1)}, f32[32,1024]{1,0:T(8,128)}, u32[]{:S(2)}) copy-start(f32[32,1024]{1,0:T(8,128)} %accum_ref.2) | copy-start | bytes 393220
  67.2 2.0 %collective-permute-start.13 = (bf16[8,16,2048]{2,1,0:T(8,128)(2,1)S(1)}, bf16[8,16,2048]{2,1,0:T(8,128)(2,1)S(1)}, u32[]{:S(2)}, u32[]{:S(2)}) collective-permute-start(bf16[8,16,2048]{2,1,0:T(8,128)(2,1)S(1)} %get-tuple-element.50), channel_id=1, source_target_pairs={{0,8},{8,0},{1,9},{9,1},{2,10},{10,2},{3,11},{11,3},{4,12},{12,4},... | collective-permute-start | bytes 1572872 | tf_op jit(solution)/shard_map/ppermute | solution.py:253
  101.4 28.2 %collective-permute-start.14 = (bf16[8,16,2048]{2,1,0:T(8,128)(2,1)S(1)}, bf16[8,16,2048]{2,1,0:T(8,128)(2,1)S(1)}, u32[]{:S(2)}, u32[]{:S(2)}) collective-permute-start(bf16[8,16,2048]{2,1,0:T(8,128)(2,1)S(1)} %all_to_all.27.mine_ref), channel_id=1, source_target_pairs={{0,8},{8,0},{1,9},{9,1},{2,10},{10,2},{3,11},{11,3},{4,12},{12,4},... | collective-permute-start | bytes 1572872 | tf_op jit(solution)/shard_map/ppermute | solution.py:272
  101.4 7.9 %collective-permute-start.5 = (bf16[2,32,1024]{2,1,0:T(8,128)(2,1)S(1)}, bf16[2,32,1024]{2,1,0:T(8,128)(2,1)S(1)}, u32[]{:S(2)}, u32[]{:S(2)}) collective-permute-start(bf16[2,32,1024]{2,1,0:T(8,128)(2,1)S(1)} %get-tuple-element.41), channel_id=1, source_target_pairs={{0,4},{2,6},{4,0},{6,2},{1,5},{3,7},{5,1},{7,3},{8,12},{10,14},{12... | collective-permute-start | bytes 393224 | tf_op jit(solution)/shard_map/ppermute | solution.py:37
  102.0 9.6 %collective-permute-start.6 = (bf16[2,32,1024]{2,1,0:T(8,128)(2,1)S(1)}, bf16[2,32,1024]{2,1,0:T(8,128)(2,1)S(1)}, u32[]{:S(2)}, u32[]{:S(2)}) collective-permute-start(bf16[2,32,1024]{2,1,0:T(8,128)(2,1)S(1)} %get-tuple-element.42), channel_id=1, source_target_pairs={{0,2},{2,4},{4,6},{6,0},{1,3},{3,5},{5,7},{7,1},{8,10},{10,12},{12... | collective-permute-start | bytes 393224 | tf_op jit(solution)/shard_map/ppermute | solution.py:37
  103.2 8.5 %collective-permute-start.7 = (bf16[2,32,1024]{2,1,0:T(8,128)(2,1)S(1)}, bf16[2,32,1024]{2,1,0:T(8,128)(2,1)S(1)}, u32[]{:S(2)}, u32[]{:S(2)}) collective-permute-start(bf16[2,32,1024]{2,1,0:T(8,128)(2,1)S(1)} %get-tuple-element.43), channel_id=1, source_target_pairs={{0,6},{2,0},{4,2},{6,4},{1,7},{3,1},{5,3},{7,5},{8,14},{10,8},{12,... | collective-permute-start | bytes 393224 | tf_op jit(solution)/shard_map/ppermute | solution.py:37
  111.7 4.3 %collective-permute-start.8 = (bf16[32,1024]{1,0:T(8,128)(2,1)S(1)}, bf16[32,1024]{1,0:T(8,128)(2,1)S(1)}, u32[]{:S(2)}, u32[]{:S(2)}) collective-permute-start(bf16[32,1024]{1,0:T(8,128)(2,1)S(1)} %get-tuple-element.45), channel_id=1, source_target_pairs={{0,1},{1,0},{2,3},{3,2},{4,5},{5,4},{6,7},{7,6},{8,9},{9,8},{10,11... | collective-permute-start | bytes 196616 | tf_op jit(solution)/shard_map/ppermute | solution.py:260
  116.2 4.3 %collective-permute-start.9 = (bf16[32,1024]{1,0:T(8,128)(2,1)S(1)}, bf16[32,1024]{1,0:T(8,128)(2,1)S(1)}, u32[]{:S(2)}, u32[]{:S(2)}) collective-permute-start(bf16[32,1024]{1,0:T(8,128)(2,1)S(1)} %get-tuple-element.46.own_ref), channel_id=1, source_target_pairs={{0,1},{1,0},{2,3},{3,2},{4,5},{5,4},{6,7},{7,6},{8,9},{9,8},{10,11... | collective-permute-start | bytes 196616 | tf_op jit(solution)/shard_map/ppermute | solution.py:266
  120.5 5.0 %collective-permute-start.12 = (bf16[64,1024]{1,0:T(8,128)(2,1)S(1)}, bf16[64,1024]{1,0:T(8,128)(2,1)S(1)}, u32[]{:S(2)}, u32[]{:S(2)}) collective-permute-start(bf16[64,1024]{1,0:T(8,128)(2,1)S(1)} %shard_map.74.refs_0_), channel_id=1, source_target_pairs={{0,6},{2,0},{4,2},{6,4},{1,7},{3,1},{5,3},{7,5},{8,14},{10,8},{12,... | collective-permute-start | bytes 393224 | tf_op jit(solution)/shard_map/ppermute | solution.py:37
  121.5 6.6 %collective-permute-start.11 = (bf16[64,1024]{1,0:T(8,128)(2,1)S(1)}, bf16[64,1024]{1,0:T(8,128)(2,1)S(1)}, u32[]{:S(2)}, u32[]{:S(2)}) collective-permute-start(bf16[64,1024]{1,0:T(8,128)(2,1)S(1)} %shard_map.74.refs_0_), channel_id=1, source_target_pairs={{0,4},{2,6},{4,0},{6,2},{1,5},{3,7},{5,1},{7,3},{8,12},{10,14},{12... | collective-permute-start | bytes 393224 | tf_op jit(solution)/shard_map/ppermute | solution.py:37
  121.7 7.6 %collective-permute-start.10 = (bf16[64,1024]{1,0:T(8,128)(2,1)S(1)}, bf16[64,1024]{1,0:T(8,128)(2,1)S(1)}, u32[]{:S(2)}, u32[]{:S(2)}) collective-permute-start(bf16[64,1024]{1,0:T(8,128)(2,1)S(1)} %shard_map.74.refs_0_), channel_id=1, source_target_pairs={{0,2},{2,4},{4,6},{6,0},{1,3},{3,5},{5,7},{7,1},{8,10},{10,12},{12... | collective-permute-start | bytes 393224 | tf_op jit(solution)/shard_map/ppermute | solution.py:37
  138.7 2.0 %collective-permute-start.19 = (bf16[8,16,2048]{2,1,0:T(8,128)(2,1)S(1)}, bf16[8,16,2048]{2,1,0:T(8,128)(2,1)S(1)}, u32[]{:S(2)}, u32[]{:S(2)}) collective-permute-start(bf16[8,16,2048]{2,1,0:T(8,128)(2,1)S(1)} %get-tuple-element.62), channel_id=1, source_target_pairs={{0,8},{8,0},{1,9},{9,1},{2,10},{10,2},{3,11},{11,3},{4,12},{12,4},... | collective-permute-start | bytes 1572872 | tf_op jit(solution)/shard_map/ppermute | solution.py:253
  141.6 18.6 %all-to-all-start.4 = ((bf16[8,16,2048]{2,1,0:T(8,128)(2,1)}), bf16[8,16,2048]{2,1,0:T(8,128)(2,1)S(1)}, u32[]{:S(2)}, u32[]{:S(2)}) async-start(bf16[8,16,2048]{2,1,0:T(8,128)(2,1)} %shard_map.80), calls=%async_computation.4 | async-start | bytes 1048576 | tf_op jit(solution)/shard_map/all_to_all | solution.py:33
  145.1 8.0 %collective-permute-start.15 = (bf16[2,32,1024]{2,1,0:T(8,128)(2,1)S(1)}, bf16[2,32,1024]{2,1,0:T(8,128)(2,1)S(1)}, u32[]{:S(2)}, u32[]{:S(2)}) collective-permute-start(bf16[2,32,1024]{2,1,0:T(8,128)(2,1)S(1)} %get-tuple-element.53), channel_id=1, source_target_pairs={{0,4},{2,6},{4,0},{6,2},{1,5},{3,7},{5,1},{7,3},{8,12},{10,14},{12... | collective-permute-start | bytes 393224 | tf_op jit(solution)/shard_map/ppermute | solution.py:37
  145.8 9.2 %collective-permute-start.16 = (bf16[2,32,1024]{2,1,0:T(8,128)(2,1)S(1)}, bf16[2,32,1024]{2,1,0:T(8,128)(2,1)S(1)}, u32[]{:S(2)}, u32[]{:S(2)}) collective-permute-start(bf16[2,32,1024]{2,1,0:T(8,128)(2,1)S(1)} %get-tuple-element.54), channel_id=1, source_target_pairs={{0,2},{2,4},{4,6},{6,0},{1,3},{3,5},{5,7},{7,1},{8,10},{10,12},{12... | collective-permute-start | bytes 393224 | tf_op jit(solution)/shard_map/ppermute | solution.py:37
  146.9 8.1 %collective-permute-start.17 = (bf16[2,32,1024]{2,1,0:T(8,128)(2,1)S(1)}, bf16[2,32,1024]{2,1,0:T(8,128)(2,1)S(1)}, u32[]{:S(2)}, u32[]{:S(2)}) collective-permute-start(bf16[2,32,1024]{2,1,0:T(8,128)(2,1)S(1)} %get-tuple-element.55), channel_id=1, source_target_pairs={{0,6},{2,0},{4,2},{6,4},{1,7},{3,1},{5,3},{7,5},{8,14},{10,8},{12,... | collective-permute-start | bytes 393224 | tf_op jit(solution)/shard_map/ppermute | solution.py:37
  155.1 4.3 %collective-permute-start.18 = (bf16[32,1024]{1,0:T(8,128)(2,1)S(1)}, bf16[32,1024]{1,0:T(8,128)(2,1)S(1)}, u32[]{:S(2)}, u32[]{:S(2)}) collective-permute-start(bf16[32,1024]{1,0:T(8,128)(2,1)S(1)} %get-tuple-element.57), channel_id=1, source_target_pairs={{0,1},{1,0},{2,3},{3,2},{4,5},{5,4},{6,7},{7,6},{8,9},{9,8},{10,11... | collective-permute-start | bytes 196616 | tf_op jit(solution)/shard_map/ppermute | solution.py:260

commit v5 on v4

--- a/solution.py
+++ b/solution.py
@@ -13,7 +13,7 @@
 SIZES = (4, 2, 2, 4, 2)
 SWAP = [(0, 1), (1, 0)]
 D, BR, COLS = 256, 1024, 2048
-TN, RC, BLOCK = 256, 256, 128
+TN, RC = 256, 256
 VMEM = pl.BlockSpec(memory_space=pltpu.VMEM)
 
 
@@ -42,25 +42,6 @@
     for at in range(1, ref.shape[0]):
         total += ref[at, rows, :].astype(jnp.float32)
     return total
-
-
-def prepared_kernel(counts_ref, out_ref):
-    values = counts_ref[...].astype(jnp.float32).astype(jnp.bfloat16)
-    for at in range(COLS // TN):
-        out_ref[at] = values[:, at * TN : at * TN + TN]
-
-
-def prepared(counts):
-    return pl.pallas_call(
-        prepared_kernel,
-        grid=(BR // BLOCK,),
-        out_shape=pltpu.HBM((COLS // TN, BR, TN), jnp.bfloat16),
-        in_specs=[pl.BlockSpec((BLOCK, COLS), lambda at: (at, 0))],
-        out_specs=pl.BlockSpec((COLS // TN, BLOCK, TN), lambda at: (0, at, 0)),
-        compiler_params=pltpu.CompilerParams(vmem_limit_bytes=6 * 2**20),
-        cost_estimate=cost(BR * COLS, 12 * 2**20),
-        name="prepared",
-    )(in_hbm(counts))
 
 
 def first_kernel(row_emb_ref, row_sums_ref, col_emb_ref, col_sums_ref, row_ref, col_ref):
@@ -81,18 +62,17 @@
     out_ref[64:] = (own_ref[32:].astype(jnp.float32) + other_ref[32:].astype(jnp.float32)).astype(jnp.bfloat16)
 
 
-def placed(row_refs, flat_ref, tall_ref):
+def placed(row_refs, flat_ref):
     z, yl = lax.axis_index("z"), lax.axis_index("yl")
     for shift in range(4):
         for other in range(2):
             place = lax.rem(z + 4 - shift, 4) * 2 + lax.rem(yl + other, 2)
             flat_ref[pl.ds(place, 1)] = row_refs[shift][pl.ds(32 * other, 32), :][None]
-    tall_ref[...] = (flat_ref[...].reshape(D, BR) * jnp.bfloat16(0.5)).T
 
 
 def arranged_first_kernel(*refs):
-    row_refs, (flat_ref, tall_ref, row_log_ref, total_ref) = refs[:4], refs[4:]
-    placed(row_refs, flat_ref, tall_ref)
+    row_refs, (flat_ref, row_log_ref, total_ref) = refs[:4], refs[4:]
+    placed(row_refs, flat_ref)
     digits = row_refs[0][64:, :].astype(jnp.float32)
     for ref in row_refs[1:]:
         digits += ref[64:, :].astype(jnp.float32)
@@ -104,14 +84,11 @@
     parcel = parts.astype(jnp.float32).astype(jnp.bfloat16)
     for at in range(16):
         total_ref[at] = parcel
-    logs = 0.5 * jnp.log(marg)
-    for at in range(BR // 128):
-        here = slice(at * 128, at * 128 + 128)
-        row_log_ref[here, :] = jnp.broadcast_to(logs[:, here], (128, 128)).T
+    row_log_ref[...] = 0.5 * jnp.log(marg)
 
 
 def arranged_kernel(*refs):
-    placed(refs[:4], refs[4], refs[5])
+    placed(refs[:4], refs[4])
 
 
 def col_log_kernel(mine_ref, theirs_ref, out_ref):
@@ -119,13 +96,17 @@
     out_ref[...] = 0.5 * jnp.log(digits[0:1] + 256.0 * digits[1:2])
 
 
-def sweep_kernel(row_flat, row_tall, mine_ref, theirs_ref, row_log_ref, col_log_ref, total_ref, counts_ref, *refs):
+def sweep_kernel(row_flat, mine_ref, theirs_ref, row_logs, col_log_ref, total_ref, counts_ref, *refs):
     outs, home_out, away_out = refs[:4], refs[4], refs[5]
-    col_flat, col_tall, grads, turned, counts, arrived = refs[6:]
-    copies = [pltpu.make_async_copy(counts_ref.at[at], counts.at[at], arrived.at[at]) for at in range(COLS // TN)]
+    col_flat, col_tall, grads, turned, counts, row_tall, row_log_ref, arrived = refs[6:]
+    copies = [pltpu.make_async_copy(counts_ref.at[:, pl.ds(at * TN, TN)], counts.at[at], arrived.at[at]) for at in range(COLS // TN)]
     for copy in copies:
         copy.start()
     core, z, yl = lax.axis_index("c"), lax.axis_index("z"), lax.axis_index("yl")
+    row_tall[...] = (row_flat[...].reshape(D, BR) * jnp.bfloat16(0.5)).T
+    for at in range(BR // 128):
+        here = slice(at * 128, at * 128 + 128)
+        row_log_ref[here, :] = jnp.broadcast_to(row_logs[:, here], (128, 128)).T
     col_flat[:, pl.ds(core, 1)] = mine_ref[:, :16, :][:, None]
     col_flat[:, pl.ds(1 - core, 1)] = theirs_ref[:, :16, :][:, None]
     lane = lax.broadcasted_iota(jnp.int32, (1, 128), 1)
@@ -168,17 +149,19 @@
         sweep_kernel,
         out_shape=(shape((2, 32, BR), jnp.bfloat16),) * 4
         + (shape((8, 16, COLS), jnp.float32), shape((8, 16, COLS), jnp.bfloat16)),
-        in_specs=[VMEM] * 7 + [pl.BlockSpec(memory_space=pltpu.HBM)],
+        in_specs=[VMEM] * 6 + [pl.BlockSpec(memory_space=pltpu.HBM)],
         out_specs=(VMEM,) * 6,
         scratch_shapes=[
             pltpu.VMEM((8, 2, 16, COLS), jnp.bfloat16),
             pltpu.VMEM((COLS, D), jnp.bfloat16),
             pltpu.VMEM((BR, COLS), jnp.bfloat16),
             pltpu.VMEM((8, 32, BR), jnp.bfloat16),
-            pltpu.VMEM((COLS // TN, BR, TN), jnp.bfloat16),
+            pltpu.VMEM((COLS // TN, BR, TN), jnp.int32),
+            pltpu.VMEM((BR, D), jnp.bfloat16),
+            pltpu.VMEM((BR, 128), jnp.float32),
             pltpu.SemaphoreType.DMA((COLS // TN,)),
         ],
-        compiler_params=pltpu.CompilerParams(vmem_limit_bytes=24 * 2**20),
+        compiler_params=pltpu.CompilerParams(vmem_limit_bytes=28 * 2**20),
         cost_estimate=cost(6 * D * BR * COLS, 20 * 2**20),
         name="sweep",
     )(*args)
@@ -242,19 +225,17 @@
     mine = to_each(copies, CHIPS)
     pair = small(joined_first_kernel, shape((72, BR), jnp.bfloat16))(parcel, other)
     row = [pair, over_z(pair, 1), over_z(pair, 2), over_z(pair, 3)]
-    outs = (shape((8, 32, BR), jnp.bfloat16), shape((BR, D), jnp.bfloat16), shape((BR, 128), jnp.float32), shape((16, 8, 128), jnp.bfloat16))
-    *row, row_log, total = small(arranged_first_kernel, outs)(*row)
+    outs = (shape((8, 32, BR), jnp.bfloat16), shape((1, BR), jnp.float32), shape((16, 8, 128), jnp.bfloat16))
+    row, row_log, total = small(arranged_first_kernel, outs)(*row)
     theirs = lax.ppermute(mine, "c", SWAP)
     total = to_each(total, ROW)
-    small_counts = prepared(counts)
     col_log = small(col_log_kernel, shape((1, COLS), jnp.float32))(mine, theirs)
     for sweep in range(2):
-        *parts, home, away = swept(*row, mine, theirs, row_log, col_log, total, in_hbm(small_counts))
+        *parts, home, away = swept(row, mine, theirs, row_log, col_log, total, in_hbm(counts))
         theirs = lax.ppermute(away, "c", SWAP)
-        far = over_z(parts[2], 2)
         both = small(home_kernel, shape((8, 16, COLS), jnp.bfloat16))(home, theirs)
         came = to_each(both, CHIPS)
-        parts = [parts[0], far, over_z(parts[1], 1), over_z(parts[3], 3)]
+        parts = parts[:1] + [over_z(parts[shift], shift) for shift in (2, 1, 3)]
         outs = (shape((32, BR), jnp.float32), shape((32, BR), jnp.bfloat16))
         keep, send = small(z_kernel, outs)(*parts)
         from_pair = lax.ppermute(send, "yl", SWAP)
@@ -267,8 +248,7 @@
             pair = small(joined_kernel, shape((64, BR), jnp.bfloat16))(half, pair)
             mine = to_each(copies, CHIPS)
             row = [pair, over_z(pair, 1), over_z(pair, 2), over_z(pair, 3)]
-            outs = (shape((8, 32, BR), jnp.bfloat16), shape((BR, D), jnp.bfloat16))
-            row = small(arranged_kernel, outs)(*row)
+            row = small(arranged_kernel, shape((8, 32, BR), jnp.bfloat16))(*row)
             theirs = lax.ppermute(mine, "c", SWAP)
     return row_emb, col_emb
 

time: 162 us -> 156 us (0.963)
  waiting for transfers between devices: 45.8 us -> 53.5 us
  Pallas kernels: 30.1 us -> 23.2 us
  blocking collectives: 52.9 us -> 48.7 us
  local copies, waits for them, and re-layouts: 1.86 us -> 0.02 us
    pallas_call x3 -> x2, Pallas kernels: 8.73 us -> 0.77 us  [the longest x1 0.72 us: on_device(): row, row_log, total = small(arranged_first_kernel, outs)(*row)]
    all_to_all x2, waiting for transfers between devices: 0.01 us -> 7.45 us  [to_each(): return lax.all_to_all(copies, axes, 0, 0, tiled=True)]
    all_to_all x3, blocking collectives: 52.9 us -> 48.7 us  [to_each(): return lax.all_to_all(copies, axes, 0, 0, tiled=True)]
    unnamed x12 -> x8, local copies, waits for them, and re-layouts: 1.86 us -> 0.02 us
  transfers between devices with their start and end apart: 22 -> 22, of which waited for: 16 -> 17; matrix products, arithmetic and copies ran while one was open for 0% -> 0% of each run, Pallas kernels for 6% -> 1%
where the time goes in v5:
time: 156 us
  waiting for transfers between devices  53.5 us (34%)
  blocking collectives  48.7 us (31%)
  starting transfers between devices  25.5 us (16%)
  Pallas kernels  23.2 us (15%)
  other arithmetic  4.05 us (3%)
    all_to_all x3, blocking collectives, to_each(): return lax.all_to_all(copies, axes, 0, 0, tiled=True)  48.7 us
    ppermute x12, waiting for transfers between devices, over_z(): return lax.ppermute(value, 'z', [(at, (at + shift) % 4) for at in range(4)])  27.4 us
    pallas_call x2, Pallas kernels, swept(): pl.pallas_call(sweep_kernel, out_shape=(shape((2, 32, BR), jnp.bfloat16),...  19.1 us
    ppermute x12, starting transfers between devices, over_z(): return lax.ppermute(value, 'z', [(at, (at + shift) % 4) for at in range(4)])  15.2 us
    all_to_all x2, waiting for transfers between devices, to_each(): return lax.all_to_all(copies, axes, 0, 0, tiled=True)  7.45 us
    ppermute x2, waiting for transfers between devices, on_device(): from_pair = lax.ppermute(send, 'yl', SWAP)  7.19 us
    all_to_all x2, starting transfers between devices, to_each(): return lax.all_to_all(copies, axes, 0, 0, tiled=True)  7.12 us
    ppermute x1, waiting for transfers between devices, on_device(): other = lax.ppermute(parcel, 'yl', SWAP)  4.18 us
  transfers between devices with their start and end apart: 22, of which 17 were waited for; matrix products, arithmetic and copies ran while one was open for 0% of the time, Pallas kernels for 1%

profile of v5, /device:TPU:0, one launch (start us, length us, event | category | flops | bytes accessed | tf_op | source)
XLA Modules:
  0.0 155.8 jit_solution(3947048595802101301)
XLA Ops:
  0.6 4.1 %fusion = (s32[2048]{0:T(1024)S(1)}, s32[1024]{0:T(1024)S(1)}) fusion(s32[1024,2048]{1,0:T(8,128)} %counts_ref.3), kind=kLoop, calls=%fused_computation | loop fusion | flops 4191232 | bytes 8400896 | tf_op jit(solution)/shard_map/reduce_sum | solution.py:221
  4.8 20.9 %all_to_all.25.mine_ref = bf16[8,24,2048]{2,1,0:T(8,128)(2,1)S(1)} all-to-all(bf16[8,24,2048]{2,1,0:T(8,128)(2,1)S(1)} %get-tuple-element.33), channel_id=1, replica_groups=mesh['x'=4,'yh'=2,'c'=2,'z'=4,'yl'=2] {'x','yh'}, dimensions={0} | all-to-all | bytes 1572864 | tf_op jit(solution)/shard_map/all_to_all | solution.py:33
  25.7 0.7 collective-permute-start
  26.4 4.2 %collective-permute-done.other_ref = bf16[40,1024]{1,0:T(8,128)(2,1)S(1)} collective-permute-done((bf16[40,1024]{1,0:T(8,128)(2,1)S(1)}, bf16[40,1024]{1,0:T(8,128)(2,1)S(1)}, u32[]{:S(2)}, u32[]{:S(2)}) %collective-permute-start) | collective-permute-done | bytes 81952 | tf_op jit(solution)/shard_map/ppermute | solution.py:224
  30.6 4.1 %collective-permute-start.3 = (bf16[72,1024]{1,0:T(8,128)(2,1)S(1)}, bf16[72,1024]{1,0:T(8,128)(2,1)S(1)}, u32[]{:S(2)}, u32[]{:S(2)}) collective-permute-start(bf16[72,1024]{1,0:T(8,128)(2,1)S(1)} %shard_map.69.refs_0_), channel_id=1, source_target_pairs={{0,6},{2,0},{4,2},{6,4},{1,7},{3,1},{5,3},{7,5},{8,14},{10,8},{12,... | collective-permute-start | bytes 442376 | tf_op jit(solution)/shard_map/ppermute | solution.py:37
  34.7 1.3 collective-permute-start.1
  35.9 4.8 %collective-permute-done.3.refs_3_ = bf16[72,1024]{1,0:T(8,128)(2,1)S(1)} collective-permute-done((bf16[72,1024]{1,0:T(8,128)(2,1)S(1)}, bf16[72,1024]{1,0:T(8,128)(2,1)S(1)}, u32[]{:S(2)}, u32[]{:S(2)}) %collective-permute-start.3) | collective-permute-done | bytes 147488 | tf_op jit(solution)/shard_map/ppermute | solution.py:37
  40.7 2.1 %collective-permute-done.2.refs_2_ = bf16[72,1024]{1,0:T(8,128)(2,1)S(1)} collective-permute-done((bf16[72,1024]{1,0:T(8,128)(2,1)S(1)}, bf16[72,1024]{1,0:T(8,128)(2,1)S(1)}, u32[]{:S(2)}, u32[]{:S(2)}) %collective-permute-start.2) | collective-permute-done | bytes 147488 | tf_op jit(solution)/shard_map/ppermute | solution.py:37
  42.9 1.3 collective-permute-done.1.refs_1_
  44.2 0.7 shard_map.70
  44.9 3.6 %all-to-all-start.1 = ((bf16[16,8,128]{2,1,0:T(8,128)(2,1)}), bf16[16,8,128]{2,1,0:T(8,128)(2,1)S(1)}, u32[]{:S(2)}, u32[]{:S(2)}) async-start(bf16[16,8,128]{2,1,0:T(8,128)(2,1)} %get-tuple-element.35), calls=%async_computation.1 | async-start | bytes 65536 | tf_op jit(solution)/shard_map/all_to_all | solution.py:33
  48.5 0.1 shard_map.71.col_log_ref
  48.6 7.4 %all-to-all-done.1.total_ref = bf16[16,8,128]{2,1,0:T(8,128)(2,1)S(1)} async-done(((bf16[16,8,128]{2,1,0:T(8,128)(2,1)}), bf16[16,8,128]{2,1,0:T(8,128)(2,1)S(1)}, u32[]{:S(2)}, u32[]{:S(2)}) %all-to-all-start.1) | async-done | bytes 32800 | tf_op jit(solution)/shard_map/all_to_all | solution.py:33
  56.1 9.6 %sweep.2 = (bf16[2,32,1024]{2,1,0:T(8,128)(2,1)S(1)}, bf16[2,32,1024]{2,1,0:T(8,128)(2,1)S(1)}, bf16[2,32,1024]{2,1,0:T(8,128)(2,1)S(1)}, bf16[2,32,1024]{2,1,0:...) custom-call(bf16[8,32,1024]{2,1,0:T(8,128)(2,1)S(1)} %get-tuple-element.32.row_flat, ...), custom_call_target="tpu_custom_call" | custom-call | flops 3221225472 | bytes 20971520 | tf_op jit(solution)/shard_map/sweep/pallas_call | solution.py:148
  65.7 0.2 collective-permute-start.13
  65.9 1.8 %collective-permute-done.13.theirs_ref = bf16[8,16,2048]{2,1,0:T(8,128)(2,1)S(1)} collective-permute-done((bf16[8,16,2048]{2,1,0:T(8,128)(2,1)S(1)}, bf16[8,16,2048]{2,1,0:T(8,128)(2,1)S(1)}, u32[]{:S(2)}, u32[]{:S(2)}) %collective-permute-start.13) | collective-permute-done | bytes 524320 | tf_op jit(solution)/shard_map/ppermute | solution.py:235
  67.6 0.1 shard_map.76
  67.8 14.2 %all_to_all.26.came_ref = bf16[8,16,2048]{2,1,0:T(8,128)(2,1)S(1)} all-to-all(bf16[8,16,2048]{2,1,0:T(8,128)(2,1)S(1)} %shard_map.76), channel_id=1, replica_groups=mesh['x'=4,'yh'=2,'c'=2,'z'=4,'yl'=2] {'x','yh'}, dimensions={0} | all-to-all | bytes 1048576 | tf_op jit(solution)/shard_map/all_to_all | solution.py:33
  82.0 0.1 shard_map.77
  82.2 13.6 %all_to_all.27.mine_ref = bf16[8,16,2048]{2,1,0:T(8,128)(2,1)S(1)} all-to-all(bf16[8,16,2048]{2,1,0:T(8,128)(2,1)S(1)} %get-tuple-element.45), channel_id=1, replica_groups=mesh['x'=4,'yh'=2,'c'=2,'z'=4,'yl'=2] {'x','yh'}, dimensions={0} | all-to-all | bytes 1048576 | tf_op jit(solution)/shard_map/all_to_all | solution.py:33
  95.7 0.6 collective-permute-start.5
  96.3 1.2 collective-permute-start.6
  97.5 2.0 %collective-permute-start.7 = (bf16[2,32,1024]{2,1,0:T(8,128)(2,1)S(1)}, bf16[2,32,1024]{2,1,0:T(8,128)(2,1)S(1)}, u32[]{:S(2)}, u32[]{:S(2)}) collective-permute-start(bf16[2,32,1024]{2,1,0:T(8,128)(2,1)S(1)} %get-tuple-element.39), channel_id=1, source_target_pairs={{0,6},{2,0},{4,2},{6,4},{1,7},{3,1},{5,3},{7,5},{8,14},{10,8},{12,... | collective-permute-start | bytes 393224 | tf_op jit(solution)/shard_map/ppermute | solution.py:37
  99.5 4.1 %collective-permute-done.5.b_ref = bf16[2,32,1024]{2,1,0:T(8,128)(2,1)S(1)} collective-permute-done((bf16[2,32,1024]{2,1,0:T(8,128)(2,1)S(1)}, bf16[2,32,1024]{2,1,0:T(8,128)(2,1)S(1)}, u32[]{:S(2)}, u32[]{:S(2)}) %collective-permute-start.5) | collective-permute-done | bytes 131104 | tf_op jit(solution)/shard_map/ppermute | solution.py:37
  103.6 2.3 %collective-permute-done.6.c_ref = bf16[2,32,1024]{2,1,0:T(8,128)(2,1)S(1)} collective-permute-done((bf16[2,32,1024]{2,1,0:T(8,128)(2,1)S(1)}, bf16[2,32,1024]{2,1,0:T(8,128)(2,1)S(1)}, u32[]{:S(2)}, u32[]{:S(2)}) %collective-permute-start.6) | collective-permute-done | bytes 131104 | tf_op jit(solution)/shard_map/ppermute | solution.py:37
  106.0 0.8 collective-permute-start.8
  106.8 3.6 %collective-permute-done.8.came_ref = bf16[32,1024]{1,0:T(8,128)(2,1)S(1)} collective-permute-done((bf16[32,1024]{1,0:T(8,128)(2,1)S(1)}, bf16[32,1024]{1,0:T(8,128)(2,1)S(1)}, u32[]{:S(2)}, u32[]{:S(2)}) %collective-permute-start.8) | collective-permute-done | bytes 65568 | tf_op jit(solution)/shard_map/ppermute | solution.py:241
  110.4 0.8 collective-permute-start.9
  111.2 3.6 %collective-permute-done.9.other_ref = bf16[32,1024]{1,0:T(8,128)(2,1)S(1)} collective-permute-done((bf16[32,1024]{1,0:T(8,128)(2,1)S(1)}, bf16[32,1024]{1,0:T(8,128)(2,1)S(1)}, u32[]{:S(2)}, u32[]{:S(2)}) %collective-permute-start.9) | collective-permute-done | bytes 65568 | tf_op jit(solution)/shard_map/ppermute | solution.py:247
  114.8 1.0 collective-permute-start.12
  115.8 0.2 collective-permute-start.11
  116.0 0.9 collective-permute-start.10
  116.9 2.9 %collective-permute-done.12.refs_3_ = bf16[64,1024]{1,0:T(8,128)(2,1)S(1)} collective-permute-done((bf16[64,1024]{1,0:T(8,128)(2,1)S(1)}, bf16[64,1024]{1,0:T(8,128)(2,1)S(1)}, u32[]{:S(2)}, u32[]{:S(2)}) %collective-permute-start.12) | collective-permute-done | bytes 131104 | tf_op jit(solution)/shard_map/ppermute | solution.py:37
  119.8 2.5 %collective-permute-done.11.refs_2_ = bf16[64,1024]{1,0:T(8,128)(2,1)S(1)} collective-permute-done((bf16[64,1024]{1,0:T(8,128)(2,1)S(1)}, bf16[64,1024]{1,0:T(8,128)(2,1)S(1)}, u32[]{:S(2)}, u32[]{:S(2)}) %collective-permute-start.11) | collective-permute-done | bytes 131104 | tf_op jit(solution)/shard_map/ppermute | solution.py:37
  122.4 1.3 collective-permute-done.10.refs_1_
  123.7 9.6 %sweep.3 = (bf16[2,32,1024]{2,1,0:T(8,128)(2,1)S(1)}, bf16[2,32,1024]{2,1,0:T(8,128)(2,1)S(1)}, bf16[2,32,1024]{2,1,0:T(8,128)(2,1)S(1)}, bf16[2,32,1024]{2,1,0:...) custom-call(bf16[8,32,1024]{2,1,0:T(8,128)(2,1)S(1)} %shard_map.75.row_flat, ...), custom_call_target="tpu_custom_call" | custom-call | flops 3221225472 | bytes 20971520 | tf_op jit(solution)/shard_map/sweep/pallas_call | solution.py:148
  133.4 1.9 %collective-permute-done.19.theirs_ref = bf16[8,16,2048]{2,1,0:T(8,128)(2,1)S(1)} collective-permute-done((bf16[8,16,2048]{2,1,0:T(8,128)(2,1)S(1)}, bf16[8,16,2048]{2,1,0:T(8,128)(2,1)S(1)}, u32[]{:S(2)}, u32[]{:S(2)}) %collective-permute-start.19) | collective-permute-done | bytes 524320 | tf_op jit(solution)/shard_map/ppermute | solution.py:235
  135.3 0.9 shard_map.80
  136.2 3.5 %all-to-all-start.4 = ((bf16[8,16,2048]{2,1,0:T(8,128)(2,1)}), bf16[8,16,2048]{2,1,0:T(8,128)(2,1)S(1)}, u32[]{:S(2)}, u32[]{:S(2)}) async-start(bf16[8,16,2048]{2,1,0:T(8,128)(2,1)} %shard_map.80), calls=%async_computation.4 | async-start | bytes 1048576 | tf_op jit(solution)/shard_map/all_to_all | solution.py:33
  139.7 0.7 collective-permute-start.15
  140.4 1.1 collective-permute-start.16
  141.5 2.1 %collective-permute-start.17 = (bf16[2,32,1024]{2,1,0:T(8,128)(2,1)S(1)}, bf16[2,32,1024]{2,1,0:T(8,128)(2,1)S(1)}, u32[]{:S(2)}, u32[]{:S(2)}) collective-permute-start(bf16[2,32,1024]{2,1,0:T(8,128)(2,1)S(1)} %get-tuple-element.49), channel_id=1, source_target_pairs={{0,6},{2,0},{4,2},{6,4},{1,7},{3,1},{5,3},{7,5},{8,14},{10,8},{12,... | collective-permute-start | bytes 393224 | tf_op jit(solution)/shard_map/ppermute | solution.py:37
  143.6 4.1 %collective-permute-done.15.b_ref = bf16[2,32,1024]{2,1,0:T(8,128)(2,1)S(1)} collective-permute-done((bf16[2,32,1024]{2,1,0:T(8,128)(2,1)S(1)}, bf16[2,32,1024]{2,1,0:T(8,128)(2,1)S(1)}, u32[]{:S(2)}, u32[]{:S(2)}) %collective-permute-start.15) | collective-permute-done | bytes 131104 | tf_op jit(solution)/shard_map/ppermute | solution.py:37
  147.7 1.9 %collective-permute-done.16.c_ref = bf16[2,32,1024]{2,1,0:T(8,128)(2,1)S(1)} collective-permute-done((bf16[2,32,1024]{2,1,0:T(8,128)(2,1)S(1)}, bf16[2,32,1024]{2,1,0:T(8,128)(2,1)S(1)}, u32[]{:S(2)}, u32[]{:S(2)}) %collective-permute-start.16) | collective-permute-done | bytes 131104 | tf_op jit(solution)/shard_map/ppermute | solution.py:37
  149.7 0.7 collective-permute-start.18
  150.4 3.6 %collective-permute-done.18.came_ref = bf16[32,1024]{1,0:T(8,128)(2,1)S(1)} collective-permute-done((bf16[32,1024]{1,0:T(8,128)(2,1)S(1)}, bf16[32,1024]{1,0:T(8,128)(2,1)S(1)}, u32[]{:S(2)}, u32[]{:S(2)}) %collective-permute-start.18) | collective-permute-done | bytes 65568 | tf_op jit(solution)/shard_map/ppermute | solution.py:241
  154.1 0.7 shard_map.79
  154.8 1.0 shard_map.81
  (24 shorter events, 0.5 us)
Async XLA Ops:
  0.6 4.1 %copy-start.1 = (f32[16,2048]{1,0:T(8,128)S(1)}, f32[16,2048]{1,0:T(8,128)}, u32[]{:S(2)}) copy-start(f32[16,2048]{1,0:T(8,128)} %emb_ref.3) | copy-start | bytes 393220
  0.6 4.1 %copy-start = (f32[32,1024]{1,0:T(8,128)S(1)}, f32[32,1024]{1,0:T(8,128)}, u32[]{:S(2)}) copy-start(f32[32,1024]{1,0:T(8,128)} %emb_ref.2) | copy-start | bytes 393220
  25.7 22.8 %collective-permute-start.4 = (bf16[8,24,2048]{2,1,0:T(8,128)(2,1)S(1)}, bf16[8,24,2048]{2,1,0:T(8,128)(2,1)S(1)}, u32[]{:S(2)}, u32[]{:S(2)}) collective-permute-start(bf16[8,24,2048]{2,1,0:T(8,128)(2,1)S(1)} %all_to_all.25.mine_ref), channel_id=1, source_target_pairs={{0,8},{8,0},{1,9},{9,1},{2,10},{10,2},{3,11},{11,3},{4,12},{12,4},... | collective-permute-start | bytes 2359304 | tf_op jit(solution)/shard_map/ppermute | solution.py:230
  25.7 4.9 %collective-permute-start = (bf16[40,1024]{1,0:T(8,128)(2,1)S(1)}, bf16[40,1024]{1,0:T(8,128)(2,1)S(1)}, u32[]{:S(2)}, u32[]{:S(2)}) collective-permute-start(bf16[40,1024]{1,0:T(8,128)(2,1)S(1)} %get-tuple-element.31.own_ref), channel_id=1, source_target_pairs={{0,1},{1,0},{2,3},{3,2},{4,5},{5,4},{6,7},{7,6},{8,9},{9,8},{10,11... | collective-permute-start | bytes 245768 | tf_op jit(solution)/shard_map/ppermute | solution.py:224
  30.6 10.2 %collective-permute-start.3 = (bf16[72,1024]{1,0:T(8,128)(2,1)S(1)}, bf16[72,1024]{1,0:T(8,128)(2,1)S(1)}, u32[]{:S(2)}, u32[]{:S(2)}) collective-permute-start(bf16[72,1024]{1,0:T(8,128)(2,1)S(1)} %shard_map.69.refs_0_), channel_id=1, source_target_pairs={{0,6},{2,0},{4,2},{6,4},{1,7},{3,1},{5,3},{7,5},{8,14},{10,8},{12,... | collective-permute-start | bytes 442376 | tf_op jit(solution)/shard_map/ppermute | solution.py:37
  34.7 8.2 %collective-permute-start.2 = (bf16[72,1024]{1,0:T(8,128)(2,1)S(1)}, bf16[72,1024]{1,0:T(8,128)(2,1)S(1)}, u32[]{:S(2)}, u32[]{:S(2)}) collective-permute-start(bf16[72,1024]{1,0:T(8,128)(2,1)S(1)} %shard_map.69.refs_0_), channel_id=1, source_target_pairs={{0,4},{2,6},{4,0},{6,2},{1,5},{3,7},{5,1},{7,3},{8,12},{10,14},{12... | collective-permute-start | bytes 442376 | tf_op jit(solution)/shard_map/ppermute | solution.py:37
  34.7 9.5 %collective-permute-start.1 = (bf16[72,1024]{1,0:T(8,128)(2,1)S(1)}, bf16[72,1024]{1,0:T(8,128)(2,1)S(1)}, u32[]{:S(2)}, u32[]{:S(2)}) collective-permute-start(bf16[72,1024]{1,0:T(8,128)(2,1)S(1)} %shard_map.69.refs_0_), channel_id=1, source_target_pairs={{0,2},{2,4},{4,6},{6,0},{1,3},{3,5},{5,7},{7,1},{8,10},{10,12},{12... | collective-permute-start | bytes 442376 | tf_op jit(solution)/shard_map/ppermute | solution.py:37
  44.9 37.1 %copy-start.3 = (f32[16,2048]{1,0:T(8,128)S(1)}, f32[16,2048]{1,0:T(8,128)}, u32[]{:S(2)}) copy-start(f32[16,2048]{1,0:T(8,128)} %accum_ref.3) | copy-start | bytes 393220
  44.9 11.2 %all-to-all-start.1 = ((bf16[16,8,128]{2,1,0:T(8,128)(2,1)}), bf16[16,8,128]{2,1,0:T(8,128)(2,1)S(1)}, u32[]{:S(2)}, u32[]{:S(2)}) async-start(bf16[16,8,128]{2,1,0:T(8,128)(2,1)} %get-tuple-element.35), calls=%async_computation.1 | async-start | bytes 65536 | tf_op jit(solution)/shard_map/all_to_all | solution.py:33
  56.1 54.3 %copy-start.2 = (f32[32,1024]{1,0:T(8,128)S(1)}, f32[32,1024]{1,0:T(8,128)}, u32[]{:S(2)}) copy-start(f32[32,1024]{1,0:T(8,128)} %accum_ref.2) | copy-start | bytes 393220
  65.7 2.0 %collective-permute-start.13 = (bf16[8,16,2048]{2,1,0:T(8,128)(2,1)S(1)}, bf16[8,16,2048]{2,1,0:T(8,128)(2,1)S(1)}, u32[]{:S(2)}, u32[]{:S(2)}) collective-permute-start(bf16[8,16,2048]{2,1,0:T(8,128)(2,1)S(1)} %get-tuple-element.44), channel_id=1, source_target_pairs={{0,8},{8,0},{1,9},{9,1},{2,10},{10,2},{3,11},{11,3},{4,12},{12,4},... | collective-permute-start | bytes 1572872 | tf_op jit(solution)/shard_map/ppermute | solution.py:235
  95.7 28.0 %collective-permute-start.14 = (bf16[8,16,2048]{2,1,0:T(8,128)(2,1)S(1)}, bf16[8,16,2048]{2,1,0:T(8,128)(2,1)S(1)}, u32[]{:S(2)}, u32[]{:S(2)}) collective-permute-start(bf16[8,16,2048]{2,1,0:T(8,128)(2,1)S(1)} %all_to_all.27.mine_ref), channel_id=1, source_target_pairs={{0,8},{8,0},{1,9},{9,1},{2,10},{10,2},{3,11},{11,3},{4,12},{12,4},... | collective-permute-start | bytes 1572872 | tf_op jit(solution)/shard_map/ppermute | solution.py:252
  95.7 7.9 %collective-permute-start.5 = (bf16[2,32,1024]{2,1,0:T(8,128)(2,1)S(1)}, bf16[2,32,1024]{2,1,0:T(8,128)(2,1)S(1)}, u32[]{:S(2)}, u32[]{:S(2)}) collective-permute-start(bf16[2,32,1024]{2,1,0:T(8,128)(2,1)S(1)} %get-tuple-element.37), channel_id=1, source_target_pairs={{0,4},{2,6},{4,0},{6,2},{1,5},{3,7},{5,1},{7,3},{8,12},{10,14},{12... | collective-permute-start | bytes 393224 | tf_op jit(solution)/shard_map/ppermute | solution.py:37
  96.3 9.6 %collective-permute-start.6 = (bf16[2,32,1024]{2,1,0:T(8,128)(2,1)S(1)}, bf16[2,32,1024]{2,1,0:T(8,128)(2,1)S(1)}, u32[]{:S(2)}, u32[]{:S(2)}) collective-permute-start(bf16[2,32,1024]{2,1,0:T(8,128)(2,1)S(1)} %get-tuple-element.38), channel_id=1, source_target_pairs={{0,2},{2,4},{4,6},{6,0},{1,3},{3,5},{5,7},{7,1},{8,10},{10,12},{12... | collective-permute-start | bytes 393224 | tf_op jit(solution)/shard_map/ppermute | solution.py:37
  97.5 8.5 %collective-permute-start.7 = (bf16[2,32,1024]{2,1,0:T(8,128)(2,1)S(1)}, bf16[2,32,1024]{2,1,0:T(8,128)(2,1)S(1)}, u32[]{:S(2)}, u32[]{:S(2)}) collective-permute-start(bf16[2,32,1024]{2,1,0:T(8,128)(2,1)S(1)} %get-tuple-element.39), channel_id=1, source_target_pairs={{0,6},{2,0},{4,2},{6,4},{1,7},{3,1},{5,3},{7,5},{8,14},{10,8},{12,... | collective-permute-start | bytes 393224 | tf_op jit(solution)/shard_map/ppermute | solution.py:37
  106.0 4.3 %collective-permute-start.8 = (bf16[32,1024]{1,0:T(8,128)(2,1)S(1)}, bf16[32,1024]{1,0:T(8,128)(2,1)S(1)}, u32[]{:S(2)}, u32[]{:S(2)}) collective-permute-start(bf16[32,1024]{1,0:T(8,128)(2,1)S(1)} %get-tuple-element.41), channel_id=1, source_target_pairs={{0,1},{1,0},{2,3},{3,2},{4,5},{5,4},{6,7},{7,6},{8,9},{9,8},{10,11... | collective-permute-start | bytes 196616 | tf_op jit(solution)/shard_map/ppermute | solution.py:241
  110.4 4.3 %collective-permute-start.9 = (bf16[32,1024]{1,0:T(8,128)(2,1)S(1)}, bf16[32,1024]{1,0:T(8,128)(2,1)S(1)}, u32[]{:S(2)}, u32[]{:S(2)}) collective-permute-start(bf16[32,1024]{1,0:T(8,128)(2,1)S(1)} %get-tuple-element.42.own_ref), channel_id=1, source_target_pairs={{0,1},{1,0},{2,3},{3,2},{4,5},{5,4},{6,7},{7,6},{8,9},{9,8},{10,11... | collective-permute-start | bytes 196616 | tf_op jit(solution)/shard_map/ppermute | solution.py:247
  114.8 5.0 %collective-permute-start.12 = (bf16[64,1024]{1,0:T(8,128)(2,1)S(1)}, bf16[64,1024]{1,0:T(8,128)(2,1)S(1)}, u32[]{:S(2)}, u32[]{:S(2)}) collective-permute-start(bf16[64,1024]{1,0:T(8,128)(2,1)S(1)} %shard_map.74.refs_0_), channel_id=1, source_target_pairs={{0,6},{2,0},{4,2},{6,4},{1,7},{3,1},{5,3},{7,5},{8,14},{10,8},{12,... | collective-permute-start | bytes 393224 | tf_op jit(solution)/shard_map/ppermute | solution.py:37
  115.8 6.6 %collective-permute-start.11 = (bf16[64,1024]{1,0:T(8,128)(2,1)S(1)}, bf16[64,1024]{1,0:T(8,128)(2,1)S(1)}, u32[]{:S(2)}, u32[]{:S(2)}) collective-permute-start(bf16[64,1024]{1,0:T(8,128)(2,1)S(1)} %shard_map.74.refs_0_), channel_id=1, source_target_pairs={{0,4},{2,6},{4,0},{6,2},{1,5},{3,7},{5,1},{7,3},{8,12},{10,14},{12... | collective-permute-start | bytes 393224 | tf_op jit(solution)/shard_map/ppermute | solution.py:37
  116.0 7.6 %collective-permute-start.10 = (bf16[64,1024]{1,0:T(8,128)(2,1)S(1)}, bf16[64,1024]{1,0:T(8,128)(2,1)S(1)}, u32[]{:S(2)}, u32[]{:S(2)}) collective-permute-start(bf16[64,1024]{1,0:T(8,128)(2,1)S(1)} %shard_map.74.refs_0_), channel_id=1, source_target_pairs={{0,2},{2,4},{4,6},{6,0},{1,3},{3,5},{5,7},{7,1},{8,10},{10,12},{12... | collective-permute-start | bytes 393224 | tf_op jit(solution)/shard_map/ppermute | solution.py:37
  133.3 2.0 %collective-permute-start.19 = (bf16[8,16,2048]{2,1,0:T(8,128)(2,1)S(1)}, bf16[8,16,2048]{2,1,0:T(8,128)(2,1)S(1)}, u32[]{:S(2)}, u32[]{:S(2)}) collective-permute-start(bf16[8,16,2048]{2,1,0:T(8,128)(2,1)S(1)} %get-tuple-element.56), channel_id=1, source_target_pairs={{0,8},{8,0},{1,9},{9,1},{2,10},{10,2},{3,11},{11,3},{4,12},{12,4},... | collective-permute-start | bytes 1572872 | tf_op jit(solution)/shard_map/ppermute | solution.py:235
  136.2 18.6 %all-to-all-start.4 = ((bf16[8,16,2048]{2,1,0:T(8,128)(2,1)}), bf16[8,16,2048]{2,1,0:T(8,128)(2,1)S(1)}, u32[]{:S(2)}, u32[]{:S(2)}) async-start(bf16[8,16,2048]{2,1,0:T(8,128)(2,1)} %shard_map.80), calls=%async_computation.4 | async-start | bytes 1048576 | tf_op jit(solution)/shard_map/all_to_all | solution.py:33
  139.7 8.0 %collective-permute-start.15 = (bf16[2,32,1024]{2,1,0:T(8,128)(2,1)S(1)}, bf16[2,32,1024]{2,1,0:T(8,128)(2,1)S(1)}, u32[]{:S(2)}, u32[]{:S(2)}) collective-permute-start(bf16[2,32,1024]{2,1,0:T(8,128)(2,1)S(1)} %get-tuple-element.47), channel_id=1, source_target_pairs={{0,4},{2,6},{4,0},{6,2},{1,5},{3,7},{5,1},{7,3},{8,12},{10,14},{12... | collective-permute-start | bytes 393224 | tf_op jit(solution)/shard_map/ppermute | solution.py:37
  140.4 9.2 %collective-permute-start.16 = (bf16[2,32,1024]{2,1,0:T(8,128)(2,1)S(1)}, bf16[2,32,1024]{2,1,0:T(8,128)(2,1)S(1)}, u32[]{:S(2)}, u32[]{:S(2)}) collective-permute-start(bf16[2,32,1024]{2,1,0:T(8,128)(2,1)S(1)} %get-tuple-element.48), channel_id=1, source_target_pairs={{0,2},{2,4},{4,6},{6,0},{1,3},{3,5},{5,7},{7,1},{8,10},{10,12},{12... | collective-permute-start | bytes 393224 | tf_op jit(solution)/shard_map/ppermute | solution.py:37
  141.5 8.1 %collective-permute-start.17 = (bf16[2,32,1024]{2,1,0:T(8,128)(2,1)S(1)}, bf16[2,32,1024]{2,1,0:T(8,128)(2,1)S(1)}, u32[]{:S(2)}, u32[]{:S(2)}) collective-permute-start(bf16[2,32,1024]{2,1,0:T(8,128)(2,1)S(1)} %get-tuple-element.49), channel_id=1, source_target_pairs={{0,6},{2,0},{4,2},{6,4},{1,7},{3,1},{5,3},{7,5},{8,14},{10,8},{12,... | collective-permute-start | bytes 393224 | tf_op jit(solution)/shard_map/ppermute | solution.py:37
  149.7 4.3 %collective-permute-start.18 = (bf16[32,1024]{1,0:T(8,128)(2,1)S(1)}, bf16[32,1024]{1,0:T(8,128)(2,1)S(1)}, u32[]{:S(2)}, u32[]{:S(2)}) collective-permute-start(bf16[32,1024]{1,0:T(8,128)(2,1)S(1)} %get-tuple-element.51), channel_id=1, source_target_pairs={{0,1},{1,0},{2,3},{3,2},{4,5},{5,4},{6,7},{7,6},{8,9},{9,8},{10,11... | collective-permute-start | bytes 196616 | tf_op jit(solution)/shard_map/ppermute | solution.py:241

commit v6 on v4

v6 whole, which is shorter than its diff:
```python
import jax
import jax.numpy as jnp
from jax import lax
from jax.experimental import pallas as pl
from jax.experimental.pallas import tpu as pltpu
from jax.sharding import Mesh, PartitionSpec as P


ROW = ("x", "yh", "c")
COL = ("z", "yl")
CHIPS = ("x", "yh")
AXES = (*ROW, *COL)
SIZES = (4, 2, 2, 4, 2)
SWAP = [(0, 1), (1, 0)]
D, BR, COLS = 256, 1024, 2048
TN, RC, BLOCK = 256, 256, 128
VMEM = pl.BlockSpec(memory_space=pltpu.VMEM)


def shape(dims, kind):
    return jax.ShapeDtypeStruct(dims, kind)


def cost(flops, moved):
    return pl.CostEstimate(flops=flops, bytes_accessed=moved, transcendentals=0)


def in_hbm(value):
    return pltpu.with_memory_space_constraint(value, pltpu.HBM)


def to_each(copies, axes):
    return lax.all_to_all(copies, axes, 0, 0, tiled=True)


def over_z(value, shift):
    return lax.ppermute(value, "z", [(at, (at + shift) % 4) for at in range(4)])


def rows_sum(ref, rows):
    total = ref[0, rows, :].astype(jnp.float32)
    for at in range(1, ref.shape[0]):
        total += ref[at, rows, :].astype(jnp.float32)
    return total


def prepared_kernel(counts_ref, out_ref):
    values = counts_ref[...].astype(jnp.float32).astype(jnp.bfloat16)
    for at in range(COLS // TN):
        out_ref[at] = values[:, at * TN : at * TN + TN]


def prepared(counts):
    return pl.pallas_call(
        prepared_kernel,
        grid=(BR // BLOCK,),
        out_shape=pltpu.HBM((COLS // TN, BR, TN), jnp.bfloat16),
        in_specs=[pl.BlockSpec((BLOCK, COLS), lambda at: (at, 0))],
        out_specs=pl.BlockSpec((COLS // TN, BLOCK, TN), lambda at: (0, at, 0)),
        compiler_params=pltpu.CompilerParams(vmem_limit_bytes=6 * 2**20),
        cost_estimate=cost(BR * COLS, 12 * 2**20),
        name="prepared",
    )(in_hbm(counts))


def first_kernel(emb_ref, sums_ref, out_ref):
    sums = sums_ref[...]
    digits = [(sums & 127).astype(jnp.float32), ((sums >> 7) & 127).astype(jnp.float32), (sums >> 14).astype(jnp.float32)]
    out_ref[...] = jnp.concatenate([emb_ref[...]] + digits + [jnp.zeros((5, BR), jnp.float32)]).astype(jnp.bfloat16)


def joined_first_kernel(own_ref, other_ref, out_ref):
    out_ref[:32] = own_ref[:32]
    out_ref[32:64] = other_ref[:32]
    out_ref[64:] = (own_ref[32:].astype(jnp.float32) + other_ref[32:].astype(jnp.float32)).astype(jnp.bfloat16)


def placed(row_refs, flat_ref):
    z, yl = lax.axis_index("z"), lax.axis_index("yl")
    for shift in range(4):
        for other in range(2):
            place = lax.rem(z + 4 - shift, 4) * 2 + lax.rem(yl + other, 2)
            flat_ref[pl.ds(place, 1)] = row_refs[shift][pl.ds(32 * other, 32), :][None]


def second_kernel(*refs):
    row_refs, (emb_ref, sums_ref, flat_ref, row_log_ref, out_ref) = refs[:4], refs[4:]
    placed(row_refs, flat_ref)
    digits = row_refs[0][64:, :].astype(jnp.float32)
    for ref in row_refs[1:]:
        digits += ref[64:, :].astype(jnp.float32)
    marg = digits[0:1] + 128.0 * digits[1:2] + 16384.0 * digits[2:3]
    row_log_ref[...] = 0.5 * jnp.log(marg)
    total = jnp.broadcast_to(jnp.sum(marg.astype(jnp.int32), axis=1, keepdims=True), (1, COLS))
    lane = lax.broadcasted_iota(jnp.int32, (1, COLS), 1)
    parts = jnp.where(lane < 4, (total >> (8 * jnp.minimum(lane, 3))) & 255, 0)
    sums = sums_ref[...]
    rows = [emb_ref[...], (sums & 255).astype(jnp.float32), (sums >> 8).astype(jnp.float32), parts.astype(jnp.float32)]
    parcel = jnp.concatenate(rows + [jnp.zeros((5, COLS), jnp.float32)]).astype(jnp.bfloat16)
    for at in range(8):
        out_ref[at] = parcel


def arranged_kernel(*refs):
    placed(refs[:4], refs[4])


def col_log_kernel(mine_ref, theirs_ref, out_ref):
    digits = rows_sum(mine_ref, slice(16, 24)) + rows_sum(theirs_ref, slice(16, 24))
    lane = lax.broadcasted_iota(jnp.int32, (1, 128), 1)
    scale = jnp.where(lane == 0, 1.0, jnp.where(lane == 1, 256.0, jnp.where(lane == 2, 65536.0, 16777216.0)))
    total = jnp.sum(jnp.where(lane < 4, digits[2:3, :128] * scale, 0.0), axis=1, keepdims=True)
    total_log = jnp.log(jnp.broadcast_to(total, (1, COLS)))
    out_ref[...] = 0.5 * jnp.log(digits[0:1] + 256.0 * digits[1:2]) - 0.5 * total_log


def sweep_kernel(row_flat, mine_ref, theirs_ref, row_logs, col_log_ref, counts_ref, *refs):
    own_out, pair_out, home_out, away_out = refs[:4]
    col_flat, col_tall, grads, turned, counts, row_tall, row_log_ref, arrived = refs[4:]
    copies = [pltpu.make_async_copy(counts_ref.at[at], counts.at[at], arrived.at[at]) for at in range(COLS // TN)]
    for copy in copies:
        copy.start()
    core, z, yl = lax.axis_index("c"), lax.axis_index("z"), lax.axis_index("yl")
    row_tall[...] = (row_flat[...].reshape(D, BR) * jnp.bfloat16(0.5)).T
    for at in range(BR // 128):
        here = slice(at * 128, at * 128 + 128)
        row_log_ref[here, :] = jnp.broadcast_to(row_logs[:, here], (128, 128)).T
    col_flat[:, pl.ds(core, 1)] = mine_ref[:, :16, :][:, None]
    col_flat[:, pl.ds(1 - core, 1)] = theirs_ref[:, :16, :][:, None]
    for at in range(COLS // TN):
        here = slice(at * TN, at * TN + TN)
        col = col_flat[:, :, :, here].reshape(D, TN)
        col_tall[here, :] = col.T
        shift = col_log_ref[:, here]
        copies[at].wait()
        for chunk in range(BR // RC):
            rows = slice(chunk * RC, chunk * RC + RC)
            scores = jnp.dot(row_tall[rows, :], col, preferred_element_type=jnp.float32)
            values = counts[at, rows, :].astype(jnp.float32)
            least = jnp.maximum(values, 1.0)
            errors = scores - 0.5 * jnp.log(least) + (shift + jnp.tile(row_log_ref[rows, :], (1, TN // 128)))
            weight = 0.2 + 0.5 * (least * lax.rsqrt(least))
            grad = jnp.where(values > 0.0, weight * errors, 0.5 * jnp.tanh(errors) + 0.5)
            grads[rows, here] = grad.astype(jnp.bfloat16)
    col_grad = jnp.dot(row_flat[...].reshape(D, BR), grads[...], preferred_element_type=jnp.float32).reshape(8, 2, 16, COLS)
    even, odd = col_grad[:, 0], col_grad[:, 1]
    home_out[...] = jnp.where(core == 0, even, odd).astype(jnp.bfloat16)
    away_out[...] = jnp.where(core == 0, odd, even).astype(jnp.bfloat16)
    for chunk in range(BR // 256):
        rows = slice(chunk * 256, chunk * 256 + 256)
        part = jnp.dot(grads[rows, :], col_tall[...], preferred_element_type=jnp.float32)
        turned[:, :, rows] = part.astype(jnp.bfloat16).T.reshape(8, 32, 256)
    for shift in range(4):
        place = lax.rem(z + shift, 4) * 2
        own_out[shift : shift + 1] = turned[pl.ds(place + yl, 1)]
        pair_out[shift : shift + 1] = turned[pl.ds(place + 1 - yl, 1)]


def swept(*args):
    return pl.pallas_call(
        sweep_kernel,
        out_shape=(shape((4, 32, BR), jnp.bfloat16),) * 2 + (shape((8, 16, COLS), jnp.bfloat16),) * 2,
        in_specs=[VMEM] * 5 + [pl.BlockSpec(memory_space=pltpu.HBM)],
        out_specs=(VMEM,) * 4,
        scratch_shapes=[
            pltpu.VMEM((8, 2, 16, COLS), jnp.bfloat16),
            pltpu.VMEM((COLS, D), jnp.bfloat16),
            pltpu.VMEM((BR, COLS), jnp.bfloat16),
            pltpu.VMEM((8, 32, BR), jnp.bfloat16),
            pltpu.VMEM((COLS // TN, BR, TN), jnp.bfloat16),
            pltpu.VMEM((BR, D), jnp.bfloat16),
            pltpu.VMEM((BR, 128), jnp.float32),
            pltpu.SemaphoreType.DMA((COLS // TN,)),
        ],
        compiler_params=pltpu.CompilerParams(vmem_limit_bytes=24 * 2**20),
        cost_estimate=cost(6 * D * BR * COLS, 20 * 2**20),
        name="sweep",
    )(*args)


def joined_kernel(own_ref, other_ref, out_ref):
    out_ref[:32] = own_ref[...]
    out_ref[32:] = other_ref[...]


def home_kernel(home_ref, theirs_ref, out_ref):
    out_ref[...] = (home_ref[...].astype(jnp.float32) + theirs_ref[...].astype(jnp.float32)).astype(jnp.bfloat16)


def pairs_kernel(own_ref, came_ref, keep_ref, *out_refs):
    keep_ref[...] = own_ref[0].astype(jnp.float32) + came_ref[0].astype(jnp.float32)
    for shift in range(1, 4):
        both = own_ref[shift].astype(jnp.float32) + came_ref[shift].astype(jnp.float32)
        out_refs[shift - 1][...] = both.astype(jnp.bfloat16)


def moved(emb_ref, accum_ref, grad):
    accum = accum_ref[...] + grad * grad
    return emb_ref[...] - 0.05 * grad / jnp.sqrt(accum), accum


def row_kernel(keep_ref, first_ref, second_ref, third_ref, emb_ref, accum_ref, new_emb_ref, new_accum_ref, half_ref):
    grad = keep_ref[...]
    for ref in (first_ref, second_ref, third_ref):
        grad += ref[...].astype(jnp.float32)
    emb, accum = moved(emb_ref, accum_ref, grad)
    new_emb_ref[...] = emb
    new_accum_ref[...] = accum
    half_ref[...] = emb.astype(jnp.bfloat16)


def col_kernel(came_ref, emb_ref, accum_ref, new_emb_ref, new_accum_ref, half_ref):
    grad = came_ref[0].astype(jnp.float32)
    for at in range(1, 8):
        grad += came_ref[at].astype(jnp.float32)
    emb, accum = moved(emb_ref, accum_ref, grad)
    new_emb_ref[...] = emb
    new_accum_ref[...] = accum
    half = emb.astype(jnp.bfloat16)
    for at in range(8):
        half_ref[at] = half


def small(kernel, outs):
    return pl.pallas_call(
        kernel,
        out_shape=outs,
        compiler_params=pltpu.CompilerParams(vmem_limit_bytes=6 * 2**20),
        cost_estimate=cost(2**20, 2**20),
    )


def on_device(counts, row_emb, col_emb, row_accum, col_accum):
    row_sums = jnp.sum(counts, axis=1)[None]
    col_sums = jnp.sum(counts, axis=0)[None]
    parcel = small(first_kernel, shape((40, BR), jnp.bfloat16))(row_emb, row_sums)
    other = lax.ppermute(parcel, "yl", SWAP)
    pair = small(joined_first_kernel, shape((72, BR), jnp.bfloat16))(parcel, other)
    row = [pair, over_z(pair, 1), over_z(pair, 2), over_z(pair, 3)]
    outs = (shape((8, 32, BR), jnp.bfloat16), shape((1, BR), jnp.float32), shape((8, 24, COLS), jnp.bfloat16))
    row, row_log, copies = small(second_kernel, outs)(*row, col_emb, col_sums)
    mine = to_each(copies, CHIPS)
    small_counts = prepared(counts)
    theirs = lax.ppermute(mine, "c", SWAP)
    col_log = small(col_log_kernel, shape((1, COLS), jnp.float32))(mine, theirs)
    for sweep in range(2):
        own, away_pair, home, away = swept(row, mine, theirs, row_log, col_log, in_hbm(small_counts))
        theirs = lax.ppermute(away, "c", SWAP)
        from_pair = lax.ppermute(away_pair, "yl", SWAP)
        both = small(home_kernel, shape((8, 16, COLS), jnp.bfloat16))(home, theirs)
        came = to_each(both, CHIPS)
        outs = (shape((32, BR), jnp.float32),) + (shape((32, BR), jnp.bfloat16),) * 3
        keep, *parts = small(pairs_kernel, outs)(own, from_pair)
        parts = [over_z(parts[shift - 1], shift) for shift in (2, 1, 3)]
        outs = (shape((32, BR), jnp.float32),) * 2 + (shape((32, BR), jnp.bfloat16),)
        row_emb, row_accum, half = small(row_kernel, outs)(keep, *parts, row_emb, row_accum)
        outs = (shape((16, COLS), jnp.float32),) * 2 + (shape((8, 16, COLS), jnp.bfloat16),)
        col_emb, col_accum, copies = small(col_kernel, outs)(came, col_emb, col_accum)
        if sweep == 0:
            pair = lax.ppermute(half, "yl", SWAP)
            pair = small(joined_kernel, shape((64, BR), jnp.bfloat16))(half, pair)
            mine = to_each(copies, CHIPS)
            row = [pair, over_z(pair, 1), over_z(pair, 2), over_z(pair, 3)]
            row = small(arranged_kernel, shape((8, 32, BR), jnp.bfloat16))(*row)
            theirs = lax.ppermute(mine, "c", SWAP)
    return row_emb, col_emb


def solution(mesh):
    fine = Mesh(mesh.devices.reshape(SIZES), AXES)
    tall, wide = P(ROW, COL), P(COL, ROW)
    return jax.shard_map(
        on_device,
        mesh=fine,
        in_specs=(tall, wide, tall, wide, tall),
        out_specs=(wide, tall),
        check_vma=False,
    )
```

time: 162 us -> 156 us (0.963)
  blocking collectives: 52.9 us -> 34.7 us
  waiting for transfers between devices: 45.8 us -> 52.6 us
  starting transfers between devices: 25.6 us -> 32 us
  local copies, waits for them, and re-layouts: 1.86 us -> 0.02 us
    all_to_all x3 -> x2, blocking collectives: 52.9 us -> 34.7 us  [to_each(): return lax.all_to_all(copies, axes, 0, 0, tiled=True)]
    all_to_all x2, waiting for transfers between devices: 0.01 us -> 10 us  [to_each(): return lax.all_to_all(copies, axes, 0, 0, tiled=True)]
    ppermute x12, waiting for transfers between devices: 27.4 us -> 19.6 us  [over_z(): return lax.ppermute(value, 'z', [(at, (at + shift) % 4) for at in range(4)])]
    ppermute x2, waiting for transfers between devices: 7.19 us -> 13.6 us  [on_device(): from_pair = lax.ppermute(away_pair, 'yl', SWAP)]
    all_to_all x2, starting transfers between devices: 6.99 us -> 10.7 us  [to_each(): return lax.all_to_all(copies, axes, 0, 0, tiled=True)]
    unnamed x12 -> x8, local copies, waits for them, and re-layouts: 1.86 us -> 0.02 us
  transfers between devices with their start and end apart: 22 -> 22, of which waited for: 16 -> 17; matrix products, arithmetic and copies ran while one was open for 0% -> 0% of each run, Pallas kernels for 6% -> 6%
where the time goes in v6:
time: 156 us; the launch traced here: 155 us
  waiting for transfers between devices  52.6 us (34%)
  blocking collectives  34.7 us (22%)
  starting transfers between devices  32 us (21%)
  Pallas kernels  30.6 us (20%)
  other arithmetic  4.05 us (3%)
    all_to_all x2, blocking collectives, to_each(): return lax.all_to_all(copies, axes, 0, 0, tiled=True)  34.7 us
    ppermute x12, waiting for transfers between devices, over_z(): return lax.ppermute(value, 'z', [(at, (at + shift) % 4) for at in range(4)])  19.6 us
    pallas_call x2, Pallas kernels, swept(): pl.pallas_call(sweep_kernel, out_shape=(shape((4, 32, BR), jnp.bfloat16),...  18.5 us
    ppermute x12, starting transfers between devices, over_z(): return lax.ppermute(value, 'z', [(at, (at + shift) % 4) for at in range(4)])  16.8 us
    ppermute x2, waiting for transfers between devices, on_device(): from_pair = lax.ppermute(away_pair, 'yl', SWAP)  13.6 us
    all_to_all x2, starting transfers between devices, to_each(): return lax.all_to_all(copies, axes, 0, 0, tiled=True)  10.7 us
    all_to_all x2, waiting for transfers between devices, to_each(): return lax.all_to_all(copies, axes, 0, 0, tiled=True)  10 us
    pallas_call x1, Pallas kernels, prepared(): pl.pallas_call(prepared_kernel, grid=(BR // BLOCK,), out_shape=pltpu.HBM(...  7.73 us
  transfers between devices with their start and end apart: 22, of which 17 were waited for; matrix products, arithmetic and copies ran while one was open for 0% of the time, Pallas kernels for 6%

profile of v6, /device:TPU:0, one launch (start us, length us, event | category | flops | bytes accessed | tf_op | source)
XLA Modules:
  0.0 154.8 jit_solution(4642920491422904281)
XLA Ops:
  0.6 4.1 %fusion = (s32[2048]{0:T(1024)S(1)}, s32[1024]{0:T(1024)S(1)}) fusion(s32[1024,2048]{1,0:T(8,128)} %counts_ref.1), kind=kLoop, calls=%fused_computation | loop fusion | flops 4191232 | bytes 8400896 | tf_op jit(solution)/shard_map/reduce_sum | solution.py:235
  4.7 1.8 %collective-permute-start = (bf16[40,1024]{1,0:T(8,128)(2,1)S(1)}, bf16[40,1024]{1,0:T(8,128)(2,1)S(1)}, u32[]{:S(2)}, u32[]{:S(2)}) collective-permute-start(bf16[40,1024]{1,0:T(8,128)(2,1)S(1)} %shard_map.68.own_ref), channel_id=1, source_target_pairs={{0,1},{1,0},{2,3},{3,2},{4,5},{5,4},{6,7},{7,6},{8,9},{9,8},{10,11... | collective-permute-start | bytes 245768 | tf_op jit(solution)/shard_map/ppermute | solution.py:237
  6.5 2.8 %collective-permute-done.other_ref = bf16[40,1024]{1,0:T(8,128)(2,1)S(1)} collective-permute-done((bf16[40,1024]{1,0:T(8,128)(2,1)S(1)}, bf16[40,1024]{1,0:T(8,128)(2,1)S(1)}, u32[]{:S(2)}, u32[]{:S(2)}) %collective-permute-start) | collective-permute-done | bytes 81952 | tf_op jit(solution)/shard_map/ppermute | solution.py:237
  9.3 4.2 %collective-permute-start.3 = (bf16[72,1024]{1,0:T(8,128)(2,1)S(1)}, bf16[72,1024]{1,0:T(8,128)(2,1)S(1)}, u32[]{:S(2)}, u32[]{:S(2)}) collective-permute-start(bf16[72,1024]{1,0:T(8,128)(2,1)S(1)} %shard_map.69.refs_0_), channel_id=1, source_target_pairs={{0,6},{2,0},{4,2},{6,4},{1,7},{3,1},{5,3},{7,5},{8,14},{10,8},{12,... | collective-permute-start | bytes 442376 | tf_op jit(solution)/shard_map/ppermute | solution.py:37
  13.5 1.3 collective-permute-start.1
  14.8 3.9 %collective-permute-done.3.refs_3_ = bf16[72,1024]{1,0:T(8,128)(2,1)S(1)} collective-permute-done((bf16[72,1024]{1,0:T(8,128)(2,1)S(1)}, bf16[72,1024]{1,0:T(8,128)(2,1)S(1)}, u32[]{:S(2)}, u32[]{:S(2)}) %collective-permute-start.3) | collective-permute-done | bytes 147488 | tf_op jit(solution)/shard_map/ppermute | solution.py:37
  18.6 2.2 %collective-permute-done.2.refs_2_ = bf16[72,1024]{1,0:T(8,128)(2,1)S(1)} collective-permute-done((bf16[72,1024]{1,0:T(8,128)(2,1)S(1)}, bf16[72,1024]{1,0:T(8,128)(2,1)S(1)}, u32[]{:S(2)}, u32[]{:S(2)}) %collective-permute-start.2) | collective-permute-done | bytes 147488 | tf_op jit(solution)/shard_map/ppermute | solution.py:37
  20.8 1.2 collective-permute-done.1.refs_1_
  22.0 0.1 shard_map.70
  22.1 20.1 %all_to_all.20.mine_ref = bf16[8,24,2048]{2,1,0:T(8,128)(2,1)S(1)} all-to-all(bf16[8,24,2048]{2,1,0:T(8,128)(2,1)S(1)} %get-tuple-element.30), channel_id=1, replica_groups=mesh['x'=4,'yh'=2,'c'=2,'z'=4,'yl'=2] {'x','yh'}, dimensions={0} | all-to-all | bytes 1572864 | tf_op jit(solution)/shard_map/all_to_all | solution.py:33
  42.2 7.7 %prepared.1.counts_ref = bf16[8,1024,256]{2,1,0:T(8,128)(2,1)} custom-call(s32[1024,2048]{1,0:T(8,128)} %counts_ref.1), custom_call_target="tpu_custom_call" | custom-call | flops 2097152 | bytes 12582912 | tf_op jit(solution)/shard_map/prepared/pallas_call | solution.py:54
  50.0 0.2 shard_map.71.col_log_ref
  50.1 9.2 %sweep.2 = (bf16[4,32,1024]{2,1,0:T(8,128)(2,1)S(1)}, bf16[4,32,1024]{2,1,0:T(8,128)(2,1)S(1)}, bf16[8,16,2048]{2,1,0:T(8,128)(2,1)S(1)}, bf16[8,16,2048]{2,1,0:T(8,128)(2,1)S(1)}) custom-call(bf16[8,32,1024]{2,1,0:T(8,128)(2,1)S(1)} %get-tuple-element.29.row_flat, bf16[8,24,2048]{2,1,0:T(8,128)(2,1)S(1)} %all_to_all.20.mine_ref, ...), custom_call_target="tpu_custom_call" | custom-call | flops 3221225472 | bytes 20971520 | tf_op jit(solution)/shard_map/sweep/pallas_call | solution.py:160
  59.4 0.6 collective-permute-start.13
  59.9 1.5 collective-permute-done.13.theirs_ref
  61.5 0.1 shard_map.76
  61.6 14.7 %all_to_all.21.came_ref = bf16[8,16,2048]{2,1,0:T(8,128)(2,1)S(1)} all-to-all(bf16[8,16,2048]{2,1,0:T(8,128)(2,1)S(1)} %shard_map.76), channel_id=1, replica_groups=mesh['x'=4,'yh'=2,'c'=2,'z'=4,'yl'=2] {'x','yh'}, dimensions={0} | all-to-all | bytes 1048576 | tf_op jit(solution)/shard_map/all_to_all | solution.py:33
  76.3 1.0 shard_map.77
  77.2 3.5 %all-to-all-start.2 = ((bf16[8,16,2048]{2,1,0:T(8,128)(2,1)}), bf16[8,16,2048]{2,1,0:T(8,128)(2,1)S(1)}, u32[]{:S(2)}, u32[]{:S(2)}) async-start(bf16[8,16,2048]{2,1,0:T(8,128)(2,1)} %get-tuple-element.41), calls=%async_computation.2 | async-start | bytes 1048576 | tf_op jit(solution)/shard_map/all_to_all | solution.py:33
  80.7 0.8 collective-permute-start.5
  81.5 10.0 %all-to-all-done.2.mine_ref = bf16[8,16,2048]{2,1,0:T(8,128)(2,1)S(1)} async-done(((bf16[8,16,2048]{2,1,0:T(8,128)(2,1)}), bf16[8,16,2048]{2,1,0:T(8,128)(2,1)S(1)}, u32[]{:S(2)}, u32[]{:S(2)}) %all-to-all-start.2) | async-done | bytes 524320 | tf_op jit(solution)/shard_map/all_to_all | solution.py:33
  91.5 1.4 collective-permute-done.5.came_ref
  92.9 0.1 collective-permute-start.6
  93.0 0.8 collective-permute-start.7
  93.8 2.5 %collective-permute-start.8 = (bf16[32,1024]{1,0:T(8,128)(2,1)S(1)}, bf16[32,1024]{1,0:T(8,128)(2,1)S(1)}, u32[]{:S(2)}, u32[]{:S(2)}) collective-permute-start(bf16[32,1024]{1,0:T(8,128)(2,1)S(1)} %get-tuple-element.37), channel_id=1, source_target_pairs={{0,6},{2,0},{4,2},{6,4},{1,7},{3,1},{5,3},{7,5},{8,14},{10,8},{12,... | collective-permute-start | bytes 196616 | tf_op jit(solution)/shard_map/ppermute | solution.py:37
  96.3 2.5 %collective-permute-done.6.first_ref = bf16[32,1024]{1,0:T(8,128)(2,1)S(1)} collective-permute-done((bf16[32,1024]{1,0:T(8,128)(2,1)S(1)}, bf16[32,1024]{1,0:T(8,128)(2,1)S(1)}, u32[]{:S(2)}, u32[]{:S(2)}) %collective-permute-start.6) | collective-permute-done | bytes 65568 | tf_op jit(solution)/shard_map/ppermute | solution.py:37
  98.8 0.5 collective-permute-done.7.second_ref
  99.3 0.1 shard_map.73
  99.4 1.2 collective-permute-start.9
  100.6 3.2 %collective-permute-done.9.other_ref = bf16[32,1024]{1,0:T(8,128)(2,1)S(1)} collective-permute-done((bf16[32,1024]{1,0:T(8,128)(2,1)S(1)}, bf16[32,1024]{1,0:T(8,128)(2,1)S(1)}, u32[]{:S(2)}, u32[]{:S(2)}) %collective-permute-start.9) | collective-permute-done | bytes 65568 | tf_op jit(solution)/shard_map/ppermute | solution.py:260
  103.8 2.6 %collective-permute-start.12 = (bf16[64,1024]{1,0:T(8,128)(2,1)S(1)}, bf16[64,1024]{1,0:T(8,128)(2,1)S(1)}, u32[]{:S(2)}, u32[]{:S(2)}) collective-permute-start(bf16[64,1024]{1,0:T(8,128)(2,1)S(1)} %shard_map.74.refs_0_), channel_id=1, source_target_pairs={{0,6},{2,0},{4,2},{6,4},{1,7},{3,1},{5,3},{7,5},{8,14},{10,8},{12,... | collective-permute-start | bytes 393224 | tf_op jit(solution)/shard_map/ppermute | solution.py:37
  106.4 1.0 collective-permute-start.11
  107.4 2.9 %collective-permute-done.12.refs_3_ = bf16[64,1024]{1,0:T(8,128)(2,1)S(1)} collective-permute-done((bf16[64,1024]{1,0:T(8,128)(2,1)S(1)}, bf16[64,1024]{1,0:T(8,128)(2,1)S(1)}, u32[]{:S(2)}, u32[]{:S(2)}) %collective-permute-start.12) | collective-permute-done | bytes 131104 | tf_op jit(solution)/shard_map/ppermute | solution.py:37
  110.3 2.6 %collective-permute-done.11.refs_2_ = bf16[64,1024]{1,0:T(8,128)(2,1)S(1)} collective-permute-done((bf16[64,1024]{1,0:T(8,128)(2,1)S(1)}, bf16[64,1024]{1,0:T(8,128)(2,1)S(1)}, u32[]{:S(2)}, u32[]{:S(2)}) %collective-permute-start.11) | collective-permute-done | bytes 131104 | tf_op jit(solution)/shard_map/ppermute | solution.py:37
  112.9 1.3 collective-permute-done.10.refs_1_
  114.3 9.2 %sweep.3 = (bf16[4,32,1024]{2,1,0:T(8,128)(2,1)S(1)}, bf16[4,32,1024]{2,1,0:T(8,128)(2,1)S(1)}, bf16[8,16,2048]{2,1,0:T(8,128)(2,1)S(1)}, bf16[8,16,2048]{2,1,0:T(8,128)(2,1)S(1)}) custom-call(bf16[8,32,1024]{2,1,0:T(8,128)(2,1)S(1)} %shard_map.75.row_flat, bf16[8,16,2048]{2,1,0:T(8,128)(2,1)S(1)} %all-to-all-done.2.mine_ref, ...), custom_call_target="tpu_custom_call" | custom-call | flops 3221225472 | bytes 20971520 | tf_op jit(solution)/shard_map/sweep/pallas_call | solution.py:160
  123.6 1.9 %collective-permute-done.19.theirs_ref = bf16[8,16,2048]{2,1,0:T(8,128)(2,1)S(1)} collective-permute-done((bf16[8,16,2048]{2,1,0:T(8,128)(2,1)S(1)}, bf16[8,16,2048]{2,1,0:T(8,128)(2,1)S(1)}, u32[]{:S(2)}, u32[]{:S(2)}) %collective-permute-start.19) | collective-permute-done | bytes 524320 | tf_op jit(solution)/shard_map/ppermute | solution.py:248
  125.5 0.9 shard_map.80
  126.5 7.2 %all-to-all-start.3 = ((bf16[8,16,2048]{2,1,0:T(8,128)(2,1)}), bf16[8,16,2048]{2,1,0:T(8,128)(2,1)S(1)}, u32[]{:S(2)}, u32[]{:S(2)}) async-start(bf16[8,16,2048]{2,1,0:T(8,128)(2,1)} %shard_map.80), calls=%async_computation.3 | async-start | bytes 1048576 | tf_op jit(solution)/shard_map/all_to_all | solution.py:33
  133.7 0.1 collective-permute-start.15
  133.8 12.3 %collective-permute-done.15.came_ref = bf16[4,32,1024]{2,1,0:T(8,128)(2,1)S(1)} collective-permute-done((bf16[4,32,1024]{2,1,0:T(8,128)(2,1)S(1)}, bf16[4,32,1024]{2,1,0:T(8,128)(2,1)S(1)}, u32[]{:S(2)}, u32[]{:S(2)}) %collective-permute-start.15) | collective-permute-done | bytes 262176 | tf_op jit(solution)/shard_map/ppermute | solution.py:249
  146.2 1.1 collective-permute-start.16
  147.3 0.4 collective-permute-start.17
  147.7 2.8 %collective-permute-start.18 = (bf16[32,1024]{1,0:T(8,128)(2,1)S(1)}, bf16[32,1024]{1,0:T(8,128)(2,1)S(1)}, u32[]{:S(2)}, u32[]{:S(2)}) collective-permute-start(bf16[32,1024]{1,0:T(8,128)(2,1)S(1)} %get-tuple-element.47), channel_id=1, source_target_pairs={{0,6},{2,0},{4,2},{6,4},{1,7},{3,1},{5,3},{7,5},{8,14},{10,8},{12,... | collective-permute-start | bytes 196616 | tf_op jit(solution)/shard_map/ppermute | solution.py:37
  150.5 1.8 %collective-permute-done.16.first_ref = bf16[32,1024]{1,0:T(8,128)(2,1)S(1)} collective-permute-done((bf16[32,1024]{1,0:T(8,128)(2,1)S(1)}, bf16[32,1024]{1,0:T(8,128)(2,1)S(1)}, u32[]{:S(2)}, u32[]{:S(2)}) %collective-permute-start.16) | collective-permute-done | bytes 65568 | tf_op jit(solution)/shard_map/ppermute | solution.py:37
  152.3 0.7 collective-permute-done.17.second_ref
  153.0 0.8 shard_map.79
  153.8 1.0 shard_map.81
  (24 shorter events, 0.3 us)
Async XLA Ops:
  0.6 4.1 %copy-start = (f32[32,1024]{1,0:T(8,128)S(1)}, f32[32,1024]{1,0:T(8,128)}, u32[]{:S(2)}) copy-start(f32[32,1024]{1,0:T(8,128)} %emb_ref.4) | copy-start | bytes 393220
  0.6 21.4 %copy-start.1 = (f32[16,2048]{1,0:T(8,128)S(1)}, f32[16,2048]{1,0:T(8,128)}, u32[]{:S(2)}) copy-start(f32[16,2048]{1,0:T(8,128)} %emb_ref.5) | copy-start | bytes 393220
  4.7 4.5 %collective-permute-start = (bf16[40,1024]{1,0:T(8,128)(2,1)S(1)}, bf16[40,1024]{1,0:T(8,128)(2,1)S(1)}, u32[]{:S(2)}, u32[]{:S(2)}) collective-permute-start(bf16[40,1024]{1,0:T(8,128)(2,1)S(1)} %shard_map.68.own_ref), channel_id=1, source_target_pairs={{0,1},{1,0},{2,3},{3,2},{4,5},{5,4},{6,7},{7,6},{8,9},{9,8},{10,11... | collective-permute-start | bytes 245768 | tf_op jit(solution)/shard_map/ppermute | solution.py:237
  9.3 9.3 %collective-permute-start.3 = (bf16[72,1024]{1,0:T(8,128)(2,1)S(1)}, bf16[72,1024]{1,0:T(8,128)(2,1)S(1)}, u32[]{:S(2)}, u32[]{:S(2)}) collective-permute-start(bf16[72,1024]{1,0:T(8,128)(2,1)S(1)} %shard_map.69.refs_0_), channel_id=1, source_target_pairs={{0,6},{2,0},{4,2},{6,4},{1,7},{3,1},{5,3},{7,5},{8,14},{10,8},{12,... | collective-permute-start | bytes 442376 | tf_op jit(solution)/shard_map/ppermute | solution.py:37
  13.5 7.3 %collective-permute-start.2 = (bf16[72,1024]{1,0:T(8,128)(2,1)S(1)}, bf16[72,1024]{1,0:T(8,128)(2,1)S(1)}, u32[]{:S(2)}, u32[]{:S(2)}) collective-permute-start(bf16[72,1024]{1,0:T(8,128)(2,1)S(1)} %shard_map.69.refs_0_), channel_id=1, source_target_pairs={{0,4},{2,6},{4,0},{6,2},{1,5},{3,7},{5,1},{7,3},{8,12},{10,14},{12... | collective-permute-start | bytes 442376 | tf_op jit(solution)/shard_map/ppermute | solution.py:37
  13.5 8.5 %collective-permute-start.1 = (bf16[72,1024]{1,0:T(8,128)(2,1)S(1)}, bf16[72,1024]{1,0:T(8,128)(2,1)S(1)}, u32[]{:S(2)}, u32[]{:S(2)}) collective-permute-start(bf16[72,1024]{1,0:T(8,128)(2,1)S(1)} %shard_map.69.refs_0_), channel_id=1, source_target_pairs={{0,2},{2,4},{4,6},{6,0},{1,3},{3,5},{5,7},{7,1},{8,10},{10,12},{12... | collective-permute-start | bytes 442376 | tf_op jit(solution)/shard_map/ppermute | solution.py:37
  42.2 7.7 %collective-permute-start.4 = (bf16[8,24,2048]{2,1,0:T(8,128)(2,1)S(1)}, bf16[8,24,2048]{2,1,0:T(8,128)(2,1)S(1)}, u32[]{:S(2)}, u32[]{:S(2)}) collective-permute-start(bf16[8,24,2048]{2,1,0:T(8,128)(2,1)S(1)} %all_to_all.20.mine_ref), channel_id=1, source_target_pairs={{0,8},{8,0},{1,9},{9,1},{2,10},{10,2},{3,11},{11,3},{4,12},{12,4},... | collective-permute-start | bytes 2359304 | tf_op jit(solution)/shard_map/ppermute | solution.py:244
  49.9 26.3 %copy-start.2 = (f32[16,2048]{1,0:T(8,128)S(1)}, f32[16,2048]{1,0:T(8,128)}, u32[]{:S(2)}) copy-start(f32[16,2048]{1,0:T(8,128)} %accum_ref.3) | copy-start | bytes 393220
  50.1 49.2 %copy-start.3 = (f32[32,1024]{1,0:T(8,128)S(1)}, f32[32,1024]{1,0:T(8,128)}, u32[]{:S(2)}) copy-start(f32[32,1024]{1,0:T(8,128)} %accum_ref.2) | copy-start | bytes 393220
  59.4 2.1 %collective-permute-start.13 = (bf16[8,16,2048]{2,1,0:T(8,128)(2,1)S(1)}, bf16[8,16,2048]{2,1,0:T(8,128)(2,1)S(1)}, u32[]{:S(2)}, u32[]{:S(2)}) collective-permute-start(bf16[8,16,2048]{2,1,0:T(8,128)(2,1)S(1)} %get-tuple-element.40), channel_id=1, source_target_pairs={{0,8},{8,0},{1,9},{9,1},{2,10},{10,2},{3,11},{11,3},{4,12},{12,4},... | collective-permute-start | bytes 1572872 | tf_op jit(solution)/shard_map/ppermute | solution.py:248
  77.2 14.3 %all-to-all-start.2 = ((bf16[8,16,2048]{2,1,0:T(8,128)(2,1)}), bf16[8,16,2048]{2,1,0:T(8,128)(2,1)S(1)}, u32[]{:S(2)}, u32[]{:S(2)}) async-start(bf16[8,16,2048]{2,1,0:T(8,128)(2,1)} %get-tuple-element.41), calls=%async_computation.2 | async-start | bytes 1048576 | tf_op jit(solution)/shard_map/all_to_all | solution.py:33
  80.7 12.1 %collective-permute-start.5 = (bf16[4,32,1024]{2,1,0:T(8,128)(2,1)S(1)}, bf16[4,32,1024]{2,1,0:T(8,128)(2,1)S(1)}, u32[]{:S(2)}, u32[]{:S(2)}) collective-permute-start(bf16[4,32,1024]{2,1,0:T(8,128)(2,1)S(1)} %get-tuple-element.33), channel_id=1, source_target_pairs={{0,1},{1,0},{2,3},{3,2},{4,5},{5,4},{6,7},{7,6},{8,9},{9,8},{10,11... | collective-permute-start | bytes 786440 | tf_op jit(solution)/shard_map/ppermute | solution.py:249
  91.5 22.8 %collective-permute-start.14 = (bf16[8,16,2048]{2,1,0:T(8,128)(2,1)S(1)}, bf16[8,16,2048]{2,1,0:T(8,128)(2,1)S(1)}, u32[]{:S(2)}, u32[]{:S(2)}) collective-permute-start(bf16[8,16,2048]{2,1,0:T(8,128)(2,1)S(1)} %all-to-all-done.2.mine_ref), channel_id=1, source_target_pairs={{0,8},{8,0},{1,9},{9,1},{2,10},{10,2},{3,11},{11,3},{4,12},{12,4},... | collective-permute-start | bytes 1572872 | tf_op jit(solution)/shard_map/ppermute | solution.py:265
  92.9 5.9 %collective-permute-start.6 = (bf16[32,1024]{1,0:T(8,128)(2,1)S(1)}, bf16[32,1024]{1,0:T(8,128)(2,1)S(1)}, u32[]{:S(2)}, u32[]{:S(2)}) collective-permute-start(bf16[32,1024]{1,0:T(8,128)(2,1)S(1)} %get-tuple-element.35), channel_id=1, source_target_pairs={{0,4},{2,6},{4,0},{6,2},{1,5},{3,7},{5,1},{7,3},{8,12},{10,14},{12... | collective-permute-start | bytes 196616 | tf_op jit(solution)/shard_map/ppermute | solution.py:37
  93.0 6.2 %collective-permute-start.7 = (bf16[32,1024]{1,0:T(8,128)(2,1)S(1)}, bf16[32,1024]{1,0:T(8,128)(2,1)S(1)}, u32[]{:S(2)}, u32[]{:S(2)}) collective-permute-start(bf16[32,1024]{1,0:T(8,128)(2,1)S(1)} %get-tuple-element.36), channel_id=1, source_target_pairs={{0,2},{2,4},{4,6},{6,0},{1,3},{3,5},{5,7},{7,1},{8,10},{10,12},{12... | collective-permute-start | bytes 196616 | tf_op jit(solution)/shard_map/ppermute | solution.py:37
  93.8 5.5 %collective-permute-start.8 = (bf16[32,1024]{1,0:T(8,128)(2,1)S(1)}, bf16[32,1024]{1,0:T(8,128)(2,1)S(1)}, u32[]{:S(2)}, u32[]{:S(2)}) collective-permute-start(bf16[32,1024]{1,0:T(8,128)(2,1)S(1)} %get-tuple-element.37), channel_id=1, source_target_pairs={{0,6},{2,0},{4,2},{6,4},{1,7},{3,1},{5,3},{7,5},{8,14},{10,8},{12,... | collective-permute-start | bytes 196616 | tf_op jit(solution)/shard_map/ppermute | solution.py:37
  99.4 4.3 %collective-permute-start.9 = (bf16[32,1024]{1,0:T(8,128)(2,1)S(1)}, bf16[32,1024]{1,0:T(8,128)(2,1)S(1)}, u32[]{:S(2)}, u32[]{:S(2)}) collective-permute-start(bf16[32,1024]{1,0:T(8,128)(2,1)S(1)} %get-tuple-element.38.own_ref), channel_id=1, source_target_pairs={{0,1},{1,0},{2,3},{3,2},{4,5},{5,4},{6,7},{7,6},{8,9},{9,8},{10,11... | collective-permute-start | bytes 196616 | tf_op jit(solution)/shard_map/ppermute | solution.py:260
  103.8 6.5 %collective-permute-start.12 = (bf16[64,1024]{1,0:T(8,128)(2,1)S(1)}, bf16[64,1024]{1,0:T(8,128)(2,1)S(1)}, u32[]{:S(2)}, u32[]{:S(2)}) collective-permute-start(bf16[64,1024]{1,0:T(8,128)(2,1)S(1)} %shard_map.74.refs_0_), channel_id=1, source_target_pairs={{0,6},{2,0},{4,2},{6,4},{1,7},{3,1},{5,3},{7,5},{8,14},{10,8},{12,... | collective-permute-start | bytes 393224 | tf_op jit(solution)/shard_map/ppermute | solution.py:37
  106.4 6.5 %collective-permute-start.11 = (bf16[64,1024]{1,0:T(8,128)(2,1)S(1)}, bf16[64,1024]{1,0:T(8,128)(2,1)S(1)}, u32[]{:S(2)}, u32[]{:S(2)}) collective-permute-start(bf16[64,1024]{1,0:T(8,128)(2,1)S(1)} %shard_map.74.refs_0_), channel_id=1, source_target_pairs={{0,4},{2,6},{4,0},{6,2},{1,5},{3,7},{5,1},{7,3},{8,12},{10,14},{12... | collective-permute-start | bytes 393224 | tf_op jit(solution)/shard_map/ppermute | solution.py:37
  107.4 6.8 %collective-permute-start.10 = (bf16[64,1024]{1,0:T(8,128)(2,1)S(1)}, bf16[64,1024]{1,0:T(8,128)(2,1)S(1)}, u32[]{:S(2)}, u32[]{:S(2)}) collective-permute-start(bf16[64,1024]{1,0:T(8,128)(2,1)S(1)} %shard_map.74.refs_0_), channel_id=1, source_target_pairs={{0,2},{2,4},{4,6},{6,0},{1,3},{3,5},{5,7},{7,1},{8,10},{10,12},{12... | collective-permute-start | bytes 393224 | tf_op jit(solution)/shard_map/ppermute | solution.py:37
  123.5 2.0 %collective-permute-start.19 = (bf16[8,16,2048]{2,1,0:T(8,128)(2,1)S(1)}, bf16[8,16,2048]{2,1,0:T(8,128)(2,1)S(1)}, u32[]{:S(2)}, u32[]{:S(2)}) collective-permute-start(bf16[8,16,2048]{2,1,0:T(8,128)(2,1)S(1)} %get-tuple-element.52), channel_id=1, source_target_pairs={{0,8},{8,0},{1,9},{9,1},{2,10},{10,2},{3,11},{11,3},{4,12},{12,4},... | collective-permute-start | bytes 1572872 | tf_op jit(solution)/shard_map/ppermute | solution.py:248
  126.5 27.3 %all-to-all-start.3 = ((bf16[8,16,2048]{2,1,0:T(8,128)(2,1)}), bf16[8,16,2048]{2,1,0:T(8,128)(2,1)S(1)}, u32[]{:S(2)}, u32[]{:S(2)}) async-start(bf16[8,16,2048]{2,1,0:T(8,128)(2,1)} %shard_map.80), calls=%async_computation.3 | async-start | bytes 1048576 | tf_op jit(solution)/shard_map/all_to_all | solution.py:33
  133.7 12.4 %collective-permute-start.15 = (bf16[4,32,1024]{2,1,0:T(8,128)(2,1)S(1)}, bf16[4,32,1024]{2,1,0:T(8,128)(2,1)S(1)}, u32[]{:S(2)}, u32[]{:S(2)}) collective-permute-start(bf16[4,32,1024]{2,1,0:T(8,128)(2,1)S(1)} %get-tuple-element.43), channel_id=1, source_target_pairs={{0,1},{1,0},{2,3},{3,2},{4,5},{5,4},{6,7},{7,6},{8,9},{9,8},{10,11... | collective-permute-start | bytes 786440 | tf_op jit(solution)/shard_map/ppermute | solution.py:249
  146.2 6.1 %collective-permute-start.16 = (bf16[32,1024]{1,0:T(8,128)(2,1)S(1)}, bf16[32,1024]{1,0:T(8,128)(2,1)S(1)}, u32[]{:S(2)}, u32[]{:S(2)}) collective-permute-start(bf16[32,1024]{1,0:T(8,128)(2,1)S(1)} %get-tuple-element.45), channel_id=1, source_target_pairs={{0,4},{2,6},{4,0},{6,2},{1,5},{3,7},{5,1},{7,3},{8,12},{10,14},{12... | collective-permute-start | bytes 196616 | tf_op jit(solution)/shard_map/ppermute | solution.py:37
  147.3 5.7 %collective-permute-start.17 = (bf16[32,1024]{1,0:T(8,128)(2,1)S(1)}, bf16[32,1024]{1,0:T(8,128)(2,1)S(1)}, u32[]{:S(2)}, u32[]{:S(2)}) collective-permute-start(bf16[32,1024]{1,0:T(8,128)(2,1)S(1)} %get-tuple-element.46), channel_id=1, source_target_pairs={{0,2},{2,4},{4,6},{6,0},{1,3},{3,5},{5,7},{7,1},{8,10},{10,12},{12... | collective-permute-start | bytes 196616 | tf_op jit(solution)/shard_map/ppermute | solution.py:37
  147.7 5.3 %collective-permute-start.18 = (bf16[32,1024]{1,0:T(8,128)(2,1)S(1)}, bf16[32,1024]{1,0:T(8,128)(2,1)S(1)}, u32[]{:S(2)}, u32[]{:S(2)}) collective-permute-start(bf16[32,1024]{1,0:T(8,128)(2,1)S(1)} %get-tuple-element.47), channel_id=1, source_target_pairs={{0,6},{2,0},{4,2},{6,4},{1,7},{3,1},{5,3},{7,5},{8,14},{10,8},{12,... | collective-permute-start | bytes 196616 | tf_op jit(solution)/shard_map/ppermute | solution.py:37

commit v7 on v6

--- a/solution.py
+++ b/solution.py
@@ -13,7 +13,7 @@
 SIZES = (4, 2, 2, 4, 2)
 SWAP = [(0, 1), (1, 0)]
 D, BR, COLS = 256, 1024, 2048
-TN, RC, BLOCK = 256, 256, 128
+TN, RC = 512, 256
 VMEM = pl.BlockSpec(memory_space=pltpu.VMEM)
 
 
@@ -44,29 +44,15 @@
     return total
 
 
-def prepared_kernel(counts_ref, out_ref):
-    values = counts_ref[...].astype(jnp.float32).astype(jnp.bfloat16)
-    for at in range(COLS // TN):
-        out_ref[at] = values[:, at * TN : at * TN + TN]
-
-
-def prepared(counts):
-    return pl.pallas_call(
-        prepared_kernel,
-        grid=(BR // BLOCK,),
-        out_shape=pltpu.HBM((COLS // TN, BR, TN), jnp.bfloat16),
-        in_specs=[pl.BlockSpec((BLOCK, COLS), lambda at: (at, 0))],
-        out_specs=pl.BlockSpec((COLS // TN, BLOCK, TN), lambda at: (0, at, 0)),
-        compiler_params=pltpu.CompilerParams(vmem_limit_bytes=6 * 2**20),
-        cost_estimate=cost(BR * COLS, 12 * 2**20),
-        name="prepared",
-    )(in_hbm(counts))
-
-
-def first_kernel(emb_ref, sums_ref, out_ref):
+def first_kernel(emb_ref, sums_ref, out_ref, total_ref):
     sums = sums_ref[...]
     digits = [(sums & 127).astype(jnp.float32), ((sums >> 7) & 127).astype(jnp.float32), (sums >> 14).astype(jnp.float32)]
     out_ref[...] = jnp.concatenate([emb_ref[...]] + digits + [jnp.zeros((5, BR), jnp.float32)]).astype(jnp.bfloat16)
+    total_ref[...] = jnp.broadcast_to(jnp.sum(sums, axis=1, keepdims=True), (8, 128))
+
+
+def added_kernel(one_ref, other_ref, out_ref):
+    out_ref[...] = one_ref[...] + other_ref[...]
 
 
 def joined_first_kernel(own_ref, other_ref, out_ref):
@@ -83,15 +69,12 @@
             flat_ref[pl.ds(place, 1)] = row_refs[shift][pl.ds(32 * other, 32), :][None]
 
 
-def second_kernel(*refs):
-    row_refs, (emb_ref, sums_ref, flat_ref, row_log_ref, out_ref) = refs[:4], refs[4:]
-    placed(row_refs, flat_ref)
-    digits = row_refs[0][64:, :].astype(jnp.float32)
-    for ref in row_refs[1:]:
-        digits += ref[64:, :].astype(jnp.float32)
-    marg = digits[0:1] + 128.0 * digits[1:2] + 16384.0 * digits[2:3]
-    row_log_ref[...] = 0.5 * jnp.log(marg)
-    total = jnp.broadcast_to(jnp.sum(marg.astype(jnp.int32), axis=1, keepdims=True), (1, COLS))
+def second_kernel(emb_ref, sums_ref, *refs):
+    total_refs, out_ref = refs[:4], refs[4]
+    total = total_refs[0][...]
+    for ref in total_refs[1:]:
+        total += ref[...]
+    total = jnp.tile(total[:1], (1, COLS // 128))
     lane = lax.broadcasted_iota(jnp.int32, (1, COLS), 1)
     parts = jnp.where(lane < 4, (total >> (8 * jnp.minimum(lane, 3))) & 255, 0)
     sums = sums_ref[...]
@@ -101,23 +84,37 @@
         out_ref[at] = parcel
 
 
+def arranged_first_kernel(*refs):
+    row_refs, (flat_ref, row_log_ref) = refs[:4], refs[4:]
+    placed(row_refs, flat_ref)
+    digits = row_refs[0][64:, :].astype(jnp.float32)
+    for ref in row_refs[1:]:
+        digits += ref[64:, :].astype(jnp.float32)
+    row_log_ref[...] = 0.5 * jnp.log(digits[0:1] + 128.0 * digits[1:2] + 16384.0 * digits[2:3])
+
+
+def total_kernel(mine_ref, out_ref):
+    digits = rows_sum(mine_ref, slice(16, 24))[2:3, :128]
+    lane = lax.broadcasted_iota(jnp.int32, (1, 128), 1)
+    scale = jnp.where(lane == 0, 1.0, jnp.where(lane == 1, 256.0, jnp.where(lane == 2, 65536.0, 16777216.0)))
+    total = jnp.sum(jnp.where(lane < 4, digits * scale, 0.0), axis=1, keepdims=True)
+    out_ref[...] = jnp.broadcast_to(total, (8, 128))
+
+
 def arranged_kernel(*refs):
     placed(refs[:4], refs[4])
 
 
-def col_log_kernel(mine_ref, theirs_ref, out_ref):
+def col_log_kernel(mine_ref, theirs_ref, total_ref, other_ref, out_ref):
     digits = rows_sum(mine_ref, slice(16, 24)) + rows_sum(theirs_ref, slice(16, 24))
-    lane = lax.broadcasted_iota(jnp.int32, (1, 128), 1)
-    scale = jnp.where(lane == 0, 1.0, jnp.where(lane == 1, 256.0, jnp.where(lane == 2, 65536.0, 16777216.0)))
-    total = jnp.sum(jnp.where(lane < 4, digits[2:3, :128] * scale, 0.0), axis=1, keepdims=True)
-    total_log = jnp.log(jnp.broadcast_to(total, (1, COLS)))
-    out_ref[...] = 0.5 * jnp.log(digits[0:1] + 256.0 * digits[1:2]) - 0.5 * total_log
+    total = jnp.tile(jnp.log(total_ref[:1] + other_ref[:1]), (1, COLS // 128))
+    out_ref[...] = 0.5 * jnp.log(digits[0:1] + 256.0 * digits[1:2]) - 0.5 * total
 
 
 def sweep_kernel(row_flat, mine_ref, theirs_ref, row_logs, col_log_ref, counts_ref, *refs):
     own_out, pair_out, home_out, away_out = refs[:4]
     col_flat, col_tall, grads, turned, counts, row_tall, row_log_ref, arrived = refs[4:]
-    copies = [pltpu.make_async_copy(counts_ref.at[at], counts.at[at], arrived.at[at]) for at in range(COLS // TN)]
+    copies = [pltpu.make_async_copy(counts_ref.at[:, pl.ds(at * TN, TN)], counts.at[at], arrived.at[at]) for at in range(COLS // TN)]
     for copy in copies:
         copy.start()
     core, z, yl = lax.axis_index("c"), lax.axis_index("z"), lax.axis_index("yl")
@@ -127,6 +124,13 @@
         row_log_ref[here, :] = jnp.broadcast_to(row_logs[:, here], (128, 128)).T
     col_flat[:, pl.ds(core, 1)] = mine_ref[:, :16, :][:, None]
     col_flat[:, pl.ds(1 - core, 1)] = theirs_ref[:, :16, :][:, None]
+    def col_part(start):
+        here = slice(start, start + 256)
+        part = jnp.dot(row_flat[...].reshape(D, BR), grads[:, here], preferred_element_type=jnp.float32).reshape(8, 2, 16, 256)
+        even, odd = part[:, 0].astype(jnp.bfloat16), part[:, 1].astype(jnp.bfloat16)
+        home_out[:, :, here] = jnp.where(core == 0, even, odd)
+        away_out[:, :, here] = jnp.where(core == 0, odd, even)
+
     for at in range(COLS // TN):
         here = slice(at * TN, at * TN + TN)
         col = col_flat[:, :, :, here].reshape(D, TN)
@@ -136,16 +140,16 @@
         for chunk in range(BR // RC):
             rows = slice(chunk * RC, chunk * RC + RC)
             scores = jnp.dot(row_tall[rows, :], col, preferred_element_type=jnp.float32)
+            if at and chunk % 2 == 0:
+                col_part((at - 1) * TN + chunk * 128)
             values = counts[at, rows, :].astype(jnp.float32)
             least = jnp.maximum(values, 1.0)
             errors = scores - 0.5 * jnp.log(least) + (shift + jnp.tile(row_log_ref[rows, :], (1, TN // 128)))
             weight = 0.2 + 0.5 * (least * lax.rsqrt(least))
             grad = jnp.where(values > 0.0, weight * errors, 0.5 * jnp.tanh(errors) + 0.5)
             grads[rows, here] = grad.astype(jnp.bfloat16)
-    col_grad = jnp.dot(row_flat[...].reshape(D, BR), grads[...], preferred_element_type=jnp.float32).reshape(8, 2, 16, COLS)
-    even, odd = col_grad[:, 0], col_grad[:, 1]
-    home_out[...] = jnp.where(core == 0, even, odd).astype(jnp.bfloat16)
-    away_out[...] = jnp.where(core == 0, odd, even).astype(jnp.bfloat16)
+    for start in range(COLS - TN, COLS, 256):
+        col_part(start)
     for chunk in range(BR // 256):
         rows = slice(chunk * 256, chunk * 256 + 256)
         part = jnp.dot(grads[rows, :], col_tall[...], preferred_element_type=jnp.float32)
@@ -167,12 +171,12 @@
             pltpu.VMEM((COLS, D), jnp.bfloat16),
             pltpu.VMEM((BR, COLS), jnp.bfloat16),
             pltpu.VMEM((8, 32, BR), jnp.bfloat16),
-            pltpu.VMEM((COLS // TN, BR, TN), jnp.bfloat16),
+            pltpu.VMEM((COLS // TN, BR, TN), jnp.int32),
             pltpu.VMEM((BR, D), jnp.bfloat16),
             pltpu.VMEM((BR, 128), jnp.float32),
             pltpu.SemaphoreType.DMA((COLS // TN,)),
         ],
-        compiler_params=pltpu.CompilerParams(vmem_limit_bytes=24 * 2**20),
+        compiler_params=pltpu.CompilerParams(vmem_limit_bytes=32 * 2**20),
         cost_estimate=cost(6 * D * BR * COLS, 20 * 2**20),
         name="sweep",
     )(*args)
@@ -233,18 +237,24 @@
 def on_device(counts, row_emb, col_emb, row_accum, col_accum):
     row_sums = jnp.sum(counts, axis=1)[None]
     col_sums = jnp.sum(counts, axis=0)[None]
-    parcel = small(first_kernel, shape((40, BR), jnp.bfloat16))(row_emb, row_sums)
+    outs = (shape((40, BR), jnp.bfloat16), shape((8, 128), jnp.int32))
+    parcel, total = small(first_kernel, outs)(row_emb, row_sums)
+    other_total = lax.ppermute(total, "c", SWAP)
     other = lax.ppermute(parcel, "yl", SWAP)
+    total = small(added_kernel, shape((8, 128), jnp.int32))(total, other_total)
+    totals = [total, over_z(total, 1), over_z(total, 2), over_z(total, 3)]
+    copies = small(second_kernel, shape((8, 24, COLS), jnp.bfloat16))(col_emb, col_sums, *totals)
     pair = small(joined_first_kernel, shape((72, BR), jnp.bfloat16))(parcel, other)
+    mine = to_each(copies, CHIPS)
     row = [pair, over_z(pair, 1), over_z(pair, 2), over_z(pair, 3)]
-    outs = (shape((8, 32, BR), jnp.bfloat16), shape((1, BR), jnp.float32), shape((8, 24, COLS), jnp.bfloat16))
-    row, row_log, copies = small(second_kernel, outs)(*row, col_emb, col_sums)
-    mine = to_each(copies, CHIPS)
-    small_counts = prepared(counts)
+    outs = (shape((8, 32, BR), jnp.bfloat16), shape((1, BR), jnp.float32))
+    row, row_log = small(arranged_first_kernel, outs)(*row)
     theirs = lax.ppermute(mine, "c", SWAP)
-    col_log = small(col_log_kernel, shape((1, COLS), jnp.float32))(mine, theirs)
+    total = small(total_kernel, shape((8, 128), jnp.float32))(mine)
+    other_total = lax.ppermute(total, "yl", SWAP)
+    col_log = small(col_log_kernel, shape((1, COLS), jnp.float32))(mine, theirs, total, other_total)
     for sweep in range(2):
-        own, away_pair, home, away = swept(row, mine, theirs, row_log, col_log, in_hbm(small_counts))
+        own, away_pair, home, away = swept(row, mine, theirs, row_log, col_log, in_hbm(counts))
         theirs = lax.ppermute(away, "c", SWAP)
         from_pair = lax.ppermute(away_pair, "yl", SWAP)
         both = small(home_kernel, shape((8, 16, COLS), jnp.bfloat16))(home, theirs)

time: 156 us -> 156 us (level)
  Pallas kernels: 30.6 us -> 22.6 us
  waiting for transfers between devices: 52.6 us -> 57.6 us
  starting transfers between devices: 32 us -> 36.5 us
    pallas_call x4 -> x6, Pallas kernels: 8.02 us -> 0.4 us  [the longest x1 0.1 us: on_device(): small(col_log_kernel, shape((1, COLS), jnp.float32))]
    ppermute x12 -> x15, starting transfers between devices: 16.8 us -> 21.7 us  [over_z(): return lax.ppermute(value, 'z', [(at, (at + shift) % 4) for at in range(4)])]
    ppermute x12 -> x15, waiting for transfers between devices: 19.6 us -> 22.1 us  [over_z(): return lax.ppermute(value, 'z', [(at, (at + shift) % 4) for at in range(4)])]
  transfers between devices with their start and end apart: 22 -> 27, of which waited for: 17 -> 20; matrix products, arithmetic and copies ran while one was open for 0% -> 0% of each run, Pallas kernels for 6% -> 1%
where the time goes in v7:
time: 156 us
  waiting for transfers between devices  57.6 us (37%)
  starting transfers between devices  36.5 us (23%)
  blocking collectives  34.1 us (22%)
  Pallas kernels  22.6 us (14%)
  other arithmetic  4.05 us (3%)
    all_to_all x2, blocking collectives, to_each(): return lax.all_to_all(copies, axes, 0, 0, tiled=True)  34.1 us
    ppermute x15, waiting for transfers between devices, over_z(): return lax.ppermute(value, 'z', [(at, (at + shift) % 4) for at in range(4)])  22.1 us
    ppermute x15, starting transfers between devices, over_z(): return lax.ppermute(value, 'z', [(at, (at + shift) % 4) for at in range(4)])  21.7 us
    pallas_call x2, Pallas kernels, swept(): pl.pallas_call(sweep_kernel, out_shape=(shape((4, 32, BR), jnp.bfloat16),...  18.2 us
    ppermute x2, waiting for transfers between devices, on_device(): from_pair = lax.ppermute(away_pair, 'yl', SWAP)  13.3 us
    all_to_all x2, starting transfers between devices, to_each(): return lax.all_to_all(copies, axes, 0, 0, tiled=True)  10.9 us
    all_to_all x2, waiting for transfers between devices, to_each(): return lax.all_to_all(copies, axes, 0, 0, tiled=True)  10 us
    ppermute x1, waiting for transfers between devices, on_device(): other = lax.ppermute(parcel, 'yl', SWAP)  4.18 us
  transfers between devices with their start and end apart: 27, of which 20 were waited for; matrix products, arithmetic and copies ran while one was open for 0% of the time, Pallas kernels for 1%

profile of v7, /device:TPU:0, one launch (start us, length us, event | category | flops | bytes accessed | tf_op | source)
XLA Modules:
  0.0 155.6 jit_solution(6892728627085863497)
XLA Ops:
  0.6 4.1 %fusion = (s32[2048]{0:T(1024)S(1)}, s32[1024]{0:T(1024)S(1)}) fusion(s32[1024,2048]{1,0:T(8,128)} %counts_ref.3), kind=kLoop, calls=%fused_computation | loop fusion | flops 4191232 | bytes 8400896 | tf_op jit(solution)/shard_map/reduce_sum | solution.py:239
  4.8 1.2 collective-permute-done.4.other_ref
  6.0 4.1 %collective-permute-start.7 = (s32[8,128]{1,0:T(8,128)S(1)}, s32[8,128]{1,0:T(8,128)S(1)}, u32[]{:S(2)}, u32[]{:S(2)}) collective-permute-start(s32[8,128]{1,0:T(8,128)S(1)} %shard_map.71.refs_0_), channel_id=1, source_target_pairs={{0,6},{2,0},{4,2},{6,4},{1,7},{3,1},{5,3},{7,5},{8,14},{10,8},{12,... | collective-permute-start | bytes 12296 | tf_op jit(solution)/shard_map/ppermute | solution.py:37
  10.1 1.3 collective-permute-start.5
  11.5 3.8 %collective-permute-done.6.refs_2_ = s32[8,128]{1,0:T(8,128)S(1)} collective-permute-done((s32[8,128]{1,0:T(8,128)S(1)}, s32[8,128]{1,0:T(8,128)S(1)}, u32[]{:S(2)}, u32[]{:S(2)}) %collective-permute-start.6) | collective-permute-done | bytes 4128 | tf_op jit(solution)/shard_map/ppermute | solution.py:37
  15.3 19.7 %all_to_all.20.mine_ref = bf16[8,24,2048]{2,1,0:T(8,128)(2,1)S(1)} all-to-all(bf16[8,24,2048]{2,1,0:T(8,128)(2,1)S(1)} %shard_map.72), channel_id=1, replica_groups=mesh['x'=4,'yh'=2,'c'=2,'z'=4,'yl'=2] {'x','yh'}, dimensions={0} | all-to-all | bytes 1572864 | tf_op jit(solution)/shard_map/all_to_all | solution.py:33
  35.0 0.7 collective-permute-start
  35.7 4.2 %collective-permute-done.other_ref = bf16[40,1024]{1,0:T(8,128)(2,1)S(1)} collective-permute-done((bf16[40,1024]{1,0:T(8,128)(2,1)S(1)}, bf16[40,1024]{1,0:T(8,128)(2,1)S(1)}, u32[]{:S(2)}, u32[]{:S(2)}) %collective-permute-start) | collective-permute-done | bytes 81952 | tf_op jit(solution)/shard_map/ppermute | solution.py:243
  39.9 1.0 collective-permute-start.3
  40.8 0.9 collective-permute-start.2
  41.8 1.3 collective-permute-start.1
  43.2 0.7 collective-permute-start.9
  43.9 2.8 %collective-permute-done.3.refs_3_ = bf16[72,1024]{1,0:T(8,128)(2,1)S(1)} collective-permute-done((bf16[72,1024]{1,0:T(8,128)(2,1)S(1)}, bf16[72,1024]{1,0:T(8,128)(2,1)S(1)}, u32[]{:S(2)}, u32[]{:S(2)}) %collective-permute-start.3) | collective-permute-done | bytes 147488 | tf_op jit(solution)/shard_map/ppermute | solution.py:37
  46.7 2.4 %collective-permute-done.2.refs_2_ = bf16[72,1024]{1,0:T(8,128)(2,1)S(1)} collective-permute-done((bf16[72,1024]{1,0:T(8,128)(2,1)S(1)}, bf16[72,1024]{1,0:T(8,128)(2,1)S(1)}, u32[]{:S(2)}, u32[]{:S(2)}) %collective-permute-start.2) | collective-permute-done | bytes 147488 | tf_op jit(solution)/shard_map/ppermute | solution.py:37
  49.0 1.6 %collective-permute-done.1.refs_1_ = bf16[72,1024]{1,0:T(8,128)(2,1)S(1)} collective-permute-done((bf16[72,1024]{1,0:T(8,128)(2,1)S(1)}, bf16[72,1024]{1,0:T(8,128)(2,1)S(1)}, u32[]{:S(2)}, u32[]{:S(2)}) %collective-permute-start.1) | collective-permute-done | bytes 147488 | tf_op jit(solution)/shard_map/ppermute | solution.py:37
  50.8 9.0 %sweep.2 = (bf16[4,32,1024]{2,1,0:T(8,128)(2,1)S(1)}, bf16[4,32,1024]{2,1,0:T(8,128)(2,1)S(1)}, bf16[8,16,2048]{2,1,0:T(8,128)(2,1)S(1)}, bf16[8,16,2048]{2,1,0:T(8,128)(2,1)S(1)}) custom-call(bf16[8,32,1024]{2,1,0:T(8,128)(2,1)S(1)} %get-tuple-element.31.row_flat, bf16[8,24,2048]{2,1,0:T(8,128)(2,1)S(1)} %all_to_all.20.mine_ref, ...), custom_call_target="tpu_custom_call" | custom-call | flops 3221225472 | bytes 20971520 | tf_op jit(solution)/shard_map/sweep/pallas_call | solution.py:164
  59.9 0.3 collective-permute-start.18
  60.2 1.9 %collective-permute-done.18.theirs_ref = bf16[8,16,2048]{2,1,0:T(8,128)(2,1)S(1)} collective-permute-done((bf16[8,16,2048]{2,1,0:T(8,128)(2,1)S(1)}, bf16[8,16,2048]{2,1,0:T(8,128)(2,1)S(1)}, u32[]{:S(2)}, u32[]{:S(2)}) %collective-permute-start.18) | collective-permute-done | bytes 524320 | tf_op jit(solution)/shard_map/ppermute | solution.py:258
  62.2 14.4 %all_to_all.21.came_ref = bf16[8,16,2048]{2,1,0:T(8,128)(2,1)S(1)} all-to-all(bf16[8,16,2048]{2,1,0:T(8,128)(2,1)S(1)} %shard_map.79), channel_id=1, replica_groups=mesh['x'=4,'yh'=2,'c'=2,'z'=4,'yl'=2] {'x','yh'}, dimensions={0} | all-to-all | bytes 1048576 | tf_op jit(solution)/shard_map/all_to_all | solution.py:33
  76.6 0.9 shard_map.80
  77.6 3.5 %all-to-all-start.2 = ((bf16[8,16,2048]{2,1,0:T(8,128)(2,1)}), bf16[8,16,2048]{2,1,0:T(8,128)(2,1)S(1)}, u32[]{:S(2)}, u32[]{:S(2)}) async-start(bf16[8,16,2048]{2,1,0:T(8,128)(2,1)} %get-tuple-element.43), calls=%async_computation.2 | async-start | bytes 1048576 | tf_op jit(solution)/shard_map/all_to_all | solution.py:33
  81.0 0.8 collective-permute-start.10
  81.8 10.0 %all-to-all-done.2.mine_ref = bf16[8,16,2048]{2,1,0:T(8,128)(2,1)S(1)} async-done(((bf16[8,16,2048]{2,1,0:T(8,128)(2,1)}), bf16[8,16,2048]{2,1,0:T(8,128)(2,1)S(1)}, u32[]{:S(2)}, u32[]{:S(2)}) %all-to-all-start.2) | async-done | bytes 524320 | tf_op jit(solution)/shard_map/all_to_all | solution.py:33
  91.8 1.0 collective-permute-done.10.came_ref
  92.9 1.3 collective-permute-start.11
  94.2 0.2 collective-permute-start.12
  94.4 3.1 %collective-permute-start.13 = (bf16[32,1024]{1,0:T(8,128)(2,1)S(1)}, bf16[32,1024]{1,0:T(8,128)(2,1)S(1)}, u32[]{:S(2)}, u32[]{:S(2)}) collective-permute-start(bf16[32,1024]{1,0:T(8,128)(2,1)S(1)} %get-tuple-element.39), channel_id=1, source_target_pairs={{0,6},{2,0},{4,2},{6,4},{1,7},{3,1},{5,3},{7,5},{8,14},{10,8},{12,... | collective-permute-start | bytes 196616 | tf_op jit(solution)/shard_map/ppermute | solution.py:37
  97.5 1.3 collective-permute-done.11.first_ref
  98.7 1.0 collective-permute-done.12.second_ref
  99.8 1.3 collective-permute-start.14
  101.1 3.1 %collective-permute-done.14.other_ref = bf16[32,1024]{1,0:T(8,128)(2,1)S(1)} collective-permute-done((bf16[32,1024]{1,0:T(8,128)(2,1)S(1)}, bf16[32,1024]{1,0:T(8,128)(2,1)S(1)}, u32[]{:S(2)}, u32[]{:S(2)}) %collective-permute-start.14) | collective-permute-done | bytes 65568 | tf_op jit(solution)/shard_map/ppermute | solution.py:270
  104.2 3.3 %collective-permute-start.17 = (bf16[64,1024]{1,0:T(8,128)(2,1)S(1)}, bf16[64,1024]{1,0:T(8,128)(2,1)S(1)}, u32[]{:S(2)}, u32[]{:S(2)}) collective-permute-start(bf16[64,1024]{1,0:T(8,128)(2,1)S(1)} %shard_map.77.refs_0_), channel_id=1, source_target_pairs={{0,6},{2,0},{4,2},{6,4},{1,7},{3,1},{5,3},{7,5},{8,14},{10,8},{12,... | collective-permute-start | bytes 393224 | tf_op jit(solution)/shard_map/ppermute | solution.py:37
  107.5 0.9 collective-permute-start.15
  108.4 3.0 %collective-permute-done.17.refs_3_ = bf16[64,1024]{1,0:T(8,128)(2,1)S(1)} collective-permute-done((bf16[64,1024]{1,0:T(8,128)(2,1)S(1)}, bf16[64,1024]{1,0:T(8,128)(2,1)S(1)}, u32[]{:S(2)}, u32[]{:S(2)}) %collective-permute-start.17) | collective-permute-done | bytes 131104 | tf_op jit(solution)/shard_map/ppermute | solution.py:37
  111.4 2.6 %collective-permute-done.16.refs_2_ = bf16[64,1024]{1,0:T(8,128)(2,1)S(1)} collective-permute-done((bf16[64,1024]{1,0:T(8,128)(2,1)S(1)}, bf16[64,1024]{1,0:T(8,128)(2,1)S(1)}, u32[]{:S(2)}, u32[]{:S(2)}) %collective-permute-start.16) | collective-permute-done | bytes 131104 | tf_op jit(solution)/shard_map/ppermute | solution.py:37
  114.0 1.0 collective-permute-done.15.refs_1_
  115.1 9.1 %sweep.3 = (bf16[4,32,1024]{2,1,0:T(8,128)(2,1)S(1)}, bf16[4,32,1024]{2,1,0:T(8,128)(2,1)S(1)}, bf16[8,16,2048]{2,1,0:T(8,128)(2,1)S(1)}, bf16[8,16,2048]{2,1,0:T(8,128)(2,1)S(1)}) custom-call(bf16[8,32,1024]{2,1,0:T(8,128)(2,1)S(1)} %shard_map.78.row_flat, bf16[8,16,2048]{2,1,0:T(8,128)(2,1)S(1)} %all-to-all-done.2.mine_ref, ...), custom_call_target="tpu_custom_call" | custom-call | flops 3221225472 | bytes 20971520 | tf_op jit(solution)/shard_map/sweep/pallas_call | solution.py:164
  124.3 1.9 %collective-permute-done.24.theirs_ref = bf16[8,16,2048]{2,1,0:T(8,128)(2,1)S(1)} collective-permute-done((bf16[8,16,2048]{2,1,0:T(8,128)(2,1)S(1)}, bf16[8,16,2048]{2,1,0:T(8,128)(2,1)S(1)}, u32[]{:S(2)}, u32[]{:S(2)}) %collective-permute-start.24) | collective-permute-done | bytes 524320 | tf_op jit(solution)/shard_map/ppermute | solution.py:258
  126.2 0.9 shard_map.83
  127.2 7.4 %all-to-all-start.3 = ((bf16[8,16,2048]{2,1,0:T(8,128)(2,1)}), bf16[8,16,2048]{2,1,0:T(8,128)(2,1)S(1)}, u32[]{:S(2)}, u32[]{:S(2)}) async-start(bf16[8,16,2048]{2,1,0:T(8,128)(2,1)} %shard_map.83), calls=%async_computation.3 | async-start | bytes 1048576 | tf_op jit(solution)/shard_map/all_to_all | solution.py:33
  134.7 12.3 %collective-permute-done.20.came_ref = bf16[4,32,1024]{2,1,0:T(8,128)(2,1)S(1)} collective-permute-done((bf16[4,32,1024]{2,1,0:T(8,128)(2,1)S(1)}, bf16[4,32,1024]{2,1,0:T(8,128)(2,1)S(1)}, u32[]{:S(2)}, u32[]{:S(2)}) %collective-permute-start.20) | collective-permute-done | bytes 262176 | tf_op jit(solution)/shard_map/ppermute | solution.py:259
  147.0 1.0 collective-permute-start.21
  148.0 0.8 collective-permute-start.22
  148.9 2.4 %collective-permute-start.23 = (bf16[32,1024]{1,0:T(8,128)(2,1)S(1)}, bf16[32,1024]{1,0:T(8,128)(2,1)S(1)}, u32[]{:S(2)}, u32[]{:S(2)}) collective-permute-start(bf16[32,1024]{1,0:T(8,128)(2,1)S(1)} %get-tuple-element.49), channel_id=1, source_target_pairs={{0,6},{2,0},{4,2},{6,4},{1,7},{3,1},{5,3},{7,5},{8,14},{10,8},{12,... | collective-permute-start | bytes 196616 | tf_op jit(solution)/shard_map/ppermute | solution.py:37
  151.3 1.9 %collective-permute-done.21.first_ref = bf16[32,1024]{1,0:T(8,128)(2,1)S(1)} collective-permute-done((bf16[32,1024]{1,0:T(8,128)(2,1)S(1)}, bf16[32,1024]{1,0:T(8,128)(2,1)S(1)}, u32[]{:S(2)}, u32[]{:S(2)}) %collective-permute-start.21) | collective-permute-done | bytes 65568 | tf_op jit(solution)/shard_map/ppermute | solution.py:37
  153.2 0.7 collective-permute-done.22.second_ref
  153.9 0.8 shard_map.82
  154.6 1.0 shard_map.84
  (36 shorter events, 1.2 us)
Async XLA Ops:
  0.6 4.1 %copy-start.1 = (f32[32,1024]{1,0:T(8,128)S(1)}, f32[32,1024]{1,0:T(8,128)}, u32[]{:S(2)}) copy-start(f32[32,1024]{1,0:T(8,128)} %emb_ref.6) | copy-start | bytes 393220
  0.6 14.6 %copy-start = (f32[16,2048]{1,0:T(8,128)S(1)}, f32[16,2048]{1,0:T(8,128)}, u32[]{:S(2)}) copy-start(f32[16,2048]{1,0:T(8,128)} %emb_ref.7) | copy-start | bytes 393220
  4.8 1.2 collective-permute-start.4
  6.0 5.5 %collective-permute-start.7 = (s32[8,128]{1,0:T(8,128)S(1)}, s32[8,128]{1,0:T(8,128)S(1)}, u32[]{:S(2)}, u32[]{:S(2)}) collective-permute-start(s32[8,128]{1,0:T(8,128)S(1)} %shard_map.71.refs_0_), channel_id=1, source_target_pairs={{0,6},{2,0},{4,2},{6,4},{1,7},{3,1},{5,3},{7,5},{8,14},{10,8},{12,... | collective-permute-start | bytes 12296 | tf_op jit(solution)/shard_map/ppermute | solution.py:37
  10.1 5.1 %collective-permute-start.6 = (s32[8,128]{1,0:T(8,128)S(1)}, s32[8,128]{1,0:T(8,128)S(1)}, u32[]{:S(2)}, u32[]{:S(2)}) collective-permute-start(s32[8,128]{1,0:T(8,128)S(1)} %shard_map.71.refs_0_), channel_id=1, source_target_pairs={{0,4},{2,6},{4,0},{6,2},{1,5},{3,7},{5,1},{7,3},{8,12},{10,14},{12... | collective-permute-start | bytes 12296 | tf_op jit(solution)/shard_map/ppermute | solution.py:37
  10.1 5.1 %collective-permute-start.5 = (s32[8,128]{1,0:T(8,128)S(1)}, s32[8,128]{1,0:T(8,128)S(1)}, u32[]{:S(2)}, u32[]{:S(2)}) collective-permute-start(s32[8,128]{1,0:T(8,128)S(1)} %shard_map.71.refs_0_), channel_id=1, source_target_pairs={{0,2},{2,4},{4,6},{6,0},{1,3},{3,5},{5,7},{7,1},{8,10},{10,12},{12... | collective-permute-start | bytes 12296 | tf_op jit(solution)/shard_map/ppermute | solution.py:37
  35.0 15.7 %collective-permute-start.8 = (bf16[8,24,2048]{2,1,0:T(8,128)(2,1)S(1)}, bf16[8,24,2048]{2,1,0:T(8,128)(2,1)S(1)}, u32[]{:S(2)}, u32[]{:S(2)}) collective-permute-start(bf16[8,24,2048]{2,1,0:T(8,128)(2,1)S(1)} %all_to_all.20.mine_ref), channel_id=1, source_target_pairs={{0,8},{8,0},{1,9},{9,1},{2,10},{10,2},{3,11},{11,3},{4,12},{12,4},... | collective-permute-start | bytes 2359304 | tf_op jit(solution)/shard_map/ppermute | solution.py:252
  35.0 4.9 %collective-permute-start = (bf16[40,1024]{1,0:T(8,128)(2,1)S(1)}, bf16[40,1024]{1,0:T(8,128)(2,1)S(1)}, u32[]{:S(2)}, u32[]{:S(2)}) collective-permute-start(bf16[40,1024]{1,0:T(8,128)(2,1)S(1)} %get-tuple-element.30.own_ref), channel_id=1, source_target_pairs={{0,1},{1,0},{2,3},{3,2},{4,5},{5,4},{6,7},{7,6},{8,9},{9,8},{10,11... | collective-permute-start | bytes 245768 | tf_op jit(solution)/shard_map/ppermute | solution.py:243
  39.9 6.8 %collective-permute-start.3 = (bf16[72,1024]{1,0:T(8,128)(2,1)S(1)}, bf16[72,1024]{1,0:T(8,128)(2,1)S(1)}, u32[]{:S(2)}, u32[]{:S(2)}) collective-permute-start(bf16[72,1024]{1,0:T(8,128)(2,1)S(1)} %shard_map.69.refs_0_), channel_id=1, source_target_pairs={{0,6},{2,0},{4,2},{6,4},{1,7},{3,1},{5,3},{7,5},{8,14},{10,8},{12,... | collective-permute-start | bytes 442376 | tf_op jit(solution)/shard_map/ppermute | solution.py:37
  40.8 8.2 %collective-permute-start.2 = (bf16[72,1024]{1,0:T(8,128)(2,1)S(1)}, bf16[72,1024]{1,0:T(8,128)(2,1)S(1)}, u32[]{:S(2)}, u32[]{:S(2)}) collective-permute-start(bf16[72,1024]{1,0:T(8,128)(2,1)S(1)} %shard_map.69.refs_0_), channel_id=1, source_target_pairs={{0,4},{2,6},{4,0},{6,2},{1,5},{3,7},{5,1},{7,3},{8,12},{10,14},{12... | collective-permute-start | bytes 442376 | tf_op jit(solution)/shard_map/ppermute | solution.py:37
  41.8 8.8 %collective-permute-start.1 = (bf16[72,1024]{1,0:T(8,128)(2,1)S(1)}, bf16[72,1024]{1,0:T(8,128)(2,1)S(1)}, u32[]{:S(2)}, u32[]{:S(2)}) collective-permute-start(bf16[72,1024]{1,0:T(8,128)(2,1)S(1)} %shard_map.69.refs_0_), channel_id=1, source_target_pairs={{0,2},{2,4},{4,6},{6,0},{1,3},{3,5},{5,7},{7,1},{8,10},{10,12},{12... | collective-permute-start | bytes 442376 | tf_op jit(solution)/shard_map/ppermute | solution.py:37
  43.2 33.4 %copy-start.2 = (f32[16,2048]{1,0:T(8,128)S(1)}, f32[16,2048]{1,0:T(8,128)}, u32[]{:S(2)}) copy-start(f32[16,2048]{1,0:T(8,128)} %accum_ref.3) | copy-start | bytes 393220
  43.2 7.5 %collective-permute-start.9 = (f32[8,128]{1,0:T(8,128)S(1)}, f32[8,128]{1,0:T(8,128)S(1)}, u32[]{:S(2)}, u32[]{:S(2)}) collective-permute-start(f32[8,128]{1,0:T(8,128)S(1)} %shard_map.73.total_ref), channel_id=1, source_target_pairs={{0,1},{1,0},{2,3},{3,2},{4,5},{5,4},{6,7},{7,6},{8,9},{9,8},{10,11... | collective-permute-start | bytes 12296 | tf_op jit(solution)/shard_map/ppermute | solution.py:254
  50.8 48.9 %copy-start.3 = (f32[32,1024]{1,0:T(8,128)S(1)}, f32[32,1024]{1,0:T(8,128)}, u32[]{:S(2)}) copy-start(f32[32,1024]{1,0:T(8,128)} %accum_ref.2) | copy-start | bytes 393220
  59.9 2.2 %collective-permute-start.18 = (bf16[8,16,2048]{2,1,0:T(8,128)(2,1)S(1)}, bf16[8,16,2048]{2,1,0:T(8,128)(2,1)S(1)}, u32[]{:S(2)}, u32[]{:S(2)}) collective-permute-start(bf16[8,16,2048]{2,1,0:T(8,128)(2,1)S(1)} %get-tuple-element.42), channel_id=1, source_target_pairs={{0,8},{8,0},{1,9},{9,1},{2,10},{10,2},{3,11},{11,3},{4,12},{12,4},... | collective-permute-start | bytes 1572872 | tf_op jit(solution)/shard_map/ppermute | solution.py:258
  77.6 14.3 %all-to-all-start.2 = ((bf16[8,16,2048]{2,1,0:T(8,128)(2,1)}), bf16[8,16,2048]{2,1,0:T(8,128)(2,1)S(1)}, u32[]{:S(2)}, u32[]{:S(2)}) async-start(bf16[8,16,2048]{2,1,0:T(8,128)(2,1)} %get-tuple-element.43), calls=%async_computation.2 | async-start | bytes 1048576 | tf_op jit(solution)/shard_map/all_to_all | solution.py:33
  81.0 11.8 %collective-permute-start.10 = (bf16[4,32,1024]{2,1,0:T(8,128)(2,1)S(1)}, bf16[4,32,1024]{2,1,0:T(8,128)(2,1)S(1)}, u32[]{:S(2)}, u32[]{:S(2)}) collective-permute-start(bf16[4,32,1024]{2,1,0:T(8,128)(2,1)S(1)} %get-tuple-element.35), channel_id=1, source_target_pairs={{0,1},{1,0},{2,3},{3,2},{4,5},{5,4},{6,7},{7,6},{8,9},{9,8},{10,11... | collective-permute-start | bytes 786440 | tf_op jit(solution)/shard_map/ppermute | solution.py:259
  91.8 23.3 %collective-permute-start.19 = (bf16[8,16,2048]{2,1,0:T(8,128)(2,1)S(1)}, bf16[8,16,2048]{2,1,0:T(8,128)(2,1)S(1)}, u32[]{:S(2)}, u32[]{:S(2)}) collective-permute-start(bf16[8,16,2048]{2,1,0:T(8,128)(2,1)S(1)} %all-to-all-done.2.mine_ref), channel_id=1, source_target_pairs={{0,8},{8,0},{1,9},{9,1},{2,10},{10,2},{3,11},{11,3},{4,12},{12,4},... | collective-permute-start | bytes 1572872 | tf_op jit(solution)/shard_map/ppermute | solution.py:275
  92.9 5.8 %collective-permute-start.11 = (bf16[32,1024]{1,0:T(8,128)(2,1)S(1)}, bf16[32,1024]{1,0:T(8,128)(2,1)S(1)}, u32[]{:S(2)}, u32[]{:S(2)}) collective-permute-start(bf16[32,1024]{1,0:T(8,128)(2,1)S(1)} %get-tuple-element.37), channel_id=1, source_target_pairs={{0,4},{2,6},{4,0},{6,2},{1,5},{3,7},{5,1},{7,3},{8,12},{10,14},{12... | collective-permute-start | bytes 196616 | tf_op jit(solution)/shard_map/ppermute | solution.py:37
  94.2 5.5 %collective-permute-start.12 = (bf16[32,1024]{1,0:T(8,128)(2,1)S(1)}, bf16[32,1024]{1,0:T(8,128)(2,1)S(1)}, u32[]{:S(2)}, u32[]{:S(2)}) collective-permute-start(bf16[32,1024]{1,0:T(8,128)(2,1)S(1)} %get-tuple-element.38), channel_id=1, source_target_pairs={{0,2},{2,4},{4,6},{6,0},{1,3},{3,5},{5,7},{7,1},{8,10},{10,12},{12... | collective-permute-start | bytes 196616 | tf_op jit(solution)/shard_map/ppermute | solution.py:37
  94.4 5.3 %collective-permute-start.13 = (bf16[32,1024]{1,0:T(8,128)(2,1)S(1)}, bf16[32,1024]{1,0:T(8,128)(2,1)S(1)}, u32[]{:S(2)}, u32[]{:S(2)}) collective-permute-start(bf16[32,1024]{1,0:T(8,128)(2,1)S(1)} %get-tuple-element.39), channel_id=1, source_target_pairs={{0,6},{2,0},{4,2},{6,4},{1,7},{3,1},{5,3},{7,5},{8,14},{10,8},{12,... | collective-permute-start | bytes 196616 | tf_op jit(solution)/shard_map/ppermute | solution.py:37
  99.8 4.3 %collective-permute-start.14 = (bf16[32,1024]{1,0:T(8,128)(2,1)S(1)}, bf16[32,1024]{1,0:T(8,128)(2,1)S(1)}, u32[]{:S(2)}, u32[]{:S(2)}) collective-permute-start(bf16[32,1024]{1,0:T(8,128)(2,1)S(1)} %get-tuple-element.40.own_ref), channel_id=1, source_target_pairs={{0,1},{1,0},{2,3},{3,2},{4,5},{5,4},{6,7},{7,6},{8,9},{9,8},{10,11... | collective-permute-start | bytes 196616 | tf_op jit(solution)/shard_map/ppermute | solution.py:270
  104.2 7.2 %collective-permute-start.17 = (bf16[64,1024]{1,0:T(8,128)(2,1)S(1)}, bf16[64,1024]{1,0:T(8,128)(2,1)S(1)}, u32[]{:S(2)}, u32[]{:S(2)}) collective-permute-start(bf16[64,1024]{1,0:T(8,128)(2,1)S(1)} %shard_map.77.refs_0_), channel_id=1, source_target_pairs={{0,6},{2,0},{4,2},{6,4},{1,7},{3,1},{5,3},{7,5},{8,14},{10,8},{12,... | collective-permute-start | bytes 393224 | tf_op jit(solution)/shard_map/ppermute | solution.py:37
  107.5 6.6 %collective-permute-start.16 = (bf16[64,1024]{1,0:T(8,128)(2,1)S(1)}, bf16[64,1024]{1,0:T(8,128)(2,1)S(1)}, u32[]{:S(2)}, u32[]{:S(2)}) collective-permute-start(bf16[64,1024]{1,0:T(8,128)(2,1)S(1)} %shard_map.77.refs_0_), channel_id=1, source_target_pairs={{0,4},{2,6},{4,0},{6,2},{1,5},{3,7},{5,1},{7,3},{8,12},{10,14},{12... | collective-permute-start | bytes 393224 | tf_op jit(solution)/shard_map/ppermute | solution.py:37
  107.5 7.6 %collective-permute-start.15 = (bf16[64,1024]{1,0:T(8,128)(2,1)S(1)}, bf16[64,1024]{1,0:T(8,128)(2,1)S(1)}, u32[]{:S(2)}, u32[]{:S(2)}) collective-permute-start(bf16[64,1024]{1,0:T(8,128)(2,1)S(1)} %shard_map.77.refs_0_), channel_id=1, source_target_pairs={{0,2},{2,4},{4,6},{6,0},{1,3},{3,5},{5,7},{7,1},{8,10},{10,12},{12... | collective-permute-start | bytes 393224 | tf_op jit(solution)/shard_map/ppermute | solution.py:37
  124.2 2.0 %collective-permute-start.24 = (bf16[8,16,2048]{2,1,0:T(8,128)(2,1)S(1)}, bf16[8,16,2048]{2,1,0:T(8,128)(2,1)S(1)}, u32[]{:S(2)}, u32[]{:S(2)}) collective-permute-start(bf16[8,16,2048]{2,1,0:T(8,128)(2,1)S(1)} %get-tuple-element.54), channel_id=1, source_target_pairs={{0,8},{8,0},{1,9},{9,1},{2,10},{10,2},{3,11},{11,3},{4,12},{12,4},... | collective-permute-start | bytes 1572872 | tf_op jit(solution)/shard_map/ppermute | solution.py:258
  127.2 27.5 %all-to-all-start.3 = ((bf16[8,16,2048]{2,1,0:T(8,128)(2,1)}), bf16[8,16,2048]{2,1,0:T(8,128)(2,1)S(1)}, u32[]{:S(2)}, u32[]{:S(2)}) async-start(bf16[8,16,2048]{2,1,0:T(8,128)(2,1)} %shard_map.83), calls=%async_computation.3 | async-start | bytes 1048576 | tf_op jit(solution)/shard_map/all_to_all | solution.py:33
  134.6 12.4 %collective-permute-start.20 = (bf16[4,32,1024]{2,1,0:T(8,128)(2,1)S(1)}, bf16[4,32,1024]{2,1,0:T(8,128)(2,1)S(1)}, u32[]{:S(2)}, u32[]{:S(2)}) collective-permute-start(bf16[4,32,1024]{2,1,0:T(8,128)(2,1)S(1)} %get-tuple-element.45), channel_id=1, source_target_pairs={{0,1},{1,0},{2,3},{3,2},{4,5},{5,4},{6,7},{7,6},{8,9},{9,8},{10,11... | collective-permute-start | bytes 786440 | tf_op jit(solution)/shard_map/ppermute | solution.py:259
  147.0 6.1 %collective-permute-start.21 = (bf16[32,1024]{1,0:T(8,128)(2,1)S(1)}, bf16[32,1024]{1,0:T(8,128)(2,1)S(1)}, u32[]{:S(2)}, u32[]{:S(2)}) collective-permute-start(bf16[32,1024]{1,0:T(8,128)(2,1)S(1)} %get-tuple-element.47), channel_id=1, source_target_pairs={{0,4},{2,6},{4,0},{6,2},{1,5},{3,7},{5,1},{7,3},{8,12},{10,14},{12... | collective-permute-start | bytes 196616 | tf_op jit(solution)/shard_map/ppermute | solution.py:37
  148.0 5.9 %collective-permute-start.22 = (bf16[32,1024]{1,0:T(8,128)(2,1)S(1)}, bf16[32,1024]{1,0:T(8,128)(2,1)S(1)}, u32[]{:S(2)}, u32[]{:S(2)}) collective-permute-start(bf16[32,1024]{1,0:T(8,128)(2,1)S(1)} %get-tuple-element.48), channel_id=1, source_target_pairs={{0,2},{2,4},{4,6},{6,0},{1,3},{3,5},{5,7},{7,1},{8,10},{10,12},{12... | collective-permute-start | bytes 196616 | tf_op jit(solution)/shard_map/ppermute | solution.py:37
  148.9 5.0 %collective-permute-start.23 = (bf16[32,1024]{1,0:T(8,128)(2,1)S(1)}, bf16[32,1024]{1,0:T(8,128)(2,1)S(1)}, u32[]{:S(2)}, u32[]{:S(2)}) collective-permute-start(bf16[32,1024]{1,0:T(8,128)(2,1)S(1)} %get-tuple-element.49), channel_id=1, source_target_pairs={{0,6},{2,0},{4,2},{6,4},{1,7},{3,1},{5,3},{7,5},{8,14},{10,8},{12,... | collective-permute-start | bytes 196616 | tf_op jit(solution)/shard_map/ppermute | solution.py:37

commit v8 on v7

--- a/solution.py
+++ b/solution.py
@@ -61,12 +61,13 @@
     out_ref[64:] = (own_ref[32:].astype(jnp.float32) + other_ref[32:].astype(jnp.float32)).astype(jnp.bfloat16)
 
 
-def placed(row_refs, flat_ref):
+def placed(row_refs, flat_ref, tall_ref):
     z, yl = lax.axis_index("z"), lax.axis_index("yl")
     for shift in range(4):
         for other in range(2):
             place = lax.rem(z + 4 - shift, 4) * 2 + lax.rem(yl + other, 2)
             flat_ref[pl.ds(place, 1)] = row_refs[shift][pl.ds(32 * other, 32), :][None]
+    tall_ref[...] = (flat_ref[...].reshape(D, BR) * jnp.bfloat16(0.5)).T
 
 
 def second_kernel(emb_ref, sums_ref, *refs):
@@ -85,8 +86,8 @@
 
 
 def arranged_first_kernel(*refs):
-    row_refs, (flat_ref, row_log_ref) = refs[:4], refs[4:]
-    placed(row_refs, flat_ref)
+    row_refs, (flat_ref, tall_ref, row_log_ref) = refs[:4], refs[4:]
+    placed(row_refs, flat_ref, tall_ref)
     digits = row_refs[0][64:, :].astype(jnp.float32)
     for ref in row_refs[1:]:
         digits += ref[64:, :].astype(jnp.float32)
@@ -102,7 +103,7 @@
 
 
 def arranged_kernel(*refs):
-    placed(refs[:4], refs[4])
+    placed(refs[:4], refs[4], refs[5])
 
 
 def col_log_kernel(mine_ref, theirs_ref, total_ref, other_ref, out_ref):
@@ -111,14 +112,17 @@
     out_ref[...] = 0.5 * jnp.log(digits[0:1] + 256.0 * digits[1:2]) - 0.5 * total
 
 
-def sweep_kernel(row_flat, mine_ref, theirs_ref, row_logs, col_log_ref, counts_ref, *refs):
+def sweep_kernel(row_flat, row_tall, mine_ref, theirs_ref, row_logs, col_log_ref, counts_ref, *refs):
     own_out, pair_out, home_out, away_out = refs[:4]
-    col_flat, col_tall, grads, turned, counts, row_tall, row_log_ref, arrived = refs[4:]
-    copies = [pltpu.make_async_copy(counts_ref.at[:, pl.ds(at * TN, TN)], counts.at[at], arrived.at[at]) for at in range(COLS // TN)]
-    for copy in copies:
-        copy.start()
+    col_flat, col_tall, grads, turned, counts, row_log_ref, arrived = refs[4:]
+    copies = {}
+    for at in range(COLS // TN):
+        for chunk in range(BR // RC):
+            source = counts_ref.at[pl.ds(chunk * RC, RC), pl.ds(at * TN, TN)]
+            target = counts.at[at, pl.ds(chunk * RC, RC)]
+            copies[at, chunk] = pltpu.make_async_copy(source, target, arrived.at[at, chunk])
+            copies[at, chunk].start()
     core, z, yl = lax.axis_index("c"), lax.axis_index("z"), lax.axis_index("yl")
-    row_tall[...] = (row_flat[...].reshape(D, BR) * jnp.bfloat16(0.5)).T
     for at in range(BR // 128):
         here = slice(at * 128, at * 128 + 128)
         row_log_ref[here, :] = jnp.broadcast_to(row_logs[:, here], (128, 128)).T
@@ -136,16 +140,17 @@
         col = col_flat[:, :, :, here].reshape(D, TN)
         col_tall[here, :] = col.T
         shift = col_log_ref[:, here]
-        copies[at].wait()
         for chunk in range(BR // RC):
             rows = slice(chunk * RC, chunk * RC + RC)
             scores = jnp.dot(row_tall[rows, :], col, preferred_element_type=jnp.float32)
             if at and chunk % 2 == 0:
                 col_part((at - 1) * TN + chunk * 128)
+            copies[at, chunk].wait()
             values = counts[at, rows, :].astype(jnp.float32)
             least = jnp.maximum(values, 1.0)
-            errors = scores - 0.5 * jnp.log(least) + (shift + jnp.tile(row_log_ref[rows, :], (1, TN // 128)))
-            weight = 0.2 + 0.5 * (least * lax.rsqrt(least))
+            root = least * lax.rsqrt(least)
+            errors = scores - jnp.log(root) + (shift + jnp.tile(row_log_ref[rows, :], (1, TN // 128)))
+            weight = 0.2 + 0.5 * root
             grad = jnp.where(values > 0.0, weight * errors, 0.5 * jnp.tanh(errors) + 0.5)
             grads[rows, here] = grad.astype(jnp.bfloat16)
     for start in range(COLS - TN, COLS, 256):
@@ -164,7 +169,7 @@
     return pl.pallas_call(
         sweep_kernel,
         out_shape=(shape((4, 32, BR), jnp.bfloat16),) * 2 + (shape((8, 16, COLS), jnp.bfloat16),) * 2,
-        in_specs=[VMEM] * 5 + [pl.BlockSpec(memory_space=pltpu.HBM)],
+        in_specs=[VMEM] * 6 + [pl.BlockSpec(memory_space=pltpu.HBM)],
         out_specs=(VMEM,) * 4,
         scratch_shapes=[
             pltpu.VMEM((8, 2, 16, COLS), jnp.bfloat16),
@@ -172,9 +177,8 @@
             pltpu.VMEM((BR, COLS), jnp.bfloat16),
             pltpu.VMEM((8, 32, BR), jnp.bfloat16),
             pltpu.VMEM((COLS // TN, BR, TN), jnp.int32),
-            pltpu.VMEM((BR, D), jnp.bfloat16),
             pltpu.VMEM((BR, 128), jnp.float32),
-            pltpu.SemaphoreType.DMA((COLS // TN,)),
+            pltpu.SemaphoreType.DMA((COLS // TN, BR // RC)),
         ],
         compiler_params=pltpu.CompilerParams(vmem_limit_bytes=32 * 2**20),
         cost_estimate=cost(6 * D * BR * COLS, 20 * 2**20),
@@ -247,14 +251,14 @@
     pair = small(joined_first_kernel, shape((72, BR), jnp.bfloat16))(parcel, other)
     mine = to_each(copies, CHIPS)
     row = [pair, over_z(pair, 1), over_z(pair, 2), over_z(pair, 3)]
-    outs = (shape((8, 32, BR), jnp.bfloat16), shape((1, BR), jnp.float32))
-    row, row_log = small(arranged_first_kernel, outs)(*row)
+    outs = (shape((8, 32, BR), jnp.bfloat16), shape((BR, D), jnp.bfloat16), shape((1, BR), jnp.float32))
+    *row, row_log = small(arranged_first_kernel, outs)(*row)
     theirs = lax.ppermute(mine, "c", SWAP)
     total = small(total_kernel, shape((8, 128), jnp.float32))(mine)
     other_total = lax.ppermute(total, "yl", SWAP)
     col_log = small(col_log_kernel, shape((1, COLS), jnp.float32))(mine, theirs, total, other_total)
     for sweep in range(2):
-        own, away_pair, home, away = swept(row, mine, theirs, row_log, col_log, in_hbm(counts))
+        own, away_pair, home, away = swept(*row, mine, theirs, row_log, col_log, in_hbm(counts))
         theirs = lax.ppermute(away, "c", SWAP)
         from_pair = lax.ppermute(away_pair, "yl", SWAP)
         both = small(home_kernel, shape((8, 16, COLS), jnp.bfloat16))(home, theirs)
@@ -271,7 +275,8 @@
             pair = small(joined_kernel, shape((64, BR), jnp.bfloat16))(half, pair)
             mine = to_each(copies, CHIPS)
             row = [pair, over_z(pair, 1), over_z(pair, 2), over_z(pair, 3)]
-            row = small(arranged_kernel, shape((8, 32, BR), jnp.bfloat16))(*row)
+            outs = (shape((8, 32, BR), jnp.bfloat16), shape((BR, D), jnp.bfloat16))
+            row = small(arranged_kernel, outs)(*row)
             theirs = lax.ppermute(mine, "c", SWAP)
     return row_emb, col_emb
 

time: 156 us -> 162 us (1.038)
  Pallas kernels: 22.6 us -> 28.5 us
    pallas_call x2, Pallas kernels: 18.2 us -> 23.7 us  [swept(): pl.pallas_call(sweep_kernel, out_shape=(shape((4, 32, BR), jnp.bfloat16),...]
where the time goes in v8:
time: 162 us; the launch traced here: 161 us
  waiting for transfers between devices  57.4 us (35%)
  starting transfers between devices  36.5 us (23%)
  blocking collectives  34.1 us (21%)
  Pallas kernels  28.5 us (18%)
  other arithmetic  4.05 us (2%)
    all_to_all x2, blocking collectives, to_each(): return lax.all_to_all(copies, axes, 0, 0, tiled=True)  34.1 us
    pallas_call x2, Pallas kernels, swept(): pl.pallas_call(sweep_kernel, out_shape=(shape((4, 32, BR), jnp.bfloat16),...  23.7 us
    ppermute x15, waiting for transfers between devices, over_z(): return lax.ppermute(value, 'z', [(at, (at + shift) % 4) for at in range(4)])  21.9 us
    ppermute x15, starting transfers between devices, over_z(): return lax.ppermute(value, 'z', [(at, (at + shift) % 4) for at in range(4)])  21.7 us
    ppermute x2, waiting for transfers between devices, on_device(): from_pair = lax.ppermute(away_pair, 'yl', SWAP)  13.3 us
    all_to_all x2, starting transfers between devices, to_each(): return lax.all_to_all(copies, axes, 0, 0, tiled=True)  10.9 us
    all_to_all x2, waiting for transfers between devices, to_each(): return lax.all_to_all(copies, axes, 0, 0, tiled=True)  10 us
    ppermute x1, waiting for transfers between devices, on_device(): other = lax.ppermute(parcel, 'yl', SWAP)  4.18 us
  transfers between devices with their start and end apart: 27, of which 20 were waited for; matrix products, arithmetic and copies ran while one was open for 0% of the time, Pallas kernels for 1%

profile of v8, /device:TPU:0, one launch (start us, length us, event | category | flops | bytes accessed | tf_op | source)
XLA Modules:
  0.0 161.3 jit_solution(171723585490075511)
XLA Ops:
  0.6 4.1 %fusion = (s32[2048]{0:T(1024)S(1)}, s32[1024]{0:T(1024)S(1)}) fusion(s32[1024,2048]{1,0:T(8,128)} %counts_ref.3), kind=kLoop, calls=%fused_computation | loop fusion | flops 4191232 | bytes 8400896 | tf_op jit(solution)/shard_map/reduce_sum | solution.py:243
  4.8 1.2 collective-permute-done.4.other_ref
  6.0 4.1 %collective-permute-start.7 = (s32[8,128]{1,0:T(8,128)S(1)}, s32[8,128]{1,0:T(8,128)S(1)}, u32[]{:S(2)}, u32[]{:S(2)}) collective-permute-start(s32[8,128]{1,0:T(8,128)S(1)} %shard_map.71.refs_0_), channel_id=1, source_target_pairs={{0,6},{2,0},{4,2},{6,4},{1,7},{3,1},{5,3},{7,5},{8,14},{10,8},{12,... | collective-permute-start | bytes 12296 | tf_op jit(solution)/shard_map/ppermute | solution.py:37
  10.1 1.3 collective-permute-start.5
  11.5 3.8 %collective-permute-done.6.refs_2_ = s32[8,128]{1,0:T(8,128)S(1)} collective-permute-done((s32[8,128]{1,0:T(8,128)S(1)}, s32[8,128]{1,0:T(8,128)S(1)}, u32[]{:S(2)}, u32[]{:S(2)}) %collective-permute-start.6) | collective-permute-done | bytes 4128 | tf_op jit(solution)/shard_map/ppermute | solution.py:37
  15.3 19.7 %all_to_all.20.mine_ref = bf16[8,24,2048]{2,1,0:T(8,128)(2,1)S(1)} all-to-all(bf16[8,24,2048]{2,1,0:T(8,128)(2,1)S(1)} %shard_map.72), channel_id=1, replica_groups=mesh['x'=4,'yh'=2,'c'=2,'z'=4,'yl'=2] {'x','yh'}, dimensions={0} | all-to-all | bytes 1572864 | tf_op jit(solution)/shard_map/all_to_all | solution.py:33
  35.0 0.7 collective-permute-start
  35.7 4.2 %collective-permute-done.other_ref = bf16[40,1024]{1,0:T(8,128)(2,1)S(1)} collective-permute-done((bf16[40,1024]{1,0:T(8,128)(2,1)S(1)}, bf16[40,1024]{1,0:T(8,128)(2,1)S(1)}, u32[]{:S(2)}, u32[]{:S(2)}) %collective-permute-start) | collective-permute-done | bytes 81952 | tf_op jit(solution)/shard_map/ppermute | solution.py:247
  39.9 1.0 collective-permute-start.3
  40.8 0.9 collective-permute-start.2
  41.8 1.3 collective-permute-start.1
  43.2 0.9 collective-permute-start.9
  44.1 2.6 %collective-permute-done.3.refs_3_ = bf16[72,1024]{1,0:T(8,128)(2,1)S(1)} collective-permute-done((bf16[72,1024]{1,0:T(8,128)(2,1)S(1)}, bf16[72,1024]{1,0:T(8,128)(2,1)S(1)}, u32[]{:S(2)}, u32[]{:S(2)}) %collective-permute-start.3) | collective-permute-done | bytes 147488 | tf_op jit(solution)/shard_map/ppermute | solution.py:37
  46.7 2.4 %collective-permute-done.2.refs_2_ = bf16[72,1024]{1,0:T(8,128)(2,1)S(1)} collective-permute-done((bf16[72,1024]{1,0:T(8,128)(2,1)S(1)}, bf16[72,1024]{1,0:T(8,128)(2,1)S(1)}, u32[]{:S(2)}, u32[]{:S(2)}) %collective-permute-start.2) | collective-permute-done | bytes 147488 | tf_op jit(solution)/shard_map/ppermute | solution.py:37
  49.0 1.6 collective-permute-done.1.refs_1_
  50.6 0.2 shard_map.70
  51.0 11.7 %sweep.2 = (bf16[4,32,1024]{2,1,0:T(8,128)(2,1)S(1)}, bf16[4,32,1024]{2,1,0:T(8,128)(2,1)S(1)}, bf16[8,16,2048]{2,1,0:T(8,128)(2,1)S(1)}, bf16[8,16,2048]{2,1,0:T(8,128)(2,1)S(1)}) custom-call(bf16[8,32,1024]{2,1,0:T(8,128)(2,1)S(1)} %get-tuple-element.34.row_flat, bf16[1024,256]{1,0:T(8,128)(2,1)S(1)} %get-tuple-element.35.row_tall, ...), custom_call_target="tpu_custom_call" | custom-call | flops 3221225472 | bytes 20971520 | tf_op jit(solution)/shard_map/sweep/pallas_call | solution.py:169
  62.8 1.9 %collective-permute-done.18.theirs_ref = bf16[8,16,2048]{2,1,0:T(8,128)(2,1)S(1)} collective-permute-done((bf16[8,16,2048]{2,1,0:T(8,128)(2,1)S(1)}, bf16[8,16,2048]{2,1,0:T(8,128)(2,1)S(1)}, u32[]{:S(2)}, u32[]{:S(2)}) %collective-permute-start.18) | collective-permute-done | bytes 524320 | tf_op jit(solution)/shard_map/ppermute | solution.py:262
  64.9 14.4 %all_to_all.21.came_ref = bf16[8,16,2048]{2,1,0:T(8,128)(2,1)S(1)} all-to-all(bf16[8,16,2048]{2,1,0:T(8,128)(2,1)S(1)} %shard_map.79), channel_id=1, replica_groups=mesh['x'=4,'yh'=2,'c'=2,'z'=4,'yl'=2] {'x','yh'}, dimensions={0} | all-to-all | bytes 1048576 | tf_op jit(solution)/shard_map/all_to_all | solution.py:33
  79.3 0.9 shard_map.80
  80.2 3.5 %all-to-all-start.2 = ((bf16[8,16,2048]{2,1,0:T(8,128)(2,1)}), bf16[8,16,2048]{2,1,0:T(8,128)(2,1)S(1)}, u32[]{:S(2)}, u32[]{:S(2)}) async-start(bf16[8,16,2048]{2,1,0:T(8,128)(2,1)} %get-tuple-element.49), calls=%async_computation.2 | async-start | bytes 1048576 | tf_op jit(solution)/shard_map/all_to_all | solution.py:33
  83.7 0.8 collective-permute-start.10
  84.5 10.0 %all-to-all-done.2.mine_ref = bf16[8,16,2048]{2,1,0:T(8,128)(2,1)S(1)} async-done(((bf16[8,16,2048]{2,1,0:T(8,128)(2,1)}), bf16[8,16,2048]{2,1,0:T(8,128)(2,1)S(1)}, u32[]{:S(2)}, u32[]{:S(2)}) %all-to-all-start.2) | async-done | bytes 524320 | tf_op jit(solution)/shard_map/all_to_all | solution.py:33
  94.5 1.0 collective-permute-done.10.came_ref
  95.6 1.3 collective-permute-start.11
  97.1 3.1 %collective-permute-start.13 = (bf16[32,1024]{1,0:T(8,128)(2,1)S(1)}, bf16[32,1024]{1,0:T(8,128)(2,1)S(1)}, u32[]{:S(2)}, u32[]{:S(2)}) collective-permute-start(bf16[32,1024]{1,0:T(8,128)(2,1)S(1)} %get-tuple-element.43), channel_id=1, source_target_pairs={{0,6},{2,0},{4,2},{6,4},{1,7},{3,1},{5,3},{7,5},{8,14},{10,8},{12,... | collective-permute-start | bytes 196616 | tf_op jit(solution)/shard_map/ppermute | solution.py:37
  100.2 1.3 collective-permute-done.11.first_ref
  101.4 1.0 collective-permute-done.12.second_ref
  102.5 1.3 collective-permute-start.14
  103.8 3.1 %collective-permute-done.14.other_ref = bf16[32,1024]{1,0:T(8,128)(2,1)S(1)} collective-permute-done((bf16[32,1024]{1,0:T(8,128)(2,1)S(1)}, bf16[32,1024]{1,0:T(8,128)(2,1)S(1)}, u32[]{:S(2)}, u32[]{:S(2)}) %collective-permute-start.14) | collective-permute-done | bytes 65568 | tf_op jit(solution)/shard_map/ppermute | solution.py:274
  106.9 3.3 %collective-permute-start.17 = (bf16[64,1024]{1,0:T(8,128)(2,1)S(1)}, bf16[64,1024]{1,0:T(8,128)(2,1)S(1)}, u32[]{:S(2)}, u32[]{:S(2)}) collective-permute-start(bf16[64,1024]{1,0:T(8,128)(2,1)S(1)} %shard_map.77.refs_0_), channel_id=1, source_target_pairs={{0,6},{2,0},{4,2},{6,4},{1,7},{3,1},{5,3},{7,5},{8,14},{10,8},{12,... | collective-permute-start | bytes 393224 | tf_op jit(solution)/shard_map/ppermute | solution.py:37
  110.2 0.9 collective-permute-start.15
  111.1 3.0 %collective-permute-done.17.refs_3_ = bf16[64,1024]{1,0:T(8,128)(2,1)S(1)} collective-permute-done((bf16[64,1024]{1,0:T(8,128)(2,1)S(1)}, bf16[64,1024]{1,0:T(8,128)(2,1)S(1)}, u32[]{:S(2)}, u32[]{:S(2)}) %collective-permute-start.17) | collective-permute-done | bytes 131104 | tf_op jit(solution)/shard_map/ppermute | solution.py:37
  114.1 2.6 %collective-permute-done.16.refs_2_ = bf16[64,1024]{1,0:T(8,128)(2,1)S(1)} collective-permute-done((bf16[64,1024]{1,0:T(8,128)(2,1)S(1)}, bf16[64,1024]{1,0:T(8,128)(2,1)S(1)}, u32[]{:S(2)}, u32[]{:S(2)}) %collective-permute-start.16) | collective-permute-done | bytes 131104 | tf_op jit(solution)/shard_map/ppermute | solution.py:37
  116.7 1.0 collective-permute-done.15.refs_1_
  117.7 0.2 shard_map.78
  118.0 12.0 %sweep.3 = (bf16[4,32,1024]{2,1,0:T(8,128)(2,1)S(1)}, bf16[4,32,1024]{2,1,0:T(8,128)(2,1)S(1)}, bf16[8,16,2048]{2,1,0:T(8,128)(2,1)S(1)}, bf16[8,16,2048]{2,1,0:T(8,128)(2,1)S(1)}) custom-call(bf16[8,32,1024]{2,1,0:T(8,128)(2,1)S(1)} %get-tuple-element.45.row_flat, bf16[1024,256]{1,0:T(8,128)(2,1)S(1)} %get-tuple-element.46.row_tall, ...), custom_call_target="tpu_custom_call" | custom-call | flops 3221225472 | bytes 20971520 | tf_op jit(solution)/shard_map/sweep/pallas_call | solution.py:169
  130.1 1.9 %collective-permute-done.24.theirs_ref = bf16[8,16,2048]{2,1,0:T(8,128)(2,1)S(1)} collective-permute-done((bf16[8,16,2048]{2,1,0:T(8,128)(2,1)S(1)}, bf16[8,16,2048]{2,1,0:T(8,128)(2,1)S(1)}, u32[]{:S(2)}, u32[]{:S(2)}) %collective-permute-start.24) | collective-permute-done | bytes 524320 | tf_op jit(solution)/shard_map/ppermute | solution.py:262
  132.0 0.9 shard_map.83
  132.9 7.4 %all-to-all-start.3 = ((bf16[8,16,2048]{2,1,0:T(8,128)(2,1)}), bf16[8,16,2048]{2,1,0:T(8,128)(2,1)S(1)}, u32[]{:S(2)}, u32[]{:S(2)}) async-start(bf16[8,16,2048]{2,1,0:T(8,128)(2,1)} %shard_map.83), calls=%async_computation.3 | async-start | bytes 1048576 | tf_op jit(solution)/shard_map/all_to_all | solution.py:33
  140.4 12.3 %collective-permute-done.20.came_ref = bf16[4,32,1024]{2,1,0:T(8,128)(2,1)S(1)} collective-permute-done((bf16[4,32,1024]{2,1,0:T(8,128)(2,1)S(1)}, bf16[4,32,1024]{2,1,0:T(8,128)(2,1)S(1)}, u32[]{:S(2)}, u32[]{:S(2)}) %collective-permute-start.20) | collective-permute-done | bytes 262176 | tf_op jit(solution)/shard_map/ppermute | solution.py:263
  152.8 1.0 collective-permute-start.21
  153.8 0.8 collective-permute-start.22
  154.6 2.4 %collective-permute-start.23 = (bf16[32,1024]{1,0:T(8,128)(2,1)S(1)}, bf16[32,1024]{1,0:T(8,128)(2,1)S(1)}, u32[]{:S(2)}, u32[]{:S(2)}) collective-permute-start(bf16[32,1024]{1,0:T(8,128)(2,1)S(1)} %get-tuple-element.55), channel_id=1, source_target_pairs={{0,6},{2,0},{4,2},{6,4},{1,7},{3,1},{5,3},{7,5},{8,14},{10,8},{12,... | collective-permute-start | bytes 196616 | tf_op jit(solution)/shard_map/ppermute | solution.py:37
  157.0 1.9 %collective-permute-done.21.first_ref = bf16[32,1024]{1,0:T(8,128)(2,1)S(1)} collective-permute-done((bf16[32,1024]{1,0:T(8,128)(2,1)S(1)}, bf16[32,1024]{1,0:T(8,128)(2,1)S(1)}, u32[]{:S(2)}, u32[]{:S(2)}) %collective-permute-start.21) | collective-permute-done | bytes 65568 | tf_op jit(solution)/shard_map/ppermute | solution.py:37
  158.9 0.7 collective-permute-done.22.second_ref
  159.6 0.8 shard_map.82
  160.4 1.0 shard_map.84
  (36 shorter events, 1.3 us)
Async XLA Ops:
  0.6 4.1 %copy-start.1 = (f32[32,1024]{1,0:T(8,128)S(1)}, f32[32,1024]{1,0:T(8,128)}, u32[]{:S(2)}) copy-start(f32[32,1024]{1,0:T(8,128)} %emb_ref.6) | copy-start | bytes 393220
  0.6 14.6 %copy-start = (f32[16,2048]{1,0:T(8,128)S(1)}, f32[16,2048]{1,0:T(8,128)}, u32[]{:S(2)}) copy-start(f32[16,2048]{1,0:T(8,128)} %emb_ref.7) | copy-start | bytes 393220
  4.8 1.2 collective-permute-start.4
  6.0 5.5 %collective-permute-start.7 = (s32[8,128]{1,0:T(8,128)S(1)}, s32[8,128]{1,0:T(8,128)S(1)}, u32[]{:S(2)}, u32[]{:S(2)}) collective-permute-start(s32[8,128]{1,0:T(8,128)S(1)} %shard_map.71.refs_0_), channel_id=1, source_target_pairs={{0,6},{2,0},{4,2},{6,4},{1,7},{3,1},{5,3},{7,5},{8,14},{10,8},{12,... | collective-permute-start | bytes 12296 | tf_op jit(solution)/shard_map/ppermute | solution.py:37
  10.1 5.1 %collective-permute-start.6 = (s32[8,128]{1,0:T(8,128)S(1)}, s32[8,128]{1,0:T(8,128)S(1)}, u32[]{:S(2)}, u32[]{:S(2)}) collective-permute-start(s32[8,128]{1,0:T(8,128)S(1)} %shard_map.71.refs_0_), channel_id=1, source_target_pairs={{0,4},{2,6},{4,0},{6,2},{1,5},{3,7},{5,1},{7,3},{8,12},{10,14},{12... | collective-permute-start | bytes 12296 | tf_op jit(solution)/shard_map/ppermute | solution.py:37
  10.1 5.1 %collective-permute-start.5 = (s32[8,128]{1,0:T(8,128)S(1)}, s32[8,128]{1,0:T(8,128)S(1)}, u32[]{:S(2)}, u32[]{:S(2)}) collective-permute-start(s32[8,128]{1,0:T(8,128)S(1)} %shard_map.71.refs_0_), channel_id=1, source_target_pairs={{0,2},{2,4},{4,6},{6,0},{1,3},{3,5},{5,7},{7,1},{8,10},{10,12},{12... | collective-permute-start | bytes 12296 | tf_op jit(solution)/shard_map/ppermute | solution.py:37
  35.0 15.9 %collective-permute-start.8 = (bf16[8,24,2048]{2,1,0:T(8,128)(2,1)S(1)}, bf16[8,24,2048]{2,1,0:T(8,128)(2,1)S(1)}, u32[]{:S(2)}, u32[]{:S(2)}) collective-permute-start(bf16[8,24,2048]{2,1,0:T(8,128)(2,1)S(1)} %all_to_all.20.mine_ref), channel_id=1, source_target_pairs={{0,8},{8,0},{1,9},{9,1},{2,10},{10,2},{3,11},{11,3},{4,12},{12,4},... | collective-permute-start | bytes 2359304 | tf_op jit(solution)/shard_map/ppermute | solution.py:256
  35.0 4.9 %collective-permute-start = (bf16[40,1024]{1,0:T(8,128)(2,1)S(1)}, bf16[40,1024]{1,0:T(8,128)(2,1)S(1)}, u32[]{:S(2)}, u32[]{:S(2)}) collective-permute-start(bf16[40,1024]{1,0:T(8,128)(2,1)S(1)} %get-tuple-element.33.own_ref), channel_id=1, source_target_pairs={{0,1},{1,0},{2,3},{3,2},{4,5},{5,4},{6,7},{7,6},{8,9},{9,8},{10,11... | collective-permute-start | bytes 245768 | tf_op jit(solution)/shard_map/ppermute | solution.py:247
  39.9 6.8 %collective-permute-start.3 = (bf16[72,1024]{1,0:T(8,128)(2,1)S(1)}, bf16[72,1024]{1,0:T(8,128)(2,1)S(1)}, u32[]{:S(2)}, u32[]{:S(2)}) collective-permute-start(bf16[72,1024]{1,0:T(8,128)(2,1)S(1)} %shard_map.69.refs_0_), channel_id=1, source_target_pairs={{0,6},{2,0},{4,2},{6,4},{1,7},{3,1},{5,3},{7,5},{8,14},{10,8},{12,... | collective-permute-start | bytes 442376 | tf_op jit(solution)/shard_map/ppermute | solution.py:37
  40.8 8.2 %collective-permute-start.2 = (bf16[72,1024]{1,0:T(8,128)(2,1)S(1)}, bf16[72,1024]{1,0:T(8,128)(2,1)S(1)}, u32[]{:S(2)}, u32[]{:S(2)}) collective-permute-start(bf16[72,1024]{1,0:T(8,128)(2,1)S(1)} %shard_map.69.refs_0_), channel_id=1, source_target_pairs={{0,4},{2,6},{4,0},{6,2},{1,5},{3,7},{5,1},{7,3},{8,12},{10,14},{12... | collective-permute-start | bytes 442376 | tf_op jit(solution)/shard_map/ppermute | solution.py:37
  41.8 8.8 %collective-permute-start.1 = (bf16[72,1024]{1,0:T(8,128)(2,1)S(1)}, bf16[72,1024]{1,0:T(8,128)(2,1)S(1)}, u32[]{:S(2)}, u32[]{:S(2)}) collective-permute-start(bf16[72,1024]{1,0:T(8,128)(2,1)S(1)} %shard_map.69.refs_0_), channel_id=1, source_target_pairs={{0,2},{2,4},{4,6},{6,0},{1,3},{3,5},{5,7},{7,1},{8,10},{10,12},{12... | collective-permute-start | bytes 442376 | tf_op jit(solution)/shard_map/ppermute | solution.py:37
  43.2 36.1 %copy-start.2 = (f32[16,2048]{1,0:T(8,128)S(1)}, f32[16,2048]{1,0:T(8,128)}, u32[]{:S(2)}) copy-start(f32[16,2048]{1,0:T(8,128)} %accum_ref.3) | copy-start | bytes 393220
  43.2 7.7 %collective-permute-start.9 = (f32[8,128]{1,0:T(8,128)S(1)}, f32[8,128]{1,0:T(8,128)S(1)}, u32[]{:S(2)}, u32[]{:S(2)}) collective-permute-start(f32[8,128]{1,0:T(8,128)S(1)} %shard_map.73.total_ref), channel_id=1, source_target_pairs={{0,1},{1,0},{2,3},{3,2},{4,5},{5,4},{6,7},{7,6},{8,9},{9,8},{10,11... | collective-permute-start | bytes 12296 | tf_op jit(solution)/shard_map/ppermute | solution.py:258
  51.0 51.4 %copy-start.3 = (f32[32,1024]{1,0:T(8,128)S(1)}, f32[32,1024]{1,0:T(8,128)}, u32[]{:S(2)}) copy-start(f32[32,1024]{1,0:T(8,128)} %accum_ref.2) | copy-start | bytes 393220
  62.8 2.0 %collective-permute-start.18 = (bf16[8,16,2048]{2,1,0:T(8,128)(2,1)S(1)}, bf16[8,16,2048]{2,1,0:T(8,128)(2,1)S(1)}, u32[]{:S(2)}, u32[]{:S(2)}) collective-permute-start(bf16[8,16,2048]{2,1,0:T(8,128)(2,1)S(1)} %get-tuple-element.48), channel_id=1, source_target_pairs={{0,8},{8,0},{1,9},{9,1},{2,10},{10,2},{3,11},{11,3},{4,12},{12,4},... | collective-permute-start | bytes 1572872 | tf_op jit(solution)/shard_map/ppermute | solution.py:262
  80.2 14.3 %all-to-all-start.2 = ((bf16[8,16,2048]{2,1,0:T(8,128)(2,1)}), bf16[8,16,2048]{2,1,0:T(8,128)(2,1)S(1)}, u32[]{:S(2)}, u32[]{:S(2)}) async-start(bf16[8,16,2048]{2,1,0:T(8,128)(2,1)} %get-tuple-element.49), calls=%async_computation.2 | async-start | bytes 1048576 | tf_op jit(solution)/shard_map/all_to_all | solution.py:33
  83.7 11.8 %collective-permute-start.10 = (bf16[4,32,1024]{2,1,0:T(8,128)(2,1)S(1)}, bf16[4,32,1024]{2,1,0:T(8,128)(2,1)S(1)}, u32[]{:S(2)}, u32[]{:S(2)}) collective-permute-start(bf16[4,32,1024]{2,1,0:T(8,128)(2,1)S(1)} %get-tuple-element.39), channel_id=1, source_target_pairs={{0,1},{1,0},{2,3},{3,2},{4,5},{5,4},{6,7},{7,6},{8,9},{9,8},{10,11... | collective-permute-start | bytes 786440 | tf_op jit(solution)/shard_map/ppermute | solution.py:263
  94.5 23.5 %collective-permute-start.19 = (bf16[8,16,2048]{2,1,0:T(8,128)(2,1)S(1)}, bf16[8,16,2048]{2,1,0:T(8,128)(2,1)S(1)}, u32[]{:S(2)}, u32[]{:S(2)}) collective-permute-start(bf16[8,16,2048]{2,1,0:T(8,128)(2,1)S(1)} %all-to-all-done.2.mine_ref), channel_id=1, source_target_pairs={{0,8},{8,0},{1,9},{9,1},{2,10},{10,2},{3,11},{11,3},{4,12},{12,4},... | collective-permute-start | bytes 1572872 | tf_op jit(solution)/shard_map/ppermute | solution.py:280
  95.6 5.8 %collective-permute-start.11 = (bf16[32,1024]{1,0:T(8,128)(2,1)S(1)}, bf16[32,1024]{1,0:T(8,128)(2,1)S(1)}, u32[]{:S(2)}, u32[]{:S(2)}) collective-permute-start(bf16[32,1024]{1,0:T(8,128)(2,1)S(1)} %get-tuple-element.41), channel_id=1, source_target_pairs={{0,4},{2,6},{4,0},{6,2},{1,5},{3,7},{5,1},{7,3},{8,12},{10,14},{12... | collective-permute-start | bytes 196616 | tf_op jit(solution)/shard_map/ppermute | solution.py:37
  96.9 5.5 %collective-permute-start.12 = (bf16[32,1024]{1,0:T(8,128)(2,1)S(1)}, bf16[32,1024]{1,0:T(8,128)(2,1)S(1)}, u32[]{:S(2)}, u32[]{:S(2)}) collective-permute-start(bf16[32,1024]{1,0:T(8,128)(2,1)S(1)} %get-tuple-element.42), channel_id=1, source_target_pairs={{0,2},{2,4},{4,6},{6,0},{1,3},{3,5},{5,7},{7,1},{8,10},{10,12},{12... | collective-permute-start | bytes 196616 | tf_op jit(solution)/shard_map/ppermute | solution.py:37
  97.1 5.3 %collective-permute-start.13 = (bf16[32,1024]{1,0:T(8,128)(2,1)S(1)}, bf16[32,1024]{1,0:T(8,128)(2,1)S(1)}, u32[]{:S(2)}, u32[]{:S(2)}) collective-permute-start(bf16[32,1024]{1,0:T(8,128)(2,1)S(1)} %get-tuple-element.43), channel_id=1, source_target_pairs={{0,6},{2,0},{4,2},{6,4},{1,7},{3,1},{5,3},{7,5},{8,14},{10,8},{12,... | collective-permute-start | bytes 196616 | tf_op jit(solution)/shard_map/ppermute | solution.py:37
  102.5 4.3 %collective-permute-start.14 = (bf16[32,1024]{1,0:T(8,128)(2,1)S(1)}, bf16[32,1024]{1,0:T(8,128)(2,1)S(1)}, u32[]{:S(2)}, u32[]{:S(2)}) collective-permute-start(bf16[32,1024]{1,0:T(8,128)(2,1)S(1)} %get-tuple-element.44.own_ref), channel_id=1, source_target_pairs={{0,1},{1,0},{2,3},{3,2},{4,5},{5,4},{6,7},{7,6},{8,9},{9,8},{10,11... | collective-permute-start | bytes 196616 | tf_op jit(solution)/shard_map/ppermute | solution.py:274
  106.9 7.2 %collective-permute-start.17 = (bf16[64,1024]{1,0:T(8,128)(2,1)S(1)}, bf16[64,1024]{1,0:T(8,128)(2,1)S(1)}, u32[]{:S(2)}, u32[]{:S(2)}) collective-permute-start(bf16[64,1024]{1,0:T(8,128)(2,1)S(1)} %shard_map.77.refs_0_), channel_id=1, source_target_pairs={{0,6},{2,0},{4,2},{6,4},{1,7},{3,1},{5,3},{7,5},{8,14},{10,8},{12,... | collective-permute-start | bytes 393224 | tf_op jit(solution)/shard_map/ppermute | solution.py:37
  110.2 6.6 %collective-permute-start.16 = (bf16[64,1024]{1,0:T(8,128)(2,1)S(1)}, bf16[64,1024]{1,0:T(8,128)(2,1)S(1)}, u32[]{:S(2)}, u32[]{:S(2)}) collective-permute-start(bf16[64,1024]{1,0:T(8,128)(2,1)S(1)} %shard_map.77.refs_0_), channel_id=1, source_target_pairs={{0,4},{2,6},{4,0},{6,2},{1,5},{3,7},{5,1},{7,3},{8,12},{10,14},{12... | collective-permute-start | bytes 393224 | tf_op jit(solution)/shard_map/ppermute | solution.py:37
  110.2 7.6 %collective-permute-start.15 = (bf16[64,1024]{1,0:T(8,128)(2,1)S(1)}, bf16[64,1024]{1,0:T(8,128)(2,1)S(1)}, u32[]{:S(2)}, u32[]{:S(2)}) collective-permute-start(bf16[64,1024]{1,0:T(8,128)(2,1)S(1)} %shard_map.77.refs_0_), channel_id=1, source_target_pairs={{0,2},{2,4},{4,6},{6,0},{1,3},{3,5},{5,7},{7,1},{8,10},{10,12},{12... | collective-permute-start | bytes 393224 | tf_op jit(solution)/shard_map/ppermute | solution.py:37
  130.0 2.0 %collective-permute-start.24 = (bf16[8,16,2048]{2,1,0:T(8,128)(2,1)S(1)}, bf16[8,16,2048]{2,1,0:T(8,128)(2,1)S(1)}, u32[]{:S(2)}, u32[]{:S(2)}) collective-permute-start(bf16[8,16,2048]{2,1,0:T(8,128)(2,1)S(1)} %get-tuple-element.60), channel_id=1, source_target_pairs={{0,8},{8,0},{1,9},{9,1},{2,10},{10,2},{3,11},{11,3},{4,12},{12,4},... | collective-permute-start | bytes 1572872 | tf_op jit(solution)/shard_map/ppermute | solution.py:262
  132.9 27.5 %all-to-all-start.3 = ((bf16[8,16,2048]{2,1,0:T(8,128)(2,1)}), bf16[8,16,2048]{2,1,0:T(8,128)(2,1)S(1)}, u32[]{:S(2)}, u32[]{:S(2)}) async-start(bf16[8,16,2048]{2,1,0:T(8,128)(2,1)} %shard_map.83), calls=%async_computation.3 | async-start | bytes 1048576 | tf_op jit(solution)/shard_map/all_to_all | solution.py:33
  140.3 12.4 %collective-permute-start.20 = (bf16[4,32,1024]{2,1,0:T(8,128)(2,1)S(1)}, bf16[4,32,1024]{2,1,0:T(8,128)(2,1)S(1)}, u32[]{:S(2)}, u32[]{:S(2)}) collective-permute-start(bf16[4,32,1024]{2,1,0:T(8,128)(2,1)S(1)} %get-tuple-element.51), channel_id=1, source_target_pairs={{0,1},{1,0},{2,3},{3,2},{4,5},{5,4},{6,7},{7,6},{8,9},{9,8},{10,11... | collective-permute-start | bytes 786440 | tf_op jit(solution)/shard_map/ppermute | solution.py:263
  152.8 6.1 %collective-permute-start.21 = (bf16[32,1024]{1,0:T(8,128)(2,1)S(1)}, bf16[32,1024]{1,0:T(8,128)(2,1)S(1)}, u32[]{:S(2)}, u32[]{:S(2)}) collective-permute-start(bf16[32,1024]{1,0:T(8,128)(2,1)S(1)} %get-tuple-element.53), channel_id=1, source_target_pairs={{0,4},{2,6},{4,0},{6,2},{1,5},{3,7},{5,1},{7,3},{8,12},{10,14},{12... | collective-permute-start | bytes 196616 | tf_op jit(solution)/shard_map/ppermute | solution.py:37
  153.8 5.8 %collective-permute-start.22 = (bf16[32,1024]{1,0:T(8,128)(2,1)S(1)}, bf16[32,1024]{1,0:T(8,128)(2,1)S(1)}, u32[]{:S(2)}, u32[]{:S(2)}) collective-permute-start(bf16[32,1024]{1,0:T(8,128)(2,1)S(1)} %get-tuple-element.54), channel_id=1, source_target_pairs={{0,2},{2,4},{4,6},{6,0},{1,3},{3,5},{5,7},{7,1},{8,10},{10,12},{12... | collective-permute-start | bytes 196616 | tf_op jit(solution)/shard_map/ppermute | solution.py:37
  154.6 5.0 %collective-permute-start.23 = (bf16[32,1024]{1,0:T(8,128)(2,1)S(1)}, bf16[32,1024]{1,0:T(8,128)(2,1)S(1)}, u32[]{:S(2)}, u32[]{:S(2)}) collective-permute-start(bf16[32,1024]{1,0:T(8,128)(2,1)S(1)} %get-tuple-element.55), channel_id=1, source_target_pairs={{0,6},{2,0},{4,2},{6,4},{1,7},{3,1},{5,3},{7,5},{8,14},{10,8},{12,... | collective-permute-start | bytes 196616 | tf_op jit(solution)/shard_map/ppermute | solution.py:37

commit v9 on v8

--- a/solution.py
+++ b/solution.py
@@ -70,11 +70,8 @@
     tall_ref[...] = (flat_ref[...].reshape(D, BR) * jnp.bfloat16(0.5)).T
 
 
-def second_kernel(emb_ref, sums_ref, *refs):
-    total_refs, out_ref = refs[:4], refs[4]
-    total = total_refs[0][...]
-    for ref in total_refs[1:]:
-        total += ref[...]
+def second_kernel(emb_ref, sums_ref, total_ref, other_ref, out_ref):
+    total = total_ref[...] + other_ref[...]
     total = jnp.tile(total[:1], (1, COLS // 128))
     lane = lax.broadcasted_iota(jnp.int32, (1, COLS), 1)
     parts = jnp.where(lane < 4, (total >> (8 * jnp.minimum(lane, 3))) & 255, 0)
@@ -106,22 +103,21 @@
     placed(refs[:4], refs[4], refs[5])
 
 
-def col_log_kernel(mine_ref, theirs_ref, total_ref, other_ref, out_ref):
+def col_log_kernel(mine_ref, theirs_ref, first_ref, second_ref, third_ref, fourth_ref, out_ref):
     digits = rows_sum(mine_ref, slice(16, 24)) + rows_sum(theirs_ref, slice(16, 24))
-    total = jnp.tile(jnp.log(total_ref[:1] + other_ref[:1]), (1, COLS // 128))
+    total = first_ref[:1] + second_ref[:1] + third_ref[:1] + fourth_ref[:1]
+    total = jnp.tile(jnp.log(total), (1, COLS // 128))
     out_ref[...] = 0.5 * jnp.log(digits[0:1] + 256.0 * digits[1:2]) - 0.5 * total
 
 
 def sweep_kernel(row_flat, row_tall, mine_ref, theirs_ref, row_logs, col_log_ref, counts_ref, *refs):
     own_out, pair_out, home_out, away_out = refs[:4]
     col_flat, col_tall, grads, turned, counts, row_log_ref, arrived = refs[4:]
-    copies = {}
-    for at in range(COLS // TN):
-        for chunk in range(BR // RC):
-            source = counts_ref.at[pl.ds(chunk * RC, RC), pl.ds(at * TN, TN)]
-            target = counts.at[at, pl.ds(chunk * RC, RC)]
-            copies[at, chunk] = pltpu.make_async_copy(source, target, arrived.at[at, chunk])
-            copies[at, chunk].start()
+    copies = [
+        pltpu.make_async_copy(counts_ref.at[:, pl.ds(at * TN, TN)], counts.at[at], arrived.at[at]) for at in range(COLS // TN)
+    ]
+    for copy in copies:
+        copy.start()
     core, z, yl = lax.axis_index("c"), lax.axis_index("z"), lax.axis_index("yl")
     for at in range(BR // 128):
         here = slice(at * 128, at * 128 + 128)
@@ -140,12 +136,12 @@
         col = col_flat[:, :, :, here].reshape(D, TN)
         col_tall[here, :] = col.T
         shift = col_log_ref[:, here]
+        copies[at].wait()
         for chunk in range(BR // RC):
             rows = slice(chunk * RC, chunk * RC + RC)
             scores = jnp.dot(row_tall[rows, :], col, preferred_element_type=jnp.float32)
             if at and chunk % 2 == 0:
                 col_part((at - 1) * TN + chunk * 128)
-            copies[at, chunk].wait()
             values = counts[at, rows, :].astype(jnp.float32)
             least = jnp.maximum(values, 1.0)
             root = least * lax.rsqrt(least)
@@ -178,7 +174,7 @@
             pltpu.VMEM((8, 32, BR), jnp.bfloat16),
             pltpu.VMEM((COLS // TN, BR, TN), jnp.int32),
             pltpu.VMEM((BR, 128), jnp.float32),
-            pltpu.SemaphoreType.DMA((COLS // TN, BR // RC)),
+            pltpu.SemaphoreType.DMA((COLS // TN,)),
         ],
         compiler_params=pltpu.CompilerParams(vmem_limit_bytes=32 * 2**20),
         cost_estimate=cost(6 * D * BR * COLS, 20 * 2**20),
@@ -246,8 +242,8 @@
     other_total = lax.ppermute(total, "c", SWAP)
     other = lax.ppermute(parcel, "yl", SWAP)
     total = small(added_kernel, shape((8, 128), jnp.int32))(total, other_total)
-    totals = [total, over_z(total, 1), over_z(total, 2), over_z(total, 3)]
-    copies = small(second_kernel, shape((8, 24, COLS), jnp.bfloat16))(col_emb, col_sums, *totals)
+    other_total = lax.ppermute(total, "yl", SWAP)
+    copies = small(second_kernel, shape((8, 24, COLS), jnp.bfloat16))(col_emb, col_sums, total, other_total)
     pair = small(joined_first_kernel, shape((72, BR), jnp.bfloat16))(parcel, other)
     mine = to_each(copies, CHIPS)
     row = [pair, over_z(pair, 1), over_z(pair, 2), over_z(pair, 3)]
@@ -255,8 +251,8 @@
     *row, row_log = small(arranged_first_kernel, outs)(*row)
     theirs = lax.ppermute(mine, "c", SWAP)
     total = small(total_kernel, shape((8, 128), jnp.float32))(mine)
-    other_total = lax.ppermute(total, "yl", SWAP)
-    col_log = small(col_log_kernel, shape((1, COLS), jnp.float32))(mine, theirs, total, other_total)
+    totals = [total, over_z(total, 1), over_z(total, 2), over_z(total, 3)]
+    col_log = small(col_log_kernel, shape((1, COLS), jnp.float32))(mine, theirs, *totals)
     for sweep in range(2):
         own, away_pair, home, away = swept(*row, mine, theirs, row_log, col_log, in_hbm(counts))
         theirs = lax.ppermute(away, "c", SWAP)

time: 162 us -> 157 us (0.969)
  Pallas kernels: 28.5 us -> 22.6 us
  starting transfers between devices: 36.5 us -> 38.8 us
    pallas_call x2, Pallas kernels: 23.7 us -> 17.9 us  [swept(): pl.pallas_call(sweep_kernel, out_shape=(shape((4, 32, BR), jnp.bfloat16),...]
    ppermute x15, waiting for transfers between devices: 21.9 us -> 18.5 us  [over_z(): return lax.ppermute(value, 'z', [(at, (at + shift) % 4) for at in range(4)])]
    ppermute x1, waiting for transfers between devices: 0.01 us -> 1.92 us  [on_device(): other_total = lax.ppermute(total, 'yl', SWAP)]
  transfers between devices with their start and end apart: 27 -> 27, of which waited for: 20 -> 21; matrix products, arithmetic and copies ran while one was open for 0% -> 0% of each run, Pallas kernels for 1% -> 1%
where the time goes in v9:
time: 157 us
  waiting for transfers between devices  55.9 us (36%)
  starting transfers between devices  38.8 us (25%)
  blocking collectives  34.5 us (22%)
  Pallas kernels  22.6 us (14%)
  other arithmetic  4.05 us (3%)
    all_to_all x2, blocking collectives, to_each(): return lax.all_to_all(copies, axes, 0, 0, tiled=True)  34.5 us
    ppermute x15, starting transfers between devices, over_z(): return lax.ppermute(value, 'z', [(at, (at + shift) % 4) for at in range(4)])  23 us
    ppermute x15, waiting for transfers between devices, over_z(): return lax.ppermute(value, 'z', [(at, (at + shift) % 4) for at in range(4)])  18.5 us
    pallas_call x2, Pallas kernels, swept(): pl.pallas_call(sweep_kernel, out_shape=(shape((4, 32, BR), jnp.bfloat16),...  17.9 us
    ppermute x2, waiting for transfers between devices, on_device(): from_pair = lax.ppermute(away_pair, 'yl', SWAP)  13.3 us
    all_to_all x2, starting transfers between devices, to_each(): return lax.all_to_all(copies, axes, 0, 0, tiled=True)  10.9 us
    all_to_all x2, waiting for transfers between devices, to_each(): return lax.all_to_all(copies, axes, 0, 0, tiled=True)  10 us
    ppermute x1, waiting for transfers between devices, on_device(): other = lax.ppermute(parcel, 'yl', SWAP)  4.18 us
  transfers between devices with their start and end apart: 27, of which 21 were waited for; matrix products, arithmetic and copies ran while one was open for 0% of the time, Pallas kernels for 1%

profile of v9, /device:TPU:0, one launch (start us, length us, event | category | flops | bytes accessed | tf_op | source)
XLA Modules:
  0.0 156.7 jit_solution(1045939794997286554)
XLA Ops:
  0.6 4.1 %fusion = (s32[2048]{0:T(1024)S(1)}, s32[1024]{0:T(1024)S(1)}) fusion(s32[1024,2048]{1,0:T(8,128)} %counts_ref.3), kind=kLoop, calls=%fused_computation | loop fusion | flops 4191232 | bytes 8400896 | tf_op jit(solution)/shard_map/reduce_sum | solution.py:239
  4.8 1.2 collective-permute-done.4.other_ref
  6.0 1.7 %collective-permute-start.5 = (s32[8,128]{1,0:T(8,128)S(1)}, s32[8,128]{1,0:T(8,128)S(1)}, u32[]{:S(2)}, u32[]{:S(2)}) collective-permute-start(s32[8,128]{1,0:T(8,128)S(1)} %shard_map.71.total_ref), channel_id=1, source_target_pairs={{0,1},{1,0},{2,3},{3,2},{4,5},{5,4},{6,7},{7,6},{8,9},{9,8},{10,11... | collective-permute-start | bytes 12296 | tf_op jit(solution)/shard_map/ppermute | solution.py:245
  7.7 1.9 %collective-permute-done.5.other_ref = s32[8,128]{1,0:T(8,128)S(1)} collective-permute-done((s32[8,128]{1,0:T(8,128)S(1)}, s32[8,128]{1,0:T(8,128)S(1)}, u32[]{:S(2)}, u32[]{:S(2)}) %collective-permute-start.5) | collective-permute-done | bytes 4128 | tf_op jit(solution)/shard_map/ppermute | solution.py:245
  9.7 20.1 %all_to_all.20.mine_ref = bf16[8,24,2048]{2,1,0:T(8,128)(2,1)S(1)} all-to-all(bf16[8,24,2048]{2,1,0:T(8,128)(2,1)S(1)} %shard_map.72), channel_id=1, replica_groups=mesh['x'=4,'yh'=2,'c'=2,'z'=4,'yl'=2] {'x','yh'}, dimensions={0} | all-to-all | bytes 1572864 | tf_op jit(solution)/shard_map/all_to_all | solution.py:33
  29.7 0.7 collective-permute-start
  30.4 4.2 %collective-permute-done.other_ref = bf16[40,1024]{1,0:T(8,128)(2,1)S(1)} collective-permute-done((bf16[40,1024]{1,0:T(8,128)(2,1)S(1)}, bf16[40,1024]{1,0:T(8,128)(2,1)S(1)}, u32[]{:S(2)}, u32[]{:S(2)}) %collective-permute-start) | collective-permute-done | bytes 81952 | tf_op jit(solution)/shard_map/ppermute | solution.py:243
  34.6 4.1 %collective-permute-start.3 = (bf16[72,1024]{1,0:T(8,128)(2,1)S(1)}, bf16[72,1024]{1,0:T(8,128)(2,1)S(1)}, u32[]{:S(2)}, u32[]{:S(2)}) collective-permute-start(bf16[72,1024]{1,0:T(8,128)(2,1)S(1)} %shard_map.69.refs_0_), channel_id=1, source_target_pairs={{0,6},{2,0},{4,2},{6,4},{1,7},{3,1},{5,3},{7,5},{8,14},{10,8},{12,... | collective-permute-start | bytes 442376 | tf_op jit(solution)/shard_map/ppermute | solution.py:37
  38.7 1.3 collective-permute-start.1
  40.1 2.0 %collective-permute-start.9 = (f32[8,128]{1,0:T(8,128)S(1)}, f32[8,128]{1,0:T(8,128)S(1)}, u32[]{:S(2)}, u32[]{:S(2)}) collective-permute-start(f32[8,128]{1,0:T(8,128)S(1)} %shard_map.73.first_ref), channel_id=1, source_target_pairs={{0,6},{2,0},{4,2},{6,4},{1,7},{3,1},{5,3},{7,5},{8,14},{10,8},{12,... | collective-permute-start | bytes 12296 | tf_op jit(solution)/shard_map/ppermute | solution.py:37
  42.1 2.8 %collective-permute-done.3.refs_3_ = bf16[72,1024]{1,0:T(8,128)(2,1)S(1)} collective-permute-done((bf16[72,1024]{1,0:T(8,128)(2,1)S(1)}, bf16[72,1024]{1,0:T(8,128)(2,1)S(1)}, u32[]{:S(2)}, u32[]{:S(2)}) %collective-permute-start.3) | collective-permute-done | bytes 147488 | tf_op jit(solution)/shard_map/ppermute | solution.py:37
  44.8 0.4 collective-permute-start.8
  45.3 1.7 %collective-permute-done.2.refs_2_ = bf16[72,1024]{1,0:T(8,128)(2,1)S(1)} collective-permute-done((bf16[72,1024]{1,0:T(8,128)(2,1)S(1)}, bf16[72,1024]{1,0:T(8,128)(2,1)S(1)}, u32[]{:S(2)}, u32[]{:S(2)}) %collective-permute-start.2) | collective-permute-done | bytes 147488 | tf_op jit(solution)/shard_map/ppermute | solution.py:37
  46.9 2.5 %collective-permute-start.7 = (f32[8,128]{1,0:T(8,128)S(1)}, f32[8,128]{1,0:T(8,128)S(1)}, u32[]{:S(2)}, u32[]{:S(2)}) collective-permute-start(f32[8,128]{1,0:T(8,128)S(1)} %shard_map.73.first_ref), channel_id=1, source_target_pairs={{0,2},{2,4},{4,6},{6,0},{1,3},{3,5},{5,7},{7,1},{8,10},{10,12},{12... | collective-permute-start | bytes 12296 | tf_op jit(solution)/shard_map/ppermute | solution.py:37
  49.6 0.3 collective-permute-done.8.third_ref
  50.0 1.8 %collective-permute-done.7.second_ref = f32[8,128]{1,0:T(8,128)S(1)} collective-permute-done((f32[8,128]{1,0:T(8,128)S(1)}, f32[8,128]{1,0:T(8,128)S(1)}, u32[]{:S(2)}, u32[]{:S(2)}) %collective-permute-start.7) | collective-permute-done | bytes 4128 | tf_op jit(solution)/shard_map/ppermute | solution.py:37
  51.9 8.9 %sweep.2 = (bf16[4,32,1024]{2,1,0:T(8,128)(2,1)S(1)}, bf16[4,32,1024]{2,1,0:T(8,128)(2,1)S(1)}, bf16[8,16,2048]{2,1,0:T(8,128)(2,1)S(1)}, bf16[8,16,2048]{2,1,0:T(8,128)(2,1)S(1)}) custom-call(bf16[8,32,1024]{2,1,0:T(8,128)(2,1)S(1)} %get-tuple-element.34.row_flat, bf16[1024,256]{1,0:T(8,128)(2,1)S(1)} %get-tuple-element.35.row_tall, ...), custom_call_target="tpu_custom_call" | custom-call | flops 3221225472 | bytes 20971520 | tf_op jit(solution)/shard_map/sweep/pallas_call | solution.py:165
  61.0 1.9 %collective-permute-done.18.theirs_ref = bf16[8,16,2048]{2,1,0:T(8,128)(2,1)S(1)} collective-permute-done((bf16[8,16,2048]{2,1,0:T(8,128)(2,1)S(1)}, bf16[8,16,2048]{2,1,0:T(8,128)(2,1)S(1)}, u32[]{:S(2)}, u32[]{:S(2)}) %collective-permute-start.18) | collective-permute-done | bytes 524320 | tf_op jit(solution)/shard_map/ppermute | solution.py:258
  63.0 14.4 %all_to_all.21.came_ref = bf16[8,16,2048]{2,1,0:T(8,128)(2,1)S(1)} all-to-all(bf16[8,16,2048]{2,1,0:T(8,128)(2,1)S(1)} %shard_map.79), channel_id=1, replica_groups=mesh['x'=4,'yh'=2,'c'=2,'z'=4,'yl'=2] {'x','yh'}, dimensions={0} | all-to-all | bytes 1048576 | tf_op jit(solution)/shard_map/all_to_all | solution.py:33
  77.5 0.9 shard_map.80
  78.4 3.5 %all-to-all-start.2 = ((bf16[8,16,2048]{2,1,0:T(8,128)(2,1)}), bf16[8,16,2048]{2,1,0:T(8,128)(2,1)S(1)}, u32[]{:S(2)}, u32[]{:S(2)}) async-start(bf16[8,16,2048]{2,1,0:T(8,128)(2,1)} %get-tuple-element.49), calls=%async_computation.2 | async-start | bytes 1048576 | tf_op jit(solution)/shard_map/all_to_all | solution.py:33
  81.9 0.8 collective-permute-start.10
  82.7 10.0 %all-to-all-done.2.mine_ref = bf16[8,16,2048]{2,1,0:T(8,128)(2,1)S(1)} async-done(((bf16[8,16,2048]{2,1,0:T(8,128)(2,1)}), bf16[8,16,2048]{2,1,0:T(8,128)(2,1)S(1)}, u32[]{:S(2)}, u32[]{:S(2)}) %all-to-all-start.2) | async-done | bytes 524320 | tf_op jit(solution)/shard_map/all_to_all | solution.py:33
  92.7 1.0 collective-permute-done.10.came_ref
  93.7 1.4 collective-permute-start.11
  95.1 1.5 collective-permute-start.12
  96.6 1.8 %collective-permute-start.13 = (bf16[32,1024]{1,0:T(8,128)(2,1)S(1)}, bf16[32,1024]{1,0:T(8,128)(2,1)S(1)}, u32[]{:S(2)}, u32[]{:S(2)}) collective-permute-start(bf16[32,1024]{1,0:T(8,128)(2,1)S(1)} %get-tuple-element.43), channel_id=1, source_target_pairs={{0,6},{2,0},{4,2},{6,4},{1,7},{3,1},{5,3},{7,5},{8,14},{10,8},{12,... | collective-permute-start | bytes 196616 | tf_op jit(solution)/shard_map/ppermute | solution.py:37
  98.3 1.8 %collective-permute-done.11.first_ref = bf16[32,1024]{1,0:T(8,128)(2,1)S(1)} collective-permute-done((bf16[32,1024]{1,0:T(8,128)(2,1)S(1)}, bf16[32,1024]{1,0:T(8,128)(2,1)S(1)}, u32[]{:S(2)}, u32[]{:S(2)}) %collective-permute-start.11) | collective-permute-done | bytes 65568 | tf_op jit(solution)/shard_map/ppermute | solution.py:37
  100.2 0.6 collective-permute-done.12.second_ref
  100.9 1.3 collective-permute-start.14
  102.2 3.1 %collective-permute-done.14.other_ref = bf16[32,1024]{1,0:T(8,128)(2,1)S(1)} collective-permute-done((bf16[32,1024]{1,0:T(8,128)(2,1)S(1)}, bf16[32,1024]{1,0:T(8,128)(2,1)S(1)}, u32[]{:S(2)}, u32[]{:S(2)}) %collective-permute-start.14) | collective-permute-done | bytes 65568 | tf_op jit(solution)/shard_map/ppermute | solution.py:270
  105.3 3.1 %collective-permute-start.17 = (bf16[64,1024]{1,0:T(8,128)(2,1)S(1)}, bf16[64,1024]{1,0:T(8,128)(2,1)S(1)}, u32[]{:S(2)}, u32[]{:S(2)}) collective-permute-start(bf16[64,1024]{1,0:T(8,128)(2,1)S(1)} %shard_map.77.refs_0_), channel_id=1, source_target_pairs={{0,6},{2,0},{4,2},{6,4},{1,7},{3,1},{5,3},{7,5},{8,14},{10,8},{12,... | collective-permute-start | bytes 393224 | tf_op jit(solution)/shard_map/ppermute | solution.py:37
  108.5 0.9 collective-permute-start.15
  109.4 2.9 %collective-permute-done.17.refs_3_ = bf16[64,1024]{1,0:T(8,128)(2,1)S(1)} collective-permute-done((bf16[64,1024]{1,0:T(8,128)(2,1)S(1)}, bf16[64,1024]{1,0:T(8,128)(2,1)S(1)}, u32[]{:S(2)}, u32[]{:S(2)}) %collective-permute-start.17) | collective-permute-done | bytes 131104 | tf_op jit(solution)/shard_map/ppermute | solution.py:37
  112.3 2.6 %collective-permute-done.16.refs_2_ = bf16[64,1024]{1,0:T(8,128)(2,1)S(1)} collective-permute-done((bf16[64,1024]{1,0:T(8,128)(2,1)S(1)}, bf16[64,1024]{1,0:T(8,128)(2,1)S(1)}, u32[]{:S(2)}, u32[]{:S(2)}) %collective-permute-start.16) | collective-permute-done | bytes 131104 | tf_op jit(solution)/shard_map/ppermute | solution.py:37
  114.9 1.2 collective-permute-done.15.refs_1_
  116.3 9.0 %sweep.3 = (bf16[4,32,1024]{2,1,0:T(8,128)(2,1)S(1)}, bf16[4,32,1024]{2,1,0:T(8,128)(2,1)S(1)}, bf16[8,16,2048]{2,1,0:T(8,128)(2,1)S(1)}, bf16[8,16,2048]{2,1,0:T(8,128)(2,1)S(1)}) custom-call(bf16[8,32,1024]{2,1,0:T(8,128)(2,1)S(1)} %get-tuple-element.45.row_flat, bf16[1024,256]{1,0:T(8,128)(2,1)S(1)} %get-tuple-element.46.row_tall, ...), custom_call_target="tpu_custom_call" | custom-call | flops 3221225472 | bytes 20971520 | tf_op jit(solution)/shard_map/sweep/pallas_call | solution.py:165
  125.4 1.9 %collective-permute-done.24.theirs_ref = bf16[8,16,2048]{2,1,0:T(8,128)(2,1)S(1)} collective-permute-done((bf16[8,16,2048]{2,1,0:T(8,128)(2,1)S(1)}, bf16[8,16,2048]{2,1,0:T(8,128)(2,1)S(1)}, u32[]{:S(2)}, u32[]{:S(2)}) %collective-permute-start.24) | collective-permute-done | bytes 524320 | tf_op jit(solution)/shard_map/ppermute | solution.py:258
  127.3 0.9 shard_map.83
  128.3 7.4 %all-to-all-start.3 = ((bf16[8,16,2048]{2,1,0:T(8,128)(2,1)}), bf16[8,16,2048]{2,1,0:T(8,128)(2,1)S(1)}, u32[]{:S(2)}, u32[]{:S(2)}) async-start(bf16[8,16,2048]{2,1,0:T(8,128)(2,1)} %shard_map.83), calls=%async_computation.3 | async-start | bytes 1048576 | tf_op jit(solution)/shard_map/all_to_all | solution.py:33
  135.8 12.3 %collective-permute-done.20.came_ref = bf16[4,32,1024]{2,1,0:T(8,128)(2,1)S(1)} collective-permute-done((bf16[4,32,1024]{2,1,0:T(8,128)(2,1)S(1)}, bf16[4,32,1024]{2,1,0:T(8,128)(2,1)S(1)}, u32[]{:S(2)}, u32[]{:S(2)}) %collective-permute-start.20) | collective-permute-done | bytes 262176 | tf_op jit(solution)/shard_map/ppermute | solution.py:259
  148.1 0.8 collective-permute-start.21
  149.0 0.8 collective-permute-start.22
  149.8 2.4 %collective-permute-start.23 = (bf16[32,1024]{1,0:T(8,128)(2,1)S(1)}, bf16[32,1024]{1,0:T(8,128)(2,1)S(1)}, u32[]{:S(2)}, u32[]{:S(2)}) collective-permute-start(bf16[32,1024]{1,0:T(8,128)(2,1)S(1)} %get-tuple-element.55), channel_id=1, source_target_pairs={{0,6},{2,0},{4,2},{6,4},{1,7},{3,1},{5,3},{7,5},{8,14},{10,8},{12,... | collective-permute-start | bytes 196616 | tf_op jit(solution)/shard_map/ppermute | solution.py:37
  152.2 2.1 %collective-permute-done.21.first_ref = bf16[32,1024]{1,0:T(8,128)(2,1)S(1)} collective-permute-done((bf16[32,1024]{1,0:T(8,128)(2,1)S(1)}, bf16[32,1024]{1,0:T(8,128)(2,1)S(1)}, u32[]{:S(2)}, u32[]{:S(2)}) %collective-permute-start.21) | collective-permute-done | bytes 65568 | tf_op jit(solution)/shard_map/ppermute | solution.py:37
  154.3 0.7 collective-permute-done.22.second_ref
  155.0 0.8 shard_map.82
  155.7 1.0 shard_map.84
  (36 shorter events, 2.0 us)
Async XLA Ops:
  0.6 4.1 %copy-start.1 = (f32[32,1024]{1,0:T(8,128)S(1)}, f32[32,1024]{1,0:T(8,128)}, u32[]{:S(2)}) copy-start(f32[32,1024]{1,0:T(8,128)} %emb_ref.6) | copy-start | bytes 393220
  0.6 9.0 %copy-start = (f32[16,2048]{1,0:T(8,128)S(1)}, f32[16,2048]{1,0:T(8,128)}, u32[]{:S(2)}) copy-start(f32[16,2048]{1,0:T(8,128)} %emb_ref.7) | copy-start | bytes 393220
  4.8 1.2 collective-permute-start.4
  6.0 3.6 %collective-permute-start.5 = (s32[8,128]{1,0:T(8,128)S(1)}, s32[8,128]{1,0:T(8,128)S(1)}, u32[]{:S(2)}, u32[]{:S(2)}) collective-permute-start(s32[8,128]{1,0:T(8,128)S(1)} %shard_map.71.total_ref), channel_id=1, source_target_pairs={{0,1},{1,0},{2,3},{3,2},{4,5},{5,4},{6,7},{7,6},{8,9},{9,8},{10,11... | collective-permute-start | bytes 12296 | tf_op jit(solution)/shard_map/ppermute | solution.py:245
  29.7 22.0 %collective-permute-start.6 = (bf16[8,24,2048]{2,1,0:T(8,128)(2,1)S(1)}, bf16[8,24,2048]{2,1,0:T(8,128)(2,1)S(1)}, u32[]{:S(2)}, u32[]{:S(2)}) collective-permute-start(bf16[8,24,2048]{2,1,0:T(8,128)(2,1)S(1)} %all_to_all.20.mine_ref), channel_id=1, source_target_pairs={{0,8},{8,0},{1,9},{9,1},{2,10},{10,2},{3,11},{11,3},{4,12},{12,4},... | collective-permute-start | bytes 2359304 | tf_op jit(solution)/shard_map/ppermute | solution.py:252
  29.7 4.9 %collective-permute-start = (bf16[40,1024]{1,0:T(8,128)(2,1)S(1)}, bf16[40,1024]{1,0:T(8,128)(2,1)S(1)}, u32[]{:S(2)}, u32[]{:S(2)}) collective-permute-start(bf16[40,1024]{1,0:T(8,128)(2,1)S(1)} %get-tuple-element.33.own_ref), channel_id=1, source_target_pairs={{0,1},{1,0},{2,3},{3,2},{4,5},{5,4},{6,7},{7,6},{8,9},{9,8},{10,11... | collective-permute-start | bytes 245768 | tf_op jit(solution)/shard_map/ppermute | solution.py:243
  34.6 10.2 %collective-permute-start.3 = (bf16[72,1024]{1,0:T(8,128)(2,1)S(1)}, bf16[72,1024]{1,0:T(8,128)(2,1)S(1)}, u32[]{:S(2)}, u32[]{:S(2)}) collective-permute-start(bf16[72,1024]{1,0:T(8,128)(2,1)S(1)} %shard_map.69.refs_0_), channel_id=1, source_target_pairs={{0,6},{2,0},{4,2},{6,4},{1,7},{3,1},{5,3},{7,5},{8,14},{10,8},{12,... | collective-permute-start | bytes 442376 | tf_op jit(solution)/shard_map/ppermute | solution.py:37
  38.7 8.2 %collective-permute-start.2 = (bf16[72,1024]{1,0:T(8,128)(2,1)S(1)}, bf16[72,1024]{1,0:T(8,128)(2,1)S(1)}, u32[]{:S(2)}, u32[]{:S(2)}) collective-permute-start(bf16[72,1024]{1,0:T(8,128)(2,1)S(1)} %shard_map.69.refs_0_), channel_id=1, source_target_pairs={{0,4},{2,6},{4,0},{6,2},{1,5},{3,7},{5,1},{7,3},{8,12},{10,14},{12... | collective-permute-start | bytes 442376 | tf_op jit(solution)/shard_map/ppermute | solution.py:37
  38.7 10.7 %collective-permute-start.1 = (bf16[72,1024]{1,0:T(8,128)(2,1)S(1)}, bf16[72,1024]{1,0:T(8,128)(2,1)S(1)}, u32[]{:S(2)}, u32[]{:S(2)}) collective-permute-start(bf16[72,1024]{1,0:T(8,128)(2,1)S(1)} %shard_map.69.refs_0_), channel_id=1, source_target_pairs={{0,2},{2,4},{4,6},{6,0},{1,3},{3,5},{5,7},{7,1},{8,10},{10,12},{12... | collective-permute-start | bytes 442376 | tf_op jit(solution)/shard_map/ppermute | solution.py:37
  40.1 37.4 %copy-start.2 = (f32[16,2048]{1,0:T(8,128)S(1)}, f32[16,2048]{1,0:T(8,128)}, u32[]{:S(2)}) copy-start(f32[16,2048]{1,0:T(8,128)} %accum_ref.3) | copy-start | bytes 393220
  40.1 9.6 %collective-permute-start.9 = (f32[8,128]{1,0:T(8,128)S(1)}, f32[8,128]{1,0:T(8,128)S(1)}, u32[]{:S(2)}, u32[]{:S(2)}) collective-permute-start(f32[8,128]{1,0:T(8,128)S(1)} %shard_map.73.first_ref), channel_id=1, source_target_pairs={{0,6},{2,0},{4,2},{6,4},{1,7},{3,1},{5,3},{7,5},{8,14},{10,8},{12,... | collective-permute-start | bytes 12296 | tf_op jit(solution)/shard_map/ppermute | solution.py:37
  44.8 5.1 %collective-permute-start.8 = (f32[8,128]{1,0:T(8,128)S(1)}, f32[8,128]{1,0:T(8,128)S(1)}, u32[]{:S(2)}, u32[]{:S(2)}) collective-permute-start(f32[8,128]{1,0:T(8,128)S(1)} %shard_map.73.first_ref), channel_id=1, source_target_pairs={{0,4},{2,6},{4,0},{6,2},{1,5},{3,7},{5,1},{7,3},{8,12},{10,14},{12... | collective-permute-start | bytes 12296 | tf_op jit(solution)/shard_map/ppermute | solution.py:37
  46.9 4.8 %collective-permute-start.7 = (f32[8,128]{1,0:T(8,128)S(1)}, f32[8,128]{1,0:T(8,128)S(1)}, u32[]{:S(2)}, u32[]{:S(2)}) collective-permute-start(f32[8,128]{1,0:T(8,128)S(1)} %shard_map.73.first_ref), channel_id=1, source_target_pairs={{0,2},{2,4},{4,6},{6,0},{1,3},{3,5},{5,7},{7,1},{8,10},{10,12},{12... | collective-permute-start | bytes 12296 | tf_op jit(solution)/shard_map/ppermute | solution.py:37
  51.9 49.0 %copy-start.3 = (f32[32,1024]{1,0:T(8,128)S(1)}, f32[32,1024]{1,0:T(8,128)}, u32[]{:S(2)}) copy-start(f32[32,1024]{1,0:T(8,128)} %accum_ref.2) | copy-start | bytes 393220
  60.7 2.2 %collective-permute-start.18 = (bf16[8,16,2048]{2,1,0:T(8,128)(2,1)S(1)}, bf16[8,16,2048]{2,1,0:T(8,128)(2,1)S(1)}, u32[]{:S(2)}, u32[]{:S(2)}) collective-permute-start(bf16[8,16,2048]{2,1,0:T(8,128)(2,1)S(1)} %get-tuple-element.48), channel_id=1, source_target_pairs={{0,8},{8,0},{1,9},{9,1},{2,10},{10,2},{3,11},{11,3},{4,12},{12,4},... | collective-permute-start | bytes 1572872 | tf_op jit(solution)/shard_map/ppermute | solution.py:258
  78.4 14.3 %all-to-all-start.2 = ((bf16[8,16,2048]{2,1,0:T(8,128)(2,1)}), bf16[8,16,2048]{2,1,0:T(8,128)(2,1)S(1)}, u32[]{:S(2)}, u32[]{:S(2)}) async-start(bf16[8,16,2048]{2,1,0:T(8,128)(2,1)} %get-tuple-element.49), calls=%async_computation.2 | async-start | bytes 1048576 | tf_op jit(solution)/shard_map/all_to_all | solution.py:33
  81.9 11.8 %collective-permute-start.10 = (bf16[4,32,1024]{2,1,0:T(8,128)(2,1)S(1)}, bf16[4,32,1024]{2,1,0:T(8,128)(2,1)S(1)}, u32[]{:S(2)}, u32[]{:S(2)}) collective-permute-start(bf16[4,32,1024]{2,1,0:T(8,128)(2,1)S(1)} %get-tuple-element.39), channel_id=1, source_target_pairs={{0,1},{1,0},{2,3},{3,2},{4,5},{5,4},{6,7},{7,6},{8,9},{9,8},{10,11... | collective-permute-start | bytes 786440 | tf_op jit(solution)/shard_map/ppermute | solution.py:259
  92.7 23.6 %collective-permute-start.19 = (bf16[8,16,2048]{2,1,0:T(8,128)(2,1)S(1)}, bf16[8,16,2048]{2,1,0:T(8,128)(2,1)S(1)}, u32[]{:S(2)}, u32[]{:S(2)}) collective-permute-start(bf16[8,16,2048]{2,1,0:T(8,128)(2,1)S(1)} %all-to-all-done.2.mine_ref), channel_id=1, source_target_pairs={{0,8},{8,0},{1,9},{9,1},{2,10},{10,2},{3,11},{11,3},{4,12},{12,4},... | collective-permute-start | bytes 1572872 | tf_op jit(solution)/shard_map/ppermute | solution.py:276
  93.7 6.4 %collective-permute-start.11 = (bf16[32,1024]{1,0:T(8,128)(2,1)S(1)}, bf16[32,1024]{1,0:T(8,128)(2,1)S(1)}, u32[]{:S(2)}, u32[]{:S(2)}) collective-permute-start(bf16[32,1024]{1,0:T(8,128)(2,1)S(1)} %get-tuple-element.41), channel_id=1, source_target_pairs={{0,4},{2,6},{4,0},{6,2},{1,5},{3,7},{5,1},{7,3},{8,12},{10,14},{12... | collective-permute-start | bytes 196616 | tf_op jit(solution)/shard_map/ppermute | solution.py:37
  95.1 5.6 %collective-permute-start.12 = (bf16[32,1024]{1,0:T(8,128)(2,1)S(1)}, bf16[32,1024]{1,0:T(8,128)(2,1)S(1)}, u32[]{:S(2)}, u32[]{:S(2)}) collective-permute-start(bf16[32,1024]{1,0:T(8,128)(2,1)S(1)} %get-tuple-element.42), channel_id=1, source_target_pairs={{0,2},{2,4},{4,6},{6,0},{1,3},{3,5},{5,7},{7,1},{8,10},{10,12},{12... | collective-permute-start | bytes 196616 | tf_op jit(solution)/shard_map/ppermute | solution.py:37
  96.6 4.3 %collective-permute-start.13 = (bf16[32,1024]{1,0:T(8,128)(2,1)S(1)}, bf16[32,1024]{1,0:T(8,128)(2,1)S(1)}, u32[]{:S(2)}, u32[]{:S(2)}) collective-permute-start(bf16[32,1024]{1,0:T(8,128)(2,1)S(1)} %get-tuple-element.43), channel_id=1, source_target_pairs={{0,6},{2,0},{4,2},{6,4},{1,7},{3,1},{5,3},{7,5},{8,14},{10,8},{12,... | collective-permute-start | bytes 196616 | tf_op jit(solution)/shard_map/ppermute | solution.py:37
  100.9 4.3 %collective-permute-start.14 = (bf16[32,1024]{1,0:T(8,128)(2,1)S(1)}, bf16[32,1024]{1,0:T(8,128)(2,1)S(1)}, u32[]{:S(2)}, u32[]{:S(2)}) collective-permute-start(bf16[32,1024]{1,0:T(8,128)(2,1)S(1)} %get-tuple-element.44.own_ref), channel_id=1, source_target_pairs={{0,1},{1,0},{2,3},{3,2},{4,5},{5,4},{6,7},{7,6},{8,9},{9,8},{10,11... | collective-permute-start | bytes 196616 | tf_op jit(solution)/shard_map/ppermute | solution.py:270
  105.3 7.0 %collective-permute-start.17 = (bf16[64,1024]{1,0:T(8,128)(2,1)S(1)}, bf16[64,1024]{1,0:T(8,128)(2,1)S(1)}, u32[]{:S(2)}, u32[]{:S(2)}) collective-permute-start(bf16[64,1024]{1,0:T(8,128)(2,1)S(1)} %shard_map.77.refs_0_), channel_id=1, source_target_pairs={{0,6},{2,0},{4,2},{6,4},{1,7},{3,1},{5,3},{7,5},{8,14},{10,8},{12,... | collective-permute-start | bytes 393224 | tf_op jit(solution)/shard_map/ppermute | solution.py:37
  108.3 6.6 %collective-permute-start.16 = (bf16[64,1024]{1,0:T(8,128)(2,1)S(1)}, bf16[64,1024]{1,0:T(8,128)(2,1)S(1)}, u32[]{:S(2)}, u32[]{:S(2)}) collective-permute-start(bf16[64,1024]{1,0:T(8,128)(2,1)S(1)} %shard_map.77.refs_0_), channel_id=1, source_target_pairs={{0,4},{2,6},{4,0},{6,2},{1,5},{3,7},{5,1},{7,3},{8,12},{10,14},{12... | collective-permute-start | bytes 393224 | tf_op jit(solution)/shard_map/ppermute | solution.py:37
  108.5 7.6 %collective-permute-start.15 = (bf16[64,1024]{1,0:T(8,128)(2,1)S(1)}, bf16[64,1024]{1,0:T(8,128)(2,1)S(1)}, u32[]{:S(2)}, u32[]{:S(2)}) collective-permute-start(bf16[64,1024]{1,0:T(8,128)(2,1)S(1)} %shard_map.77.refs_0_), channel_id=1, source_target_pairs={{0,2},{2,4},{4,6},{6,0},{1,3},{3,5},{5,7},{7,1},{8,10},{10,12},{12... | collective-permute-start | bytes 393224 | tf_op jit(solution)/shard_map/ppermute | solution.py:37
  125.3 2.0 %collective-permute-start.24 = (bf16[8,16,2048]{2,1,0:T(8,128)(2,1)S(1)}, bf16[8,16,2048]{2,1,0:T(8,128)(2,1)S(1)}, u32[]{:S(2)}, u32[]{:S(2)}) collective-permute-start(bf16[8,16,2048]{2,1,0:T(8,128)(2,1)S(1)} %get-tuple-element.60), channel_id=1, source_target_pairs={{0,8},{8,0},{1,9},{9,1},{2,10},{10,2},{3,11},{11,3},{4,12},{12,4},... | collective-permute-start | bytes 1572872 | tf_op jit(solution)/shard_map/ppermute | solution.py:258
  128.3 27.5 %all-to-all-start.3 = ((bf16[8,16,2048]{2,1,0:T(8,128)(2,1)}), bf16[8,16,2048]{2,1,0:T(8,128)(2,1)S(1)}, u32[]{:S(2)}, u32[]{:S(2)}) async-start(bf16[8,16,2048]{2,1,0:T(8,128)(2,1)} %shard_map.83), calls=%async_computation.3 | async-start | bytes 1048576 | tf_op jit(solution)/shard_map/all_to_all | solution.py:33
  135.6 12.4 %collective-permute-start.20 = (bf16[4,32,1024]{2,1,0:T(8,128)(2,1)S(1)}, bf16[4,32,1024]{2,1,0:T(8,128)(2,1)S(1)}, u32[]{:S(2)}, u32[]{:S(2)}) collective-permute-start(bf16[4,32,1024]{2,1,0:T(8,128)(2,1)S(1)} %get-tuple-element.51), channel_id=1, source_target_pairs={{0,1},{1,0},{2,3},{3,2},{4,5},{5,4},{6,7},{7,6},{8,9},{9,8},{10,11... | collective-permute-start | bytes 786440 | tf_op jit(solution)/shard_map/ppermute | solution.py:259
  148.1 6.1 %collective-permute-start.21 = (bf16[32,1024]{1,0:T(8,128)(2,1)S(1)}, bf16[32,1024]{1,0:T(8,128)(2,1)S(1)}, u32[]{:S(2)}, u32[]{:S(2)}) collective-permute-start(bf16[32,1024]{1,0:T(8,128)(2,1)S(1)} %get-tuple-element.53), channel_id=1, source_target_pairs={{0,4},{2,6},{4,0},{6,2},{1,5},{3,7},{5,1},{7,3},{8,12},{10,14},{12... | collective-permute-start | bytes 196616 | tf_op jit(solution)/shard_map/ppermute | solution.py:37
  149.0 6.0 %collective-permute-start.22 = (bf16[32,1024]{1,0:T(8,128)(2,1)S(1)}, bf16[32,1024]{1,0:T(8,128)(2,1)S(1)}, u32[]{:S(2)}, u32[]{:S(2)}) collective-permute-start(bf16[32,1024]{1,0:T(8,128)(2,1)S(1)} %get-tuple-element.54), channel_id=1, source_target_pairs={{0,2},{2,4},{4,6},{6,0},{1,3},{3,5},{5,7},{7,1},{8,10},{10,12},{12... | collective-permute-start | bytes 196616 | tf_op jit(solution)/shard_map/ppermute | solution.py:37
  149.8 5.1 %collective-permute-start.23 = (bf16[32,1024]{1,0:T(8,128)(2,1)S(1)}, bf16[32,1024]{1,0:T(8,128)(2,1)S(1)}, u32[]{:S(2)}, u32[]{:S(2)}) collective-permute-start(bf16[32,1024]{1,0:T(8,128)(2,1)S(1)} %get-tuple-element.55), channel_id=1, source_target_pairs={{0,6},{2,0},{4,2},{6,4},{1,7},{3,1},{5,3},{7,5},{8,14},{10,8},{12,... | collective-permute-start | bytes 196616 | tf_op jit(solution)/shard_map/ppermute | solution.py:37

commit v10 on v9

--- a/solution.py
+++ b/solution.py
@@ -44,11 +44,48 @@
     return total
 
 
-def first_kernel(emb_ref, sums_ref, out_ref, total_ref):
-    sums = sums_ref[...]
+def first_kernel(counts_ref, emb_source, out_ref, total_ref, col_ref, blocks, emb_ref, sums_ref, arrived, emb_arrived):
+    copies = [
+        pltpu.make_async_copy(counts_ref.at[pl.ds(at * 128, 128)], blocks.at[at], arrived.at[at]) for at in range(BR // 128)
+    ]
+    for copy in copies:
+        copy.start()
+    emb_copy = pltpu.make_async_copy(emb_source, emb_ref, emb_arrived)
+    emb_copy.start()
+    col = jnp.zeros((8, COLS), jnp.int32)
+    for at in range(BR // 128):
+        copies[at].wait()
+        block = blocks[at]
+        col += jnp.sum(block.reshape(16, 8, COLS), axis=0)
+        across = block[:, :128]
+        for lane in range(128, COLS, 128):
+            across += block[:, lane : lane + 128]
+        sums_ref[:, at * 128 : at * 128 + 128] = jnp.sum(across.astype(jnp.float32).T, axis=0, keepdims=True)
+    col_ref[...] = jnp.sum(col.astype(jnp.float32), axis=0, keepdims=True).astype(jnp.int32)
+    sums = sums_ref[...].astype(jnp.int32)
     digits = [(sums & 127).astype(jnp.float32), ((sums >> 7) & 127).astype(jnp.float32), (sums >> 14).astype(jnp.float32)]
+    emb_copy.wait()
     out_ref[...] = jnp.concatenate([emb_ref[...]] + digits + [jnp.zeros((5, BR), jnp.float32)]).astype(jnp.bfloat16)
     total_ref[...] = jnp.broadcast_to(jnp.sum(sums, axis=1, keepdims=True), (8, 128))
+
+
+def first(counts, emb):
+    return pl.pallas_call(
+        first_kernel,
+        out_shape=(shape((40, BR), jnp.bfloat16), shape((8, 128), jnp.int32), shape((1, COLS), jnp.int32)),
+        in_specs=[pl.BlockSpec(memory_space=pltpu.HBM)] * 2,
+        out_specs=(VMEM,) * 3,
+        scratch_shapes=[
+            pltpu.VMEM((BR // 128, 128, COLS), jnp.int32),
+            pltpu.VMEM((32, BR), jnp.float32),
+            pltpu.VMEM((1, BR), jnp.float32),
+            pltpu.SemaphoreType.DMA((BR // 128,)),
+            pltpu.SemaphoreType.DMA(()),
+        ],
+        compiler_params=pltpu.CompilerParams(vmem_limit_bytes=16 * 2**20),
+        cost_estimate=cost(4 * BR * COLS, 8 * 2**20),
+        name="first",
+    )(in_hbm(counts), in_hbm(emb))
 
 
 def added_kernel(one_ref, other_ref, out_ref):
@@ -70,14 +107,21 @@
     tall_ref[...] = (flat_ref[...].reshape(D, BR) * jnp.bfloat16(0.5)).T
 
 
-def second_kernel(emb_ref, sums_ref, total_ref, other_ref, out_ref):
-    total = total_ref[...] + other_ref[...]
-    total = jnp.tile(total[:1], (1, COLS // 128))
-    lane = lax.broadcasted_iota(jnp.int32, (1, COLS), 1)
+def packed(wide):
+    return jnp.concatenate([wide[:, lane : lane + 128] for lane in range(0, COLS, 128)])
+
+
+def second_kernel(emb_ref, sums_ref, *refs):
+    total_refs, out_ref = refs[:4], refs[4]
+    total = total_refs[0][...]
+    for ref in total_refs[1:]:
+        total += ref[...]
+    lane = lax.broadcasted_iota(jnp.int32, (16, 128), 1)
+    total = jnp.broadcast_to(total[:1], (16, 128))
     parts = jnp.where(lane < 4, (total >> (8 * jnp.minimum(lane, 3))) & 255, 0)
-    sums = sums_ref[...]
-    rows = [emb_ref[...], (sums & 255).astype(jnp.float32), (sums >> 8).astype(jnp.float32), parts.astype(jnp.float32)]
-    parcel = jnp.concatenate(rows + [jnp.zeros((5, COLS), jnp.float32)]).astype(jnp.bfloat16)
+    sums = packed(sums_ref[...])
+    blocks = [packed(emb_ref[...]), (sums & 255).astype(jnp.float32), (sums >> 8).astype(jnp.float32), parts.astype(jnp.float32)]
+    parcel = jnp.concatenate(blocks).astype(jnp.bfloat16)
     for at in range(8):
         out_ref[at] = parcel
 
@@ -91,23 +135,23 @@
     row_log_ref[...] = 0.5 * jnp.log(digits[0:1] + 128.0 * digits[1:2] + 16384.0 * digits[2:3])
 
 
+def arranged_kernel(*refs):
+    placed(refs[:4], refs[4], refs[5])
+
+
 def total_kernel(mine_ref, out_ref):
-    digits = rows_sum(mine_ref, slice(16, 24))[2:3, :128]
+    digits = rows_sum(mine_ref, slice(288, 304))[:1]
     lane = lax.broadcasted_iota(jnp.int32, (1, 128), 1)
     scale = jnp.where(lane == 0, 1.0, jnp.where(lane == 1, 256.0, jnp.where(lane == 2, 65536.0, 16777216.0)))
     total = jnp.sum(jnp.where(lane < 4, digits * scale, 0.0), axis=1, keepdims=True)
     out_ref[...] = jnp.broadcast_to(total, (8, 128))
 
 
-def arranged_kernel(*refs):
-    placed(refs[:4], refs[4], refs[5])
-
-
-def col_log_kernel(mine_ref, theirs_ref, first_ref, second_ref, third_ref, fourth_ref, out_ref):
-    digits = rows_sum(mine_ref, slice(16, 24)) + rows_sum(theirs_ref, slice(16, 24))
-    total = first_ref[:1] + second_ref[:1] + third_ref[:1] + fourth_ref[:1]
-    total = jnp.tile(jnp.log(total), (1, COLS // 128))
-    out_ref[...] = 0.5 * jnp.log(digits[0:1] + 256.0 * digits[1:2]) - 0.5 * total
+def col_log_kernel(mine_ref, theirs_ref, total_ref, other_ref, out_ref):
+    digits = rows_sum(mine_ref, slice(256, 288)) + rows_sum(theirs_ref, slice(256, 288))
+    logs = 0.5 * jnp.log(digits[:16] + 256.0 * digits[16:]) - 0.5 * jnp.log(total_ref[:1] + other_ref[:1])
+    for at in range(COLS // 128):
+        out_ref[:, at * 128 : at * 128 + 128] = logs[at : at + 1]
 
 
 def sweep_kernel(row_flat, row_tall, mine_ref, theirs_ref, row_logs, col_log_ref, counts_ref, *refs):
@@ -122,8 +166,10 @@
     for at in range(BR // 128):
         here = slice(at * 128, at * 128 + 128)
         row_log_ref[here, :] = jnp.broadcast_to(row_logs[:, here], (128, 128)).T
-    col_flat[:, pl.ds(core, 1)] = mine_ref[:, :16, :][:, None]
-    col_flat[:, pl.ds(1 - core, 1)] = theirs_ref[:, :16, :][:, None]
+    for at in range(COLS // 128):
+        rows, here = slice(at * 16, at * 16 + 16), slice(at * 128, at * 128 + 128)
+        col_flat[:, pl.ds(core, 1), :, here] = mine_ref[:, rows, :][:, None]
+        col_flat[:, pl.ds(1 - core, 1), :, here] = theirs_ref[:, rows, :][:, None]
     def col_part(start):
         here = slice(start, start + 256)
         part = jnp.dot(row_flat[...].reshape(D, BR), grads[:, here], preferred_element_type=jnp.float32).reshape(8, 2, 16, 256)
@@ -220,7 +266,7 @@
     emb, accum = moved(emb_ref, accum_ref, grad)
     new_emb_ref[...] = emb
     new_accum_ref[...] = accum
-    half = emb.astype(jnp.bfloat16)
+    half = packed(emb).astype(jnp.bfloat16)
     for at in range(8):
         half_ref[at] = half
 
@@ -235,15 +281,12 @@
 
 
 def on_device(counts, row_emb, col_emb, row_accum, col_accum):
-    row_sums = jnp.sum(counts, axis=1)[None]
-    col_sums = jnp.sum(counts, axis=0)[None]
-    outs = (shape((40, BR), jnp.bfloat16), shape((8, 128), jnp.int32))
-    parcel, total = small(first_kernel, outs)(row_emb, row_sums)
+    parcel, total, col_sums = first(counts, row_emb)
     other_total = lax.ppermute(total, "c", SWAP)
     other = lax.ppermute(parcel, "yl", SWAP)
     total = small(added_kernel, shape((8, 128), jnp.int32))(total, other_total)
-    other_total = lax.ppermute(total, "yl", SWAP)
-    copies = small(second_kernel, shape((8, 24, COLS), jnp.bfloat16))(col_emb, col_sums, total, other_total)
+    totals = [total, over_z(total, 1), over_z(total, 2), over_z(total, 3)]
+    copies = small(second_kernel, shape((8, 304, 128), jnp.bfloat16))(col_emb, col_sums, *totals)
     pair = small(joined_first_kernel, shape((72, BR), jnp.bfloat16))(parcel, other)
     mine = to_each(copies, CHIPS)
     row = [pair, over_z(pair, 1), over_z(pair, 2), over_z(pair, 3)]
@@ -251,8 +294,8 @@
     *row, row_log = small(arranged_first_kernel, outs)(*row)
     theirs = lax.ppermute(mine, "c", SWAP)
     total = small(total_kernel, shape((8, 128), jnp.float32))(mine)
-    totals = [total, over_z(total, 1), over_z(total, 2), over_z(total, 3)]
-    col_log = small(col_log_kernel, shape((1, COLS), jnp.float32))(mine, theirs, *totals)
+    other_total = lax.ppermute(total, "yl", SWAP)
+    col_log = small(col_log_kernel, shape((1, COLS), jnp.float32))(mine, theirs, total, other_total)
     for sweep in range(2):
         own, away_pair, home, away = swept(*row, mine, theirs, row_log, col_log, in_hbm(counts))
         theirs = lax.ppermute(away, "c", SWAP)
@@ -264,7 +307,7 @@
         parts = [over_z(parts[shift - 1], shift) for shift in (2, 1, 3)]
         outs = (shape((32, BR), jnp.float32),) * 2 + (shape((32, BR), jnp.bfloat16),)
         row_emb, row_accum, half = small(row_kernel, outs)(keep, *parts, row_emb, row_accum)
-        outs = (shape((16, COLS), jnp.float32),) * 2 + (shape((8, 16, COLS), jnp.bfloat16),)
+        outs = (shape((16, COLS), jnp.float32),) * 2 + (shape((8, 256, 128), jnp.bfloat16),)
         col_emb, col_accum, copies = small(col_kernel, outs)(came, col_emb, col_accum)
         if sweep == 0:
             pair = lax.ppermute(half, "yl", SWAP)

time: 157 us -> 154 us (0.981)
  other arithmetic: 4.05 us -> 0 us
  Pallas kernels: 22.6 us -> 26.3 us
  starting transfers between devices: 38.8 us -> 36.5 us
  blocking collectives: 34.5 us -> 32.4 us
    reduce_sum x1 -> x0, other arithmetic: 4.05 us -> none  [on_device(): col_sums = jnp.sum(counts, axis=0)[None]]
    pallas_call x3, Pallas kernels: 0.24 us -> 3.86 us  [the longest x1 3.77 us: first(): pl.pallas_call(first_kernel, out_shape=(shape((40, BR), jnp.bfloat16), sh...]
    ppermute x15, waiting for transfers between devices: 18.5 us -> 21.9 us  [over_z(): return lax.ppermute(value, 'z', [(at, (at + shift) % 4) for at in range(4)])]
    all_to_all x2, blocking collectives: 34.5 us -> 32.4 us  [to_each(): return lax.all_to_all(copies, axes, 0, 0, tiled=True)]
    ppermute x1, waiting for transfers between devices: 1.92 us -> 0.01 us  [on_device(): other_total = lax.ppermute(total, 'yl', SWAP)]
  transfers between devices with their start and end apart: 27 -> 27, of which waited for: 21 -> 20; matrix products, arithmetic and copies ran while one was open for 0% -> 0% of each run, Pallas kernels for 1% -> 1%
where the time goes in v10:
time: 154 us; the launch traced here: 153 us
  waiting for transfers between devices  57.4 us (37%)
  starting transfers between devices  36.5 us (24%)
  blocking collectives  32.4 us (21%)
  Pallas kernels  26.3 us (17%)
    all_to_all x2, blocking collectives, to_each(): return lax.all_to_all(copies, axes, 0, 0, tiled=True)  32.4 us
    ppermute x15, waiting for transfers between devices, over_z(): return lax.ppermute(value, 'z', [(at, (at + shift) % 4) for at in range(4)])  21.9 us
    ppermute x15, starting transfers between devices, over_z(): return lax.ppermute(value, 'z', [(at, (at + shift) % 4) for at in range(4)])  21.6 us
    pallas_call x2, Pallas kernels, swept(): pl.pallas_call(sweep_kernel, out_shape=(shape((4, 32, BR), jnp.bfloat16),...  17.9 us
    ppermute x2, waiting for transfers between devices, on_device(): from_pair = lax.ppermute(away_pair, 'yl', SWAP)  13.2 us
    all_to_all x2, starting transfers between devices, to_each(): return lax.all_to_all(copies, axes, 0, 0, tiled=True)  10.9 us
    all_to_all x2, waiting for transfers between devices, to_each(): return lax.all_to_all(copies, axes, 0, 0, tiled=True)  10 us
    ppermute x1, waiting for transfers between devices, on_device(): other = lax.ppermute(parcel, 'yl', SWAP)  4.18 us
  transfers between devices with their start and end apart: 27, of which 20 were waited for; matrix products, arithmetic and copies ran while one was open for 0% of the time, Pallas kernels for 1%

profile of v10, /device:TPU:0, one launch (start us, length us, event | category | flops | bytes accessed | tf_op | source)
XLA Modules:
  0.0 153.4 jit_solution(6523280658549763998)
XLA Ops:
  0.6 3.8 %first.1 = (bf16[40,1024]{1,0:T(8,128)(2,1)S(1)}, s32[8,128]{1,0:T(8,128)S(1)}, s32[1,2048]{1,0:T(1,128)S(1)}) custom-call(s32[1024,2048]{1,0:T(8,128)} %counts_ref.5, f32[32,1024]{1,0:T(8,128)} %emb_ref.4), custom_call_target="tpu_custom_call" | custom-call | flops 8388608 | bytes 8388608 | tf_op jit(solution)/shard_map/first/pallas_call | solution.py:73
  4.5 1.2 collective-permute-done.4.other_ref
  5.7 4.1 %collective-permute-start.7 = (s32[8,128]{1,0:T(8,128)S(1)}, s32[8,128]{1,0:T(8,128)S(1)}, u32[]{:S(2)}, u32[]{:S(2)}) collective-permute-start(s32[8,128]{1,0:T(8,128)S(1)} %shard_map.70.refs_0_), channel_id=1, source_target_pairs={{0,6},{2,0},{4,2},{6,4},{1,7},{3,1},{5,3},{7,5},{8,14},{10,8},{12,... | collective-permute-start | bytes 12296 | tf_op jit(solution)/shard_map/ppermute | solution.py:37
  9.8 1.3 collective-permute-start.5
  11.2 3.8 %collective-permute-done.6.refs_2_ = s32[8,128]{1,0:T(8,128)S(1)} collective-permute-done((s32[8,128]{1,0:T(8,128)S(1)}, s32[8,128]{1,0:T(8,128)S(1)}, u32[]{:S(2)}, u32[]{:S(2)}) %collective-permute-start.6) | collective-permute-done | bytes 4128 | tf_op jit(solution)/shard_map/ppermute | solution.py:37
  15.0 18.2 %all_to_all.20.mine_ref = bf16[8,304,128]{2,1,0:T(8,128)(2,1)S(1)} all-to-all(bf16[8,304,128]{2,1,0:T(8,128)(2,1)S(1)} %shard_map.71), channel_id=1, replica_groups=mesh['x'=4,'yh'=2,'c'=2,'z'=4,'yl'=2] {'x','yh'}, dimensions={0} | all-to-all | bytes 1245184 | tf_op jit(solution)/shard_map/all_to_all | solution.py:33
  33.2 0.7 collective-permute-start
  33.8 4.2 %collective-permute-done.other_ref = bf16[40,1024]{1,0:T(8,128)(2,1)S(1)} collective-permute-done((bf16[40,1024]{1,0:T(8,128)(2,1)S(1)}, bf16[40,1024]{1,0:T(8,128)(2,1)S(1)}, u32[]{:S(2)}, u32[]{:S(2)}) %collective-permute-start) | collective-permute-done | bytes 81952 | tf_op jit(solution)/shard_map/ppermute | solution.py:286
  38.0 1.0 collective-permute-start.3
  39.0 0.9 collective-permute-start.2
  40.0 1.3 collective-permute-start.1
  41.4 0.9 collective-permute-start.9
  42.2 2.6 %collective-permute-done.3.refs_3_ = bf16[72,1024]{1,0:T(8,128)(2,1)S(1)} collective-permute-done((bf16[72,1024]{1,0:T(8,128)(2,1)S(1)}, bf16[72,1024]{1,0:T(8,128)(2,1)S(1)}, u32[]{:S(2)}, u32[]{:S(2)}) %collective-permute-start.3) | collective-permute-done | bytes 147488 | tf_op jit(solution)/shard_map/ppermute | solution.py:37
  44.8 2.4 %collective-permute-done.2.refs_2_ = bf16[72,1024]{1,0:T(8,128)(2,1)S(1)} collective-permute-done((bf16[72,1024]{1,0:T(8,128)(2,1)S(1)}, bf16[72,1024]{1,0:T(8,128)(2,1)S(1)}, u32[]{:S(2)}, u32[]{:S(2)}) %collective-permute-start.2) | collective-permute-done | bytes 147488 | tf_op jit(solution)/shard_map/ppermute | solution.py:37
  47.2 1.6 %collective-permute-done.1.refs_1_ = bf16[72,1024]{1,0:T(8,128)(2,1)S(1)} collective-permute-done((bf16[72,1024]{1,0:T(8,128)(2,1)S(1)}, bf16[72,1024]{1,0:T(8,128)(2,1)S(1)}, u32[]{:S(2)}, u32[]{:S(2)}) %collective-permute-start.1) | collective-permute-done | bytes 147488 | tf_op jit(solution)/shard_map/ppermute | solution.py:37
  48.8 0.2 shard_map.69
  49.1 8.9 %sweep.2 = (bf16[4,32,1024]{2,1,0:T(8,128)(2,1)S(1)}, bf16[4,32,1024]{2,1,0:T(8,128)(2,1)S(1)}, bf16[8,16,2048]{2,1,0:T(8,128)(2,1)S(1)}, bf16[8,16,2048]{2,1,0:T(8,128)(2,1)S(1)}) custom-call(bf16[8,32,1024]{2,1,0:T(8,128)(2,1)S(1)} %get-tuple-element.35.row_flat, bf16[1024,256]{1,0:T(8,128)(2,1)S(1)} %get-tuple-element.36.row_tall, ...), custom_call_target="tpu_custom_call" | custom-call | flops 3221225472 | bytes 20971520 | tf_op jit(solution)/shard_map/sweep/pallas_call | solution.py:211
  58.1 1.9 %collective-permute-done.18.theirs_ref = bf16[8,16,2048]{2,1,0:T(8,128)(2,1)S(1)} collective-permute-done((bf16[8,16,2048]{2,1,0:T(8,128)(2,1)S(1)}, bf16[8,16,2048]{2,1,0:T(8,128)(2,1)S(1)}, u32[]{:S(2)}, u32[]{:S(2)}) %collective-permute-start.18) | collective-permute-done | bytes 524320 | tf_op jit(solution)/shard_map/ppermute | solution.py:301
  60.2 14.2 %all_to_all.21.came_ref = bf16[8,16,2048]{2,1,0:T(8,128)(2,1)S(1)} all-to-all(bf16[8,16,2048]{2,1,0:T(8,128)(2,1)S(1)} %shard_map.78), channel_id=1, replica_groups=mesh['x'=4,'yh'=2,'c'=2,'z'=4,'yl'=2] {'x','yh'}, dimensions={0} | all-to-all | bytes 1048576 | tf_op jit(solution)/shard_map/all_to_all | solution.py:33
  74.4 0.9 shard_map.79
  75.3 3.5 %all-to-all-start.2 = ((bf16[8,256,128]{2,1,0:T(8,128)(2,1)}), bf16[8,256,128]{2,1,0:T(8,128)(2,1)S(1)}, u32[]{:S(2)}, u32[]{:S(2)}) async-start(bf16[8,256,128]{2,1,0:T(8,128)(2,1)} %get-tuple-element.51), calls=%async_computation.2 | async-start | bytes 1048576 | tf_op jit(solution)/shard_map/all_to_all | solution.py:33
  78.8 0.8 collective-permute-start.10
  79.6 10.0 %all-to-all-done.2.mine_ref = bf16[8,256,128]{2,1,0:T(8,128)(2,1)S(1)} async-done(((bf16[8,256,128]{2,1,0:T(8,128)(2,1)}), bf16[8,256,128]{2,1,0:T(8,128)(2,1)S(1)}, u32[]{:S(2)}, u32[]{:S(2)}) %all-to-all-start.2) | async-done | bytes 524320 | tf_op jit(solution)/shard_map/all_to_all | solution.py:33
  89.6 0.9 collective-permute-done.10.came_ref
  90.6 1.3 collective-permute-start.11
  92.1 3.0 %collective-permute-start.13 = (bf16[32,1024]{1,0:T(8,128)(2,1)S(1)}, bf16[32,1024]{1,0:T(8,128)(2,1)S(1)}, u32[]{:S(2)}, u32[]{:S(2)}) collective-permute-start(bf16[32,1024]{1,0:T(8,128)(2,1)S(1)} %get-tuple-element.45), channel_id=1, source_target_pairs={{0,6},{2,0},{4,2},{6,4},{1,7},{3,1},{5,3},{7,5},{8,14},{10,8},{12,... | collective-permute-start | bytes 196616 | tf_op jit(solution)/shard_map/ppermute | solution.py:37
  95.1 1.3 collective-permute-done.11.first_ref
  96.5 0.9 collective-permute-done.12.second_ref
  97.5 1.3 collective-permute-start.14
  98.8 3.1 %collective-permute-done.14.other_ref = bf16[32,1024]{1,0:T(8,128)(2,1)S(1)} collective-permute-done((bf16[32,1024]{1,0:T(8,128)(2,1)S(1)}, bf16[32,1024]{1,0:T(8,128)(2,1)S(1)}, u32[]{:S(2)}, u32[]{:S(2)}) %collective-permute-start.14) | collective-permute-done | bytes 65568 | tf_op jit(solution)/shard_map/ppermute | solution.py:313
  101.9 3.3 %collective-permute-start.17 = (bf16[64,1024]{1,0:T(8,128)(2,1)S(1)}, bf16[64,1024]{1,0:T(8,128)(2,1)S(1)}, u32[]{:S(2)}, u32[]{:S(2)}) collective-permute-start(bf16[64,1024]{1,0:T(8,128)(2,1)S(1)} %shard_map.76.refs_0_), channel_id=1, source_target_pairs={{0,6},{2,0},{4,2},{6,4},{1,7},{3,1},{5,3},{7,5},{8,14},{10,8},{12,... | collective-permute-start | bytes 393224 | tf_op jit(solution)/shard_map/ppermute | solution.py:37
  105.1 0.9 collective-permute-start.15
  106.1 3.0 %collective-permute-done.17.refs_3_ = bf16[64,1024]{1,0:T(8,128)(2,1)S(1)} collective-permute-done((bf16[64,1024]{1,0:T(8,128)(2,1)S(1)}, bf16[64,1024]{1,0:T(8,128)(2,1)S(1)}, u32[]{:S(2)}, u32[]{:S(2)}) %collective-permute-start.17) | collective-permute-done | bytes 131104 | tf_op jit(solution)/shard_map/ppermute | solution.py:37
  109.1 2.6 %collective-permute-done.16.refs_2_ = bf16[64,1024]{1,0:T(8,128)(2,1)S(1)} collective-permute-done((bf16[64,1024]{1,0:T(8,128)(2,1)S(1)}, bf16[64,1024]{1,0:T(8,128)(2,1)S(1)}, u32[]{:S(2)}, u32[]{:S(2)}) %collective-permute-start.16) | collective-permute-done | bytes 131104 | tf_op jit(solution)/shard_map/ppermute | solution.py:37
  111.7 1.0 collective-permute-done.15.refs_1_
  112.7 0.2 shard_map.77
  113.0 9.0 %sweep.3 = (bf16[4,32,1024]{2,1,0:T(8,128)(2,1)S(1)}, bf16[4,32,1024]{2,1,0:T(8,128)(2,1)S(1)}, bf16[8,16,2048]{2,1,0:T(8,128)(2,1)S(1)}, bf16[8,16,2048]{2,1,0:T(8,128)(2,1)S(1)}) custom-call(bf16[8,32,1024]{2,1,0:T(8,128)(2,1)S(1)} %get-tuple-element.47.row_flat, bf16[1024,256]{1,0:T(8,128)(2,1)S(1)} %get-tuple-element.48.row_tall, ...), custom_call_target="tpu_custom_call" | custom-call | flops 3221225472 | bytes 20971520 | tf_op jit(solution)/shard_map/sweep/pallas_call | solution.py:211
  122.1 1.9 %collective-permute-done.24.theirs_ref = bf16[8,16,2048]{2,1,0:T(8,128)(2,1)S(1)} collective-permute-done((bf16[8,16,2048]{2,1,0:T(8,128)(2,1)S(1)}, bf16[8,16,2048]{2,1,0:T(8,128)(2,1)S(1)}, u32[]{:S(2)}, u32[]{:S(2)}) %collective-permute-start.24) | collective-permute-done | bytes 524320 | tf_op jit(solution)/shard_map/ppermute | solution.py:301
  124.0 0.9 shard_map.82
  124.9 7.4 %all-to-all-start.3 = ((bf16[8,16,2048]{2,1,0:T(8,128)(2,1)}), bf16[8,16,2048]{2,1,0:T(8,128)(2,1)S(1)}, u32[]{:S(2)}, u32[]{:S(2)}) async-start(bf16[8,16,2048]{2,1,0:T(8,128)(2,1)} %shard_map.82), calls=%async_computation.3 | async-start | bytes 1048576 | tf_op jit(solution)/shard_map/all_to_all | solution.py:33
  132.4 12.3 %collective-permute-done.20.came_ref = bf16[4,32,1024]{2,1,0:T(8,128)(2,1)S(1)} collective-permute-done((bf16[4,32,1024]{2,1,0:T(8,128)(2,1)S(1)}, bf16[4,32,1024]{2,1,0:T(8,128)(2,1)S(1)}, u32[]{:S(2)}, u32[]{:S(2)}) %collective-permute-start.20) | collective-permute-done | bytes 262176 | tf_op jit(solution)/shard_map/ppermute | solution.py:302
  144.8 1.0 collective-permute-start.21
  145.8 0.8 collective-permute-start.22
  146.6 2.4 %collective-permute-start.23 = (bf16[32,1024]{1,0:T(8,128)(2,1)S(1)}, bf16[32,1024]{1,0:T(8,128)(2,1)S(1)}, u32[]{:S(2)}, u32[]{:S(2)}) collective-permute-start(bf16[32,1024]{1,0:T(8,128)(2,1)S(1)} %get-tuple-element.57), channel_id=1, source_target_pairs={{0,6},{2,0},{4,2},{6,4},{1,7},{3,1},{5,3},{7,5},{8,14},{10,8},{12,... | collective-permute-start | bytes 196616 | tf_op jit(solution)/shard_map/ppermute | solution.py:37
  149.0 1.9 %collective-permute-done.21.first_ref = bf16[32,1024]{1,0:T(8,128)(2,1)S(1)} collective-permute-done((bf16[32,1024]{1,0:T(8,128)(2,1)S(1)}, bf16[32,1024]{1,0:T(8,128)(2,1)S(1)}, u32[]{:S(2)}, u32[]{:S(2)}) %collective-permute-start.21) | collective-permute-done | bytes 65568 | tf_op jit(solution)/shard_map/ppermute | solution.py:37
  150.9 0.7 collective-permute-done.22.second_ref
  151.6 0.8 shard_map.81
  152.4 1.0 shard_map.83
  (35 shorter events, 1.3 us)
Async XLA Ops:
  0.6 14.3 %copy-start.1 = (f32[16,2048]{1,0:T(8,128)S(1)}, f32[16,2048]{1,0:T(8,128)}, u32[]{:S(2)}) copy-start(f32[16,2048]{1,0:T(8,128)} %emb_ref.5) | copy-start | bytes 393220
  4.4 1.2 collective-permute-start.4
  5.7 5.5 %collective-permute-start.7 = (s32[8,128]{1,0:T(8,128)S(1)}, s32[8,128]{1,0:T(8,128)S(1)}, u32[]{:S(2)}, u32[]{:S(2)}) collective-permute-start(s32[8,128]{1,0:T(8,128)S(1)} %shard_map.70.refs_0_), channel_id=1, source_target_pairs={{0,6},{2,0},{4,2},{6,4},{1,7},{3,1},{5,3},{7,5},{8,14},{10,8},{12,... | collective-permute-start | bytes 12296 | tf_op jit(solution)/shard_map/ppermute | solution.py:37
  9.8 5.1 %collective-permute-start.6 = (s32[8,128]{1,0:T(8,128)S(1)}, s32[8,128]{1,0:T(8,128)S(1)}, u32[]{:S(2)}, u32[]{:S(2)}) collective-permute-start(s32[8,128]{1,0:T(8,128)S(1)} %shard_map.70.refs_0_), channel_id=1, source_target_pairs={{0,4},{2,6},{4,0},{6,2},{1,5},{3,7},{5,1},{7,3},{8,12},{10,14},{12... | collective-permute-start | bytes 12296 | tf_op jit(solution)/shard_map/ppermute | solution.py:37
  9.8 5.1 %collective-permute-start.5 = (s32[8,128]{1,0:T(8,128)S(1)}, s32[8,128]{1,0:T(8,128)S(1)}, u32[]{:S(2)}, u32[]{:S(2)}) collective-permute-start(s32[8,128]{1,0:T(8,128)S(1)} %shard_map.70.refs_0_), channel_id=1, source_target_pairs={{0,2},{2,4},{4,6},{6,0},{1,3},{3,5},{5,7},{7,1},{8,10},{10,12},{12... | collective-permute-start | bytes 12296 | tf_op jit(solution)/shard_map/ppermute | solution.py:37
  33.2 15.9 %collective-permute-start.8 = (bf16[8,304,128]{2,1,0:T(8,128)(2,1)S(1)}, bf16[8,304,128]{2,1,0:T(8,128)(2,1)S(1)}, u32[]{:S(2)}, u32[]{:S(2)}) collective-permute-start(bf16[8,304,128]{2,1,0:T(8,128)(2,1)S(1)} %all_to_all.20.mine_ref), channel_id=1, source_target_pairs={{0,8},{8,0},{1,9},{9,1},{2,10},{10,2},{3,11},{11,3},{4,12},{12,4},... | collective-permute-start | bytes 1867784 | tf_op jit(solution)/shard_map/ppermute | solution.py:295
  33.2 4.9 %collective-permute-start = (bf16[40,1024]{1,0:T(8,128)(2,1)S(1)}, bf16[40,1024]{1,0:T(8,128)(2,1)S(1)}, u32[]{:S(2)}, u32[]{:S(2)}) collective-permute-start(bf16[40,1024]{1,0:T(8,128)(2,1)S(1)} %get-tuple-element.34.own_ref), channel_id=1, source_target_pairs={{0,1},{1,0},{2,3},{3,2},{4,5},{5,4},{6,7},{7,6},{8,9},{9,8},{10,11... | collective-permute-start | bytes 245768 | tf_op jit(solution)/shard_map/ppermute | solution.py:286
  38.0 36.4 %copy-start.2 = (f32[16,2048]{1,0:T(8,128)S(1)}, f32[16,2048]{1,0:T(8,128)}, u32[]{:S(2)}) copy-start(f32[16,2048]{1,0:T(8,128)} %accum_ref.3) | copy-start | bytes 393220
  38.0 6.8 %collective-permute-start.3 = (bf16[72,1024]{1,0:T(8,128)(2,1)S(1)}, bf16[72,1024]{1,0:T(8,128)(2,1)S(1)}, u32[]{:S(2)}, u32[]{:S(2)}) collective-permute-start(bf16[72,1024]{1,0:T(8,128)(2,1)S(1)} %shard_map.68.refs_0_), channel_id=1, source_target_pairs={{0,6},{2,0},{4,2},{6,4},{1,7},{3,1},{5,3},{7,5},{8,14},{10,8},{12,... | collective-permute-start | bytes 442376 | tf_op jit(solution)/shard_map/ppermute | solution.py:37
  39.0 8.2 %collective-permute-start.2 = (bf16[72,1024]{1,0:T(8,128)(2,1)S(1)}, bf16[72,1024]{1,0:T(8,128)(2,1)S(1)}, u32[]{:S(2)}, u32[]{:S(2)}) collective-permute-start(bf16[72,1024]{1,0:T(8,128)(2,1)S(1)} %shard_map.68.refs_0_), channel_id=1, source_target_pairs={{0,4},{2,6},{4,0},{6,2},{1,5},{3,7},{5,1},{7,3},{8,12},{10,14},{12... | collective-permute-start | bytes 442376 | tf_op jit(solution)/shard_map/ppermute | solution.py:37
  40.0 8.8 %collective-permute-start.1 = (bf16[72,1024]{1,0:T(8,128)(2,1)S(1)}, bf16[72,1024]{1,0:T(8,128)(2,1)S(1)}, u32[]{:S(2)}, u32[]{:S(2)}) collective-permute-start(bf16[72,1024]{1,0:T(8,128)(2,1)S(1)} %shard_map.68.refs_0_), channel_id=1, source_target_pairs={{0,2},{2,4},{4,6},{6,0},{1,3},{3,5},{5,7},{7,1},{8,10},{10,12},{12... | collective-permute-start | bytes 442376 | tf_op jit(solution)/shard_map/ppermute | solution.py:37
  41.4 7.7 %collective-permute-start.9 = (f32[8,128]{1,0:T(8,128)S(1)}, f32[8,128]{1,0:T(8,128)S(1)}, u32[]{:S(2)}, u32[]{:S(2)}) collective-permute-start(f32[8,128]{1,0:T(8,128)S(1)} %shard_map.72.total_ref), channel_id=1, source_target_pairs={{0,1},{1,0},{2,3},{3,2},{4,5},{5,4},{6,7},{7,6},{8,9},{9,8},{10,11... | collective-permute-start | bytes 12296 | tf_op jit(solution)/shard_map/ppermute | solution.py:297
  49.1 48.3 %copy-start = (f32[32,1024]{1,0:T(8,128)S(1)}, f32[32,1024]{1,0:T(8,128)}, u32[]{:S(2)}) copy-start(f32[32,1024]{1,0:T(8,128)} %emb_ref.4) | copy-start | bytes 393220
  49.1 48.3 %copy-start.3 = (f32[32,1024]{1,0:T(8,128)S(1)}, f32[32,1024]{1,0:T(8,128)}, u32[]{:S(2)}) copy-start(f32[32,1024]{1,0:T(8,128)} %accum_ref.2) | copy-start | bytes 393220
  58.0 2.0 %collective-permute-start.18 = (bf16[8,16,2048]{2,1,0:T(8,128)(2,1)S(1)}, bf16[8,16,2048]{2,1,0:T(8,128)(2,1)S(1)}, u32[]{:S(2)}, u32[]{:S(2)}) collective-permute-start(bf16[8,16,2048]{2,1,0:T(8,128)(2,1)S(1)} %get-tuple-element.50), channel_id=1, source_target_pairs={{0,8},{8,0},{1,9},{9,1},{2,10},{10,2},{3,11},{11,3},{4,12},{12,4},... | collective-permute-start | bytes 1572872 | tf_op jit(solution)/shard_map/ppermute | solution.py:301
  75.3 14.3 %all-to-all-start.2 = ((bf16[8,256,128]{2,1,0:T(8,128)(2,1)}), bf16[8,256,128]{2,1,0:T(8,128)(2,1)S(1)}, u32[]{:S(2)}, u32[]{:S(2)}) async-start(bf16[8,256,128]{2,1,0:T(8,128)(2,1)} %get-tuple-element.51), calls=%async_computation.2 | async-start | bytes 1048576 | tf_op jit(solution)/shard_map/all_to_all | solution.py:33
  78.8 11.7 %collective-permute-start.10 = (bf16[4,32,1024]{2,1,0:T(8,128)(2,1)S(1)}, bf16[4,32,1024]{2,1,0:T(8,128)(2,1)S(1)}, u32[]{:S(2)}, u32[]{:S(2)}) collective-permute-start(bf16[4,32,1024]{2,1,0:T(8,128)(2,1)S(1)} %get-tuple-element.41), channel_id=1, source_target_pairs={{0,1},{1,0},{2,3},{3,2},{4,5},{5,4},{6,7},{7,6},{8,9},{9,8},{10,11... | collective-permute-start | bytes 786440 | tf_op jit(solution)/shard_map/ppermute | solution.py:302
  89.6 23.4 %collective-permute-start.19 = (bf16[8,256,128]{2,1,0:T(8,128)(2,1)S(1)}, bf16[8,256,128]{2,1,0:T(8,128)(2,1)S(1)}, u32[]{:S(2)}, u32[]{:S(2)}) collective-permute-start(bf16[8,256,128]{2,1,0:T(8,128)(2,1)S(1)} %all-to-all-done.2.mine_ref), channel_id=1, source_target_pairs={{0,8},{8,0},{1,9},{9,1},{2,10},{10,2},{3,11},{11,3},{4,12},{12,4},... | collective-permute-start | bytes 1572872 | tf_op jit(solution)/shard_map/ppermute | solution.py:319
  90.6 5.9 %collective-permute-start.11 = (bf16[32,1024]{1,0:T(8,128)(2,1)S(1)}, bf16[32,1024]{1,0:T(8,128)(2,1)S(1)}, u32[]{:S(2)}, u32[]{:S(2)}) collective-permute-start(bf16[32,1024]{1,0:T(8,128)(2,1)S(1)} %get-tuple-element.43), channel_id=1, source_target_pairs={{0,4},{2,6},{4,0},{6,2},{1,5},{3,7},{5,1},{7,3},{8,12},{10,14},{12... | collective-permute-start | bytes 196616 | tf_op jit(solution)/shard_map/ppermute | solution.py:37
  91.9 5.5 %collective-permute-start.12 = (bf16[32,1024]{1,0:T(8,128)(2,1)S(1)}, bf16[32,1024]{1,0:T(8,128)(2,1)S(1)}, u32[]{:S(2)}, u32[]{:S(2)}) collective-permute-start(bf16[32,1024]{1,0:T(8,128)(2,1)S(1)} %get-tuple-element.44), channel_id=1, source_target_pairs={{0,2},{2,4},{4,6},{6,0},{1,3},{3,5},{5,7},{7,1},{8,10},{10,12},{12... | collective-permute-start | bytes 196616 | tf_op jit(solution)/shard_map/ppermute | solution.py:37
  92.1 5.3 %collective-permute-start.13 = (bf16[32,1024]{1,0:T(8,128)(2,1)S(1)}, bf16[32,1024]{1,0:T(8,128)(2,1)S(1)}, u32[]{:S(2)}, u32[]{:S(2)}) collective-permute-start(bf16[32,1024]{1,0:T(8,128)(2,1)S(1)} %get-tuple-element.45), channel_id=1, source_target_pairs={{0,6},{2,0},{4,2},{6,4},{1,7},{3,1},{5,3},{7,5},{8,14},{10,8},{12,... | collective-permute-start | bytes 196616 | tf_op jit(solution)/shard_map/ppermute | solution.py:37
  97.5 4.3 %collective-permute-start.14 = (bf16[32,1024]{1,0:T(8,128)(2,1)S(1)}, bf16[32,1024]{1,0:T(8,128)(2,1)S(1)}, u32[]{:S(2)}, u32[]{:S(2)}) collective-permute-start(bf16[32,1024]{1,0:T(8,128)(2,1)S(1)} %get-tuple-element.46.own_ref), channel_id=1, source_target_pairs={{0,1},{1,0},{2,3},{3,2},{4,5},{5,4},{6,7},{7,6},{8,9},{9,8},{10,11... | collective-permute-start | bytes 196616 | tf_op jit(solution)/shard_map/ppermute | solution.py:313
  101.9 7.2 %collective-permute-start.17 = (bf16[64,1024]{1,0:T(8,128)(2,1)S(1)}, bf16[64,1024]{1,0:T(8,128)(2,1)S(1)}, u32[]{:S(2)}, u32[]{:S(2)}) collective-permute-start(bf16[64,1024]{1,0:T(8,128)(2,1)S(1)} %shard_map.76.refs_0_), channel_id=1, source_target_pairs={{0,6},{2,0},{4,2},{6,4},{1,7},{3,1},{5,3},{7,5},{8,14},{10,8},{12,... | collective-permute-start | bytes 393224 | tf_op jit(solution)/shard_map/ppermute | solution.py:37
  105.1 6.6 %collective-permute-start.16 = (bf16[64,1024]{1,0:T(8,128)(2,1)S(1)}, bf16[64,1024]{1,0:T(8,128)(2,1)S(1)}, u32[]{:S(2)}, u32[]{:S(2)}) collective-permute-start(bf16[64,1024]{1,0:T(8,128)(2,1)S(1)} %shard_map.76.refs_0_), channel_id=1, source_target_pairs={{0,4},{2,6},{4,0},{6,2},{1,5},{3,7},{5,1},{7,3},{8,12},{10,14},{12... | collective-permute-start | bytes 393224 | tf_op jit(solution)/shard_map/ppermute | solution.py:37
  105.1 7.6 %collective-permute-start.15 = (bf16[64,1024]{1,0:T(8,128)(2,1)S(1)}, bf16[64,1024]{1,0:T(8,128)(2,1)S(1)}, u32[]{:S(2)}, u32[]{:S(2)}) collective-permute-start(bf16[64,1024]{1,0:T(8,128)(2,1)S(1)} %shard_map.76.refs_0_), channel_id=1, source_target_pairs={{0,2},{2,4},{4,6},{6,0},{1,3},{3,5},{5,7},{7,1},{8,10},{10,12},{12... | collective-permute-start | bytes 393224 | tf_op jit(solution)/shard_map/ppermute | solution.py:37
  122.0 2.0 %collective-permute-start.24 = (bf16[8,16,2048]{2,1,0:T(8,128)(2,1)S(1)}, bf16[8,16,2048]{2,1,0:T(8,128)(2,1)S(1)}, u32[]{:S(2)}, u32[]{:S(2)}) collective-permute-start(bf16[8,16,2048]{2,1,0:T(8,128)(2,1)S(1)} %get-tuple-element.62), channel_id=1, source_target_pairs={{0,8},{8,0},{1,9},{9,1},{2,10},{10,2},{3,11},{11,3},{4,12},{12,4},... | collective-permute-start | bytes 1572872 | tf_op jit(solution)/shard_map/ppermute | solution.py:301
  124.9 27.5 %all-to-all-start.3 = ((bf16[8,16,2048]{2,1,0:T(8,128)(2,1)}), bf16[8,16,2048]{2,1,0:T(8,128)(2,1)S(1)}, u32[]{:S(2)}, u32[]{:S(2)}) async-start(bf16[8,16,2048]{2,1,0:T(8,128)(2,1)} %shard_map.82), calls=%async_computation.3 | async-start | bytes 1048576 | tf_op jit(solution)/shard_map/all_to_all | solution.py:33
  132.3 12.4 %collective-permute-start.20 = (bf16[4,32,1024]{2,1,0:T(8,128)(2,1)S(1)}, bf16[4,32,1024]{2,1,0:T(8,128)(2,1)S(1)}, u32[]{:S(2)}, u32[]{:S(2)}) collective-permute-start(bf16[4,32,1024]{2,1,0:T(8,128)(2,1)S(1)} %get-tuple-element.53), channel_id=1, source_target_pairs={{0,1},{1,0},{2,3},{3,2},{4,5},{5,4},{6,7},{7,6},{8,9},{9,8},{10,11... | collective-permute-start | bytes 786440 | tf_op jit(solution)/shard_map/ppermute | solution.py:302
  144.8 6.1 %collective-permute-start.21 = (bf16[32,1024]{1,0:T(8,128)(2,1)S(1)}, bf16[32,1024]{1,0:T(8,128)(2,1)S(1)}, u32[]{:S(2)}, u32[]{:S(2)}) collective-permute-start(bf16[32,1024]{1,0:T(8,128)(2,1)S(1)} %get-tuple-element.55), channel_id=1, source_target_pairs={{0,4},{2,6},{4,0},{6,2},{1,5},{3,7},{5,1},{7,3},{8,12},{10,14},{12... | collective-permute-start | bytes 196616 | tf_op jit(solution)/shard_map/ppermute | solution.py:37
  145.8 5.8 %collective-permute-start.22 = (bf16[32,1024]{1,0:T(8,128)(2,1)S(1)}, bf16[32,1024]{1,0:T(8,128)(2,1)S(1)}, u32[]{:S(2)}, u32[]{:S(2)}) collective-permute-start(bf16[32,1024]{1,0:T(8,128)(2,1)S(1)} %get-tuple-element.56), channel_id=1, source_target_pairs={{0,2},{2,4},{4,6},{6,0},{1,3},{3,5},{5,7},{7,1},{8,10},{10,12},{12... | collective-permute-start | bytes 196616 | tf_op jit(solution)/shard_map/ppermute | solution.py:37
  146.6 5.0 %collective-permute-start.23 = (bf16[32,1024]{1,0:T(8,128)(2,1)S(1)}, bf16[32,1024]{1,0:T(8,128)(2,1)S(1)}, u32[]{:S(2)}, u32[]{:S(2)}) collective-permute-start(bf16[32,1024]{1,0:T(8,128)(2,1)S(1)} %get-tuple-element.57), channel_id=1, source_target_pairs={{0,6},{2,0},{4,2},{6,4},{1,7},{3,1},{5,3},{7,5},{8,14},{10,8},{12,... | collective-permute-start | bytes 196616 | tf_op jit(solution)/shard_map/ppermute | solution.py:37

commit v11 on v10

--- a/solution.py
+++ b/solution.py
@@ -48,13 +48,15 @@
     copies = [
         pltpu.make_async_copy(counts_ref.at[pl.ds(at * 128, 128)], blocks.at[at], arrived.at[at]) for at in range(BR // 128)
     ]
-    for copy in copies:
+    for copy in copies[:3]:
         copy.start()
     emb_copy = pltpu.make_async_copy(emb_source, emb_ref, emb_arrived)
     emb_copy.start()
     col = jnp.zeros((8, COLS), jnp.int32)
     for at in range(BR // 128):
         copies[at].wait()
+        if at + 3 < BR // 128:
+            copies[at + 3].start()
         block = blocks[at]
         col += jnp.sum(block.reshape(16, 8, COLS), axis=0)
         across = block[:, :128]
@@ -160,8 +162,7 @@
     copies = [
         pltpu.make_async_copy(counts_ref.at[:, pl.ds(at * TN, TN)], counts.at[at], arrived.at[at]) for at in range(COLS // TN)
     ]
-    for copy in copies:
-        copy.start()
+    copies[0].start()
     core, z, yl = lax.axis_index("c"), lax.axis_index("z"), lax.axis_index("yl")
     for at in range(BR // 128):
         here = slice(at * 128, at * 128 + 128)
@@ -170,6 +171,8 @@
         rows, here = slice(at * 16, at * 16 + 16), slice(at * 128, at * 128 + 128)
         col_flat[:, pl.ds(core, 1), :, here] = mine_ref[:, rows, :][:, None]
         col_flat[:, pl.ds(1 - core, 1), :, here] = theirs_ref[:, rows, :][:, None]
+    copies[1].start()
+
     def col_part(start):
         here = slice(start, start + 256)
         part = jnp.dot(row_flat[...].reshape(D, BR), grads[:, here], preferred_element_type=jnp.float32).reshape(8, 2, 16, 256)
@@ -183,6 +186,8 @@
         col_tall[here, :] = col.T
         shift = col_log_ref[:, here]
         copies[at].wait()
+        if at + 2 < COLS // TN:
+            copies[at + 2].start()
         for chunk in range(BR // RC):
             rows = slice(chunk * RC, chunk * RC + RC)
             scores = jnp.dot(row_tall[rows, :], col, preferred_element_type=jnp.float32)

time: 154 us -> 155 us (level)
  no operation moved by 1% of the time
where the time goes in v11:
time: 155 us; the launch traced here: 154 us
  waiting for transfers between devices  57.4 us (37%)
  starting transfers between devices  36.5 us (24%)
  blocking collectives  32.4 us (21%)
  Pallas kernels  27.2 us (18%)
    all_to_all x2, blocking collectives, to_each(): return lax.all_to_all(copies, axes, 0, 0, tiled=True)  32.4 us
    ppermute x15, waiting for transfers between devices, over_z(): return lax.ppermute(value, 'z', [(at, (at + shift) % 4) for at in range(4)])  21.9 us
    ppermute x15, starting transfers between devices, over_z(): return lax.ppermute(value, 'z', [(at, (at + shift) % 4) for at in range(4)])  21.6 us
    pallas_call x2, Pallas kernels, swept(): pl.pallas_call(sweep_kernel, out_shape=(shape((4, 32, BR), jnp.bfloat16),...  17.9 us
    ppermute x2, waiting for transfers between devices, on_device(): from_pair = lax.ppermute(away_pair, 'yl', SWAP)  13.2 us
    all_to_all x2, starting transfers between devices, to_each(): return lax.all_to_all(copies, axes, 0, 0, tiled=True)  10.9 us
    all_to_all x2, waiting for transfers between devices, to_each(): return lax.all_to_all(copies, axes, 0, 0, tiled=True)  10 us
    pallas_call x1, Pallas kernels, first(): pl.pallas_call(first_kernel, out_shape=(shape((40, BR), jnp.bfloat16), sh...  4.64 us
  transfers between devices with their start and end apart: 27, of which 20 were waited for; matrix products, arithmetic and copies ran while one was open for 0% of the time, Pallas kernels for 1%

profile of v11, /device:TPU:0, one launch (start us, length us, event | category | flops | bytes accessed | tf_op | source)
XLA Modules:
  0.0 154.2 jit_solution(6521827796276438502)
XLA Ops:
  0.6 4.6 %first.1 = (bf16[40,1024]{1,0:T(8,128)(2,1)S(1)}, s32[8,128]{1,0:T(8,128)S(1)}, s32[1,2048]{1,0:T(1,128)S(1)}) custom-call(s32[1024,2048]{1,0:T(8,128)} %counts_ref.5, f32[32,1024]{1,0:T(8,128)} %emb_ref.4), custom_call_target="tpu_custom_call" | custom-call | flops 8388608 | bytes 8388608 | tf_op jit(solution)/shard_map/first/pallas_call | solution.py:75
  5.4 1.2 collective-permute-done.4.other_ref
  6.5 4.1 %collective-permute-start.7 = (s32[8,128]{1,0:T(8,128)S(1)}, s32[8,128]{1,0:T(8,128)S(1)}, u32[]{:S(2)}, u32[]{:S(2)}) collective-permute-start(s32[8,128]{1,0:T(8,128)S(1)} %shard_map.70.refs_0_), channel_id=1, source_target_pairs={{0,6},{2,0},{4,2},{6,4},{1,7},{3,1},{5,3},{7,5},{8,14},{10,8},{12,... | collective-permute-start | bytes 12296 | tf_op jit(solution)/shard_map/ppermute | solution.py:37
  10.7 1.3 collective-permute-start.5
  12.0 3.8 %collective-permute-done.6.refs_2_ = s32[8,128]{1,0:T(8,128)S(1)} collective-permute-done((s32[8,128]{1,0:T(8,128)S(1)}, s32[8,128]{1,0:T(8,128)S(1)}, u32[]{:S(2)}, u32[]{:S(2)}) %collective-permute-start.6) | collective-permute-done | bytes 4128 | tf_op jit(solution)/shard_map/ppermute | solution.py:37
  15.9 18.2 %all_to_all.20.mine_ref = bf16[8,304,128]{2,1,0:T(8,128)(2,1)S(1)} all-to-all(bf16[8,304,128]{2,1,0:T(8,128)(2,1)S(1)} %shard_map.71), channel_id=1, replica_groups=mesh['x'=4,'yh'=2,'c'=2,'z'=4,'yl'=2] {'x','yh'}, dimensions={0} | all-to-all | bytes 1245184 | tf_op jit(solution)/shard_map/all_to_all | solution.py:33
  34.0 0.7 collective-permute-start
  34.7 4.2 %collective-permute-done.other_ref = bf16[40,1024]{1,0:T(8,128)(2,1)S(1)} collective-permute-done((bf16[40,1024]{1,0:T(8,128)(2,1)S(1)}, bf16[40,1024]{1,0:T(8,128)(2,1)S(1)}, u32[]{:S(2)}, u32[]{:S(2)}) %collective-permute-start) | collective-permute-done | bytes 81952 | tf_op jit(solution)/shard_map/ppermute | solution.py:291
  38.9 1.0 collective-permute-start.3
  39.9 0.9 collective-permute-start.2
  40.8 1.3 collective-permute-start.1
  42.2 0.9 collective-permute-start.9
  43.1 2.6 %collective-permute-done.3.refs_3_ = bf16[72,1024]{1,0:T(8,128)(2,1)S(1)} collective-permute-done((bf16[72,1024]{1,0:T(8,128)(2,1)S(1)}, bf16[72,1024]{1,0:T(8,128)(2,1)S(1)}, u32[]{:S(2)}, u32[]{:S(2)}) %collective-permute-start.3) | collective-permute-done | bytes 147488 | tf_op jit(solution)/shard_map/ppermute | solution.py:37
  45.7 2.4 %collective-permute-done.2.refs_2_ = bf16[72,1024]{1,0:T(8,128)(2,1)S(1)} collective-permute-done((bf16[72,1024]{1,0:T(8,128)(2,1)S(1)}, bf16[72,1024]{1,0:T(8,128)(2,1)S(1)}, u32[]{:S(2)}, u32[]{:S(2)}) %collective-permute-start.2) | collective-permute-done | bytes 147488 | tf_op jit(solution)/shard_map/ppermute | solution.py:37
  48.1 1.6 %collective-permute-done.1.refs_1_ = bf16[72,1024]{1,0:T(8,128)(2,1)S(1)} collective-permute-done((bf16[72,1024]{1,0:T(8,128)(2,1)S(1)}, bf16[72,1024]{1,0:T(8,128)(2,1)S(1)}, u32[]{:S(2)}, u32[]{:S(2)}) %collective-permute-start.1) | collective-permute-done | bytes 147488 | tf_op jit(solution)/shard_map/ppermute | solution.py:37
  49.7 0.2 shard_map.69
  50.0 8.9 %sweep.2 = (bf16[4,32,1024]{2,1,0:T(8,128)(2,1)S(1)}, bf16[4,32,1024]{2,1,0:T(8,128)(2,1)S(1)}, bf16[8,16,2048]{2,1,0:T(8,128)(2,1)S(1)}, bf16[8,16,2048]{2,1,0:T(8,128)(2,1)S(1)}) custom-call(bf16[8,32,1024]{2,1,0:T(8,128)(2,1)S(1)} %get-tuple-element.35.row_flat, bf16[1024,256]{1,0:T(8,128)(2,1)S(1)} %get-tuple-element.36.row_tall, ...), custom_call_target="tpu_custom_call" | custom-call | flops 3221225472 | bytes 20971520 | tf_op jit(solution)/shard_map/sweep/pallas_call | solution.py:216
  59.0 1.9 %collective-permute-done.18.theirs_ref = bf16[8,16,2048]{2,1,0:T(8,128)(2,1)S(1)} collective-permute-done((bf16[8,16,2048]{2,1,0:T(8,128)(2,1)S(1)}, bf16[8,16,2048]{2,1,0:T(8,128)(2,1)S(1)}, u32[]{:S(2)}, u32[]{:S(2)}) %collective-permute-start.18) | collective-permute-done | bytes 524320 | tf_op jit(solution)/shard_map/ppermute | solution.py:306
  61.0 14.2 %all_to_all.21.came_ref = bf16[8,16,2048]{2,1,0:T(8,128)(2,1)S(1)} all-to-all(bf16[8,16,2048]{2,1,0:T(8,128)(2,1)S(1)} %shard_map.78), channel_id=1, replica_groups=mesh['x'=4,'yh'=2,'c'=2,'z'=4,'yl'=2] {'x','yh'}, dimensions={0} | all-to-all | bytes 1048576 | tf_op jit(solution)/shard_map/all_to_all | solution.py:33
  75.3 0.9 shard_map.79
  76.2 3.5 %all-to-all-start.2 = ((bf16[8,256,128]{2,1,0:T(8,128)(2,1)}), bf16[8,256,128]{2,1,0:T(8,128)(2,1)S(1)}, u32[]{:S(2)}, u32[]{:S(2)}) async-start(bf16[8,256,128]{2,1,0:T(8,128)(2,1)} %get-tuple-element.51), calls=%async_computation.2 | async-start | bytes 1048576 | tf_op jit(solution)/shard_map/all_to_all | solution.py:33
  79.7 0.7 collective-permute-start.10
  80.5 10.0 %all-to-all-done.2.mine_ref = bf16[8,256,128]{2,1,0:T(8,128)(2,1)S(1)} async-done(((bf16[8,256,128]{2,1,0:T(8,128)(2,1)}), bf16[8,256,128]{2,1,0:T(8,128)(2,1)S(1)}, u32[]{:S(2)}, u32[]{:S(2)}) %all-to-all-start.2) | async-done | bytes 524320 | tf_op jit(solution)/shard_map/all_to_all | solution.py:33
  90.5 0.9 collective-permute-done.10.came_ref
  91.5 1.3 collective-permute-start.11
  93.0 3.0 %collective-permute-start.13 = (bf16[32,1024]{1,0:T(8,128)(2,1)S(1)}, bf16[32,1024]{1,0:T(8,128)(2,1)S(1)}, u32[]{:S(2)}, u32[]{:S(2)}) collective-permute-start(bf16[32,1024]{1,0:T(8,128)(2,1)S(1)} %get-tuple-element.45), channel_id=1, source_target_pairs={{0,6},{2,0},{4,2},{6,4},{1,7},{3,1},{5,3},{7,5},{8,14},{10,8},{12,... | collective-permute-start | bytes 196616 | tf_op jit(solution)/shard_map/ppermute | solution.py:37
  96.0 1.3 collective-permute-done.11.first_ref
  97.4 0.9 collective-permute-done.12.second_ref
  98.4 1.3 collective-permute-start.14
  99.6 3.1 %collective-permute-done.14.other_ref = bf16[32,1024]{1,0:T(8,128)(2,1)S(1)} collective-permute-done((bf16[32,1024]{1,0:T(8,128)(2,1)S(1)}, bf16[32,1024]{1,0:T(8,128)(2,1)S(1)}, u32[]{:S(2)}, u32[]{:S(2)}) %collective-permute-start.14) | collective-permute-done | bytes 65568 | tf_op jit(solution)/shard_map/ppermute | solution.py:318
  102.7 3.3 %collective-permute-start.17 = (bf16[64,1024]{1,0:T(8,128)(2,1)S(1)}, bf16[64,1024]{1,0:T(8,128)(2,1)S(1)}, u32[]{:S(2)}, u32[]{:S(2)}) collective-permute-start(bf16[64,1024]{1,0:T(8,128)(2,1)S(1)} %shard_map.76.refs_0_), channel_id=1, source_target_pairs={{0,6},{2,0},{4,2},{6,4},{1,7},{3,1},{5,3},{7,5},{8,14},{10,8},{12,... | collective-permute-start | bytes 393224 | tf_op jit(solution)/shard_map/ppermute | solution.py:37
  106.0 0.9 collective-permute-start.15
  107.0 3.0 %collective-permute-done.17.refs_3_ = bf16[64,1024]{1,0:T(8,128)(2,1)S(1)} collective-permute-done((bf16[64,1024]{1,0:T(8,128)(2,1)S(1)}, bf16[64,1024]{1,0:T(8,128)(2,1)S(1)}, u32[]{:S(2)}, u32[]{:S(2)}) %collective-permute-start.17) | collective-permute-done | bytes 131104 | tf_op jit(solution)/shard_map/ppermute | solution.py:37
  109.9 2.6 %collective-permute-done.16.refs_2_ = bf16[64,1024]{1,0:T(8,128)(2,1)S(1)} collective-permute-done((bf16[64,1024]{1,0:T(8,128)(2,1)S(1)}, bf16[64,1024]{1,0:T(8,128)(2,1)S(1)}, u32[]{:S(2)}, u32[]{:S(2)}) %collective-permute-start.16) | collective-permute-done | bytes 131104 | tf_op jit(solution)/shard_map/ppermute | solution.py:37
  112.6 1.0 collective-permute-done.15.refs_1_
  113.6 0.2 shard_map.77
  113.9 9.0 %sweep.3 = (bf16[4,32,1024]{2,1,0:T(8,128)(2,1)S(1)}, bf16[4,32,1024]{2,1,0:T(8,128)(2,1)S(1)}, bf16[8,16,2048]{2,1,0:T(8,128)(2,1)S(1)}, bf16[8,16,2048]{2,1,0:T(8,128)(2,1)S(1)}) custom-call(bf16[8,32,1024]{2,1,0:T(8,128)(2,1)S(1)} %get-tuple-element.47.row_flat, bf16[1024,256]{1,0:T(8,128)(2,1)S(1)} %get-tuple-element.48.row_tall, ...), custom_call_target="tpu_custom_call" | custom-call | flops 3221225472 | bytes 20971520 | tf_op jit(solution)/shard_map/sweep/pallas_call | solution.py:216
  123.0 1.9 %collective-permute-done.24.theirs_ref = bf16[8,16,2048]{2,1,0:T(8,128)(2,1)S(1)} collective-permute-done((bf16[8,16,2048]{2,1,0:T(8,128)(2,1)S(1)}, bf16[8,16,2048]{2,1,0:T(8,128)(2,1)S(1)}, u32[]{:S(2)}, u32[]{:S(2)}) %collective-permute-start.24) | collective-permute-done | bytes 524320 | tf_op jit(solution)/shard_map/ppermute | solution.py:306
  124.9 0.9 shard_map.82
  125.8 7.4 %all-to-all-start.3 = ((bf16[8,16,2048]{2,1,0:T(8,128)(2,1)}), bf16[8,16,2048]{2,1,0:T(8,128)(2,1)S(1)}, u32[]{:S(2)}, u32[]{:S(2)}) async-start(bf16[8,16,2048]{2,1,0:T(8,128)(2,1)} %shard_map.82), calls=%async_computation.3 | async-start | bytes 1048576 | tf_op jit(solution)/shard_map/all_to_all | solution.py:33
  133.3 12.3 %collective-permute-done.20.came_ref = bf16[4,32,1024]{2,1,0:T(8,128)(2,1)S(1)} collective-permute-done((bf16[4,32,1024]{2,1,0:T(8,128)(2,1)S(1)}, bf16[4,32,1024]{2,1,0:T(8,128)(2,1)S(1)}, u32[]{:S(2)}, u32[]{:S(2)}) %collective-permute-start.20) | collective-permute-done | bytes 262176 | tf_op jit(solution)/shard_map/ppermute | solution.py:307
  145.7 1.0 collective-permute-start.21
  146.6 0.8 collective-permute-start.22
  147.5 2.4 %collective-permute-start.23 = (bf16[32,1024]{1,0:T(8,128)(2,1)S(1)}, bf16[32,1024]{1,0:T(8,128)(2,1)S(1)}, u32[]{:S(2)}, u32[]{:S(2)}) collective-permute-start(bf16[32,1024]{1,0:T(8,128)(2,1)S(1)} %get-tuple-element.57), channel_id=1, source_target_pairs={{0,6},{2,0},{4,2},{6,4},{1,7},{3,1},{5,3},{7,5},{8,14},{10,8},{12,... | collective-permute-start | bytes 196616 | tf_op jit(solution)/shard_map/ppermute | solution.py:37
  149.9 1.9 %collective-permute-done.21.first_ref = bf16[32,1024]{1,0:T(8,128)(2,1)S(1)} collective-permute-done((bf16[32,1024]{1,0:T(8,128)(2,1)S(1)}, bf16[32,1024]{1,0:T(8,128)(2,1)S(1)}, u32[]{:S(2)}, u32[]{:S(2)}) %collective-permute-start.21) | collective-permute-done | bytes 65568 | tf_op jit(solution)/shard_map/ppermute | solution.py:37
  151.8 0.7 collective-permute-done.22.second_ref
  152.5 0.8 shard_map.81
  153.2 1.0 shard_map.83
  (35 shorter events, 1.3 us)
Async XLA Ops:
  0.6 15.2 %copy-start.1 = (f32[16,2048]{1,0:T(8,128)S(1)}, f32[16,2048]{1,0:T(8,128)}, u32[]{:S(2)}) copy-start(f32[16,2048]{1,0:T(8,128)} %emb_ref.5) | copy-start | bytes 393220
  5.3 1.2 collective-permute-start.4
  6.5 5.5 %collective-permute-start.7 = (s32[8,128]{1,0:T(8,128)S(1)}, s32[8,128]{1,0:T(8,128)S(1)}, u32[]{:S(2)}, u32[]{:S(2)}) collective-permute-start(s32[8,128]{1,0:T(8,128)S(1)} %shard_map.70.refs_0_), channel_id=1, source_target_pairs={{0,6},{2,0},{4,2},{6,4},{1,7},{3,1},{5,3},{7,5},{8,14},{10,8},{12,... | collective-permute-start | bytes 12296 | tf_op jit(solution)/shard_map/ppermute | solution.py:37
  10.7 5.1 %collective-permute-start.6 = (s32[8,128]{1,0:T(8,128)S(1)}, s32[8,128]{1,0:T(8,128)S(1)}, u32[]{:S(2)}, u32[]{:S(2)}) collective-permute-start(s32[8,128]{1,0:T(8,128)S(1)} %shard_map.70.refs_0_), channel_id=1, source_target_pairs={{0,4},{2,6},{4,0},{6,2},{1,5},{3,7},{5,1},{7,3},{8,12},{10,14},{12... | collective-permute-start | bytes 12296 | tf_op jit(solution)/shard_map/ppermute | solution.py:37
  10.7 5.1 %collective-permute-start.5 = (s32[8,128]{1,0:T(8,128)S(1)}, s32[8,128]{1,0:T(8,128)S(1)}, u32[]{:S(2)}, u32[]{:S(2)}) collective-permute-start(s32[8,128]{1,0:T(8,128)S(1)} %shard_map.70.refs_0_), channel_id=1, source_target_pairs={{0,2},{2,4},{4,6},{6,0},{1,3},{3,5},{5,7},{7,1},{8,10},{10,12},{12... | collective-permute-start | bytes 12296 | tf_op jit(solution)/shard_map/ppermute | solution.py:37
  34.0 15.9 %collective-permute-start.8 = (bf16[8,304,128]{2,1,0:T(8,128)(2,1)S(1)}, bf16[8,304,128]{2,1,0:T(8,128)(2,1)S(1)}, u32[]{:S(2)}, u32[]{:S(2)}) collective-permute-start(bf16[8,304,128]{2,1,0:T(8,128)(2,1)S(1)} %all_to_all.20.mine_ref), channel_id=1, source_target_pairs={{0,8},{8,0},{1,9},{9,1},{2,10},{10,2},{3,11},{11,3},{4,12},{12,4},... | collective-permute-start | bytes 1867784 | tf_op jit(solution)/shard_map/ppermute | solution.py:300
  34.0 4.9 %collective-permute-start = (bf16[40,1024]{1,0:T(8,128)(2,1)S(1)}, bf16[40,1024]{1,0:T(8,128)(2,1)S(1)}, u32[]{:S(2)}, u32[]{:S(2)}) collective-permute-start(bf16[40,1024]{1,0:T(8,128)(2,1)S(1)} %get-tuple-element.34.own_ref), channel_id=1, source_target_pairs={{0,1},{1,0},{2,3},{3,2},{4,5},{5,4},{6,7},{7,6},{8,9},{9,8},{10,11... | collective-permute-start | bytes 245768 | tf_op jit(solution)/shard_map/ppermute | solution.py:291
  38.9 36.4 %copy-start.2 = (f32[16,2048]{1,0:T(8,128)S(1)}, f32[16,2048]{1,0:T(8,128)}, u32[]{:S(2)}) copy-start(f32[16,2048]{1,0:T(8,128)} %accum_ref.3) | copy-start | bytes 393220
  38.9 6.8 %collective-permute-start.3 = (bf16[72,1024]{1,0:T(8,128)(2,1)S(1)}, bf16[72,1024]{1,0:T(8,128)(2,1)S(1)}, u32[]{:S(2)}, u32[]{:S(2)}) collective-permute-start(bf16[72,1024]{1,0:T(8,128)(2,1)S(1)} %shard_map.68.refs_0_), channel_id=1, source_target_pairs={{0,6},{2,0},{4,2},{6,4},{1,7},{3,1},{5,3},{7,5},{8,14},{10,8},{12,... | collective-permute-start | bytes 442376 | tf_op jit(solution)/shard_map/ppermute | solution.py:37
  39.9 8.2 %collective-permute-start.2 = (bf16[72,1024]{1,0:T(8,128)(2,1)S(1)}, bf16[72,1024]{1,0:T(8,128)(2,1)S(1)}, u32[]{:S(2)}, u32[]{:S(2)}) collective-permute-start(bf16[72,1024]{1,0:T(8,128)(2,1)S(1)} %shard_map.68.refs_0_), channel_id=1, source_target_pairs={{0,4},{2,6},{4,0},{6,2},{1,5},{3,7},{5,1},{7,3},{8,12},{10,14},{12... | collective-permute-start | bytes 442376 | tf_op jit(solution)/shard_map/ppermute | solution.py:37
  40.8 8.8 %collective-permute-start.1 = (bf16[72,1024]{1,0:T(8,128)(2,1)S(1)}, bf16[72,1024]{1,0:T(8,128)(2,1)S(1)}, u32[]{:S(2)}, u32[]{:S(2)}) collective-permute-start(bf16[72,1024]{1,0:T(8,128)(2,1)S(1)} %shard_map.68.refs_0_), channel_id=1, source_target_pairs={{0,2},{2,4},{4,6},{6,0},{1,3},{3,5},{5,7},{7,1},{8,10},{10,12},{12... | collective-permute-start | bytes 442376 | tf_op jit(solution)/shard_map/ppermute | solution.py:37
  42.2 7.7 %collective-permute-start.9 = (f32[8,128]{1,0:T(8,128)S(1)}, f32[8,128]{1,0:T(8,128)S(1)}, u32[]{:S(2)}, u32[]{:S(2)}) collective-permute-start(f32[8,128]{1,0:T(8,128)S(1)} %shard_map.72.total_ref), channel_id=1, source_target_pairs={{0,1},{1,0},{2,3},{3,2},{4,5},{5,4},{6,7},{7,6},{8,9},{9,8},{10,11... | collective-permute-start | bytes 12296 | tf_op jit(solution)/shard_map/ppermute | solution.py:302
  50.0 48.3 %copy-start = (f32[32,1024]{1,0:T(8,128)S(1)}, f32[32,1024]{1,0:T(8,128)}, u32[]{:S(2)}) copy-start(f32[32,1024]{1,0:T(8,128)} %emb_ref.4) | copy-start | bytes 393220
  50.0 48.3 %copy-start.3 = (f32[32,1024]{1,0:T(8,128)S(1)}, f32[32,1024]{1,0:T(8,128)}, u32[]{:S(2)}) copy-start(f32[32,1024]{1,0:T(8,128)} %accum_ref.2) | copy-start | bytes 393220
  58.9 2.0 %collective-permute-start.18 = (bf16[8,16,2048]{2,1,0:T(8,128)(2,1)S(1)}, bf16[8,16,2048]{2,1,0:T(8,128)(2,1)S(1)}, u32[]{:S(2)}, u32[]{:S(2)}) collective-permute-start(bf16[8,16,2048]{2,1,0:T(8,128)(2,1)S(1)} %get-tuple-element.50), channel_id=1, source_target_pairs={{0,8},{8,0},{1,9},{9,1},{2,10},{10,2},{3,11},{11,3},{4,12},{12,4},... | collective-permute-start | bytes 1572872 | tf_op jit(solution)/shard_map/ppermute | solution.py:306
  76.2 14.3 %all-to-all-start.2 = ((bf16[8,256,128]{2,1,0:T(8,128)(2,1)}), bf16[8,256,128]{2,1,0:T(8,128)(2,1)S(1)}, u32[]{:S(2)}, u32[]{:S(2)}) async-start(bf16[8,256,128]{2,1,0:T(8,128)(2,1)} %get-tuple-element.51), calls=%async_computation.2 | async-start | bytes 1048576 | tf_op jit(solution)/shard_map/all_to_all | solution.py:33
  79.7 11.7 %collective-permute-start.10 = (bf16[4,32,1024]{2,1,0:T(8,128)(2,1)S(1)}, bf16[4,32,1024]{2,1,0:T(8,128)(2,1)S(1)}, u32[]{:S(2)}, u32[]{:S(2)}) collective-permute-start(bf16[4,32,1024]{2,1,0:T(8,128)(2,1)S(1)} %get-tuple-element.41), channel_id=1, source_target_pairs={{0,1},{1,0},{2,3},{3,2},{4,5},{5,4},{6,7},{7,6},{8,9},{9,8},{10,11... | collective-permute-start | bytes 786440 | tf_op jit(solution)/shard_map/ppermute | solution.py:307
  90.5 23.4 %collective-permute-start.19 = (bf16[8,256,128]{2,1,0:T(8,128)(2,1)S(1)}, bf16[8,256,128]{2,1,0:T(8,128)(2,1)S(1)}, u32[]{:S(2)}, u32[]{:S(2)}) collective-permute-start(bf16[8,256,128]{2,1,0:T(8,128)(2,1)S(1)} %all-to-all-done.2.mine_ref), channel_id=1, source_target_pairs={{0,8},{8,0},{1,9},{9,1},{2,10},{10,2},{3,11},{11,3},{4,12},{12,4},... | collective-permute-start | bytes 1572872 | tf_op jit(solution)/shard_map/ppermute | solution.py:324
  91.5 5.9 %collective-permute-start.11 = (bf16[32,1024]{1,0:T(8,128)(2,1)S(1)}, bf16[32,1024]{1,0:T(8,128)(2,1)S(1)}, u32[]{:S(2)}, u32[]{:S(2)}) collective-permute-start(bf16[32,1024]{1,0:T(8,128)(2,1)S(1)} %get-tuple-element.43), channel_id=1, source_target_pairs={{0,4},{2,6},{4,0},{6,2},{1,5},{3,7},{5,1},{7,3},{8,12},{10,14},{12... | collective-permute-start | bytes 196616 | tf_op jit(solution)/shard_map/ppermute | solution.py:37
  92.8 5.5 %collective-permute-start.12 = (bf16[32,1024]{1,0:T(8,128)(2,1)S(1)}, bf16[32,1024]{1,0:T(8,128)(2,1)S(1)}, u32[]{:S(2)}, u32[]{:S(2)}) collective-permute-start(bf16[32,1024]{1,0:T(8,128)(2,1)S(1)} %get-tuple-element.44), channel_id=1, source_target_pairs={{0,2},{2,4},{4,6},{6,0},{1,3},{3,5},{5,7},{7,1},{8,10},{10,12},{12... | collective-permute-start | bytes 196616 | tf_op jit(solution)/shard_map/ppermute | solution.py:37
  93.0 5.3 %collective-permute-start.13 = (bf16[32,1024]{1,0:T(8,128)(2,1)S(1)}, bf16[32,1024]{1,0:T(8,128)(2,1)S(1)}, u32[]{:S(2)}, u32[]{:S(2)}) collective-permute-start(bf16[32,1024]{1,0:T(8,128)(2,1)S(1)} %get-tuple-element.45), channel_id=1, source_target_pairs={{0,6},{2,0},{4,2},{6,4},{1,7},{3,1},{5,3},{7,5},{8,14},{10,8},{12,... | collective-permute-start | bytes 196616 | tf_op jit(solution)/shard_map/ppermute | solution.py:37
  98.4 4.3 %collective-permute-start.14 = (bf16[32,1024]{1,0:T(8,128)(2,1)S(1)}, bf16[32,1024]{1,0:T(8,128)(2,1)S(1)}, u32[]{:S(2)}, u32[]{:S(2)}) collective-permute-start(bf16[32,1024]{1,0:T(8,128)(2,1)S(1)} %get-tuple-element.46.own_ref), channel_id=1, source_target_pairs={{0,1},{1,0},{2,3},{3,2},{4,5},{5,4},{6,7},{7,6},{8,9},{9,8},{10,11... | collective-permute-start | bytes 196616 | tf_op jit(solution)/shard_map/ppermute | solution.py:318
  102.7 7.2 %collective-permute-start.17 = (bf16[64,1024]{1,0:T(8,128)(2,1)S(1)}, bf16[64,1024]{1,0:T(8,128)(2,1)S(1)}, u32[]{:S(2)}, u32[]{:S(2)}) collective-permute-start(bf16[64,1024]{1,0:T(8,128)(2,1)S(1)} %shard_map.76.refs_0_), channel_id=1, source_target_pairs={{0,6},{2,0},{4,2},{6,4},{1,7},{3,1},{5,3},{7,5},{8,14},{10,8},{12,... | collective-permute-start | bytes 393224 | tf_op jit(solution)/shard_map/ppermute | solution.py:37
  106.0 6.6 %collective-permute-start.16 = (bf16[64,1024]{1,0:T(8,128)(2,1)S(1)}, bf16[64,1024]{1,0:T(8,128)(2,1)S(1)}, u32[]{:S(2)}, u32[]{:S(2)}) collective-permute-start(bf16[64,1024]{1,0:T(8,128)(2,1)S(1)} %shard_map.76.refs_0_), channel_id=1, source_target_pairs={{0,4},{2,6},{4,0},{6,2},{1,5},{3,7},{5,1},{7,3},{8,12},{10,14},{12... | collective-permute-start | bytes 393224 | tf_op jit(solution)/shard_map/ppermute | solution.py:37
  106.0 7.6 %collective-permute-start.15 = (bf16[64,1024]{1,0:T(8,128)(2,1)S(1)}, bf16[64,1024]{1,0:T(8,128)(2,1)S(1)}, u32[]{:S(2)}, u32[]{:S(2)}) collective-permute-start(bf16[64,1024]{1,0:T(8,128)(2,1)S(1)} %shard_map.76.refs_0_), channel_id=1, source_target_pairs={{0,2},{2,4},{4,6},{6,0},{1,3},{3,5},{5,7},{7,1},{8,10},{10,12},{12... | collective-permute-start | bytes 393224 | tf_op jit(solution)/shard_map/ppermute | solution.py:37
  122.9 2.0 %collective-permute-start.24 = (bf16[8,16,2048]{2,1,0:T(8,128)(2,1)S(1)}, bf16[8,16,2048]{2,1,0:T(8,128)(2,1)S(1)}, u32[]{:S(2)}, u32[]{:S(2)}) collective-permute-start(bf16[8,16,2048]{2,1,0:T(8,128)(2,1)S(1)} %get-tuple-element.62), channel_id=1, source_target_pairs={{0,8},{8,0},{1,9},{9,1},{2,10},{10,2},{3,11},{11,3},{4,12},{12,4},... | collective-permute-start | bytes 1572872 | tf_op jit(solution)/shard_map/ppermute | solution.py:306
  125.8 27.5 %all-to-all-start.3 = ((bf16[8,16,2048]{2,1,0:T(8,128)(2,1)}), bf16[8,16,2048]{2,1,0:T(8,128)(2,1)S(1)}, u32[]{:S(2)}, u32[]{:S(2)}) async-start(bf16[8,16,2048]{2,1,0:T(8,128)(2,1)} %shard_map.82), calls=%async_computation.3 | async-start | bytes 1048576 | tf_op jit(solution)/shard_map/all_to_all | solution.py:33
  133.2 12.4 %collective-permute-start.20 = (bf16[4,32,1024]{2,1,0:T(8,128)(2,1)S(1)}, bf16[4,32,1024]{2,1,0:T(8,128)(2,1)S(1)}, u32[]{:S(2)}, u32[]{:S(2)}) collective-permute-start(bf16[4,32,1024]{2,1,0:T(8,128)(2,1)S(1)} %get-tuple-element.53), channel_id=1, source_target_pairs={{0,1},{1,0},{2,3},{3,2},{4,5},{5,4},{6,7},{7,6},{8,9},{9,8},{10,11... | collective-permute-start | bytes 786440 | tf_op jit(solution)/shard_map/ppermute | solution.py:307
  145.7 6.1 %collective-permute-start.21 = (bf16[32,1024]{1,0:T(8,128)(2,1)S(1)}, bf16[32,1024]{1,0:T(8,128)(2,1)S(1)}, u32[]{:S(2)}, u32[]{:S(2)}) collective-permute-start(bf16[32,1024]{1,0:T(8,128)(2,1)S(1)} %get-tuple-element.55), channel_id=1, source_target_pairs={{0,4},{2,6},{4,0},{6,2},{1,5},{3,7},{5,1},{7,3},{8,12},{10,14},{12... | collective-permute-start | bytes 196616 | tf_op jit(solution)/shard_map/ppermute | solution.py:37
  146.6 5.8 %collective-permute-start.22 = (bf16[32,1024]{1,0:T(8,128)(2,1)S(1)}, bf16[32,1024]{1,0:T(8,128)(2,1)S(1)}, u32[]{:S(2)}, u32[]{:S(2)}) collective-permute-start(bf16[32,1024]{1,0:T(8,128)(2,1)S(1)} %get-tuple-element.56), channel_id=1, source_target_pairs={{0,2},{2,4},{4,6},{6,0},{1,3},{3,5},{5,7},{7,1},{8,10},{10,12},{12... | collective-permute-start | bytes 196616 | tf_op jit(solution)/shard_map/ppermute | solution.py:37
  147.5 5.0 %collective-permute-start.23 = (bf16[32,1024]{1,0:T(8,128)(2,1)S(1)}, bf16[32,1024]{1,0:T(8,128)(2,1)S(1)}, u32[]{:S(2)}, u32[]{:S(2)}) collective-permute-start(bf16[32,1024]{1,0:T(8,128)(2,1)S(1)} %get-tuple-element.57), channel_id=1, source_target_pairs={{0,6},{2,0},{4,2},{6,4},{1,7},{3,1},{5,3},{7,5},{8,14},{10,8},{12,... | collective-permute-start | bytes 196616 | tf_op jit(solution)/shard_map/ppermute | solution.py:37

commit v12 on v10

--- a/solution.py
+++ b/solution.py
@@ -249,26 +249,28 @@
     return emb_ref[...] - 0.05 * grad / jnp.sqrt(accum), accum
 
 
-def row_kernel(keep_ref, first_ref, second_ref, third_ref, emb_ref, accum_ref, new_emb_ref, new_accum_ref, half_ref):
+def row_kernel(keep_ref, first_ref, second_ref, third_ref, emb_ref, accum_ref, new_emb_ref, *more_refs):
     grad = keep_ref[...]
     for ref in (first_ref, second_ref, third_ref):
         grad += ref[...].astype(jnp.float32)
     emb, accum = moved(emb_ref, accum_ref, grad)
     new_emb_ref[...] = emb
-    new_accum_ref[...] = accum
-    half_ref[...] = emb.astype(jnp.bfloat16)
-
-
-def col_kernel(came_ref, emb_ref, accum_ref, new_emb_ref, new_accum_ref, half_ref):
+    if more_refs:
+        more_refs[0][...] = accum
+        more_refs[1][...] = emb.astype(jnp.bfloat16)
+
+
+def col_kernel(came_ref, emb_ref, accum_ref, new_emb_ref, *more_refs):
     grad = came_ref[0].astype(jnp.float32)
     for at in range(1, 8):
         grad += came_ref[at].astype(jnp.float32)
     emb, accum = moved(emb_ref, accum_ref, grad)
     new_emb_ref[...] = emb
-    new_accum_ref[...] = accum
-    half = packed(emb).astype(jnp.bfloat16)
-    for at in range(8):
-        half_ref[at] = half
+    if more_refs:
+        more_refs[0][...] = accum
+        half = packed(emb).astype(jnp.bfloat16)
+        for at in range(8):
+            more_refs[1][at] = half
 
 
 def small(kernel, outs):
@@ -305,11 +307,16 @@
         outs = (shape((32, BR), jnp.float32),) + (shape((32, BR), jnp.bfloat16),) * 3
         keep, *parts = small(pairs_kernel, outs)(own, from_pair)
         parts = [over_z(parts[shift - 1], shift) for shift in (2, 1, 3)]
+        last = sweep == 1
         outs = (shape((32, BR), jnp.float32),) * 2 + (shape((32, BR), jnp.bfloat16),)
-        row_emb, row_accum, half = small(row_kernel, outs)(keep, *parts, row_emb, row_accum)
+        step = small(row_kernel, outs[:1] if last else outs)
+        row_emb, *row_more = step(keep, *parts, row_emb, row_accum)
         outs = (shape((16, COLS), jnp.float32),) * 2 + (shape((8, 256, 128), jnp.bfloat16),)
-        col_emb, col_accum, copies = small(col_kernel, outs)(came, col_emb, col_accum)
-        if sweep == 0:
+        step = small(col_kernel, outs[:1] if last else outs)
+        col_emb, *col_more = step(came, col_emb, col_accum)
+        if not last:
+            row_accum, half = row_more
+            col_accum, copies = col_more
             pair = lax.ppermute(half, "yl", SWAP)
             pair = small(joined_kernel, shape((64, BR), jnp.bfloat16))(half, pair)
             mine = to_each(copies, CHIPS)

time: 154 us -> 154 us (level)
  no operation moved by 1% of the time
where the time goes in v12:
time: 154 us; the launch traced here: 153 us
  waiting for transfers between devices  57.4 us (37%)
  starting transfers between devices  36.5 us (24%)
  blocking collectives  32.4 us (21%)
  Pallas kernels  26.1 us (17%)
    all_to_all x2, blocking collectives, to_each(): return lax.all_to_all(copies, axes, 0, 0, tiled=True)  32.4 us
    ppermute x15, waiting for transfers between devices, over_z(): return lax.ppermute(value, 'z', [(at, (at + shift) % 4) for at in range(4)])  21.9 us
    ppermute x15, starting transfers between devices, over_z(): return lax.ppermute(value, 'z', [(at, (at + shift) % 4) for at in range(4)])  21.6 us
    pallas_call x2, Pallas kernels, swept(): pl.pallas_call(sweep_kernel, out_shape=(shape((4, 32, BR), jnp.bfloat16),...  17.9 us
    ppermute x2, waiting for transfers between devices, on_device(): from_pair = lax.ppermute(away_pair, 'yl', SWAP)  13.2 us
    all_to_all x2, starting transfers between devices, to_each(): return lax.all_to_all(copies, axes, 0, 0, tiled=True)  10.9 us
    all_to_all x2, waiting for transfers between devices, to_each(): return lax.all_to_all(copies, axes, 0, 0, tiled=True)  10 us
    ppermute x1, waiting for transfers between devices, on_device(): other = lax.ppermute(parcel, 'yl', SWAP)  4.18 us
  transfers between devices with their start and end apart: 27, of which 20 were waited for; matrix products, arithmetic and copies ran while one was open for 0% of the time, Pallas kernels for 1%

profile of v12, /device:TPU:0, one launch (start us, length us, event | category | flops | bytes accessed | tf_op | source)
XLA Modules:
  0.0 153.2 jit_solution(18343533072208835653)
XLA Ops:
  0.6 3.8 %first.1 = (bf16[40,1024]{1,0:T(8,128)(2,1)S(1)}, s32[8,128]{1,0:T(8,128)S(1)}, s32[1,2048]{1,0:T(1,128)S(1)}) custom-call(s32[1024,2048]{1,0:T(8,128)} %counts_ref.5, f32[32,1024]{1,0:T(8,128)} %emb_ref.4), custom_call_target="tpu_custom_call" | custom-call | flops 8388608 | bytes 8388608 | tf_op jit(solution)/shard_map/first/pallas_call | solution.py:73
  4.5 1.2 collective-permute-done.4.other_ref
  5.7 4.1 %collective-permute-start.7 = (s32[8,128]{1,0:T(8,128)S(1)}, s32[8,128]{1,0:T(8,128)S(1)}, u32[]{:S(2)}, u32[]{:S(2)}) collective-permute-start(s32[8,128]{1,0:T(8,128)S(1)} %shard_map.70.refs_0_), channel_id=1, source_target_pairs={{0,6},{2,0},{4,2},{6,4},{1,7},{3,1},{5,3},{7,5},{8,14},{10,8},{12,... | collective-permute-start | bytes 12296 | tf_op jit(solution)/shard_map/ppermute | solution.py:37
  9.8 1.3 collective-permute-start.5
  11.2 3.8 %collective-permute-done.6.refs_2_ = s32[8,128]{1,0:T(8,128)S(1)} collective-permute-done((s32[8,128]{1,0:T(8,128)S(1)}, s32[8,128]{1,0:T(8,128)S(1)}, u32[]{:S(2)}, u32[]{:S(2)}) %collective-permute-start.6) | collective-permute-done | bytes 4128 | tf_op jit(solution)/shard_map/ppermute | solution.py:37
  15.0 18.2 %all_to_all.20.mine_ref = bf16[8,304,128]{2,1,0:T(8,128)(2,1)S(1)} all-to-all(bf16[8,304,128]{2,1,0:T(8,128)(2,1)S(1)} %shard_map.71), channel_id=1, replica_groups=mesh['x'=4,'yh'=2,'c'=2,'z'=4,'yl'=2] {'x','yh'}, dimensions={0} | all-to-all | bytes 1245184 | tf_op jit(solution)/shard_map/all_to_all | solution.py:33
  33.2 0.7 collective-permute-start
  33.8 4.2 %collective-permute-done.other_ref = bf16[40,1024]{1,0:T(8,128)(2,1)S(1)} collective-permute-done((bf16[40,1024]{1,0:T(8,128)(2,1)S(1)}, bf16[40,1024]{1,0:T(8,128)(2,1)S(1)}, u32[]{:S(2)}, u32[]{:S(2)}) %collective-permute-start) | collective-permute-done | bytes 81952 | tf_op jit(solution)/shard_map/ppermute | solution.py:288
  38.0 1.0 collective-permute-start.3
  39.0 0.9 collective-permute-start.2
  40.0 1.3 collective-permute-start.1
  41.4 0.9 collective-permute-start.9
  42.2 2.6 %collective-permute-done.3.refs_3_ = bf16[72,1024]{1,0:T(8,128)(2,1)S(1)} collective-permute-done((bf16[72,1024]{1,0:T(8,128)(2,1)S(1)}, bf16[72,1024]{1,0:T(8,128)(2,1)S(1)}, u32[]{:S(2)}, u32[]{:S(2)}) %collective-permute-start.3) | collective-permute-done | bytes 147488 | tf_op jit(solution)/shard_map/ppermute | solution.py:37
  44.8 2.4 %collective-permute-done.2.refs_2_ = bf16[72,1024]{1,0:T(8,128)(2,1)S(1)} collective-permute-done((bf16[72,1024]{1,0:T(8,128)(2,1)S(1)}, bf16[72,1024]{1,0:T(8,128)(2,1)S(1)}, u32[]{:S(2)}, u32[]{:S(2)}) %collective-permute-start.2) | collective-permute-done | bytes 147488 | tf_op jit(solution)/shard_map/ppermute | solution.py:37
  47.2 1.6 %collective-permute-done.1.refs_1_ = bf16[72,1024]{1,0:T(8,128)(2,1)S(1)} collective-permute-done((bf16[72,1024]{1,0:T(8,128)(2,1)S(1)}, bf16[72,1024]{1,0:T(8,128)(2,1)S(1)}, u32[]{:S(2)}, u32[]{:S(2)}) %collective-permute-start.1) | collective-permute-done | bytes 147488 | tf_op jit(solution)/shard_map/ppermute | solution.py:37
  48.8 0.2 shard_map.69
  49.1 8.9 %sweep.2 = (bf16[4,32,1024]{2,1,0:T(8,128)(2,1)S(1)}, bf16[4,32,1024]{2,1,0:T(8,128)(2,1)S(1)}, bf16[8,16,2048]{2,1,0:T(8,128)(2,1)S(1)}, bf16[8,16,2048]{2,1,0:T(8,128)(2,1)S(1)}) custom-call(bf16[8,32,1024]{2,1,0:T(8,128)(2,1)S(1)} %get-tuple-element.33.row_flat, bf16[1024,256]{1,0:T(8,128)(2,1)S(1)} %get-tuple-element.34.row_tall, ...), custom_call_target="tpu_custom_call" | custom-call | flops 3221225472 | bytes 20971520 | tf_op jit(solution)/shard_map/sweep/pallas_call | solution.py:211
  58.1 1.9 %collective-permute-done.18.theirs_ref = bf16[8,16,2048]{2,1,0:T(8,128)(2,1)S(1)} collective-permute-done((bf16[8,16,2048]{2,1,0:T(8,128)(2,1)S(1)}, bf16[8,16,2048]{2,1,0:T(8,128)(2,1)S(1)}, u32[]{:S(2)}, u32[]{:S(2)}) %collective-permute-start.18) | collective-permute-done | bytes 524320 | tf_op jit(solution)/shard_map/ppermute | solution.py:303
  60.2 14.2 %all_to_all.21.came_ref = bf16[8,16,2048]{2,1,0:T(8,128)(2,1)S(1)} all-to-all(bf16[8,16,2048]{2,1,0:T(8,128)(2,1)S(1)} %shard_map.78), channel_id=1, replica_groups=mesh['x'=4,'yh'=2,'c'=2,'z'=4,'yl'=2] {'x','yh'}, dimensions={0} | all-to-all | bytes 1048576 | tf_op jit(solution)/shard_map/all_to_all | solution.py:33
  74.4 0.9 shard_map.79
  75.3 3.5 %all-to-all-start.2 = ((bf16[8,256,128]{2,1,0:T(8,128)(2,1)}), bf16[8,256,128]{2,1,0:T(8,128)(2,1)S(1)}, u32[]{:S(2)}, u32[]{:S(2)}) async-start(bf16[8,256,128]{2,1,0:T(8,128)(2,1)} %get-tuple-element.49), calls=%async_computation.2 | async-start | bytes 1048576 | tf_op jit(solution)/shard_map/all_to_all | solution.py:33
  78.8 0.8 collective-permute-start.10
  79.6 10.0 %all-to-all-done.2.mine_ref = bf16[8,256,128]{2,1,0:T(8,128)(2,1)S(1)} async-done(((bf16[8,256,128]{2,1,0:T(8,128)(2,1)}), bf16[8,256,128]{2,1,0:T(8,128)(2,1)S(1)}, u32[]{:S(2)}, u32[]{:S(2)}) %all-to-all-start.2) | async-done | bytes 524320 | tf_op jit(solution)/shard_map/all_to_all | solution.py:33
  89.6 0.9 collective-permute-done.10.came_ref
  90.6 1.3 collective-permute-start.11
  92.1 3.0 %collective-permute-start.13 = (bf16[32,1024]{1,0:T(8,128)(2,1)S(1)}, bf16[32,1024]{1,0:T(8,128)(2,1)S(1)}, u32[]{:S(2)}, u32[]{:S(2)}) collective-permute-start(bf16[32,1024]{1,0:T(8,128)(2,1)S(1)} %get-tuple-element.43), channel_id=1, source_target_pairs={{0,6},{2,0},{4,2},{6,4},{1,7},{3,1},{5,3},{7,5},{8,14},{10,8},{12,... | collective-permute-start | bytes 196616 | tf_op jit(solution)/shard_map/ppermute | solution.py:37
  95.1 1.3 collective-permute-done.11.first_ref
  96.5 0.9 collective-permute-done.12.second_ref
  97.5 1.3 collective-permute-start.14
  98.8 3.1 %collective-permute-done.14.other_ref = bf16[32,1024]{1,0:T(8,128)(2,1)S(1)} collective-permute-done((bf16[32,1024]{1,0:T(8,128)(2,1)S(1)}, bf16[32,1024]{1,0:T(8,128)(2,1)S(1)}, u32[]{:S(2)}, u32[]{:S(2)}) %collective-permute-start.14) | collective-permute-done | bytes 65568 | tf_op jit(solution)/shard_map/ppermute | solution.py:320
  101.9 3.3 %collective-permute-start.17 = (bf16[64,1024]{1,0:T(8,128)(2,1)S(1)}, bf16[64,1024]{1,0:T(8,128)(2,1)S(1)}, u32[]{:S(2)}, u32[]{:S(2)}) collective-permute-start(bf16[64,1024]{1,0:T(8,128)(2,1)S(1)} %shard_map.76.refs_0_), channel_id=1, source_target_pairs={{0,6},{2,0},{4,2},{6,4},{1,7},{3,1},{5,3},{7,5},{8,14},{10,8},{12,... | collective-permute-start | bytes 393224 | tf_op jit(solution)/shard_map/ppermute | solution.py:37
  105.1 0.9 collective-permute-start.15
  106.1 3.0 %collective-permute-done.17.refs_3_ = bf16[64,1024]{1,0:T(8,128)(2,1)S(1)} collective-permute-done((bf16[64,1024]{1,0:T(8,128)(2,1)S(1)}, bf16[64,1024]{1,0:T(8,128)(2,1)S(1)}, u32[]{:S(2)}, u32[]{:S(2)}) %collective-permute-start.17) | collective-permute-done | bytes 131104 | tf_op jit(solution)/shard_map/ppermute | solution.py:37
  109.1 2.6 %collective-permute-done.16.refs_2_ = bf16[64,1024]{1,0:T(8,128)(2,1)S(1)} collective-permute-done((bf16[64,1024]{1,0:T(8,128)(2,1)S(1)}, bf16[64,1024]{1,0:T(8,128)(2,1)S(1)}, u32[]{:S(2)}, u32[]{:S(2)}) %collective-permute-start.16) | collective-permute-done | bytes 131104 | tf_op jit(solution)/shard_map/ppermute | solution.py:37
  111.7 1.0 collective-permute-done.15.refs_1_
  112.7 0.2 shard_map.77
  113.0 9.0 %sweep.3 = (bf16[4,32,1024]{2,1,0:T(8,128)(2,1)S(1)}, bf16[4,32,1024]{2,1,0:T(8,128)(2,1)S(1)}, bf16[8,16,2048]{2,1,0:T(8,128)(2,1)S(1)}, bf16[8,16,2048]{2,1,0:T(8,128)(2,1)S(1)}) custom-call(bf16[8,32,1024]{2,1,0:T(8,128)(2,1)S(1)} %get-tuple-element.45.row_flat, bf16[1024,256]{1,0:T(8,128)(2,1)S(1)} %get-tuple-element.46.row_tall, ...), custom_call_target="tpu_custom_call" | custom-call | flops 3221225472 | bytes 20971520 | tf_op jit(solution)/shard_map/sweep/pallas_call | solution.py:211
  122.1 1.9 %collective-permute-done.24.theirs_ref = bf16[8,16,2048]{2,1,0:T(8,128)(2,1)S(1)} collective-permute-done((bf16[8,16,2048]{2,1,0:T(8,128)(2,1)S(1)}, bf16[8,16,2048]{2,1,0:T(8,128)(2,1)S(1)}, u32[]{:S(2)}, u32[]{:S(2)}) %collective-permute-start.24) | collective-permute-done | bytes 524320 | tf_op jit(solution)/shard_map/ppermute | solution.py:303
  124.0 0.9 shard_map.82
  124.9 7.4 %all-to-all-start.3 = ((bf16[8,16,2048]{2,1,0:T(8,128)(2,1)}), bf16[8,16,2048]{2,1,0:T(8,128)(2,1)S(1)}, u32[]{:S(2)}, u32[]{:S(2)}) async-start(bf16[8,16,2048]{2,1,0:T(8,128)(2,1)} %shard_map.82), calls=%async_computation.3 | async-start | bytes 1048576 | tf_op jit(solution)/shard_map/all_to_all | solution.py:33
  132.4 12.3 %collective-permute-done.20.came_ref = bf16[4,32,1024]{2,1,0:T(8,128)(2,1)S(1)} collective-permute-done((bf16[4,32,1024]{2,1,0:T(8,128)(2,1)S(1)}, bf16[4,32,1024]{2,1,0:T(8,128)(2,1)S(1)}, u32[]{:S(2)}, u32[]{:S(2)}) %collective-permute-start.20) | collective-permute-done | bytes 262176 | tf_op jit(solution)/shard_map/ppermute | solution.py:304
  144.8 1.0 collective-permute-start.21
  145.8 0.8 collective-permute-start.22
  146.6 2.4 %collective-permute-start.23 = (bf16[32,1024]{1,0:T(8,128)(2,1)S(1)}, bf16[32,1024]{1,0:T(8,128)(2,1)S(1)}, u32[]{:S(2)}, u32[]{:S(2)}) collective-permute-start(bf16[32,1024]{1,0:T(8,128)(2,1)S(1)} %get-tuple-element.55), channel_id=1, source_target_pairs={{0,6},{2,0},{4,2},{6,4},{1,7},{3,1},{5,3},{7,5},{8,14},{10,8},{12,... | collective-permute-start | bytes 196616 | tf_op jit(solution)/shard_map/ppermute | solution.py:37
  149.0 1.9 %collective-permute-done.21.first_ref = bf16[32,1024]{1,0:T(8,128)(2,1)S(1)} collective-permute-done((bf16[32,1024]{1,0:T(8,128)(2,1)S(1)}, bf16[32,1024]{1,0:T(8,128)(2,1)S(1)}, u32[]{:S(2)}, u32[]{:S(2)}) %collective-permute-start.21) | collective-permute-done | bytes 65568 | tf_op jit(solution)/shard_map/ppermute | solution.py:37
  150.9 0.7 collective-permute-done.22.second_ref
  151.6 0.7 shard_map.81
  152.4 0.8 shard_map.83
  (35 shorter events, 1.3 us)
Async XLA Ops:
  0.6 14.3 %copy-start.1 = (f32[16,2048]{1,0:T(8,128)S(1)}, f32[16,2048]{1,0:T(8,128)}, u32[]{:S(2)}) copy-start(f32[16,2048]{1,0:T(8,128)} %emb_ref.5) | copy-start | bytes 393220
  4.4 1.2 collective-permute-start.4
  5.7 5.5 %collective-permute-start.7 = (s32[8,128]{1,0:T(8,128)S(1)}, s32[8,128]{1,0:T(8,128)S(1)}, u32[]{:S(2)}, u32[]{:S(2)}) collective-permute-start(s32[8,128]{1,0:T(8,128)S(1)} %shard_map.70.refs_0_), channel_id=1, source_target_pairs={{0,6},{2,0},{4,2},{6,4},{1,7},{3,1},{5,3},{7,5},{8,14},{10,8},{12,... | collective-permute-start | bytes 12296 | tf_op jit(solution)/shard_map/ppermute | solution.py:37
  9.8 5.1 %collective-permute-start.6 = (s32[8,128]{1,0:T(8,128)S(1)}, s32[8,128]{1,0:T(8,128)S(1)}, u32[]{:S(2)}, u32[]{:S(2)}) collective-permute-start(s32[8,128]{1,0:T(8,128)S(1)} %shard_map.70.refs_0_), channel_id=1, source_target_pairs={{0,4},{2,6},{4,0},{6,2},{1,5},{3,7},{5,1},{7,3},{8,12},{10,14},{12... | collective-permute-start | bytes 12296 | tf_op jit(solution)/shard_map/ppermute | solution.py:37
  9.8 5.1 %collective-permute-start.5 = (s32[8,128]{1,0:T(8,128)S(1)}, s32[8,128]{1,0:T(8,128)S(1)}, u32[]{:S(2)}, u32[]{:S(2)}) collective-permute-start(s32[8,128]{1,0:T(8,128)S(1)} %shard_map.70.refs_0_), channel_id=1, source_target_pairs={{0,2},{2,4},{4,6},{6,0},{1,3},{3,5},{5,7},{7,1},{8,10},{10,12},{12... | collective-permute-start | bytes 12296 | tf_op jit(solution)/shard_map/ppermute | solution.py:37
  33.2 15.9 %collective-permute-start.8 = (bf16[8,304,128]{2,1,0:T(8,128)(2,1)S(1)}, bf16[8,304,128]{2,1,0:T(8,128)(2,1)S(1)}, u32[]{:S(2)}, u32[]{:S(2)}) collective-permute-start(bf16[8,304,128]{2,1,0:T(8,128)(2,1)S(1)} %all_to_all.20.mine_ref), channel_id=1, source_target_pairs={{0,8},{8,0},{1,9},{9,1},{2,10},{10,2},{3,11},{11,3},{4,12},{12,4},... | collective-permute-start | bytes 1867784 | tf_op jit(solution)/shard_map/ppermute | solution.py:297
  33.2 4.9 %collective-permute-start = (bf16[40,1024]{1,0:T(8,128)(2,1)S(1)}, bf16[40,1024]{1,0:T(8,128)(2,1)S(1)}, u32[]{:S(2)}, u32[]{:S(2)}) collective-permute-start(bf16[40,1024]{1,0:T(8,128)(2,1)S(1)} %get-tuple-element.32.own_ref), channel_id=1, source_target_pairs={{0,1},{1,0},{2,3},{3,2},{4,5},{5,4},{6,7},{7,6},{8,9},{9,8},{10,11... | collective-permute-start | bytes 245768 | tf_op jit(solution)/shard_map/ppermute | solution.py:288
  38.0 36.4 %copy-start.2 = (f32[16,2048]{1,0:T(8,128)S(1)}, f32[16,2048]{1,0:T(8,128)}, u32[]{:S(2)}) copy-start(f32[16,2048]{1,0:T(8,128)} %accum_ref.3) | copy-start | bytes 393220
  38.0 6.8 %collective-permute-start.3 = (bf16[72,1024]{1,0:T(8,128)(2,1)S(1)}, bf16[72,1024]{1,0:T(8,128)(2,1)S(1)}, u32[]{:S(2)}, u32[]{:S(2)}) collective-permute-start(bf16[72,1024]{1,0:T(8,128)(2,1)S(1)} %shard_map.68.refs_0_), channel_id=1, source_target_pairs={{0,6},{2,0},{4,2},{6,4},{1,7},{3,1},{5,3},{7,5},{8,14},{10,8},{12,... | collective-permute-start | bytes 442376 | tf_op jit(solution)/shard_map/ppermute | solution.py:37
  39.0 8.2 %collective-permute-start.2 = (bf16[72,1024]{1,0:T(8,128)(2,1)S(1)}, bf16[72,1024]{1,0:T(8,128)(2,1)S(1)}, u32[]{:S(2)}, u32[]{:S(2)}) collective-permute-start(bf16[72,1024]{1,0:T(8,128)(2,1)S(1)} %shard_map.68.refs_0_), channel_id=1, source_target_pairs={{0,4},{2,6},{4,0},{6,2},{1,5},{3,7},{5,1},{7,3},{8,12},{10,14},{12... | collective-permute-start | bytes 442376 | tf_op jit(solution)/shard_map/ppermute | solution.py:37
  40.0 8.8 %collective-permute-start.1 = (bf16[72,1024]{1,0:T(8,128)(2,1)S(1)}, bf16[72,1024]{1,0:T(8,128)(2,1)S(1)}, u32[]{:S(2)}, u32[]{:S(2)}) collective-permute-start(bf16[72,1024]{1,0:T(8,128)(2,1)S(1)} %shard_map.68.refs_0_), channel_id=1, source_target_pairs={{0,2},{2,4},{4,6},{6,0},{1,3},{3,5},{5,7},{7,1},{8,10},{10,12},{12... | collective-permute-start | bytes 442376 | tf_op jit(solution)/shard_map/ppermute | solution.py:37
  41.4 7.7 %collective-permute-start.9 = (f32[8,128]{1,0:T(8,128)S(1)}, f32[8,128]{1,0:T(8,128)S(1)}, u32[]{:S(2)}, u32[]{:S(2)}) collective-permute-start(f32[8,128]{1,0:T(8,128)S(1)} %shard_map.72.total_ref), channel_id=1, source_target_pairs={{0,1},{1,0},{2,3},{3,2},{4,5},{5,4},{6,7},{7,6},{8,9},{9,8},{10,11... | collective-permute-start | bytes 12296 | tf_op jit(solution)/shard_map/ppermute | solution.py:299
  49.1 48.3 %copy-start = (f32[32,1024]{1,0:T(8,128)S(1)}, f32[32,1024]{1,0:T(8,128)}, u32[]{:S(2)}) copy-start(f32[32,1024]{1,0:T(8,128)} %emb_ref.4) | copy-start | bytes 393220
  49.1 48.3 %copy-start.3 = (f32[32,1024]{1,0:T(8,128)S(1)}, f32[32,1024]{1,0:T(8,128)}, u32[]{:S(2)}) copy-start(f32[32,1024]{1,0:T(8,128)} %accum_ref.2) | copy-start | bytes 393220
  58.0 2.0 %collective-permute-start.18 = (bf16[8,16,2048]{2,1,0:T(8,128)(2,1)S(1)}, bf16[8,16,2048]{2,1,0:T(8,128)(2,1)S(1)}, u32[]{:S(2)}, u32[]{:S(2)}) collective-permute-start(bf16[8,16,2048]{2,1,0:T(8,128)(2,1)S(1)} %get-tuple-element.48), channel_id=1, source_target_pairs={{0,8},{8,0},{1,9},{9,1},{2,10},{10,2},{3,11},{11,3},{4,12},{12,4},... | collective-permute-start | bytes 1572872 | tf_op jit(solution)/shard_map/ppermute | solution.py:303
  75.3 14.3 %all-to-all-start.2 = ((bf16[8,256,128]{2,1,0:T(8,128)(2,1)}), bf16[8,256,128]{2,1,0:T(8,128)(2,1)S(1)}, u32[]{:S(2)}, u32[]{:S(2)}) async-start(bf16[8,256,128]{2,1,0:T(8,128)(2,1)} %get-tuple-element.49), calls=%async_computation.2 | async-start | bytes 1048576 | tf_op jit(solution)/shard_map/all_to_all | solution.py:33
  78.8 11.7 %collective-permute-start.10 = (bf16[4,32,1024]{2,1,0:T(8,128)(2,1)S(1)}, bf16[4,32,1024]{2,1,0:T(8,128)(2,1)S(1)}, u32[]{:S(2)}, u32[]{:S(2)}) collective-permute-start(bf16[4,32,1024]{2,1,0:T(8,128)(2,1)S(1)} %get-tuple-element.39), channel_id=1, source_target_pairs={{0,1},{1,0},{2,3},{3,2},{4,5},{5,4},{6,7},{7,6},{8,9},{9,8},{10,11... | collective-permute-start | bytes 786440 | tf_op jit(solution)/shard_map/ppermute | solution.py:304
  89.6 23.4 %collective-permute-start.19 = (bf16[8,256,128]{2,1,0:T(8,128)(2,1)S(1)}, bf16[8,256,128]{2,1,0:T(8,128)(2,1)S(1)}, u32[]{:S(2)}, u32[]{:S(2)}) collective-permute-start(bf16[8,256,128]{2,1,0:T(8,128)(2,1)S(1)} %all-to-all-done.2.mine_ref), channel_id=1, source_target_pairs={{0,8},{8,0},{1,9},{9,1},{2,10},{10,2},{3,11},{11,3},{4,12},{12,4},... | collective-permute-start | bytes 1572872 | tf_op jit(solution)/shard_map/ppermute | solution.py:326
  90.6 5.9 %collective-permute-start.11 = (bf16[32,1024]{1,0:T(8,128)(2,1)S(1)}, bf16[32,1024]{1,0:T(8,128)(2,1)S(1)}, u32[]{:S(2)}, u32[]{:S(2)}) collective-permute-start(bf16[32,1024]{1,0:T(8,128)(2,1)S(1)} %get-tuple-element.41), channel_id=1, source_target_pairs={{0,4},{2,6},{4,0},{6,2},{1,5},{3,7},{5,1},{7,3},{8,12},{10,14},{12... | collective-permute-start | bytes 196616 | tf_op jit(solution)/shard_map/ppermute | solution.py:37
  91.9 5.5 %collective-permute-start.12 = (bf16[32,1024]{1,0:T(8,128)(2,1)S(1)}, bf16[32,1024]{1,0:T(8,128)(2,1)S(1)}, u32[]{:S(2)}, u32[]{:S(2)}) collective-permute-start(bf16[32,1024]{1,0:T(8,128)(2,1)S(1)} %get-tuple-element.42), channel_id=1, source_target_pairs={{0,2},{2,4},{4,6},{6,0},{1,3},{3,5},{5,7},{7,1},{8,10},{10,12},{12... | collective-permute-start | bytes 196616 | tf_op jit(solution)/shard_map/ppermute | solution.py:37
  92.1 5.3 %collective-permute-start.13 = (bf16[32,1024]{1,0:T(8,128)(2,1)S(1)}, bf16[32,1024]{1,0:T(8,128)(2,1)S(1)}, u32[]{:S(2)}, u32[]{:S(2)}) collective-permute-start(bf16[32,1024]{1,0:T(8,128)(2,1)S(1)} %get-tuple-element.43), channel_id=1, source_target_pairs={{0,6},{2,0},{4,2},{6,4},{1,7},{3,1},{5,3},{7,5},{8,14},{10,8},{12,... | collective-permute-start | bytes 196616 | tf_op jit(solution)/shard_map/ppermute | solution.py:37
  97.5 4.3 %collective-permute-start.14 = (bf16[32,1024]{1,0:T(8,128)(2,1)S(1)}, bf16[32,1024]{1,0:T(8,128)(2,1)S(1)}, u32[]{:S(2)}, u32[]{:S(2)}) collective-permute-start(bf16[32,1024]{1,0:T(8,128)(2,1)S(1)} %get-tuple-element.44.own_ref), channel_id=1, source_target_pairs={{0,1},{1,0},{2,3},{3,2},{4,5},{5,4},{6,7},{7,6},{8,9},{9,8},{10,11... | collective-permute-start | bytes 196616 | tf_op jit(solution)/shard_map/ppermute | solution.py:320
  101.9 7.2 %collective-permute-start.17 = (bf16[64,1024]{1,0:T(8,128)(2,1)S(1)}, bf16[64,1024]{1,0:T(8,128)(2,1)S(1)}, u32[]{:S(2)}, u32[]{:S(2)}) collective-permute-start(bf16[64,1024]{1,0:T(8,128)(2,1)S(1)} %shard_map.76.refs_0_), channel_id=1, source_target_pairs={{0,6},{2,0},{4,2},{6,4},{1,7},{3,1},{5,3},{7,5},{8,14},{10,8},{12,... | collective-permute-start | bytes 393224 | tf_op jit(solution)/shard_map/ppermute | solution.py:37
  105.1 6.6 %collective-permute-start.16 = (bf16[64,1024]{1,0:T(8,128)(2,1)S(1)}, bf16[64,1024]{1,0:T(8,128)(2,1)S(1)}, u32[]{:S(2)}, u32[]{:S(2)}) collective-permute-start(bf16[64,1024]{1,0:T(8,128)(2,1)S(1)} %shard_map.76.refs_0_), channel_id=1, source_target_pairs={{0,4},{2,6},{4,0},{6,2},{1,5},{3,7},{5,1},{7,3},{8,12},{10,14},{12... | collective-permute-start | bytes 393224 | tf_op jit(solution)/shard_map/ppermute | solution.py:37
  105.1 7.6 %collective-permute-start.15 = (bf16[64,1024]{1,0:T(8,128)(2,1)S(1)}, bf16[64,1024]{1,0:T(8,128)(2,1)S(1)}, u32[]{:S(2)}, u32[]{:S(2)}) collective-permute-start(bf16[64,1024]{1,0:T(8,128)(2,1)S(1)} %shard_map.76.refs_0_), channel_id=1, source_target_pairs={{0,2},{2,4},{4,6},{6,0},{1,3},{3,5},{5,7},{7,1},{8,10},{10,12},{12... | collective-permute-start | bytes 393224 | tf_op jit(solution)/shard_map/ppermute | solution.py:37
  122.0 2.0 %collective-permute-start.24 = (bf16[8,16,2048]{2,1,0:T(8,128)(2,1)S(1)}, bf16[8,16,2048]{2,1,0:T(8,128)(2,1)S(1)}, u32[]{:S(2)}, u32[]{:S(2)}) collective-permute-start(bf16[8,16,2048]{2,1,0:T(8,128)(2,1)S(1)} %get-tuple-element.59), channel_id=1, source_target_pairs={{0,8},{8,0},{1,9},{9,1},{2,10},{10,2},{3,11},{11,3},{4,12},{12,4},... | collective-permute-start | bytes 1572872 | tf_op jit(solution)/shard_map/ppermute | solution.py:303
  124.9 27.5 %all-to-all-start.3 = ((bf16[8,16,2048]{2,1,0:T(8,128)(2,1)}), bf16[8,16,2048]{2,1,0:T(8,128)(2,1)S(1)}, u32[]{:S(2)}, u32[]{:S(2)}) async-start(bf16[8,16,2048]{2,1,0:T(8,128)(2,1)} %shard_map.82), calls=%async_computation.3 | async-start | bytes 1048576 | tf_op jit(solution)/shard_map/all_to_all | solution.py:33
  132.3 12.4 %collective-permute-start.20 = (bf16[4,32,1024]{2,1,0:T(8,128)(2,1)S(1)}, bf16[4,32,1024]{2,1,0:T(8,128)(2,1)S(1)}, u32[]{:S(2)}, u32[]{:S(2)}) collective-permute-start(bf16[4,32,1024]{2,1,0:T(8,128)(2,1)S(1)} %get-tuple-element.51), channel_id=1, source_target_pairs={{0,1},{1,0},{2,3},{3,2},{4,5},{5,4},{6,7},{7,6},{8,9},{9,8},{10,11... | collective-permute-start | bytes 786440 | tf_op jit(solution)/shard_map/ppermute | solution.py:304
  144.8 6.1 %collective-permute-start.21 = (bf16[32,1024]{1,0:T(8,128)(2,1)S(1)}, bf16[32,1024]{1,0:T(8,128)(2,1)S(1)}, u32[]{:S(2)}, u32[]{:S(2)}) collective-permute-start(bf16[32,1024]{1,0:T(8,128)(2,1)S(1)} %get-tuple-element.53), channel_id=1, source_target_pairs={{0,4},{2,6},{4,0},{6,2},{1,5},{3,7},{5,1},{7,3},{8,12},{10,14},{12... | collective-permute-start | bytes 196616 | tf_op jit(solution)/shard_map/ppermute | solution.py:37
  145.8 5.8 %collective-permute-start.22 = (bf16[32,1024]{1,0:T(8,128)(2,1)S(1)}, bf16[32,1024]{1,0:T(8,128)(2,1)S(1)}, u32[]{:S(2)}, u32[]{:S(2)}) collective-permute-start(bf16[32,1024]{1,0:T(8,128)(2,1)S(1)} %get-tuple-element.54), channel_id=1, source_target_pairs={{0,2},{2,4},{4,6},{6,0},{1,3},{3,5},{5,7},{7,1},{8,10},{10,12},{12... | collective-permute-start | bytes 196616 | tf_op jit(solution)/shard_map/ppermute | solution.py:37
  146.6 5.0 %collective-permute-start.23 = (bf16[32,1024]{1,0:T(8,128)(2,1)S(1)}, bf16[32,1024]{1,0:T(8,128)(2,1)S(1)}, u32[]{:S(2)}, u32[]{:S(2)}) collective-permute-start(bf16[32,1024]{1,0:T(8,128)(2,1)S(1)} %get-tuple-element.55), channel_id=1, source_target_pairs={{0,6},{2,0},{4,2},{6,4},{1,7},{3,1},{5,3},{7,5},{8,14},{10,8},{12,... | collective-permute-start | bytes 196616 | tf_op jit(solution)/shard_map/ppermute | solution.py:37

commit v13 on v12

--- a/solution.py
+++ b/solution.py
@@ -291,7 +291,8 @@
     copies = small(second_kernel, shape((8, 304, 128), jnp.bfloat16))(col_emb, col_sums, *totals)
     pair = small(joined_first_kernel, shape((72, BR), jnp.bfloat16))(parcel, other)
     mine = to_each(copies, CHIPS)
-    row = [pair, over_z(pair, 1), over_z(pair, 2), over_z(pair, 3)]
+    far = over_z(pair, 2)
+    row = [pair, over_z(pair, 1), far, over_z(pair, 3)]
     outs = (shape((8, 32, BR), jnp.bfloat16), shape((BR, D), jnp.bfloat16), shape((1, BR), jnp.float32))
     *row, row_log = small(arranged_first_kernel, outs)(*row)
     theirs = lax.ppermute(mine, "c", SWAP)
@@ -320,7 +321,8 @@
             pair = lax.ppermute(half, "yl", SWAP)
             pair = small(joined_kernel, shape((64, BR), jnp.bfloat16))(half, pair)
             mine = to_each(copies, CHIPS)
-            row = [pair, over_z(pair, 1), over_z(pair, 2), over_z(pair, 3)]
+            far = over_z(pair, 2)
+            row = [pair, over_z(pair, 1), far, over_z(pair, 3)]
             outs = (shape((8, 32, BR), jnp.bfloat16), shape((BR, D), jnp.bfloat16))
             row = small(arranged_kernel, outs)(*row)
             theirs = lax.ppermute(mine, "c", SWAP)

time: 154 us -> 154 us (level)
  no operation moved by 1% of the time
where the time goes in v13:
time: 154 us; the launch traced here: 153 us
  waiting for transfers between devices  57.4 us (37%)
  starting transfers between devices  36.5 us (24%)
  blocking collectives  32.4 us (21%)
  Pallas kernels  26.1 us (17%)
    all_to_all x2, blocking collectives, to_each(): return lax.all_to_all(copies, axes, 0, 0, tiled=True)  32.4 us
    ppermute x15, waiting for transfers between devices, over_z(): return lax.ppermute(value, 'z', [(at, (at + shift) % 4) for at in range(4)])  21.9 us
    ppermute x15, starting transfers between devices, over_z(): return lax.ppermute(value, 'z', [(at, (at + shift) % 4) for at in range(4)])  21.6 us
    pallas_call x2, Pallas kernels, swept(): pl.pallas_call(sweep_kernel, out_shape=(shape((4, 32, BR), jnp.bfloat16),...  17.9 us
    ppermute x2, waiting for transfers between devices, on_device(): from_pair = lax.ppermute(away_pair, 'yl', SWAP)  13.2 us
    all_to_all x2, starting transfers between devices, to_each(): return lax.all_to_all(copies, axes, 0, 0, tiled=True)  10.9 us
    all_to_all x2, waiting for transfers between devices, to_each(): return lax.all_to_all(copies, axes, 0, 0, tiled=True)  10 us
    ppermute x1, waiting for transfers between devices, on_device(): other = lax.ppermute(parcel, 'yl', SWAP)  4.18 us
  transfers between devices with their start and end apart: 27, of which 20 were waited for; matrix products, arithmetic and copies ran while one was open for 0% of the time, Pallas kernels for 1%

profile of v13, /device:TPU:0, one launch (start us, length us, event | category | flops | bytes accessed | tf_op | source)
XLA Modules:
  0.0 153.2 jit_solution(18343533072208835653)
XLA Ops:
  0.6 3.8 %first.1 = (bf16[40,1024]{1,0:T(8,128)(2,1)S(1)}, s32[8,128]{1,0:T(8,128)S(1)}, s32[1,2048]{1,0:T(1,128)S(1)}) custom-call(s32[1024,2048]{1,0:T(8,128)} %counts_ref.5, f32[32,1024]{1,0:T(8,128)} %emb_ref.4), custom_call_target="tpu_custom_call" | custom-call | flops 8388608 | bytes 8388608 | tf_op jit(solution)/shard_map/first/pallas_call | solution.py:73
  4.5 1.2 collective-permute-done.4.other_ref
  5.7 4.1 %collective-permute-start.7 = (s32[8,128]{1,0:T(8,128)S(1)}, s32[8,128]{1,0:T(8,128)S(1)}, u32[]{:S(2)}, u32[]{:S(2)}) collective-permute-start(s32[8,128]{1,0:T(8,128)S(1)} %shard_map.70.refs_0_), channel_id=1, source_target_pairs={{0,6},{2,0},{4,2},{6,4},{1,7},{3,1},{5,3},{7,5},{8,14},{10,8},{12,... | collective-permute-start | bytes 12296 | tf_op jit(solution)/shard_map/ppermute | solution.py:37
  9.8 1.3 collective-permute-start.5
  11.2 3.8 %collective-permute-done.6.refs_2_ = s32[8,128]{1,0:T(8,128)S(1)} collective-permute-done((s32[8,128]{1,0:T(8,128)S(1)}, s32[8,128]{1,0:T(8,128)S(1)}, u32[]{:S(2)}, u32[]{:S(2)}) %collective-permute-start.6) | collective-permute-done | bytes 4128 | tf_op jit(solution)/shard_map/ppermute | solution.py:37
  15.0 18.2 %all_to_all.20.mine_ref = bf16[8,304,128]{2,1,0:T(8,128)(2,1)S(1)} all-to-all(bf16[8,304,128]{2,1,0:T(8,128)(2,1)S(1)} %shard_map.71), channel_id=1, replica_groups=mesh['x'=4,'yh'=2,'c'=2,'z'=4,'yl'=2] {'x','yh'}, dimensions={0} | all-to-all | bytes 1245184 | tf_op jit(solution)/shard_map/all_to_all | solution.py:33
  33.2 0.7 collective-permute-start
  33.8 4.2 %collective-permute-done.other_ref = bf16[40,1024]{1,0:T(8,128)(2,1)S(1)} collective-permute-done((bf16[40,1024]{1,0:T(8,128)(2,1)S(1)}, bf16[40,1024]{1,0:T(8,128)(2,1)S(1)}, u32[]{:S(2)}, u32[]{:S(2)}) %collective-permute-start) | collective-permute-done | bytes 81952 | tf_op jit(solution)/shard_map/ppermute | solution.py:288
  38.0 1.0 collective-permute-start.3
  39.0 0.9 collective-permute-start.2
  40.0 1.3 collective-permute-start.1
  41.4 0.9 collective-permute-start.9
  42.2 2.6 %collective-permute-done.3.refs_3_ = bf16[72,1024]{1,0:T(8,128)(2,1)S(1)} collective-permute-done((bf16[72,1024]{1,0:T(8,128)(2,1)S(1)}, bf16[72,1024]{1,0:T(8,128)(2,1)S(1)}, u32[]{:S(2)}, u32[]{:S(2)}) %collective-permute-start.3) | collective-permute-done | bytes 147488 | tf_op jit(solution)/shard_map/ppermute | solution.py:37
  44.8 2.4 %collective-permute-done.2.refs_2_ = bf16[72,1024]{1,0:T(8,128)(2,1)S(1)} collective-permute-done((bf16[72,1024]{1,0:T(8,128)(2,1)S(1)}, bf16[72,1024]{1,0:T(8,128)(2,1)S(1)}, u32[]{:S(2)}, u32[]{:S(2)}) %collective-permute-start.2) | collective-permute-done | bytes 147488 | tf_op jit(solution)/shard_map/ppermute | solution.py:37
  47.2 1.6 %collective-permute-done.1.refs_1_ = bf16[72,1024]{1,0:T(8,128)(2,1)S(1)} collective-permute-done((bf16[72,1024]{1,0:T(8,128)(2,1)S(1)}, bf16[72,1024]{1,0:T(8,128)(2,1)S(1)}, u32[]{:S(2)}, u32[]{:S(2)}) %collective-permute-start.1) | collective-permute-done | bytes 147488 | tf_op jit(solution)/shard_map/ppermute | solution.py:37
  48.8 0.2 shard_map.69
  49.1 8.9 %sweep.2 = (bf16[4,32,1024]{2,1,0:T(8,128)(2,1)S(1)}, bf16[4,32,1024]{2,1,0:T(8,128)(2,1)S(1)}, bf16[8,16,2048]{2,1,0:T(8,128)(2,1)S(1)}, bf16[8,16,2048]{2,1,0:T(8,128)(2,1)S(1)}) custom-call(bf16[8,32,1024]{2,1,0:T(8,128)(2,1)S(1)} %get-tuple-element.33.row_flat, bf16[1024,256]{1,0:T(8,128)(2,1)S(1)} %get-tuple-element.34.row_tall, ...), custom_call_target="tpu_custom_call" | custom-call | flops 3221225472 | bytes 20971520 | tf_op jit(solution)/shard_map/sweep/pallas_call | solution.py:211
  58.1 1.9 %collective-permute-done.18.theirs_ref = bf16[8,16,2048]{2,1,0:T(8,128)(2,1)S(1)} collective-permute-done((bf16[8,16,2048]{2,1,0:T(8,128)(2,1)S(1)}, bf16[8,16,2048]{2,1,0:T(8,128)(2,1)S(1)}, u32[]{:S(2)}, u32[]{:S(2)}) %collective-permute-start.18) | collective-permute-done | bytes 524320 | tf_op jit(solution)/shard_map/ppermute | solution.py:304
  60.2 14.2 %all_to_all.21.came_ref = bf16[8,16,2048]{2,1,0:T(8,128)(2,1)S(1)} all-to-all(bf16[8,16,2048]{2,1,0:T(8,128)(2,1)S(1)} %shard_map.78), channel_id=1, replica_groups=mesh['x'=4,'yh'=2,'c'=2,'z'=4,'yl'=2] {'x','yh'}, dimensions={0} | all-to-all | bytes 1048576 | tf_op jit(solution)/shard_map/all_to_all | solution.py:33
  74.4 0.9 shard_map.79
  75.3 3.5 %all-to-all-start.2 = ((bf16[8,256,128]{2,1,0:T(8,128)(2,1)}), bf16[8,256,128]{2,1,0:T(8,128)(2,1)S(1)}, u32[]{:S(2)}, u32[]{:S(2)}) async-start(bf16[8,256,128]{2,1,0:T(8,128)(2,1)} %get-tuple-element.49), calls=%async_computation.2 | async-start | bytes 1048576 | tf_op jit(solution)/shard_map/all_to_all | solution.py:33
  78.8 0.8 collective-permute-start.10
  79.6 10.0 %all-to-all-done.2.mine_ref = bf16[8,256,128]{2,1,0:T(8,128)(2,1)S(1)} async-done(((bf16[8,256,128]{2,1,0:T(8,128)(2,1)}), bf16[8,256,128]{2,1,0:T(8,128)(2,1)S(1)}, u32[]{:S(2)}, u32[]{:S(2)}) %all-to-all-start.2) | async-done | bytes 524320 | tf_op jit(solution)/shard_map/all_to_all | solution.py:33
  89.6 0.9 collective-permute-done.10.came_ref
  90.6 1.3 collective-permute-start.11
  92.1 3.0 %collective-permute-start.13 = (bf16[32,1024]{1,0:T(8,128)(2,1)S(1)}, bf16[32,1024]{1,0:T(8,128)(2,1)S(1)}, u32[]{:S(2)}, u32[]{:S(2)}) collective-permute-start(bf16[32,1024]{1,0:T(8,128)(2,1)S(1)} %get-tuple-element.43), channel_id=1, source_target_pairs={{0,6},{2,0},{4,2},{6,4},{1,7},{3,1},{5,3},{7,5},{8,14},{10,8},{12,... | collective-permute-start | bytes 196616 | tf_op jit(solution)/shard_map/ppermute | solution.py:37
  95.1 1.3 collective-permute-done.11.first_ref
  96.5 0.9 collective-permute-done.12.second_ref
  97.5 1.3 collective-permute-start.14
  98.8 3.1 %collective-permute-done.14.other_ref = bf16[32,1024]{1,0:T(8,128)(2,1)S(1)} collective-permute-done((bf16[32,1024]{1,0:T(8,128)(2,1)S(1)}, bf16[32,1024]{1,0:T(8,128)(2,1)S(1)}, u32[]{:S(2)}, u32[]{:S(2)}) %collective-permute-start.14) | collective-permute-done | bytes 65568 | tf_op jit(solution)/shard_map/ppermute | solution.py:321
  101.9 3.3 %collective-permute-start.17 = (bf16[64,1024]{1,0:T(8,128)(2,1)S(1)}, bf16[64,1024]{1,0:T(8,128)(2,1)S(1)}, u32[]{:S(2)}, u32[]{:S(2)}) collective-permute-start(bf16[64,1024]{1,0:T(8,128)(2,1)S(1)} %shard_map.76.refs_0_), channel_id=1, source_target_pairs={{0,6},{2,0},{4,2},{6,4},{1,7},{3,1},{5,3},{7,5},{8,14},{10,8},{12,... | collective-permute-start | bytes 393224 | tf_op jit(solution)/shard_map/ppermute | solution.py:37
  105.1 0.9 collective-permute-start.15
  106.1 3.0 %collective-permute-done.17.refs_3_ = bf16[64,1024]{1,0:T(8,128)(2,1)S(1)} collective-permute-done((bf16[64,1024]{1,0:T(8,128)(2,1)S(1)}, bf16[64,1024]{1,0:T(8,128)(2,1)S(1)}, u32[]{:S(2)}, u32[]{:S(2)}) %collective-permute-start.17) | collective-permute-done | bytes 131104 | tf_op jit(solution)/shard_map/ppermute | solution.py:37
  109.1 2.6 %collective-permute-done.16.refs_2_ = bf16[64,1024]{1,0:T(8,128)(2,1)S(1)} collective-permute-done((bf16[64,1024]{1,0:T(8,128)(2,1)S(1)}, bf16[64,1024]{1,0:T(8,128)(2,1)S(1)}, u32[]{:S(2)}, u32[]{:S(2)}) %collective-permute-start.16) | collective-permute-done | bytes 131104 | tf_op jit(solution)/shard_map/ppermute | solution.py:37
  111.7 1.0 collective-permute-done.15.refs_1_
  112.7 0.2 shard_map.77
  113.0 9.0 %sweep.3 = (bf16[4,32,1024]{2,1,0:T(8,128)(2,1)S(1)}, bf16[4,32,1024]{2,1,0:T(8,128)(2,1)S(1)}, bf16[8,16,2048]{2,1,0:T(8,128)(2,1)S(1)}, bf16[8,16,2048]{2,1,0:T(8,128)(2,1)S(1)}) custom-call(bf16[8,32,1024]{2,1,0:T(8,128)(2,1)S(1)} %get-tuple-element.45.row_flat, bf16[1024,256]{1,0:T(8,128)(2,1)S(1)} %get-tuple-element.46.row_tall, ...), custom_call_target="tpu_custom_call" | custom-call | flops 3221225472 | bytes 20971520 | tf_op jit(solution)/shard_map/sweep/pallas_call | solution.py:211
  122.1 1.9 %collective-permute-done.24.theirs_ref = bf16[8,16,2048]{2,1,0:T(8,128)(2,1)S(1)} collective-permute-done((bf16[8,16,2048]{2,1,0:T(8,128)(2,1)S(1)}, bf16[8,16,2048]{2,1,0:T(8,128)(2,1)S(1)}, u32[]{:S(2)}, u32[]{:S(2)}) %collective-permute-start.24) | collective-permute-done | bytes 524320 | tf_op jit(solution)/shard_map/ppermute | solution.py:304
  124.0 0.9 shard_map.82
  124.9 7.4 %all-to-all-start.3 = ((bf16[8,16,2048]{2,1,0:T(8,128)(2,1)}), bf16[8,16,2048]{2,1,0:T(8,128)(2,1)S(1)}, u32[]{:S(2)}, u32[]{:S(2)}) async-start(bf16[8,16,2048]{2,1,0:T(8,128)(2,1)} %shard_map.82), calls=%async_computation.3 | async-start | bytes 1048576 | tf_op jit(solution)/shard_map/all_to_all | solution.py:33
  132.4 12.3 %collective-permute-done.20.came_ref = bf16[4,32,1024]{2,1,0:T(8,128)(2,1)S(1)} collective-permute-done((bf16[4,32,1024]{2,1,0:T(8,128)(2,1)S(1)}, bf16[4,32,1024]{2,1,0:T(8,128)(2,1)S(1)}, u32[]{:S(2)}, u32[]{:S(2)}) %collective-permute-start.20) | collective-permute-done | bytes 262176 | tf_op jit(solution)/shard_map/ppermute | solution.py:305
  144.8 1.0 collective-permute-start.21
  145.8 0.8 collective-permute-start.22
  146.6 2.4 %collective-permute-start.23 = (bf16[32,1024]{1,0:T(8,128)(2,1)S(1)}, bf16[32,1024]{1,0:T(8,128)(2,1)S(1)}, u32[]{:S(2)}, u32[]{:S(2)}) collective-permute-start(bf16[32,1024]{1,0:T(8,128)(2,1)S(1)} %get-tuple-element.55), channel_id=1, source_target_pairs={{0,6},{2,0},{4,2},{6,4},{1,7},{3,1},{5,3},{7,5},{8,14},{10,8},{12,... | collective-permute-start | bytes 196616 | tf_op jit(solution)/shard_map/ppermute | solution.py:37
  149.0 1.9 %collective-permute-done.21.first_ref = bf16[32,1024]{1,0:T(8,128)(2,1)S(1)} collective-permute-done((bf16[32,1024]{1,0:T(8,128)(2,1)S(1)}, bf16[32,1024]{1,0:T(8,128)(2,1)S(1)}, u32[]{:S(2)}, u32[]{:S(2)}) %collective-permute-start.21) | collective-permute-done | bytes 65568 | tf_op jit(solution)/shard_map/ppermute | solution.py:37
  150.9 0.7 collective-permute-done.22.second_ref
  151.6 0.7 shard_map.81
  152.4 0.8 shard_map.83
  (35 shorter events, 1.3 us)
Async XLA Ops:
  0.6 14.3 %copy-start.1 = (f32[16,2048]{1,0:T(8,128)S(1)}, f32[16,2048]{1,0:T(8,128)}, u32[]{:S(2)}) copy-start(f32[16,2048]{1,0:T(8,128)} %emb_ref.5) | copy-start | bytes 393220
  4.4 1.2 collective-permute-start.4
  5.7 5.5 %collective-permute-start.7 = (s32[8,128]{1,0:T(8,128)S(1)}, s32[8,128]{1,0:T(8,128)S(1)}, u32[]{:S(2)}, u32[]{:S(2)}) collective-permute-start(s32[8,128]{1,0:T(8,128)S(1)} %shard_map.70.refs_0_), channel_id=1, source_target_pairs={{0,6},{2,0},{4,2},{6,4},{1,7},{3,1},{5,3},{7,5},{8,14},{10,8},{12,... | collective-permute-start | bytes 12296 | tf_op jit(solution)/shard_map/ppermute | solution.py:37
  9.8 5.1 %collective-permute-start.6 = (s32[8,128]{1,0:T(8,128)S(1)}, s32[8,128]{1,0:T(8,128)S(1)}, u32[]{:S(2)}, u32[]{:S(2)}) collective-permute-start(s32[8,128]{1,0:T(8,128)S(1)} %shard_map.70.refs_0_), channel_id=1, source_target_pairs={{0,4},{2,6},{4,0},{6,2},{1,5},{3,7},{5,1},{7,3},{8,12},{10,14},{12... | collective-permute-start | bytes 12296 | tf_op jit(solution)/shard_map/ppermute | solution.py:37
  9.8 5.1 %collective-permute-start.5 = (s32[8,128]{1,0:T(8,128)S(1)}, s32[8,128]{1,0:T(8,128)S(1)}, u32[]{:S(2)}, u32[]{:S(2)}) collective-permute-start(s32[8,128]{1,0:T(8,128)S(1)} %shard_map.70.refs_0_), channel_id=1, source_target_pairs={{0,2},{2,4},{4,6},{6,0},{1,3},{3,5},{5,7},{7,1},{8,10},{10,12},{12... | collective-permute-start | bytes 12296 | tf_op jit(solution)/shard_map/ppermute | solution.py:37
  33.2 15.9 %collective-permute-start.8 = (bf16[8,304,128]{2,1,0:T(8,128)(2,1)S(1)}, bf16[8,304,128]{2,1,0:T(8,128)(2,1)S(1)}, u32[]{:S(2)}, u32[]{:S(2)}) collective-permute-start(bf16[8,304,128]{2,1,0:T(8,128)(2,1)S(1)} %all_to_all.20.mine_ref), channel_id=1, source_target_pairs={{0,8},{8,0},{1,9},{9,1},{2,10},{10,2},{3,11},{11,3},{4,12},{12,4},... | collective-permute-start | bytes 1867784 | tf_op jit(solution)/shard_map/ppermute | solution.py:298
  33.2 4.9 %collective-permute-start = (bf16[40,1024]{1,0:T(8,128)(2,1)S(1)}, bf16[40,1024]{1,0:T(8,128)(2,1)S(1)}, u32[]{:S(2)}, u32[]{:S(2)}) collective-permute-start(bf16[40,1024]{1,0:T(8,128)(2,1)S(1)} %get-tuple-element.32.own_ref), channel_id=1, source_target_pairs={{0,1},{1,0},{2,3},{3,2},{4,5},{5,4},{6,7},{7,6},{8,9},{9,8},{10,11... | collective-permute-start | bytes 245768 | tf_op jit(solution)/shard_map/ppermute | solution.py:288
  38.0 36.4 %copy-start.2 = (f32[16,2048]{1,0:T(8,128)S(1)}, f32[16,2048]{1,0:T(8,128)}, u32[]{:S(2)}) copy-start(f32[16,2048]{1,0:T(8,128)} %accum_ref.3) | copy-start | bytes 393220
  38.0 6.8 %collective-permute-start.3 = (bf16[72,1024]{1,0:T(8,128)(2,1)S(1)}, bf16[72,1024]{1,0:T(8,128)(2,1)S(1)}, u32[]{:S(2)}, u32[]{:S(2)}) collective-permute-start(bf16[72,1024]{1,0:T(8,128)(2,1)S(1)} %shard_map.68.refs_0_), channel_id=1, source_target_pairs={{0,6},{2,0},{4,2},{6,4},{1,7},{3,1},{5,3},{7,5},{8,14},{10,8},{12,... | collective-permute-start | bytes 442376 | tf_op jit(solution)/shard_map/ppermute | solution.py:37
  39.0 8.2 %collective-permute-start.2 = (bf16[72,1024]{1,0:T(8,128)(2,1)S(1)}, bf16[72,1024]{1,0:T(8,128)(2,1)S(1)}, u32[]{:S(2)}, u32[]{:S(2)}) collective-permute-start(bf16[72,1024]{1,0:T(8,128)(2,1)S(1)} %shard_map.68.refs_0_), channel_id=1, source_target_pairs={{0,4},{2,6},{4,0},{6,2},{1,5},{3,7},{5,1},{7,3},{8,12},{10,14},{12... | collective-permute-start | bytes 442376 | tf_op jit(solution)/shard_map/ppermute | solution.py:37
  40.0 8.8 %collective-permute-start.1 = (bf16[72,1024]{1,0:T(8,128)(2,1)S(1)}, bf16[72,1024]{1,0:T(8,128)(2,1)S(1)}, u32[]{:S(2)}, u32[]{:S(2)}) collective-permute-start(bf16[72,1024]{1,0:T(8,128)(2,1)S(1)} %shard_map.68.refs_0_), channel_id=1, source_target_pairs={{0,2},{2,4},{4,6},{6,0},{1,3},{3,5},{5,7},{7,1},{8,10},{10,12},{12... | collective-permute-start | bytes 442376 | tf_op jit(solution)/shard_map/ppermute | solution.py:37
  41.4 7.7 %collective-permute-start.9 = (f32[8,128]{1,0:T(8,128)S(1)}, f32[8,128]{1,0:T(8,128)S(1)}, u32[]{:S(2)}, u32[]{:S(2)}) collective-permute-start(f32[8,128]{1,0:T(8,128)S(1)} %shard_map.72.total_ref), channel_id=1, source_target_pairs={{0,1},{1,0},{2,3},{3,2},{4,5},{5,4},{6,7},{7,6},{8,9},{9,8},{10,11... | collective-permute-start | bytes 12296 | tf_op jit(solution)/shard_map/ppermute | solution.py:300
  49.1 48.3 %copy-start = (f32[32,1024]{1,0:T(8,128)S(1)}, f32[32,1024]{1,0:T(8,128)}, u32[]{:S(2)}) copy-start(f32[32,1024]{1,0:T(8,128)} %emb_ref.4) | copy-start | bytes 393220
  49.1 48.3 %copy-start.3 = (f32[32,1024]{1,0:T(8,128)S(1)}, f32[32,1024]{1,0:T(8,128)}, u32[]{:S(2)}) copy-start(f32[32,1024]{1,0:T(8,128)} %accum_ref.2) | copy-start | bytes 393220
  58.0 2.0 %collective-permute-start.18 = (bf16[8,16,2048]{2,1,0:T(8,128)(2,1)S(1)}, bf16[8,16,2048]{2,1,0:T(8,128)(2,1)S(1)}, u32[]{:S(2)}, u32[]{:S(2)}) collective-permute-start(bf16[8,16,2048]{2,1,0:T(8,128)(2,1)S(1)} %get-tuple-element.48), channel_id=1, source_target_pairs={{0,8},{8,0},{1,9},{9,1},{2,10},{10,2},{3,11},{11,3},{4,12},{12,4},... | collective-permute-start | bytes 1572872 | tf_op jit(solution)/shard_map/ppermute | solution.py:304
  75.3 14.3 %all-to-all-start.2 = ((bf16[8,256,128]{2,1,0:T(8,128)(2,1)}), bf16[8,256,128]{2,1,0:T(8,128)(2,1)S(1)}, u32[]{:S(2)}, u32[]{:S(2)}) async-start(bf16[8,256,128]{2,1,0:T(8,128)(2,1)} %get-tuple-element.49), calls=%async_computation.2 | async-start | bytes 1048576 | tf_op jit(solution)/shard_map/all_to_all | solution.py:33
  78.8 11.7 %collective-permute-start.10 = (bf16[4,32,1024]{2,1,0:T(8,128)(2,1)S(1)}, bf16[4,32,1024]{2,1,0:T(8,128)(2,1)S(1)}, u32[]{:S(2)}, u32[]{:S(2)}) collective-permute-start(bf16[4,32,1024]{2,1,0:T(8,128)(2,1)S(1)} %get-tuple-element.39), channel_id=1, source_target_pairs={{0,1},{1,0},{2,3},{3,2},{4,5},{5,4},{6,7},{7,6},{8,9},{9,8},{10,11... | collective-permute-start | bytes 786440 | tf_op jit(solution)/shard_map/ppermute | solution.py:305
  89.6 23.4 %collective-permute-start.19 = (bf16[8,256,128]{2,1,0:T(8,128)(2,1)S(1)}, bf16[8,256,128]{2,1,0:T(8,128)(2,1)S(1)}, u32[]{:S(2)}, u32[]{:S(2)}) collective-permute-start(bf16[8,256,128]{2,1,0:T(8,128)(2,1)S(1)} %all-to-all-done.2.mine_ref), channel_id=1, source_target_pairs={{0,8},{8,0},{1,9},{9,1},{2,10},{10,2},{3,11},{11,3},{4,12},{12,4},... | collective-permute-start | bytes 1572872 | tf_op jit(solution)/shard_map/ppermute | solution.py:328
  90.6 5.9 %collective-permute-start.11 = (bf16[32,1024]{1,0:T(8,128)(2,1)S(1)}, bf16[32,1024]{1,0:T(8,128)(2,1)S(1)}, u32[]{:S(2)}, u32[]{:S(2)}) collective-permute-start(bf16[32,1024]{1,0:T(8,128)(2,1)S(1)} %get-tuple-element.41), channel_id=1, source_target_pairs={{0,4},{2,6},{4,0},{6,2},{1,5},{3,7},{5,1},{7,3},{8,12},{10,14},{12... | collective-permute-start | bytes 196616 | tf_op jit(solution)/shard_map/ppermute | solution.py:37
  91.9 5.5 %collective-permute-start.12 = (bf16[32,1024]{1,0:T(8,128)(2,1)S(1)}, bf16[32,1024]{1,0:T(8,128)(2,1)S(1)}, u32[]{:S(2)}, u32[]{:S(2)}) collective-permute-start(bf16[32,1024]{1,0:T(8,128)(2,1)S(1)} %get-tuple-element.42), channel_id=1, source_target_pairs={{0,2},{2,4},{4,6},{6,0},{1,3},{3,5},{5,7},{7,1},{8,10},{10,12},{12... | collective-permute-start | bytes 196616 | tf_op jit(solution)/shard_map/ppermute | solution.py:37
  92.1 5.3 %collective-permute-start.13 = (bf16[32,1024]{1,0:T(8,128)(2,1)S(1)}, bf16[32,1024]{1,0:T(8,128)(2,1)S(1)}, u32[]{:S(2)}, u32[]{:S(2)}) collective-permute-start(bf16[32,1024]{1,0:T(8,128)(2,1)S(1)} %get-tuple-element.43), channel_id=1, source_target_pairs={{0,6},{2,0},{4,2},{6,4},{1,7},{3,1},{5,3},{7,5},{8,14},{10,8},{12,... | collective-permute-start | bytes 196616 | tf_op jit(solution)/shard_map/ppermute | solution.py:37
  97.5 4.3 %collective-permute-start.14 = (bf16[32,1024]{1,0:T(8,128)(2,1)S(1)}, bf16[32,1024]{1,0:T(8,128)(2,1)S(1)}, u32[]{:S(2)}, u32[]{:S(2)}) collective-permute-start(bf16[32,1024]{1,0:T(8,128)(2,1)S(1)} %get-tuple-element.44.own_ref), channel_id=1, source_target_pairs={{0,1},{1,0},{2,3},{3,2},{4,5},{5,4},{6,7},{7,6},{8,9},{9,8},{10,11... | collective-permute-start | bytes 196616 | tf_op jit(solution)/shard_map/ppermute | solution.py:321
  101.9 7.2 %collective-permute-start.17 = (bf16[64,1024]{1,0:T(8,128)(2,1)S(1)}, bf16[64,1024]{1,0:T(8,128)(2,1)S(1)}, u32[]{:S(2)}, u32[]{:S(2)}) collective-permute-start(bf16[64,1024]{1,0:T(8,128)(2,1)S(1)} %shard_map.76.refs_0_), channel_id=1, source_target_pairs={{0,6},{2,0},{4,2},{6,4},{1,7},{3,1},{5,3},{7,5},{8,14},{10,8},{12,... | collective-permute-start | bytes 393224 | tf_op jit(solution)/shard_map/ppermute | solution.py:37
  105.1 6.6 %collective-permute-start.16 = (bf16[64,1024]{1,0:T(8,128)(2,1)S(1)}, bf16[64,1024]{1,0:T(8,128)(2,1)S(1)}, u32[]{:S(2)}, u32[]{:S(2)}) collective-permute-start(bf16[64,1024]{1,0:T(8,128)(2,1)S(1)} %shard_map.76.refs_0_), channel_id=1, source_target_pairs={{0,4},{2,6},{4,0},{6,2},{1,5},{3,7},{5,1},{7,3},{8,12},{10,14},{12... | collective-permute-start | bytes 393224 | tf_op jit(solution)/shard_map/ppermute | solution.py:37
  105.1 7.6 %collective-permute-start.15 = (bf16[64,1024]{1,0:T(8,128)(2,1)S(1)}, bf16[64,1024]{1,0:T(8,128)(2,1)S(1)}, u32[]{:S(2)}, u32[]{:S(2)}) collective-permute-start(bf16[64,1024]{1,0:T(8,128)(2,1)S(1)} %shard_map.76.refs_0_), channel_id=1, source_target_pairs={{0,2},{2,4},{4,6},{6,0},{1,3},{3,5},{5,7},{7,1},{8,10},{10,12},{12... | collective-permute-start | bytes 393224 | tf_op jit(solution)/shard_map/ppermute | solution.py:37
  122.0 2.0 %collective-permute-start.24 = (bf16[8,16,2048]{2,1,0:T(8,128)(2,1)S(1)}, bf16[8,16,2048]{2,1,0:T(8,128)(2,1)S(1)}, u32[]{:S(2)}, u32[]{:S(2)}) collective-permute-start(bf16[8,16,2048]{2,1,0:T(8,128)(2,1)S(1)} %get-tuple-element.59), channel_id=1, source_target_pairs={{0,8},{8,0},{1,9},{9,1},{2,10},{10,2},{3,11},{11,3},{4,12},{12,4},... | collective-permute-start | bytes 1572872 | tf_op jit(solution)/shard_map/ppermute | solution.py:304
  124.9 27.5 %all-to-all-start.3 = ((bf16[8,16,2048]{2,1,0:T(8,128)(2,1)}), bf16[8,16,2048]{2,1,0:T(8,128)(2,1)S(1)}, u32[]{:S(2)}, u32[]{:S(2)}) async-start(bf16[8,16,2048]{2,1,0:T(8,128)(2,1)} %shard_map.82), calls=%async_computation.3 | async-start | bytes 1048576 | tf_op jit(solution)/shard_map/all_to_all | solution.py:33
  132.3 12.4 %collective-permute-start.20 = (bf16[4,32,1024]{2,1,0:T(8,128)(2,1)S(1)}, bf16[4,32,1024]{2,1,0:T(8,128)(2,1)S(1)}, u32[]{:S(2)}, u32[]{:S(2)}) collective-permute-start(bf16[4,32,1024]{2,1,0:T(8,128)(2,1)S(1)} %get-tuple-element.51), channel_id=1, source_target_pairs={{0,1},{1,0},{2,3},{3,2},{4,5},{5,4},{6,7},{7,6},{8,9},{9,8},{10,11... | collective-permute-start | bytes 786440 | tf_op jit(solution)/shard_map/ppermute | solution.py:305
  144.8 6.1 %collective-permute-start.21 = (bf16[32,1024]{1,0:T(8,128)(2,1)S(1)}, bf16[32,1024]{1,0:T(8,128)(2,1)S(1)}, u32[]{:S(2)}, u32[]{:S(2)}) collective-permute-start(bf16[32,1024]{1,0:T(8,128)(2,1)S(1)} %get-tuple-element.53), channel_id=1, source_target_pairs={{0,4},{2,6},{4,0},{6,2},{1,5},{3,7},{5,1},{7,3},{8,12},{10,14},{12... | collective-permute-start | bytes 196616 | tf_op jit(solution)/shard_map/ppermute | solution.py:37
  145.8 5.8 %collective-permute-start.22 = (bf16[32,1024]{1,0:T(8,128)(2,1)S(1)}, bf16[32,1024]{1,0:T(8,128)(2,1)S(1)}, u32[]{:S(2)}, u32[]{:S(2)}) collective-permute-start(bf16[32,1024]{1,0:T(8,128)(2,1)S(1)} %get-tuple-element.54), channel_id=1, source_target_pairs={{0,2},{2,4},{4,6},{6,0},{1,3},{3,5},{5,7},{7,1},{8,10},{10,12},{12... | collective-permute-start | bytes 196616 | tf_op jit(solution)/shard_map/ppermute | solution.py:37
  146.6 5.0 %collective-permute-start.23 = (bf16[32,1024]{1,0:T(8,128)(2,1)S(1)}, bf16[32,1024]{1,0:T(8,128)(2,1)S(1)}, u32[]{:S(2)}, u32[]{:S(2)}) collective-permute-start(bf16[32,1024]{1,0:T(8,128)(2,1)S(1)} %get-tuple-element.55), channel_id=1, source_target_pairs={{0,6},{2,0},{4,2},{6,4},{1,7},{3,1},{5,3},{7,5},{8,14},{10,8},{12,... | collective-permute-start | bytes 196616 | tf_op jit(solution)/shard_map/ppermute | solution.py:37
